TPU v7x, 32 devices: a whole 2x2x4 slice. The times are simulated.
32 devices in a mesh: dp: 4 (over x, core), fsdp: 8 (over z, y).
Axes of the slice: x: 2, y: 2, z: 4, core: 2. Of those that a mesh axis runs over, the one named last changes fastest.
Arguments:
- regions: bfloat16 [768, 512], P(('dp', 'fsdp')), may hold values from -6 to 6
- patches: bfloat16 [768, 49, 512], P(('dp', 'fsdp')), may hold values from -6 to 6
- cot_regions: bfloat16 [768, 512], P(('dp', 'fsdp')), may hold values from -6 to 6
- cot_patches: bfloat16 [768, 49, 512], P(('dp', 'fsdp')), may hold values from -6 to 6
- image_shape: int32 [192, 2], P(('dp', 'fsdp')), may hold values from 0 to 4, as said below
- owner: int32 [192], replicated, may hold values from 0 to 191, as said below
- slot_weights: float32 [192, 128, 128], P(('dp', 'fsdp')), may hold values from -2 to 2
- small: float32 [6144], P(('dp', 'fsdp')), may hold values from -2 to 2
- stats: float32 [192, 2, 128, 128], P(('dp', 'fsdp')), may hold values from -38400 to 652800, as said below
- roots: float32 [192, 2, 128, 128], P(('dp', 'fsdp')), may hold values from -1 to 3, as said below
- ema_slots: float32 [192, 128, 128], P(('dp', 'fsdp')), may hold values from -4 to 4
- ema_small: float32 [6144], P(('dp', 'fsdp')), may hold values from -2 to 2
Outputs:
- out_regions: bfloat16 [768, 512], P(('dp', 'fsdp'))
- out_patches: bfloat16 [768, 49, 512], P(('dp', 'fsdp'))
- grad_regions: bfloat16 [768, 512], P(('dp', 'fsdp'))
- grad_patches: bfloat16 [768, 49, 512], P(('dp', 'fsdp'))
- grad_slots: float32 [192, 128, 128], P(('dp', 'fsdp'))
- grad_small: float32 [6144], P(('dp', 'fsdp'))
- new_stats: float32 [192, 2, 128, 128], P(('dp', 'fsdp'))
- new_slots: float32 [192, 128, 128], P(('dp', 'fsdp'))
- new_small: float32 [6144], P(('dp', 'fsdp'))
- new_ema_slots: float32 [192, 128, 128], P(('dp', 'fsdp'))
- new_ema_small: float32 [6144], P(('dp', 'fsdp'))
Inputs may be any that keep to these rules, and one draw needn't show every extreme that they name: `image_shape`: each group's 6 rows hold (height, width) of 2 to 4 for its images and (0, 0) for empty image slots, the empty ones after all used ones; a group's images take its region slots in order from the first; their regions number at most 24 in each group and exactly 24 in at least one. `owner`: each slot number appears once. `stats`: each slot's two matrices are symmetric. `roots`: each slot's two matrices are symmetric.
All inputs are finite; a program needn't handle non-finite values.
Results may differ from a plain program's by a relative error of at most 0.018.
Values may be sent and summed in bfloat16 or wider, within the bound.
No kernel may reach another device: no remote copies, remote signals or barrier semaphores. Data moves between devices by JAX's collectives and lax.ppermute only.
A program may use at most 128 MiB of HBM per device.

v0:
```python
import math

import jax
import jax.numpy as jnp
from jax import lax
from jax.sharding import PartitionSpec as P

D = 512
HEAD = 32
FF = 2048
SHAMPOO_SIDE = 128
NBLOCKS = 192


EPS_NORM = 1e-05
EPS_MEAN = 1e-06
SHAMPOO_RATE = 0.5
SMALL_RATE = 0.3
EMA_DECAY = 0.8
STAT_DECAY = 0.5


def norm_forward(values, gain_row, offset):
    center = values - jnp.mean(values, axis=-1, keepdims=True)
    inverse = lax.rsqrt(jnp.mean(center * center, axis=-1, keepdims=True) + EPS_NORM)
    normed = center * inverse
    return (normed * gain_row + offset, normed, inverse)


def norm_back(grad_out, normed, inverse, gain_row):
    scaled = grad_out * gain_row
    grad_in = inverse * (
        scaled
        - jnp.mean(scaled, axis=-1, keepdims=True)
        - normed * jnp.mean(scaled * normed, axis=-1, keepdims=True)
    )
    lead_axes = tuple(range(grad_out.ndim - 1))
    return (grad_in, jnp.sum(grad_out * normed, axis=lead_axes), jnp.sum(grad_out, axis=lead_axes))


def gelu_slope(values):
    return (
        0.5 * (1.0 + lax.erf(values * 0.7071067811865476))
        + values * jnp.exp(-0.5 * values * values) * 0.3989422804014327
    )


def region_labels(shape_rows, region_slots):
    region_counts = shape_rows[:, 0] * shape_rows[:, 1]
    region_ends = jnp.cumsum(region_counts)
    places = jnp.arange(region_slots, dtype=jnp.int32)
    labels = jnp.sum((places[:, None] >= region_ends[None, :]).astype(jnp.int32), axis=1)
    return (places < region_ends[-1], labels)


def assemble(blocks):
    model_blocks = D // SHAMPOO_SIDE
    hidden_blocks = FF // SHAMPOO_SIDE
    end_qkv = model_blocks * 3 * model_blocks
    end_out = end_qkv + model_blocks * model_blocks
    end_up = end_out + model_blocks * hidden_blocks

    def block_grid(pieces, row_blocks, col_blocks):
        return (
            pieces.reshape(row_blocks, col_blocks, SHAMPOO_SIDE, SHAMPOO_SIDE)
            .transpose(0, 2, 1, 3)
            .reshape(row_blocks * SHAMPOO_SIDE, col_blocks * SHAMPOO_SIDE)
        )

    return (
        block_grid(blocks[:end_qkv], model_blocks, 3 * model_blocks),
        block_grid(blocks[end_qkv:end_out], model_blocks, model_blocks),
        block_grid(blocks[end_out:end_up], model_blocks, hidden_blocks),
        block_grid(blocks[end_up:], hidden_blocks, model_blocks),
    )


def disassemble(matrices):

    def to_blocks(matrix):
        row_blocks = matrix.shape[0] // SHAMPOO_SIDE
        col_blocks = matrix.shape[1] // SHAMPOO_SIDE
        return (
            matrix.reshape(row_blocks, SHAMPOO_SIDE, col_blocks, SHAMPOO_SIDE)
            .transpose(0, 2, 1, 3)
            .reshape(row_blocks * col_blocks, SHAMPOO_SIDE, SHAMPOO_SIDE)
        )

    return jnp.concatenate([to_blocks(matrix) for matrix in matrices], axis=0)


def split_heads(mixed):
    leading = mixed.shape[:-1]
    model_width = mixed.shape[-1] // 3
    queries = mixed[..., :model_width].reshape(leading + (model_width // HEAD, HEAD))
    keys_in = mixed[..., model_width : 2 * model_width].reshape(
        leading + (model_width // HEAD, HEAD)
    )
    values_in = mixed[..., 2 * model_width :].reshape(leading + (model_width // HEAD, HEAD))
    return (queries, keys_in, values_in)


def attend_scores(queries, keys_in, visible):
    scores = jnp.einsum(
        "bqhd,bkhd->bhqk", queries, keys_in, preferred_element_type=jnp.float32
    ) * HEAD ** (-0.5)
    if visible is not None:
        scores = jnp.where(visible, scores, -1e30)
    return scores


def attend_forward(queries, keys_in, values_in, visible):
    scores = attend_scores(queries, keys_in, visible)
    highest = jnp.max(scores, axis=-1, keepdims=True)
    weights = jnp.exp(scores - highest)
    row_total = jnp.sum(weights, axis=-1, keepdims=True)
    context = jnp.einsum(
        "bhqk,bkhd->bqhd",
        (weights / row_total).astype(jnp.bfloat16),
        values_in,
        preferred_element_type=jnp.float32,
    )
    return (context, highest + jnp.log(row_total))


def attend_back(queries, keys_in, values_in, visible, log_total, grad_context):
    score_scale = HEAD ** (-0.5)
    chances = jnp.exp(attend_scores(queries, keys_in, visible) - log_total)
    grad_chances = jnp.einsum(
        "bqhd,bkhd->bhqk", grad_context, values_in, preferred_element_type=jnp.float32
    )
    row_dot = jnp.sum(chances * grad_chances, axis=-1, keepdims=True)
    grad_scores = (chances * (grad_chances - row_dot)).astype(jnp.bfloat16)
    grad_queries = (
        jnp.einsum("bhqk,bkhd->bqhd", grad_scores, keys_in, preferred_element_type=jnp.float32)
        * score_scale
    )
    grad_keys = (
        jnp.einsum("bhqk,bqhd->bkhd", grad_scores, queries, preferred_element_type=jnp.float32)
        * score_scale
    )
    grad_values = jnp.einsum(
        "bhqk,bqhd->bkhd",
        chances.astype(jnp.bfloat16),
        grad_context,
        preferred_element_type=jnp.float32,
    )
    return (grad_queries, grad_keys, grad_values)


def merge_grads(grad_queries, grad_keys, grad_values, leading):
    return jnp.concatenate(
        [
            grad_queries.reshape(leading + (D,)),
            grad_keys.reshape(leading + (D,)),
            grad_values.reshape(leading + (D,)),
        ],
        axis=-1,
    ).astype(jnp.bfloat16)


def shards(
    regions,
    patches,
    cot_regions,
    cot_patches,
    image_shape,
    owner,
    slot_weights,
    small,
    stats,
    roots,
    ema_slots,
    ema_small,
):
    region_slots = regions.shape[0]
    window_len = patches.shape[1] + 1
    gathered = (
        lax.all_gather(slot_weights.astype(jnp.bfloat16), ("dp", "fsdp"), axis=0, tiled=True),
        lax.all_gather(small.astype(jnp.bfloat16), ("dp", "fsdp"), axis=0, tiled=True),
    )
    w_qkv, w_out, w_up, w_down = assemble(gathered[0][owner[:NBLOCKS]])
    row_params = gathered[1][: 8 * D].astype(jnp.float32).reshape(8, D)
    bias_up = gathered[1][8 * D :].astype(jnp.float32)
    live_slots, labels = region_labels(image_shape, region_slots)
    bias_mix = jnp.concatenate([row_params[4], jnp.zeros_like(row_params[4]), row_params[5]])
    reg_in = regions.astype(jnp.float32)
    normed_out, normed_reg, inverse_reg = norm_forward(reg_in, row_params[0], row_params[1])
    input_reg = normed_out.astype(jnp.bfloat16)
    mix_reg = (jnp.dot(input_reg, w_qkv, preferred_element_type=jnp.float32) + bias_mix).astype(
        jnp.bfloat16
    )
    query_reg, key_reg, value_reg = split_heads(mix_reg[None])
    visible = (labels[:, None] == labels[None, :])[None, None]
    context_reg, log_reg = attend_forward(query_reg, key_reg, value_reg, visible)
    context_reg = context_reg.reshape(region_slots, D).astype(jnp.bfloat16)
    region_mid = (
        reg_in + jnp.dot(context_reg, w_out, preferred_element_type=jnp.float32) + row_params[6]
    )
    window = jnp.concatenate([region_mid[:, None, :], patches.astype(jnp.float32)], axis=1)
    normed_out, normed_win, inverse_win = norm_forward(window, row_params[0], row_params[1])
    input_win = normed_out.astype(jnp.bfloat16)
    mix_win = (
        jnp.einsum("rtd,de->rte", input_win, w_qkv, preferred_element_type=jnp.float32) + bias_mix
    ).astype(jnp.bfloat16)
    query_win, key_win, value_win = split_heads(mix_win)
    context_win, log_win = attend_forward(query_win, key_win, value_win, None)
    context_win = context_win.reshape(region_slots, window_len, D).astype(jnp.bfloat16)
    middle = (
        window
        + jnp.einsum("rtd,de->rte", context_win, w_out, preferred_element_type=jnp.float32)
        + row_params[6]
    )
    normed_out, normed_mlp, inverse_mlp = norm_forward(middle, row_params[2], row_params[3])
    perceptron_input = normed_out.astype(jnp.bfloat16)
    hidden_pre = (
        jnp.einsum("rtd,df->rtf", perceptron_input, w_up, preferred_element_type=jnp.float32)
        + bias_up
    )
    hidden_act = jax.nn.gelu(hidden_pre, approximate=False).astype(jnp.bfloat16)
    block_out = (
        middle
        + jnp.einsum("rtf,fd->rtd", hidden_act, w_down, preferred_element_type=jnp.float32)
        + row_params[7]
    )
    keep_rows = live_slots[:, None, None]
    block_out = jnp.where(keep_rows, block_out, 0.0)
    out_regions = block_out[:, 0].astype(jnp.bfloat16)
    out_patches = block_out[:, 1:].astype(jnp.bfloat16)
    regathered = (
        lax.all_gather(slot_weights.astype(jnp.bfloat16), ("dp", "fsdp"), axis=0, tiled=True),
        lax.all_gather(small.astype(jnp.bfloat16), ("dp", "fsdp"), axis=0, tiled=True),
    )
    w_qkv, w_out, w_up, w_down = assemble(regathered[0][owner[:NBLOCKS]])
    row_params = regathered[1][: 8 * D].astype(jnp.float32).reshape(8, D)
    slot_total = owner.shape[0]
    cotangent = jnp.concatenate([cot_regions[:, None, :], cot_patches], axis=1)
    grad_final = jnp.where(keep_rows, cotangent, jnp.zeros((), jnp.bfloat16))
    grad_down = jnp.einsum(
        "rtf,rtd->fd", hidden_act, grad_final, preferred_element_type=jnp.float32
    )
    grad_bias_down = jnp.sum(grad_final.astype(jnp.float32), axis=(0, 1))
    grad_act = jnp.einsum("rtd,fd->rtf", grad_final, w_down, preferred_element_type=jnp.float32)
    grad_pre = (grad_act * gelu_slope(hidden_pre)).astype(jnp.bfloat16)
    grad_up = jnp.einsum(
        "rtd,rtf->df", perceptron_input, grad_pre, preferred_element_type=jnp.float32
    )
    grad_bias_up = jnp.sum(grad_pre.astype(jnp.float32), axis=(0, 1))
    grad_norm_mlp = jnp.einsum("rtf,df->rtd", grad_pre, w_up, preferred_element_type=jnp.float32)
    grad_middle_in, grad_gain_two, grad_offset_two = norm_back(
        grad_norm_mlp, normed_mlp, inverse_mlp, row_params[2]
    )
    grad_middle = (grad_final.astype(jnp.float32) + grad_middle_in).astype(jnp.bfloat16)
    grad_out_w = jnp.einsum(
        "rtd,rte->de", context_win, grad_middle, preferred_element_type=jnp.float32
    )
    grad_bias_o = jnp.sum(grad_middle.astype(jnp.float32), axis=(0, 1))
    grad_context_win = jnp.einsum(
        "rte,de->rtd", grad_middle, w_out, preferred_element_type=jnp.float32
    ).astype(jnp.bfloat16)
    grads_win = attend_back(
        query_win,
        key_win,
        value_win,
        None,
        log_win,
        grad_context_win.reshape(region_slots, window_len, D // HEAD, HEAD),
    )
    grad_mix_win = merge_grads(grads_win[0], grads_win[1], grads_win[2], (region_slots, window_len))
    grad_qkv = jnp.einsum(
        "rtd,rte->de", input_win, grad_mix_win, preferred_element_type=jnp.float32
    )
    grad_bias_mix = jnp.sum(grad_mix_win.astype(jnp.float32), axis=(0, 1))
    grad_norm_win = jnp.einsum(
        "rte,de->rtd", grad_mix_win, w_qkv, preferred_element_type=jnp.float32
    )
    grad_window_in, grad_gain_one, grad_offset_one = norm_back(
        grad_norm_win, normed_win, inverse_win, row_params[0]
    )
    grad_window = grad_middle.astype(jnp.float32) + grad_window_in
    grad_patches = grad_window[:, 1:].astype(jnp.bfloat16)
    grad_region_mid = grad_window[:, 0].astype(jnp.bfloat16)
    grad_out_w = grad_out_w + jnp.einsum(
        "rd,re->de", context_reg, grad_region_mid, preferred_element_type=jnp.float32
    )
    grad_bias_o = grad_bias_o + jnp.sum(grad_region_mid.astype(jnp.float32), axis=0)
    grad_context_reg = jnp.einsum(
        "re,de->rd", grad_region_mid, w_out, preferred_element_type=jnp.float32
    ).astype(jnp.bfloat16)
    grads_reg = attend_back(
        query_reg,
        key_reg,
        value_reg,
        visible,
        log_reg,
        grad_context_reg.reshape(1, region_slots, D // HEAD, HEAD),
    )
    grad_mix_reg = merge_grads(grads_reg[0], grads_reg[1], grads_reg[2], (region_slots,))
    grad_qkv = grad_qkv + jnp.einsum(
        "rd,re->de", input_reg, grad_mix_reg, preferred_element_type=jnp.float32
    )
    grad_bias_mix = grad_bias_mix + jnp.sum(grad_mix_reg.astype(jnp.float32), axis=0)
    grad_norm_reg = jnp.einsum("re,de->rd", grad_mix_reg, w_qkv, preferred_element_type=jnp.float32)
    grad_reg_in, grad_gain_reg, grad_offset_reg = norm_back(
        grad_norm_reg, normed_reg, inverse_reg, row_params[0]
    )
    grad_regions = (grad_region_mid.astype(jnp.float32) + grad_reg_in).astype(jnp.bfloat16)
    grad_gain_one = grad_gain_one + grad_gain_reg
    grad_offset_one = grad_offset_one + grad_offset_reg
    slot_every = (
        jnp.zeros((slot_total, SHAMPOO_SIDE, SHAMPOO_SIDE), jnp.float32)
        .at[owner[:NBLOCKS]]
        .set(disassemble((grad_qkv, grad_out_w, grad_up, grad_down)))
    )
    rows_every = jnp.stack(
        [
            grad_gain_one,
            grad_offset_one,
            grad_gain_two,
            grad_offset_two,
            grad_bias_mix[:D],
            grad_bias_mix[2 * D :],
            grad_bias_o,
            grad_bias_down,
        ]
    )
    small_per_device = jnp.concatenate([rows_every.reshape(-1), grad_bias_up])
    received = (
        lax.psum_scatter(slot_every, ("dp", "fsdp"), scatter_dimension=0, tiled=True),
        lax.psum_scatter(small_per_device, ("dp", "fsdp"), scatter_dimension=0, tiled=True),
    )
    grad_slot_shard = received[0]
    grad_small_shard = received[1]
    precise = lax.Precision.HIGHEST
    left_stat = jnp.einsum("sij,skj->sik", grad_slot_shard, grad_slot_shard, precision=precise)
    right_stat = jnp.einsum("sji,sjk->sik", grad_slot_shard, grad_slot_shard, precision=precise)
    new_stats = STAT_DECAY * stats + (1.0 - STAT_DECAY) * jnp.stack([left_stat, right_stat], axis=1)
    direction = jnp.einsum("sij,sjk->sik", roots[:, 0], grad_slot_shard, precision=precise)
    direction = jnp.einsum("sij,sjk->sik", direction, roots[:, 1], precision=precise)
    weight_rms = jnp.sqrt(
        jnp.mean(slot_weights * slot_weights, axis=(1, 2), keepdims=True) + EPS_MEAN
    )
    step_rms = jnp.sqrt(jnp.mean(direction * direction, axis=(1, 2), keepdims=True) + EPS_MEAN)
    new_slots = slot_weights - SHAMPOO_RATE * (weight_rms / step_rms) * direction
    token_count = region_slots * window_len * lax.axis_size(("dp", "fsdp"))
    new_small = small - SMALL_RATE / math.sqrt(token_count) * grad_small_shard
    new_ema_slots = EMA_DECAY * ema_slots + (1.0 - EMA_DECAY) * new_slots
    new_ema_small = EMA_DECAY * ema_small + (1.0 - EMA_DECAY) * new_small
    return (
        out_regions,
        out_patches,
        grad_regions,
        grad_patches,
        grad_slot_shard,
        grad_small_shard,
        new_stats,
        new_slots,
        new_small,
        new_ema_slots,
        new_ema_small,
    )


def solution(mesh):
    return jax.shard_map(
        shards,
        mesh=mesh,
        in_specs=(
            P(("dp", "fsdp"), None),
            P(("dp", "fsdp"), None, None),
            P(("dp", "fsdp"), None),
            P(("dp", "fsdp"), None, None),
            P(("dp", "fsdp"), None),
            P(),
            P(("dp", "fsdp"), None, None),
            P(("dp", "fsdp")),
            P(("dp", "fsdp"), None, None, None),
            P(("dp", "fsdp"), None, None, None),
            P(("dp", "fsdp"), None, None),
            P(("dp", "fsdp")),
        ),
        out_specs=(
            P(("dp", "fsdp"), None),
            P(("dp", "fsdp"), None, None),
            P(("dp", "fsdp"), None),
            P(("dp", "fsdp"), None, None),
            P(("dp", "fsdp"), None, None),
            P(("dp", "fsdp")),
            P(("dp", "fsdp"), None, None, None),
            P(("dp", "fsdp"), None, None),
            P(("dp", "fsdp")),
            P(("dp", "fsdp"), None, None),
            P(("dp", "fsdp")),
        ),
        check_vma=False,
    )
```

profile of v0, /device:TPU:0, one launch (start us, length us, event | category | flops | bytes accessed | tf_op | source)
XLA Modules:
  0.0 570.2 jit_solution(5332349804902089017)
XLA Ops:
  13.9 42.3 %all-reduce = bf16[6144]{0:T(1024)(128)(2,1)S(1)} all-reduce(bf16[6144]{0:T(1024)(128)(2,1)S(1)} %dynamic-update-slice), channel_id=1, replica_groups=mesh['dp'=4,'fsdp'=8] {'dp','fsdp'}, use_global_device_ids=true, to_apply=%add | all-reduce | flops 6144 | bytes 24576
  62.9 21.0 %all-gather.2.cloned.1.call-done = bf16[192,128,128]{2,1,0:T(8,128)(2,1)} async-done(((bf16[6,128,128]{2,1,0:T(8,128)(2,1)}), bf16[192,128,128]{2,1,0:T(8,128)(2,1)}) %all-gather.2.cloned.1.call-update) | async-done | bytes 6291472 | tf_op jit(solution)/shard_map/all_gather | solution.py:179
  83.9 10.8 %gather_fusion = bf16[192,128,128]{2,1,0:T(8,128)(2,1)} fusion(bf16[192,128,128]{2,1,0:T(8,128)(2,1)} %all-gather.2.cloned.1.call-done, s32[1024]{0:T(1024)S(1)} %pad_clamp_fusion), kind=kCustom, calls=%fused_computation | custom fusion | bytes 12583680 | tf_op jit(solution)/shard_map/gather | solution.py:182
  97.5 5.0 fusion.115
  103.1 4.7 copy.428
  111.9 4.3 copy.429
  149.5 4.4 copy.258
  153.9 5.9 %multiply_reduce_fusion.1 = (f32[24,16,50]{2,1,0:T(8,128)S(1)}, f32[24,16,50,50]{2,3,1,0:T(8,128)S(1)}) fusion(bf16[24,50,16,32]{1,3,2,0:T(8,128)(2,1)} %bitcast.195, bf16[24,50,16,32]{1,3,2,0:T(8,128)(2,1)} %bitcast.193), kind=kOutput, calls=%fused_computation.39 | convolution fusion | flops 63340800 | bytes 6374400 | tf_op jit(solution)/shard_map/bqhd,bkhd->bhqk/dot_general | solution.py:104
  168.7 5.2 copy.311
  177.7 5.8 %convert_reduce_fusion.1 = (u32[50,2048]{1,0:T(8,128)S(1)}, u32[50,2048]{1,0:T(8,128)S(1)}, f32[24,50,2048]{2,1,0:T(8,128)S(1)}) fusion(f32[2048]{0:T(1024)S(1)} %copy-done.44, bf16[512,2048,1]{1,0,2:T(8,128)(2,1)S(1)} %copy-done.20, bf16[24,50,512]{2,0,1:T(8,128)(2,1)S(1)} %add_convert_fusion.1), kind=kOutput, calls=%fused_computation.18 | convolution fusion | flops 2545868800 | bytes 13983744 | tf_op jit(solution)/shard_map/rtd,df->rtf/dot_general | solution.py:217
  183.6 25.0 %fusion.2 = bf16[24,50,2048]{2,1,0:T(8,128)(2,1)S(1)} fusion(f32[24,50,2048]{2,1,0:T(8,128)S(1)} %get-tuple-element.120, u32[50,2048]{1,0:T(8,128)S(1)} %get-tuple-element.67, u32[50,2048]{1,0:T(8,128)S(1)} %get-tuple-element.66, f32[2048]{0:T(1024)S(1)} %copy-done.44), kind=kLoop, calls=%fused_computation.7 | loop fusion | flops 169574400 | bytes 15572992 | tf_op jit(solution)/shard_map/convert_element_type | solution.py:220
  208.6 8.5 %convert_reduce_fusion.2 = (f32[2048]{0:T(1024)S(1)}, bf16[24,50,2048]{2,1,0:T(8,128)(2,1)S(1)}) fusion(f32[24,50,2048]{2,1,0:T(8,128)S(1)} %get-tuple-element.120, f32[2048]{0:T(1024)S(1)} %copy-done.44, bf16[2048,512,1]{1,0,2:T(8,128)(2,1)S(1)} %copy-done.22, bf16[24,50,512]{2,0,1:T(8,128)(2,1)S(1)} %copy-done.11), kind=kOutput, calls=%fused_computation.19 | convolution fusion | flops 2548529152 | bytes 18087936 | tf_op jit(solution)/shard_map/rtd,fd->rtf/dot_general | solution.py:243
  217.1 4.7 fusion.124
  221.8 5.4 convolution_bitcast_fusion
  230.4 5.4 fusion.39
  238.5 4.3 convert_reduce_fusion.4
  251.4 9.8 %fusion.34 = bf16[24,16,32,50]{3,2,1,0:T(8,128)(2,1)} fusion(bf16[24,50,16,32]{1,3,2,0:T(8,128)(2,1)} %bitcast.191, f32[24,16,50,50]{2,3,1,0:T(8,128)} %copy-done, f32[24,16,50]{2,1,0:T(8,128)S(1)} %log_add_fusion), kind=kOutput, calls=%fused_computation.81 | convolution fusion | flops 64934400 | bytes 6374400 | tf_op jit(solution)/shard_map/bhqk,bqhd->bkhd/dot_general | solution.py:142
  261.3 9.1 %multiply_reduce_fusion = (f32[24,16,50]{2,1,0:T(8,128)S(1)}, f32[24,16,50,50]{2,3,1,0:T(8,128)}) fusion(f32[24,16,50,50]{2,3,1,0:T(8,128)} %copy-done, f32[24,16,50]{2,1,0:T(8,128)S(1)} %log_add_fusion, bf16[24,50,16,32]{1,3,2,0:T(8,128)(2,1)S(1)} %bitcast.192, bf16[24,50,16,32]{1,3,2,0:T(8,128)(2,1)S(1)} %bitcast.203), kind=kOutput, calls=%fused_computation.21 | convolution fusion | flops 65260800 | bytes 10291200 | tf_op jit(solution)/shard_map/bqhd,bkhd->bhqk/dot_general | solution.py:129
  270.3 8.7 %multiply_convert_fusion = bf16[24,16,50,50]{2,3,1,0:T(8,128)(2,1)S(1)} fusion(f32[24,16,50,50]{2,3,1,0:T(8,128)} %get-tuple-element.122, f32[24,16,50,50]{2,3,1,0:T(8,128)} %copy-done, f32[24,16,50]{2,1,0:T(8,128)S(1)} %get-tuple-element.121, f32[24,16,50]{2,1,0:T(8,128)S(1)} %log_add_fusion), kind=kLoop, calls=%fused_computation.20 | loop fusion | flops 4800000 | bytes 9753600 | tf_op jit(solution)/shard_map/convert_element_type | solution.py:133
  279.1 4.2 multiply_convert_fusion.1
  286.4 4.3 copy.277
  290.8 4.4 copy.275
  295.1 4.3 copy.276
  316.5 5.4 reshape.444
  321.9 4.9 copy.298
  340.6 4.9 reshape.438
  345.5 4.9 copy.291
  350.4 9.2 %pad_maximum_fusion = f32[192,128,128]{2,1,0:T(8,128)} fusion(f32[64,128,128]{2,1,0:T(8,128)} %bitcast.200, f32[64,128,128]{2,1,0:T(8,128)} %bitcast.201, f32[16,128,128]{2,1,0:T(8,128)S(1)} %bitcast.217, f32[48,128,128]{2,1,0:T(8,128)} %bitcast.204), kind=kLoop, calls=%fused_computation.4 | loop fusion | flops 9437184 | bytes 25165824 | tf_op jit(solution)/shard_map/concatenate | solution.py:89
  359.6 6.1 %broadcast_in_dim.60 = f32[192,128,128]{2,1,0:T(8,128)} broadcast(f32[]{:T(128)} %constant.46.clone.1), dimensions={} | broadcast | bytes 12582916 | tf_op jit(solution)/shard_map/broadcast_in_dim | solution.py:311
  365.7 34.8 %scatter_fusion = f32[192,128,128]{2,1,0:T(8,128)} fusion(f32[192,128,128]{2,1,0:T(8,128)} %broadcast_in_dim.60, s32[192]{0:T(256)S(1)} %copy-done.50, f32[192,128,128]{2,1,0:T(8,128)} %pad_maximum_fusion), kind=kCustom, calls=%fused_computation.1 | custom fusion | bytes 37749504 | tf_op jit(solution)/shard_map/scatter | solution.py:313
  406.3 39.6 %all-reduce.1 = f32[6144]{0:T(1024)S(1)} all-reduce(f32[6144]{0:T(1024)S(1)} %pad_maximum_fusion.3), channel_id=3, replica_groups=mesh['dp'=4,'fsdp'=8] {'dp','fsdp'}, use_global_device_ids=true, to_apply=%region_34.35.clone | all-reduce | flops 6144 | bytes 49152
  447.9 107.0 %reduce-scatter.2.cloned.1.call-done = f32[6,128,128]{2,1,0:T(8,128)} async-done(((f32[192,128,128]{2,1,0:T(8,128)}), f32[6,128,128]{2,1,0:T(8,128)}) %reduce-scatter.2.cloned.1.call-update) | async-done | bytes 393232 | tf_op jit(solution)/shard_map/reduce_scatter | solution.py:329
  (260 shorter events, 130.4 us)
Async XLA Ops:
  7.2 49.6 %copy-start.62 = (s32[192]{0:T(256)S(1)}, s32[192]{0:T(256)}, u32[]{:S(2)}) copy-start(s32[192]{0:T(256)} %param.17) | copy-start | bytes 2308
  7.2 50.3 %copy-start.30 = (bf16[24,512]{1,0:T(8,128)(2,1)S(1)}, bf16[24,512]{1,0:T(8,128)(2,1)}, u32[]{:S(2)}) copy-start(bf16[24,512]{1,0:T(8,128)(2,1)} %param.12) | copy-start | bytes 73732
  7.2 52.0 %copy-start.45 = (bf16[24,512]{1,0:T(8,128)(2,1)S(1)}, bf16[24,512]{1,0:T(8,128)(2,1)}, u32[]{:S(2)}) copy-start(bf16[24,512]{1,0:T(8,128)(2,1)} %param.14) | copy-start | bytes 73732
  7.2 76.7 %all-gather.2.cloned.1.call-start = ((), (), s32[]{:S(2)}) async-start(), calls=%async_computation.1 | async-start | bytes 6488064 | tf_op jit(solution)/shard_map/all_gather | solution.py:179
  9.7 545.2 %reduce-scatter.2.cloned.1.call-start = ((), (), s32[]{:S(2)}) async-start(), calls=%async_computation.2 | async-start | bytes 12976128 | tf_op jit(solution)/shard_map/reduce_scatter | solution.py:329
  56.8 38.0 %copy-start.60 = (pred[24]{0:T(512)(128)(4,1)}, pred[24]{0:T(512)(128)(4,1)S(1)}, u32[]{:S(2)}) copy-start(pred[24]{0:T(512)(128)(4,1)S(1)} %iota_compare_fusion.1) | copy-start | bytes 76
  56.8 37.9 %copy-start.49 = (s32[192]{0:T(256)}, s32[192]{0:T(256)S(1)}, u32[]{:S(2)}) copy-start(s32[192]{0:T(256)S(1)} %compare_select_fusion) | copy-start | bytes 2308
  57.4 66.9 %copy-start.41 = (f32[512]{0:T(512)}, f32[512]{0:T(512)S(1)}, u32[]{:S(2)}) copy-start(f32[512]{0:T(512)S(1)} %get-tuple-element.111) | copy-start | bytes 6148
  57.5 66.9 %copy-start.46 = (f32[512]{0:T(512)}, f32[512]{0:T(512)S(1)}, u32[]{:S(2)}) copy-start(f32[512]{0:T(512)S(1)} %get-tuple-element.110) | copy-start | bytes 6148
  57.5 66.8 %copy-start.54 = (f32[1536]{0:T(1024)}, f32[1536]{0:T(1024)S(1)}, u32[]{:S(2)}) copy-start(f32[1536]{0:T(1024)S(1)} %pad_maximum_fusion.4) | copy-start | bytes 18436
  57.7 66.6 %copy-start.56 = (f32[24]{0:T(128)}, f32[24]{0:T(128)S(1)}, u32[]{:S(2)}) copy-start(f32[24]{0:T(128)S(1)} %broadcast_multiply_fusion.8) | copy-start | bytes 292
  57.9 66.4 %copy-start.58 = (f32[24]{0:T(128)}, f32[24]{0:T(128)S(1)}, u32[]{:S(2)}) copy-start(f32[24]{0:T(128)S(1)} %add_rsqrt_fusion.2) | copy-start | bytes 292
  97.5 5.0 slice-start
  102.9 30.4 %copy-start.8 = (bf16[4,4,128,128]{3,1,2,0:T(4,128)(2,1)}, bf16[4,4,128,128]{3,1,2,0:T(4,128)(2,1)S(1)}, u32[]{:S(2)}) copy-start(bf16[4,4,128,128]{3,1,2,0:T(4,128)(2,1)S(1)} %copy.430) | copy-start | bytes 1572868
  159.8 4.8 copy-start
  159.8 4.8 copy-start.5
  168.7 5.2 copy-start.48
  183.6 25.0 %copy-start.11 = (bf16[24,50,512]{2,0,1:T(8,128)(2,1)S(1)}, bf16[24,50,512]{2,0,1:T(8,128)(2,1)}, u32[]{:S(2)}) copy-start(bf16[24,50,512]{2,0,1:T(8,128)(2,1)} %get-tuple-element.84) | copy-start | bytes 3686404
  183.6 25.0 %copy-start.22 = (bf16[2048,512,1]{1,0,2:T(8,128)(2,1)S(1)}, bf16[2048,512,1]{1,0,2:T(8,128)(2,1)}, u32[]{:S(2)}) copy-start(bf16[2048,512,1]{1,0,2:T(8,128)(2,1)} %reshape.470) | copy-start | bytes 6291460
  221.8 5.4 copy-start.21
  251.4 9.8 %copy-start.1 = (bf16[24,50,512]{1,2,0:T(8,128)(2,1)S(1)}, bf16[24,50,512]{1,2,0:T(8,128)(2,1)}, u32[]{:S(2)}) copy-start(bf16[24,50,512]{1,2,0:T(8,128)(2,1)} %copy.271) | copy-start | bytes 3686404
  251.4 9.8 %copy-start.6 = (bf16[24,50,512]{1,2,0:T(8,128)(2,1)S(1)}, bf16[24,50,512]{1,2,0:T(8,128)(2,1)}, u32[]{:S(2)}) copy-start(bf16[24,50,512]{1,2,0:T(8,128)(2,1)} %copy.258) | copy-start | bytes 3686404
  270.3 8.7 %copy-start.3 = (bf16[24,50,512]{1,2,0:T(8,128)(2,1)S(1)}, bf16[24,50,512]{1,2,0:T(8,128)(2,1)}, u32[]{:S(2)}) copy-start(bf16[24,50,512]{1,2,0:T(8,128)(2,1)} %copy.259) | copy-start | bytes 3686404
  321.9 4.9 copy-start.4
  359.6 6.1 %copy-start.50 = (s32[192]{0:T(256)S(1)}, s32[192]{0:T(256)}, u32[]{:S(2)}) copy-start(s32[192]{0:T(256)} %copy-done.49) | copy-start | bytes 2308
  400.6 5.6 copy-start.51
  400.6 45.3 %copy-start.63 = (f32[192]{0:T(256)S(1)}, f32[192]{0:T(256)}, u32[]{:S(2)}) copy-start(f32[192]{0:T(256)} %param.19) | copy-start | bytes 2308
  400.6 45.3 %copy-start.64 = (f32[192]{0:T(256)S(1)}, f32[192]{0:T(256)}, u32[]{:S(2)}) copy-start(f32[192]{0:T(256)} %param.23) | copy-start | bytes 2308
  400.6 154.3 %copy-start.27 = (f32[6,2,128,128]{3,2,1,0:T(8,128)S(1)}, f32[6,2,128,128]{3,2,1,0:T(8,128)}, u32[]{:S(2)}) copy-start(f32[6,2,128,128]{3,2,1,0:T(8,128)} %param.21) | copy-start | bytes 2359300
  557.0 5.1 copy-start.65
  557.1 5.1 copy-start.25
  557.1 5.1 copy-start.35
  (37 other events, 96.0 us)
Sparse Core Ops, SparseCore 0:
  11.5 72.3 all-gather.1
  400.7 154.1 reduce-scatter.1
where the time goes:
time: 580 us; the launch traced here: 570 us
  local copies, waits for them, and re-layouts  162 us (28%)
  waiting for transfers between devices  128 us (22%)
  matrix products  102 us (18%)
  blocking collectives  81.9 us (14%)
  other arithmetic  80.7 us (14%)
  between operations  15.6 us (3%)
    reduce_scatter x1, waiting for transfers between devices, shards(): lax.psum_scatter(slot_every, ('dp', 'fsdp'), scatter_dimension=0, tiled=T...  107 us
    unnamed x2, blocking collectives  81.9 us
    scatter x1, local copies, waits for them, and re-layouts, shards(): slot_every = jnp.zeros((slot_total, SHAMPOO_SIDE, SHAMPOO_SIDE), jnp.floa...  34.8 us
    convert_element_type x1, other arithmetic, shards(): hidden_act = jax.nn.gelu(hidden_pre, approximate=False).astype(jnp.bfloat16)  25 us
    all_gather x1, waiting for transfers between devices, shards(): lax.all_gather(slot_weights.astype(jnp.bfloat16), ('dp', 'fsdp'), axis=0,...  21 us
    transpose x5, local copies, waits for them, and re-layouts, to_blocks(): return matrix.reshape(row_blocks, SHAMPOO_SIDE, col_blocks, SHAMPOO_SIDE)...  13.5 us
    reshape x4, local copies, waits for them, and re-layouts, block_grid(): pieces.reshape(row_blocks, col_blocks, SHAMPOO_SIDE, SHAMPOO_SIDE)  13.3 us
  transfers between devices with their start and end apart: 2, of which 2 were waited for; matrix products, arithmetic and copies ran while one was open for 3% of the time, Pallas kernels for 0%

commit v1 on v0

v1 whole, which is shorter than its diff:
```python
import math

import jax
import jax.numpy as jnp
from jax import lax
from jax.experimental import pallas as pl
from jax.experimental.pallas import tpu as pltpu
from jax.sharding import PartitionSpec as P

D = 512
HEAD = 32
FF = 2048
SIDE = 128
NBLOCKS = 192
LANES = 128
HEADS_PER = LANES // HEAD
GROUPS = D // LANES

EPS_NORM = 1e-05
EPS_MEAN = 1e-06
SHAMPOO_RATE = 0.5
SMALL_RATE = 0.3
EMA_DECAY = 0.8
STAT_DECAY = 0.5
SCORE_SCALE = HEAD ** (-0.5)
MASKED = -1e30

WINDOWS = 8
PAD = 64
REG_PAD = 32
WIDE = 4 * D + FF
VMEM_LIMIT = 60 * 1024 * 1024

F32 = jnp.float32
BF16 = jnp.bfloat16


def dot_nn(a, b):
    return lax.dot_general(a, b, (((1,), (0,)), ((), ())), preferred_element_type=F32)


def dot_nt(a, b):
    return lax.dot_general(a, b, (((1,), (1,)), ((), ())), preferred_element_type=F32)


def dot_tn(a, b):
    return lax.dot_general(a, b, (((0,), (0,)), ((), ())), preferred_element_type=F32)


def normalize(values):
    center = values - jnp.mean(values, axis=-1, keepdims=True)
    inverse = lax.rsqrt(jnp.mean(center * center, axis=-1, keepdims=True) + EPS_NORM)
    return center * inverse, inverse


def normalize_back(scaled, normed, inverse):
    return inverse * (
        scaled
        - jnp.mean(scaled, axis=-1, keepdims=True)
        - normed * jnp.mean(scaled * normed, axis=-1, keepdims=True)
    )


def gauss(values):
    size = jnp.abs(values)
    t = 1.0 / (1.0 + (0.3275911 * 0.7071067811865476) * size)
    bell = jnp.exp(-0.5 * values * values)
    poly = t * (
        0.127414796
        + t * (-0.142248368 + t * (0.7107068705 + t * (-0.7265760135 + t * 0.5307027145)))
    )
    tail = poly * bell
    return jnp.where(values >= 0.0, 1.0 - tail, tail), bell * 0.3989422804014327


def head_masks(rows, dtype):
    lane = lax.broadcasted_iota(jnp.int32, (rows, LANES), 1) // HEAD
    return [(lane == j).astype(F32).astype(dtype) for j in range(HEADS_PER)]


def spread(values, masks):
    return jnp.concatenate([values * mask for mask in masks], axis=0)


def collect(stacked, masks, rows):
    total = stacked[:rows] * masks[0]
    for j in range(1, HEADS_PER):
        total = total + stacked[j * rows : (j + 1) * rows] * masks[j]
    return total


def attend(queries, keys, values, valid, masks_b, masks_f):
    rows = queries.shape[0]
    scores = dot_nt(keys, spread(queries, masks_b))
    scores = jnp.where(valid, scores, MASKED)
    highest = jnp.max(scores, axis=0, keepdims=True)
    weights = jnp.exp((scores - highest) * SCORE_SCALE)
    probs = weights * (1.0 / jnp.sum(weights, axis=0, keepdims=True))
    context = collect(dot_tn(probs.astype(BF16), values), masks_f, rows)
    return context, probs


def attend_back(queries, keys, values, probs, grad_context, masks_b, masks_f):
    rows = queries.shape[0]
    grad_wide = spread(grad_context, masks_b)
    grad_probs = dot_nt(values, grad_wide)
    row_dot = jnp.sum(probs * grad_probs, axis=0, keepdims=True)
    grad_scores = (probs * (grad_probs - row_dot)).astype(BF16)
    grad_q = collect(dot_tn(grad_scores, keys), masks_f, rows) * SCORE_SCALE
    grad_k = dot_nn(grad_scores, spread(queries, masks_b)) * SCORE_SCALE
    grad_v = dot_nn(probs.astype(BF16), grad_wide)
    return grad_q, grad_k, grad_v


def layer_kernel(
    owner,
    shape,
    small,
    slots,
    regions,
    cot_regions,
    patches,
    cot_patches,
    out_regions,
    out_patches,
    grad_regions,
    grad_patches,
    grad_slots,
    grad_small,
    w_wide,
    w_down,
    vecs,
    reg_mid,
    reg_out,
    reg_grad,
    reg_norm,
    reg_inv,
    reg_mix,
    reg_probs,
    reg_ctx,
    reg_in,
    x_win,
    n_one,
    i_one,
    n_two,
    i_two,
    mix,
    probs_s,
    ctx,
    mid,
    g_fin,
    g_ctx,
    a_win_t,
    ctx_t,
    a_mlp_t,
    g_fin_t,
    g_mid,
    g_mix,
    act,
    g_pre,
    acc,
    acc_up,
    acc_mix,
    stage,
    sem,
):
    step = pl.program_id(0)
    steps = pl.num_programs(0)
    n_reg = regions.shape[0]
    win = patches.shape[1]
    rows = WINDOWS * PAD
    total_slots = slots.shape[0]
    base = pl.multiple_of(step * rows, rows)

    def place(b):
        if b < 48:
            return w_wide, b // 12, b % 12
        if b < 64:
            return w_wide, (b - 48) // 4, 12 + (b - 48) % 4
        if b < 128:
            return w_wide, (b - 64) // 16, 16 + (b - 64) % 16
        return w_down, (b - 128) // 4, (b - 128) % 4

    ends = []
    so_far = jnp.int32(0)
    for j in range(shape.shape[0]):
        so_far = so_far + shape[j, 0] * shape[j, 1]
        ends.append(so_far)
    live_count = ends[-1]

    def row(i, count=1):
        return vecs[i : i + 1, : count * D]

    reg_mask_b = head_masks(REG_PAD, BF16)
    reg_mask_f = head_masks(REG_PAD, F32)

    @pl.when(step == 0)
    def _():
        for b in range(NBLOCKS):
            ref, r, c = place(b)
            pltpu.make_async_copy(
                slots.at[owner[b]],
                ref.at[pl.ds(r * SIDE, SIDE), pl.ds(c * SIDE, SIDE)],
                sem.at[0 if b < 128 else 1],
            ).start()
        for i in range(8):
            vecs[i : i + 1, :D] = jnp.concatenate(
                [small[4 * i + j : 4 * i + j + 1, :] for j in range(4)], axis=1
            )
        vecs[8:9, :] = jnp.concatenate([small[32 + j : 33 + j, :] for j in range(16)], axis=1)
        acc[...] = jnp.zeros_like(acc)
        acc_up[...] = jnp.zeros_like(acc_up)
        acc_mix[...] = jnp.zeros_like(acc_mix)
        reg_in[...] = jnp.zeros_like(reg_in)
        reg_in[:n_reg, :] = regions[...].astype(F32)
        for w in range(WINDOWS):
            x_win[w * PAD + win + 1 : (w + 1) * PAD, :] = jnp.zeros((PAD - win - 1, D), F32)
            g_fin[w * PAD + win + 1 : (w + 1) * PAD, :] = jnp.zeros((PAD - win - 1, D), F32)
        pltpu.make_async_copy(w_wide, w_wide, sem.at[0]).wait()
        pltpu.make_async_copy(w_down, w_down, sem.at[1]).wait()

        normed, inverse = normalize(reg_in[...])
        reg_norm[...] = normed
        reg_inv[...] = inverse
        a_reg = (normed * row(0) + row(1)).astype(BF16)
        mixed = dot_nn(a_reg, w_wide[:, : 3 * D])
        reg_mix[:, :D] = (mixed[:, :D] + row(4)).astype(BF16)
        reg_mix[:, D : 2 * D] = mixed[:, D : 2 * D].astype(BF16)
        reg_mix[:, 2 * D :] = (mixed[:, 2 * D :] + row(5)).astype(BF16)
        spot = (REG_PAD, HEADS_PER * REG_PAD)
        key_at = lax.broadcasted_iota(jnp.int32, spot, 0)
        query_at = lax.broadcasted_iota(jnp.int32, spot, 1) % REG_PAD
        key_label = jnp.zeros(spot, jnp.int32)
        query_label = jnp.zeros(spot, jnp.int32)
        for end in ends:
            key_label = key_label + (key_at >= end).astype(jnp.int32)
            query_label = query_label + (query_at >= end).astype(jnp.int32)
        valid = (key_label == query_label) & ((key_at < n_reg) == (query_at < n_reg))
        for h in range(GROUPS):
            cols = slice(h * LANES, (h + 1) * LANES)
            context, probs = attend(
                reg_mix[:, h * LANES : (h + 1) * LANES],
                reg_mix[:, D + h * LANES : D + (h + 1) * LANES],
                reg_mix[:, 2 * D + h * LANES : 2 * D + (h + 1) * LANES],
                valid,
                reg_mask_b,
                reg_mask_f,
            )
            reg_probs[h] = probs
            reg_ctx[:, cols] = context.astype(BF16)
        reg_mid[...] = (
            reg_in[...] + dot_nn(reg_ctx[...], w_wide[:, 3 * D : 4 * D]) + row(6)
        )

    masks_b = head_masks(PAD, BF16)
    masks_f = head_masks(PAD, F32)
    valid = lax.broadcasted_iota(jnp.int32, (PAD, HEADS_PER * PAD), 0) < win + 1

    def window_in(w, carry):
        at = pl.multiple_of(w * PAD, PAD)
        slot = step * WINDOWS + w
        live = (slot < live_count).astype(F32)
        x_win[pl.ds(at, win), :] = patches[w].astype(F32)
        x_win[pl.ds(at + win, 1), :] = reg_mid[pl.ds(slot, 1), :]
        g_fin[pl.ds(at, win), :] = cot_patches[w].astype(F32) * live
        reg_row = reg_grad[pl.ds(slot, 1), :]
        g_fin[pl.ds(at + win, 1), :] = reg_row * live
        normed, inverse = normalize(x_win[pl.ds(at, PAD), :])
        n_one[pl.ds(at, PAD), :] = normed
        i_one[pl.ds(at, PAD), :] = inverse
        return carry

    @pl.when(step == 0)
    def _():
        reg_grad[:n_reg, :] = cot_regions[...].astype(F32)

    lax.fori_loop(0, WINDOWS, window_in, 0)

    half = rows // 2

    def project(i, carry):
        at = pl.ds(pl.multiple_of(i * half, half), half)
        a_win = (n_one[at, :] * row(0) + row(1)).astype(BF16)
        a_win_t[step * 2 + i] = a_win.T
        g_fin_t[step * 2 + i] = g_fin[at, :].astype(BF16).T
        mix[at, :D] = (dot_nn(a_win, w_wide[:, :D]) + row(4)).astype(BF16)
        mix[at, D : 2 * D] = dot_nn(a_win, w_wide[:, D : 2 * D]).astype(BF16)
        mix[at, 2 * D :] = (dot_nn(a_win, w_wide[:, 2 * D : 3 * D]) + row(5)).astype(BF16)
        return carry

    lax.fori_loop(0, 2, project, 0)

    def window_attend(w, carry):
        at = pl.ds(pl.multiple_of(w * PAD, PAD), PAD)
        for h in range(GROUPS):
            context, probs = attend(
                mix[at, h * LANES : (h + 1) * LANES],
                mix[at, D + h * LANES : D + (h + 1) * LANES],
                mix[at, 2 * D + h * LANES : 2 * D + (h + 1) * LANES],
                valid,
                masks_b,
                masks_f,
            )
            probs_s[w * GROUPS + h] = probs
            ctx[at, h * LANES : (h + 1) * LANES] = context.astype(BF16)
        return carry

    lax.fori_loop(0, WINDOWS, window_attend, 0)

    def perceptron(i, carry):
        at = pl.ds(pl.multiple_of(i * half, half), half)
        here = pl.ds(pl.multiple_of(base + i * half, half), half)
        context = ctx[at, :]
        ctx_t[step * 2 + i] = context.T
        middle = x_win[at, :] + dot_nn(context, w_wide[:, 3 * D : 4 * D]) + row(6)
        normed, inverse = normalize(middle)
        n_two[at, :] = normed
        i_two[at, :] = inverse
        a_mlp = (normed * row(2) + row(3)).astype(BF16)
        a_mlp_t[step * 2 + i] = a_mlp.T
        grad_final = g_fin[at, :]
        grad_b = grad_final.astype(BF16)
        acc[7:8, :] = acc[7:8, :] + jnp.sum(grad_final, axis=0, keepdims=True)
        final = middle + row(7)
        grad_a = jnp.zeros((half, D), F32)
        width = 256
        for c in range(FF // width):
            cols = slice(c * width, (c + 1) * width)
            up = w_wide[:, 4 * D + c * width : 4 * D + (c + 1) * width]
            down = w_down[cols, :]
            pre = dot_nn(a_mlp, up) + vecs[8:9, cols]
            big_phi, phi = gauss(pre)
            act_b = (pre * big_phi).astype(BF16)
            act[here, cols] = act_b
            grad_pre = dot_nt(grad_b, down) * (big_phi + pre * phi)
            grad_pre = grad_pre.astype(BF16)
            g_pre[here, cols] = grad_pre
            acc_up[:, cols] = acc_up[:, cols] + jnp.sum(
                grad_pre.astype(F32), axis=0, keepdims=True
            )
            final = final + dot_nn(act_b, down)
            grad_a = grad_a + dot_nt(grad_pre, up)
        mid[at, :] = final
        acc[2:3, :] = acc[2:3, :] + jnp.sum(grad_a * normed, axis=0, keepdims=True)
        acc[3:4, :] = acc[3:4, :] + jnp.sum(grad_a, axis=0, keepdims=True)
        grad_mid = (grad_final + normalize_back(grad_a * row(2), normed, inverse)).astype(BF16)
        g_mid[here, :] = grad_mid
        acc[6:7, :] = acc[6:7, :] + jnp.sum(grad_mid.astype(F32), axis=0, keepdims=True)
        g_ctx[at, :] = dot_nt(grad_mid, w_wide[:, 3 * D : 4 * D]).astype(BF16)
        return carry

    lax.fori_loop(0, 2, perceptron, 0)

    def window_back(w, carry):
        at = pl.ds(pl.multiple_of(w * PAD, PAD), PAD)
        here = pl.ds(pl.multiple_of(base + w * PAD, PAD), PAD)
        slot = step * WINDOWS + w
        live = (slot < live_count).astype(F32)
        out_patches[w] = (mid[pl.ds(w * PAD, win), :] * live).astype(BF16)
        reg_out[pl.ds(slot, 1), :] = mid[pl.ds(w * PAD + win, 1), :] * live
        for h in range(GROUPS):
            grad_q, grad_k, grad_v = attend_back(
                mix[at, h * LANES : (h + 1) * LANES],
                mix[at, D + h * LANES : D + (h + 1) * LANES],
                mix[at, 2 * D + h * LANES : 2 * D + (h + 1) * LANES],
                probs_s[w * GROUPS + h],
                g_ctx[at, h * LANES : (h + 1) * LANES],
                masks_b,
                masks_f,
            )
            g_mix[here, h * LANES : (h + 1) * LANES] = grad_q.astype(BF16)
            g_mix[here, D + h * LANES : D + (h + 1) * LANES] = grad_k.astype(BF16)
            g_mix[here, 2 * D + h * LANES : 2 * D + (h + 1) * LANES] = grad_v.astype(BF16)
        return carry

    lax.fori_loop(0, WINDOWS, window_back, 0)

    def project_back(i, carry):
        at = pl.ds(pl.multiple_of(i * half, half), half)
        here = pl.ds(pl.multiple_of(base + i * half, half), half)
        grad_mix = g_mix[here, :]
        acc_mix[...] = acc_mix[...] + jnp.sum(grad_mix.astype(F32), axis=0, keepdims=True)
        grad_a = dot_nt(grad_mix, w_wide[:, : 3 * D])
        normed = n_one[at, :]
        acc[0:1, :] = acc[0:1, :] + jnp.sum(grad_a * normed, axis=0, keepdims=True)
        acc[1:2, :] = acc[1:2, :] + jnp.sum(grad_a, axis=0, keepdims=True)
        mid[at, :] = g_mid[here, :].astype(F32) + normalize_back(
            grad_a * row(0), normed, i_one[at, :]
        )
        return carry

    lax.fori_loop(0, 2, project_back, 0)

    def window_out(w, carry):
        slot = step * WINDOWS + w
        grad_patches[w] = mid[pl.ds(w * PAD, win), :].astype(BF16)
        reg_grad[pl.ds(slot, 1), :] = mid[pl.ds(w * PAD + win, 1), :]
        return carry

    lax.fori_loop(0, WINDOWS, window_out, 0)

    @pl.when(step == steps - 1)
    def _():
        out_regions[...] = reg_out[:n_reg, :].astype(BF16)
        reg_grad[n_reg:, :] = jnp.zeros((REG_PAD - n_reg, D), F32)
        grad_mid = reg_grad[...].astype(BF16)
        grad_mid_f = grad_mid.astype(F32)
        grad_ctx = dot_nt(grad_mid, w_wide[:, 3 * D : 4 * D]).astype(BF16)
        parts = ([], [], [])
        for h in range(GROUPS):
            cols = slice(h * LANES, (h + 1) * LANES)
            grads = attend_back(
                reg_mix[:, h * LANES : (h + 1) * LANES],
                reg_mix[:, D + h * LANES : D + (h + 1) * LANES],
                reg_mix[:, 2 * D + h * LANES : 2 * D + (h + 1) * LANES],
                reg_probs[h],
                grad_ctx[:, cols],
                reg_mask_b,
                reg_mask_f,
            )
            for part, grad in zip(parts, grads):
                part.append(grad.astype(BF16))
        grad_mix = jnp.concatenate(parts[0] + parts[1] + parts[2], axis=1)
        grad_a = dot_nt(grad_mix, w_wide[:, : 3 * D])
        normed = reg_norm[...]
        inside = (lax.broadcasted_iota(jnp.int32, (REG_PAD, D), 0) < n_reg).astype(F32)
        grad_a = grad_a * inside
        grad_regions[...] = (
            grad_mid_f + normalize_back(grad_a * row(0), normed, reg_inv[...])
        )[:n_reg, :].astype(BF16)
        gain_one = acc[0:1, :] + jnp.sum(grad_a * normed, axis=0, keepdims=True)
        shift_one = acc[1:2, :] + jnp.sum(grad_a, axis=0, keepdims=True)
        bias_o = acc[6:7, :] + jnp.sum(grad_mid_f, axis=0, keepdims=True)
        bias_mix = acc_mix[...] + jnp.sum(grad_mix.astype(F32), axis=0, keepdims=True)
        rows_all = [
            gain_one,
            shift_one,
            acc[2:3, :],
            acc[3:4, :],
            bias_mix[:, :D],
            bias_mix[:, 2 * D :],
            bias_o,
            acc[7:8, :],
        ]
        for i, values in enumerate(rows_all):
            for j in range(4):
                grad_small[4 * i + j : 4 * i + j + 1, :] = values[:, j * LANES : (j + 1) * LANES]
        for j in range(FF // LANES):
            grad_small[32 + j : 33 + j, :] = acc_up[:, j * LANES : (j + 1) * LANES]

        a_reg = (normed * row(0) + row(1)).astype(BF16)

        def copy_out(b, r, c):
            return pltpu.make_async_copy(
                stage.at[pl.ds(r * SIDE, SIDE), pl.ds(c * SIDE, SIDE)],
                grad_slots.at[owner[b]],
                sem.at[2],
            )

        def contract(left, right, cols):
            total = dot_nn(left[0], right[0:half, cols])
            for i in range(1, left.shape[0]):
                total = total + dot_nn(left[i], right[i * half : (i + 1) * half, cols])
            return total

        width = 256
        for c in range(FF // width):
            cols = slice(c * width, (c + 1) * width)
            out = slice(4 * D + c * width, 4 * D + (c + 1) * width)
            stage[:, out] = contract(a_mlp_t, g_pre, cols).astype(BF16)
            flipped = contract(g_fin_t, act, cols).astype(BF16).T
            for j in range(width // SIDE):
                for k in range(4):
                    stage[
                        k * SIDE : (k + 1) * SIDE,
                        WIDE + c * width + j * SIDE : WIDE + c * width + (j + 1) * SIDE,
                    ] = flipped[j * SIDE : (j + 1) * SIDE, k * SIDE : (k + 1) * SIDE]
        for c in range(3 * D // width):
            cols = slice(c * width, (c + 1) * width)
            stage[:, cols] = (
                contract(a_win_t, g_mix, cols) + dot_tn(a_reg, grad_mix[:, cols])
            ).astype(BF16)
        for c in range(D // width):
            cols = slice(c * width, (c + 1) * width)
            stage[:, 3 * D + c * width : 3 * D + (c + 1) * width] = (
                contract(ctx_t, g_mid, cols) + dot_tn(reg_ctx[...], grad_mid[:, cols])
            ).astype(BF16)
        copies = []
        for b in range(NBLOCKS):
            ref, r, c = place(b)
            if b >= 128:
                r, c = c, WIDE // SIDE + r
            copies.append(copy_out(b, r, c))
        if total_slots > NBLOCKS:
            w_down[:SIDE, :SIDE] = jnp.zeros((SIDE, SIDE), BF16)
        for b in range(NBLOCKS, total_slots):
            copies.append(
                pltpu.make_async_copy(
                    w_down.at[pl.ds(0, SIDE), pl.ds(0, SIDE)], grad_slots.at[owner[b]], sem.at[2]
                )
            )
        for copy in copies:
            copy.start()
        pltpu.make_async_copy(grad_slots, grad_slots, sem.at[2]).wait()


def layer(owner, shape, small, slots, regions, cot_regions, patches, cot_patches):
    n_reg, win = patches.shape[:2]
    steps = n_reg // WINDOWS
    rows = WINDOWS * PAD
    half = rows // 2
    every = steps * rows
    whole = lambda i: (0, 0)
    block = pl.BlockSpec((WINDOWS, win, D), lambda i: (i, 0, 0))
    vec = lambda r, c, dtype=F32: pltpu.VMEM((r, c), dtype)
    return pl.pallas_call(
        layer_kernel,
        grid=(steps,),
        in_specs=[
            pl.BlockSpec(memory_space=pltpu.SMEM),
            pl.BlockSpec(memory_space=pltpu.SMEM),
            pl.BlockSpec(small.shape, whole),
            pl.BlockSpec(memory_space=pl.ANY),
            pl.BlockSpec(regions.shape, whole),
            pl.BlockSpec(cot_regions.shape, whole),
            block,
            block,
        ],
        out_specs=[
            pl.BlockSpec(regions.shape, whole),
            block,
            pl.BlockSpec(regions.shape, whole),
            block,
            pl.BlockSpec(memory_space=pl.ANY),
            pl.BlockSpec(small.shape, whole),
        ],
        out_shape=[
            jax.ShapeDtypeStruct(regions.shape, BF16),
            jax.ShapeDtypeStruct(patches.shape, BF16),
            jax.ShapeDtypeStruct(regions.shape, BF16),
            jax.ShapeDtypeStruct(patches.shape, BF16),
            jax.ShapeDtypeStruct(slots.shape, BF16),
            jax.ShapeDtypeStruct(small.shape, F32),
        ],
        scratch_shapes=[
            vec(D, WIDE, BF16),
            vec(FF, D, BF16),
            vec(16, FF),
            vec(REG_PAD, D),
            vec(REG_PAD, D),
            vec(REG_PAD, D),
            vec(REG_PAD, D),
            vec(REG_PAD, 1),
            vec(REG_PAD, 3 * D, BF16),
            pltpu.VMEM((GROUPS, REG_PAD, HEADS_PER * REG_PAD), F32),
            vec(REG_PAD, D, BF16),
            vec(REG_PAD, D),
            vec(rows, D),
            vec(rows, D),
            vec(rows, 1),
            vec(rows, D),
            vec(rows, 1),
            vec(rows, 3 * D, BF16),
            pltpu.VMEM((WINDOWS * GROUPS, PAD, HEADS_PER * PAD), F32),
            vec(rows, D, BF16),
            vec(rows, D),
            vec(rows, D),
            vec(rows, D, BF16),
            pltpu.VMEM((2 * steps, D, half), BF16),
            pltpu.VMEM((2 * steps, D, half), BF16),
            pltpu.VMEM((2 * steps, D, half), BF16),
            pltpu.VMEM((2 * steps, D, half), BF16),
            vec(every, D, BF16),
            vec(every, 3 * D, BF16),
            vec(every, FF, BF16),
            vec(every, FF, BF16),
            vec(8, D),
            vec(1, FF),
            vec(1, 3 * D),
            vec(D, WIDE + FF, BF16),
            pltpu.SemaphoreType.DMA((3,)),
        ],
        compiler_params=pltpu.CompilerParams(
            dimension_semantics=("arbitrary",), vmem_limit_bytes=VMEM_LIMIT
        ),
        name="layer",
    )(owner, shape, small, slots, regions, cot_regions, patches, cot_patches)


def shards(
    regions,
    patches,
    cot_regions,
    cot_patches,
    image_shape,
    owner,
    slot_weights,
    small,
    stats,
    roots,
    ema_slots,
    ema_small,
):
    axes = ("dp", "fsdp")
    devices = lax.axis_size(axes)
    me = lax.axis_index(axes)
    mine = small.shape[0]
    own_slots = slot_weights.shape[0]
    slots = lax.all_gather(slot_weights.astype(BF16), axes, axis=0, tiled=True)
    small_all = lax.all_gather(small.astype(BF16), axes, axis=0, tiled=True).astype(F32)
    out_regions, out_patches, grad_regions, grad_patches, grad_slots, grad_small = layer(
        owner,
        image_shape,
        small_all.reshape(-1, LANES),
        slots,
        regions,
        cot_regions,
        patches,
        cot_patches,
    )
    grad_slot = lax.psum_scatter(grad_slots, axes, scatter_dimension=0, tiled=True).astype(F32)
    grad_small = lax.psum_scatter(grad_small.reshape(-1), axes, scatter_dimension=0, tiled=True)
    precise = lax.Precision.HIGHEST
    left_stat = jnp.einsum("sij,skj->sik", grad_slot, grad_slot, precision=precise)
    right_stat = jnp.einsum("sji,sjk->sik", grad_slot, grad_slot, precision=precise)
    new_stats = STAT_DECAY * stats + (1.0 - STAT_DECAY) * jnp.stack([left_stat, right_stat], axis=1)
    direction = jnp.einsum("sij,sjk->sik", roots[:, 0], grad_slot, precision=precise)
    direction = jnp.einsum("sij,sjk->sik", direction, roots[:, 1], precision=precise)
    weight_rms = jnp.sqrt(
        jnp.mean(slot_weights * slot_weights, axis=(1, 2), keepdims=True) + EPS_MEAN
    )
    step_rms = jnp.sqrt(jnp.mean(direction * direction, axis=(1, 2), keepdims=True) + EPS_MEAN)
    new_slots = slot_weights - SHAMPOO_RATE * (weight_rms / step_rms) * direction
    token_count = regions.shape[0] * (patches.shape[1] + 1) * devices
    new_small = small - SMALL_RATE / math.sqrt(token_count) * grad_small
    new_ema_slots = EMA_DECAY * ema_slots + (1.0 - EMA_DECAY) * new_slots
    new_ema_small = EMA_DECAY * ema_small + (1.0 - EMA_DECAY) * new_small
    return (
        out_regions,
        out_patches,
        grad_regions,
        grad_patches,
        grad_slot,
        grad_small,
        new_stats,
        new_slots,
        new_small,
        new_ema_slots,
        new_ema_small,
    )


def solution(mesh):
    both = ("dp", "fsdp")
    ranks = (2, 3, 2, 3, 2, None, 3, 1, 4, 4, 3, 1)
    outs = (2, 3, 2, 3, 3, 1, 4, 3, 1, 3, 1)
    spec = lambda rank: P() if rank is None else P(both, *([None] * (rank - 1)))
    return jax.shard_map(
        shards,
        mesh=mesh,
        in_specs=tuple(spec(r) for r in ranks),
        out_specs=tuple(spec(r) for r in outs),
        check_vma=False,
    )
```

time: 580 us -> 318 us (0.55); the launches traced: 570 us -> 317 us
  local copies, waits for them, and re-layouts: 162 us -> 10.7 us
  Pallas kernels: 0 us -> 108 us
  matrix products: 102 us -> 2.43 us
  other arithmetic: 80.7 us -> 5.02 us
  waiting for transfers between devices: 128 us -> 95.1 us
    pallas_call x0 -> x1, Pallas kernels: none -> 108 us  [layer(): pl.pallas_call(layer_kernel, grid=(steps,), in_specs=[pl.BlockSpec(memory...]
    dot_general x33 -> x3, matrix products: 102 us -> 1.82 us  [the longest x1 1.31 us: shards(): jnp.einsum('sij,sjk->sik', roots[:, 0], grad_slot, precision=precise)]
    reshape x16 -> x0, local copies, waits for them, and re-layouts: 45.9 us -> none  [the longest x4 13.3 us: block_grid(): pieces.reshape(row_blocks, col_blocks, SHAMPOO_SIDE, SHAMPOO_SIDE)]
    reduce_scatter x1, waiting for transfers between devices: 107 us -> 68.7 us  [shards(): lax.psum_scatter(grad_slots, axes, scatter_dimension=0, tiled=True)]
    convert_element_type x10 -> x2, other arithmetic: 38.9 us -> 0.78 us  [the longest x1 0.77 us: shards(): lax.psum_scatter(grad_slots, axes, scatter_dimension=0, tiled=True)]
    scatter x1 -> x0, local copies, waits for them, and re-layouts: 34.8 us -> none  [shards(): slot_every = jnp.zeros((slot_total, SHAMPOO_SIDE, SHAMPOO_SIDE), jnp.floa...]
    slice x14 -> x0, local copies, waits for them, and re-layouts: 27.2 us -> none  [the longest x2 6.17 us: split_heads(): mixed[..., model_width:2 * model_width]]
    reduce_sum x15 -> x0, other arithmetic: 22.1 us -> none  [the longest x2 5.63 us: norm_back(): jnp.sum(grad_out * normed, axis=lead_axes)]
where the time goes in v1:
time: 318 us; the launch traced here: 317 us
  Pallas kernels  108 us (34%)
  waiting for transfers between devices  95.1 us (30%)
  blocking collectives  81.8 us (26%)
  between operations  14.2 us (4%)
  local copies, waits for them, and re-layouts  10.7 us (3%)
  other arithmetic  5.02 us (2%)
    pallas_call x1, Pallas kernels, layer(): pl.pallas_call(layer_kernel, grid=(steps,), in_specs=[pl.BlockSpec(memory...  108 us
    unnamed x2, blocking collectives  81.8 us
    reduce_scatter x1, waiting for transfers between devices, shards(): lax.psum_scatter(grad_slots, axes, scatter_dimension=0, tiled=True)  68.7 us
    all_gather x1, waiting for transfers between devices, shards(): slots = lax.all_gather(slot_weights.astype(BF16), axes, axis=0, tiled=True)  26.4 us
    unnamed x32, local copies, waits for them, and re-layouts  10.7 us
  transfers between devices with their start and end apart: 2, of which 2 were waited for; matrix products, arithmetic and copies ran while one was open for 3% of the time, Pallas kernels for 0%

profile of v1, /device:TPU:0, one launch (start us, length us, event | category | flops | bytes accessed | tf_op | source)
XLA Modules:
  0.0 317.1 jit_solution(10890066570668034634)
XLA Ops:
  7.2 0.0 all-gather.2.cloned.1.call-start
  7.2 1.9 multiply_reduce_fusion.1
  9.1 0.0 all-gather.2.cloned.1.call-update
  9.1 0.0 reduce-scatter.2.cloned.1.call-start
  9.2 2.8 copy.33.patches
  12.0 1.5 copy.34.cot_patches
  13.5 0.7 copy.32.shape
  14.2 0.2 dynamic-update-slice
  14.4 42.4 %all-reduce = bf16[6144]{0:T(1024)(128)(2,1)S(1)} all-reduce(bf16[6144]{0:T(1024)(128)(2,1)S(1)} %dynamic-update-slice), channel_id=1, replica_groups=mesh['dp'=4,'fsdp'=8] {'dp','fsdp'}, use_global_device_ids=true, to_apply=%add | all-reduce | flops 6144 | bytes 24576
  56.8 0.6 bitcast_convert_fusion.small
  57.4 26.4 %all-gather.2.cloned.1.call-done.slots = bf16[192,128,128]{2,1,0:T(8,128)(2,1)} async-done(((bf16[6,128,128]{2,1,0:T(8,128)(2,1)}), bf16[192,128,128]{2,1,0:T(8,128)(2,1)}) %all-gather.2.cloned.1.call-update) | async-done | bytes 6291472 | tf_op jit(solution)/shard_map/all_gather | solution.py:609
  83.8 107.8 %layer.1 = (bf16[24,512]{1,0:T(8,128)(2,1)}, bf16[24,49,512]{2,1,0:T(8,128)(2,1)}, bf16[24,512]{1,0:T(8,128)(2,1)}, bf16[24,49,512]{2,1,0:T(8,128)(2,1)}, bf16[1...) custom-call(s32[192]{0:T(256)} %owner.1, s32[6,2]{1,0:T(8,128)} %copy.32.shape, f32[48,128]{1,0:T(8,128)} %bitcast_convert_fusion.small, ...), custom_call_target="tpu_custom_call" | custom-call | tf_op jit(solution)/shard_map/layer/pallas_call | solution.py:516
  191.5 0.0 reduce-scatter.2.cloned.1.call-update
  191.6 1.3 copy-done.3
  192.9 1.4 copy.38
  194.3 1.4 copy.39
  195.7 39.4 %all-reduce.1 = f32[6144]{0:T(1024)S(1)} all-reduce(f32[6144]{0:T(1024)S(1)} %bitcast.24), channel_id=3, replica_groups=mesh['dp'=4,'fsdp'=8] {'dp','fsdp'}, use_global_device_ids=true, to_apply=%region_1.0.clone | all-reduce | flops 6144 | bytes 49152
  235.1 0.7 multiply_add_fusion.1
  235.7 68.7 %reduce-scatter.2.cloned.1.call-done = bf16[6,128,128]{2,1,0:T(8,128)(2,1)} async-done(((bf16[192,128,128]{2,1,0:T(8,128)(2,1)}), bf16[6,128,128]{2,1,0:T(8,128)(2,1)}) %reduce-scatter.2.cloned.1.call-update) | async-done | bytes 196624 | tf_op jit(solution)/shard_map/reduce_scatter | solution.py:621
  304.5 1.3 fusion.3
  305.8 0.0 copy-start.6
  305.8 0.6 multiply_reduce_fusion
  306.4 0.3 convolution_bitcast_fusion
  306.7 0.2 convolution_bitcast_fusion.1
  307.0 0.1 fusion
  307.1 0.0 copy-start.1
  307.1 0.0 copy-start.7
  307.1 0.9 copy.40
  308.0 0.1 copy-done.1
  308.1 0.3 copy-done.7
  308.5 1.0 multiply_add_fusion
  309.5 0.8 convert_element_type.12
  (21 shorter events, 0.1 us)
Async XLA Ops:
  7.2 76.6 %all-gather.2.cloned.1.call-start = ((), (), s32[]{:S(2)}) async-start(), calls=%async_computation.1 | async-start | bytes 6488064 | tf_op jit(solution)/shard_map/all_gather | solution.py:609
  9.1 2.9 copy-start.4
  9.1 295.4 %reduce-scatter.2.cloned.1.call-start = ((), (), s32[]{:S(2)}) async-start(), calls=%async_computation.2 | async-start | bytes 6488064 | tf_op jit(solution)/shard_map/reduce_scatter | solution.py:621
  12.0 1.5 copy-start.10
  12.0 1.5 copy-start.9
  191.5 1.3 copy-start.3
  191.6 2.7 copy-start.2
  194.3 1.4 copy-start.8
  194.3 40.8 %copy-start.11 = (f32[192]{0:T(256)S(1)}, f32[192]{0:T(256)}, u32[]{:S(2)}) copy-start(f32[192]{0:T(256)} %param.23) | copy-start | bytes 2308
  194.3 110.2 %copy-start.5 = (f32[6,2,128,128]{3,2,1,0:T(8,128)S(1)}, f32[6,2,128,128]{3,2,1,0:T(8,128)}, u32[]{:S(2)}) copy-start(f32[6,2,128,128]{3,2,1,0:T(8,128)} %param.21) | copy-start | bytes 2359300
  304.5 2.0 copy-start
  305.8 1.2 copy-start.6
  307.1 1.1 copy-start.1
  307.1 1.4 copy-start.7
Sparse Core Ops, SparseCore 0:
  11.5 72.2 all-gather.1
  191.7 112.7 reduce-scatter.1

commit v2 on v1

--- a/solution.py
+++ b/solution.py
@@ -1,3 +1,4 @@
+import functools
 import math
 
 import jax
@@ -29,6 +30,9 @@
 PAD = 64
 REG_PAD = 32
 WIDE = 4 * D + FF
+ALL = WIDE + FF
+Z_LEN = 4
+TAIL = 16
 VMEM_LIMIT = 60 * 1024 * 1024
 
 F32 = jnp.float32
@@ -112,23 +116,169 @@
     return grad_q, grad_k, grad_v
 
 
+class Plan:
+    def __init__(self, n_dp, n_fsdp, own, entries):
+        self.n_dp, self.n_fsdp, self.own, self.entries = n_dp, n_fsdp, own, entries
+        self.x_len, self.ring = n_dp // 2, n_fsdp
+        self.y_len = n_fsdp // Z_LEN
+        self.devices = n_dp * n_fsdp
+        self.empty = self.devices * own > NBLOCKS
+        self.half = self.ring // 2
+        starts = [(d * entries) % LANES for d in range(self.devices)]
+        self.small_rows = max((at + entries - 1) // LANES + 1 for at in starts)
+        order = [0] * self.ring
+        for z in range(Z_LEN):
+            for y in range(self.y_len):
+                order[y * Z_LEN + (z if y % 2 == 0 else Z_LEN - 1 - z)] = z * self.y_len + y
+        n = self.ring
+        self.forward = [(order[i], order[(i + 1) % n]) for i in range(n)]
+        self.backward = [(order[i], order[i - 1]) for i in range(n)]
+        self.flip = [(i, i ^ 1) for i in range(n_dp)]
+        self.gathered, self.scattered = [], []
+        xs = range(self.x_len)
+        h, m = self.half, self.x_len // 2
+        for flip in (0, 1):
+            put = lambda k, part: self.gathered.append([self.home(flip, k, x) for x in part])
+            put(0, xs)
+            for k in range(1, h):
+                put(-k, xs)
+                put(k, xs)
+            put(-h, xs[:m])
+            put(h, xs[m:])
+            spots = [[h, h - 1, 1 - h]]
+            spots.append([k for j in range(h - 2, 0, -1) for k in (j, -j)])
+            spots.append([0])
+            for group in spots:
+                self.scattered.append([self.home(flip, k, x) for k in group for x in xs])
+        self.spots = spots
+
+    def home(self, flip, k, x):
+        return (flip * self.ring + k % self.ring) * self.x_len + x % self.x_len
+
+    def shift(self, by):
+        return [(i, (i + 2 * by) % self.n_dp) for i in range(self.n_dp)]
+
+    def device_of_homes(self, dp, fsdp):
+        home = jnp.arange(self.devices, dtype=jnp.int32)
+        x = (home % self.x_len + dp // 2) % self.x_len
+        core = (home // (self.x_len * self.ring) + dp) % 2
+        z, y = fsdp // self.y_len, fsdp % self.y_len
+        here = y * Z_LEN + jnp.where(y % 2 == 0, z, Z_LEN - 1 - z)
+        place = (home // self.x_len + here) % self.ring
+        y, z = place // Z_LEN, place % Z_LEN
+        z = jnp.where(y % 2 == 0, z, Z_LEN - 1 - z)
+        return (x * 2 + core) * self.n_fsdp + z * self.y_len + y
+
+    def gather(self, mine):
+        stack = [mine[None]]
+        for by in range(1, self.x_len):
+            stack.append(lax.ppermute(mine[None], "dp", self.shift(-by)))
+        first = jnp.concatenate(stack, axis=0)
+        pieces = [first]
+        ahead = behind = first
+        m = self.x_len // 2
+        for _ in range(1, self.half):
+            ahead = lax.ppermute(ahead, "fsdp", self.forward)
+            behind = lax.ppermute(behind, "fsdp", self.backward)
+            pieces += [ahead, behind]
+        pieces.append(lax.ppermute(ahead[:m], "fsdp", self.forward))
+        pieces.append(lax.ppermute(behind[m:], "fsdp", self.backward))
+        return pieces + [lax.ppermute(piece, "dp", self.flip) for piece in pieces]
+
+    def scatter(self, sends):
+        n = len(self.spots)
+        mixed = [lax.ppermute(send, "dp", self.flip) for send in sends[n:]]
+        parts = {}
+        for spot, kept, came in zip(self.spots, sends[:n], mixed):
+            for i, k in enumerate(spot):
+                at = slice(i * self.x_len, (i + 1) * self.x_len)
+                parts[k] = (kept[at], came[at])
+        total = lambda k: parts[k][0].astype(F32) + parts[k][1].astype(F32)
+        m = self.x_len // 2
+        far = total(self.half).astype(BF16)
+        ahead = lax.ppermute(far[:m], "fsdp", self.forward)
+        behind = lax.ppermute(far[m:], "fsdp", self.backward)
+        none = ((0, 0), (0, 0))
+        ahead = jnp.pad(ahead, ((0, self.x_len - m),) + none)
+        behind = jnp.pad(behind, ((m, 0),) + none)
+        for k in range(self.half - 1, 0, -1):
+            ahead = (total(k) + ahead.astype(F32)).astype(BF16)
+            behind = (total(-k) + behind.astype(F32)).astype(BF16)
+            ahead = lax.ppermute(ahead, "fsdp", self.forward)
+            behind = lax.ppermute(behind, "fsdp", self.backward)
+        mine = total(0) + ahead.astype(F32) + behind.astype(F32)
+        result = mine[0]
+        for by in range(1, self.x_len):
+            came = lax.ppermute(mine[by].astype(BF16), "dp", self.shift(by))
+            result = result + came.astype(F32)
+        return result
+
+
+def block_places(block):
+    pick = jnp.where
+    row = pick(block < 48, block // 12, pick(block < 64, (block - 48) // 4, (block - 64) // 16))
+    col = pick(block < 48, block % 12, pick(block < 64, 12 + block % 4, 16 + block % 16))
+    row = pick(block < 128, row, block % 4)
+    col = pick(block < 128, col, 32 + (block - 128) // 4)
+    return pick(block < NBLOCKS, row, 0), pick(block < NBLOCKS, col, ALL // SIDE)
+
+
 def layer_kernel(
-    owner,
+    plan,
+    block_row,
+    block_col,
+    small_row,
     shape,
-    small,
-    slots,
     regions,
     cot_regions,
     patches,
     cot_patches,
+    *rest,
+):
+    n_in, n_out = len(plan.gathered), len(plan.scattered)
+    pieces = rest[:n_in]
+    out_regions, out_patches, grad_regions, grad_patches = rest[n_in : n_in + 4]
+    sends = rest[n_in + 4 : n_in + 4 + n_out]
+    layer_body(
+        plan,
+        block_row,
+        block_col,
+        small_row,
+        shape,
+        regions,
+        cot_regions,
+        patches,
+        cot_patches,
+        pieces,
+        out_regions,
+        out_patches,
+        grad_regions,
+        grad_patches,
+        sends,
+        *rest[n_in + 4 + n_out :],
+    )
+
+
+def layer_body(
+    plan,
+    block_row,
+    block_col,
+    small_row,
+    shape,
+    regions,
+    cot_regions,
+    patches,
+    cot_patches,
+    pieces,
     out_regions,
     out_patches,
     grad_regions,
     grad_patches,
-    grad_slots,
-    grad_small,
+    sends,
     w_wide,
-    w_down,
+    small_in,
+    small,
+    small_out,
     vecs,
     reg_mid,
     reg_out,
@@ -169,17 +319,7 @@
     n_reg = regions.shape[0]
     win = patches.shape[1]
     rows = WINDOWS * PAD
-    total_slots = slots.shape[0]
     base = pl.multiple_of(step * rows, rows)
-
-    def place(b):
-        if b < 48:
-            return w_wide, b // 12, b % 12
-        if b < 64:
-            return w_wide, (b - 48) // 4, 12 + (b - 48) % 4
-        if b < 128:
-            return w_wide, (b - 64) // 16, 16 + (b - 64) % 16
-        return w_down, (b - 128) // 4, (b - 128) % 4
 
     ends = []
     so_far = jnp.int32(0)
@@ -196,13 +336,36 @@
 
     @pl.when(step == 0)
     def _():
-        for b in range(NBLOCKS):
-            ref, r, c = place(b)
-            pltpu.make_async_copy(
-                slots.at[owner[b]],
-                ref.at[pl.ds(r * SIDE, SIDE), pl.ds(c * SIDE, SIDE)],
-                sem.at[0 if b < 128 else 1],
-            ).start()
+        for piece, homes in zip(pieces, plan.gathered):
+            for j, home in enumerate(homes):
+                pltpu.make_async_copy(
+                    piece.at[j, pl.ds(plan.own * SIDE, TAIL), :], small_in.at[home], sem.at[0]
+                ).start()
+        for piece, homes in zip(pieces, plan.gathered):
+            for j, home in enumerate(homes):
+                for i in range(plan.own):
+                    r = block_row[home * plan.own + i]
+                    c = block_col[home * plan.own + i]
+
+                    def fetch(piece=piece, j=j, i=i, r=r, c=c):
+                        pltpu.make_async_copy(
+                            piece.at[j, pl.ds(i * SIDE, SIDE), :],
+                            w_wide.at[
+                                pl.ds(pl.multiple_of(r * SIDE, SIDE), SIDE),
+                                pl.ds(pl.multiple_of(c * SIDE, SIDE), SIDE),
+                            ],
+                            sem.at[1],
+                        ).start()
+
+                    if plan.empty:
+                        pl.when(c < ALL // SIDE)(fetch)
+                    else:
+                        fetch()
+        small[...] = jnp.zeros_like(small)
+        pltpu.make_async_copy(small_in, small_in, sem.at[0]).wait()
+        for home in range(plan.devices):
+            at = pl.ds(small_row[home], plan.small_rows)
+            small[at, :] = small[at, :] + small_in[home].astype(F32)[: plan.small_rows, :]
         for i in range(8):
             vecs[i : i + 1, :D] = jnp.concatenate(
                 [small[4 * i + j : 4 * i + j + 1, :] for j in range(4)], axis=1
@@ -216,8 +379,7 @@
         for w in range(WINDOWS):
             x_win[w * PAD + win + 1 : (w + 1) * PAD, :] = jnp.zeros((PAD - win - 1, D), F32)
             g_fin[w * PAD + win + 1 : (w + 1) * PAD, :] = jnp.zeros((PAD - win - 1, D), F32)
-        pltpu.make_async_copy(w_wide, w_wide, sem.at[0]).wait()
-        pltpu.make_async_copy(w_down, w_down, sem.at[1]).wait()
+        pltpu.make_async_copy(w_wide, w_wide, sem.at[1]).wait()
 
         normed, inverse = normalize(reg_in[...])
         reg_norm[...] = normed
@@ -327,7 +489,19 @@
         for c in range(FF // width):
             cols = slice(c * width, (c + 1) * width)
             up = w_wide[:, 4 * D + c * width : 4 * D + (c + 1) * width]
-            down = w_down[cols, :]
+            down = jnp.concatenate(
+                [
+                    jnp.concatenate(
+                        [
+                            w_wide[k * SIDE : (k + 1) * SIDE, WIDE + r * SIDE : WIDE + (r + 1) * SIDE]
+                            for k in range(D // SIDE)
+                        ],
+                        axis=1,
+                    )
+                    for r in range(c * width // SIDE, (c + 1) * width // SIDE)
+                ],
+                axis=0,
+            )
             pre = dot_nn(a_mlp, up) + vecs[8:9, cols]
             big_phi, phi = gauss(pre)
             act_b = (pre * big_phi).astype(BF16)
@@ -444,18 +618,17 @@
         ]
         for i, values in enumerate(rows_all):
             for j in range(4):
-                grad_small[4 * i + j : 4 * i + j + 1, :] = values[:, j * LANES : (j + 1) * LANES]
+                small[4 * i + j : 4 * i + j + 1, :] = values[:, j * LANES : (j + 1) * LANES]
         for j in range(FF // LANES):
-            grad_small[32 + j : 33 + j, :] = acc_up[:, j * LANES : (j + 1) * LANES]
+            small[32 + j : 33 + j, :] = acc_up[:, j * LANES : (j + 1) * LANES]
 
         a_reg = (normed * row(0) + row(1)).astype(BF16)
 
-        def copy_out(b, r, c):
-            return pltpu.make_async_copy(
-                stage.at[pl.ds(r * SIDE, SIDE), pl.ds(c * SIDE, SIDE)],
-                grad_slots.at[owner[b]],
-                sem.at[2],
-            )
+        for home in range(plan.devices):
+            part = small[pl.ds(small_row[home], plan.small_rows), :]
+            small_out[home] = jnp.concatenate(
+                [part, jnp.zeros((TAIL - plan.small_rows, LANES), F32)], axis=0
+            ).astype(BF16)
 
         def contract(left, right, cols):
             total = dot_nn(left[0], right[0:half, cols])
@@ -485,68 +658,66 @@
             stage[:, 3 * D + c * width : 3 * D + (c + 1) * width] = (
                 contract(ctx_t, g_mid, cols) + dot_tn(reg_ctx[...], grad_mid[:, cols])
             ).astype(BF16)
-        copies = []
-        for b in range(NBLOCKS):
-            ref, r, c = place(b)
-            if b >= 128:
-                r, c = c, WIDE // SIDE + r
-            copies.append(copy_out(b, r, c))
-        if total_slots > NBLOCKS:
-            w_down[:SIDE, :SIDE] = jnp.zeros((SIDE, SIDE), BF16)
-        for b in range(NBLOCKS, total_slots):
-            copies.append(
+        if plan.empty:
+            stage[:SIDE, ALL:] = jnp.zeros((SIDE, SIDE), BF16)
+        for n, (send, homes) in enumerate(zip(sends, plan.scattered)):
+            for j, home in enumerate(homes):
                 pltpu.make_async_copy(
-                    w_down.at[pl.ds(0, SIDE), pl.ds(0, SIDE)], grad_slots.at[owner[b]], sem.at[2]
-                )
-            )
-        for copy in copies:
-            copy.start()
-        pltpu.make_async_copy(grad_slots, grad_slots, sem.at[2]).wait()
-
-
-def layer(owner, shape, small, slots, regions, cot_regions, patches, cot_patches):
+                    small_out.at[home], send.at[j, pl.ds(plan.own * SIDE, TAIL), :], sem.at[2 + n]
+                ).start()
+                for i in range(plan.own):
+                    r = block_row[home * plan.own + i]
+                    c = block_col[home * plan.own + i]
+                    pltpu.make_async_copy(
+                        stage.at[
+                            pl.ds(pl.multiple_of(r * SIDE, SIDE), SIDE),
+                            pl.ds(pl.multiple_of(c * SIDE, SIDE), SIDE),
+                        ],
+                        send.at[j, pl.ds(i * SIDE, SIDE), :],
+                        sem.at[2 + n],
+                    ).start()
+        for n, send in enumerate(sends):
+            pltpu.make_async_copy(send, send, sem.at[2 + n]).wait()
+
+
+def layer(plan, block_row, block_col, small_row, shape, regions, cot_regions, patches, cot_patches, pieces):
     n_reg, win = patches.shape[:2]
     steps = n_reg // WINDOWS
     rows = WINDOWS * PAD
     half = rows // 2
     every = steps * rows
+    length = pieces[0].shape[1]
     whole = lambda i: (0, 0)
     block = pl.BlockSpec((WINDOWS, win, D), lambda i: (i, 0, 0))
     vec = lambda r, c, dtype=F32: pltpu.VMEM((r, c), dtype)
+    in_smem = pl.BlockSpec(memory_space=pltpu.SMEM)
+    in_place = pl.BlockSpec(memory_space=pl.ANY)
     return pl.pallas_call(
-        layer_kernel,
+        functools.partial(layer_kernel, plan),
         grid=(steps,),
-        in_specs=[
-            pl.BlockSpec(memory_space=pltpu.SMEM),
-            pl.BlockSpec(memory_space=pltpu.SMEM),
-            pl.BlockSpec(small.shape, whole),
-            pl.BlockSpec(memory_space=pl.ANY),
-            pl.BlockSpec(regions.shape, whole),
-            pl.BlockSpec(cot_regions.shape, whole),
-            block,
-            block,
-        ],
+        in_specs=[in_smem] * 4
+        + [pl.BlockSpec(regions.shape, whole), pl.BlockSpec(regions.shape, whole), block, block]
+        + [in_place] * len(pieces),
         out_specs=[
             pl.BlockSpec(regions.shape, whole),
             block,
             pl.BlockSpec(regions.shape, whole),
             block,
-            pl.BlockSpec(memory_space=pl.ANY),
-            pl.BlockSpec(small.shape, whole),
-        ],
+        ]
+        + [in_place] * len(plan.scattered),
         out_shape=[
             jax.ShapeDtypeStruct(regions.shape, BF16),
             jax.ShapeDtypeStruct(patches.shape, BF16),
             jax.ShapeDtypeStruct(regions.shape, BF16),
             jax.ShapeDtypeStruct(patches.shape, BF16),
-            jax.ShapeDtypeStruct(slots.shape, BF16),
-            jax.ShapeDtypeStruct(small.shape, F32),
-        ],
+        ]
+        + [jax.ShapeDtypeStruct((len(h), length, LANES), BF16) for h in plan.scattered],
         scratch_shapes=[
-            vec(D, WIDE, BF16),
-            vec(FF, D, BF16),
-            vec(16, FF),
-            vec(REG_PAD, D),
+            vec(D, ALL, BF16),
+            pltpu.VMEM((plan.devices, TAIL, LANES), BF16),
+            vec(56, LANES),
+            pltpu.VMEM((plan.devices, TAIL, LANES), BF16),
+            vec(16, FF),            vec(REG_PAD, D),
             vec(REG_PAD, D),
             vec(REG_PAD, D),
             vec(REG_PAD, D),
@@ -577,14 +748,14 @@
             vec(8, D),
             vec(1, FF),
             vec(1, 3 * D),
-            vec(D, WIDE + FF, BF16),
-            pltpu.SemaphoreType.DMA((3,)),
+            vec(D, ALL + SIDE, BF16),
+            pltpu.SemaphoreType.DMA((2 + len(plan.scattered),)),
         ],
         compiler_params=pltpu.CompilerParams(
             dimension_semantics=("arbitrary",), vmem_limit_bytes=VMEM_LIMIT
         ),
         name="layer",
-    )(owner, shape, small, slots, regions, cot_regions, patches, cot_patches)
+    )(block_row, block_col, small_row, shape, regions, cot_regions, patches, cot_patches, *pieces)
 
 
 def shards(
@@ -603,23 +774,36 @@
 ):
     axes = ("dp", "fsdp")
     devices = lax.axis_size(axes)
-    me = lax.axis_index(axes)
-    mine = small.shape[0]
-    own_slots = slot_weights.shape[0]
-    slots = lax.all_gather(slot_weights.astype(BF16), axes, axis=0, tiled=True)
-    small_all = lax.all_gather(small.astype(BF16), axes, axis=0, tiled=True).astype(F32)
-    out_regions, out_patches, grad_regions, grad_patches, grad_slots, grad_small = layer(
-        owner,
+    entries = small.shape[0]
+    own = slot_weights.shape[0]
+    plan = Plan(lax.axis_size("dp"), lax.axis_size("fsdp"), own, entries)
+    offset = lax.rem(lax.axis_index(axes) * entries, LANES)
+    tail = lax.dynamic_update_slice(jnp.zeros(TAIL * LANES, BF16), small.astype(BF16), (offset,))
+    mine = jnp.concatenate(
+        [slot_weights.astype(BF16).reshape(own * SIDE, LANES), tail.reshape(TAIL, LANES)], axis=0
+    )
+    pieces = plan.gather(mine)
+    homes = plan.device_of_homes(lax.axis_index("dp"), lax.axis_index("fsdp"))
+    spots = (homes[:, None] * own + jnp.arange(own, dtype=jnp.int32)[None, :]).reshape(-1)
+    numbers = jnp.arange(owner.shape[0], dtype=jnp.int32)
+    block = jnp.sum(jnp.where(owner[None, :] == spots[:, None], numbers[None, :], 0), axis=1)
+    block_row, block_col = block_places(block)
+    small_row = homes * entries // LANES
+    out_regions, out_patches, grad_regions, grad_patches, *sends = layer(
+        plan,
+        block_row,
+        block_col,
+        small_row,
         image_shape,
-        small_all.reshape(-1, LANES),
-        slots,
         regions,
         cot_regions,
         patches,
         cot_patches,
+        pieces,
     )
-    grad_slot = lax.psum_scatter(grad_slots, axes, scatter_dimension=0, tiled=True).astype(F32)
-    grad_small = lax.psum_scatter(grad_small.reshape(-1), axes, scatter_dimension=0, tiled=True)
+    received = plan.scatter(sends)
+    grad_slot = received[: own * SIDE].reshape(own, SIDE, SIDE)
+    grad_small = lax.dynamic_slice(received[own * SIDE :].reshape(-1), (offset,), (entries,))
     precise = lax.Precision.HIGHEST
     left_stat = jnp.einsum("sij,skj->sik", grad_slot, grad_slot, precision=precise)
     right_stat = jnp.einsum("sji,sjk->sik", grad_slot, grad_slot, precision=precise)

time: 318 us -> 227 us (0.71)
  blocking collectives: 81.8 us -> 0 us
  starting transfers between devices: 0.08 us -> 23.1 us
  waiting for transfers between devices: 95.1 us -> 73.3 us
  between operations: 14.2 us -> 1.03 us
    unnamed x2 -> x0, blocking collectives: 81.8 us -> none
    ppermute x0 -> x30, waiting for transfers between devices: none -> 73.3 us  [the longest x3 22.7 us: gather(): behind = lax.ppermute(behind, 'fsdp', self.backward)]
    reduce_scatter x1 -> x0, waiting for transfers between devices: 68.7 us -> none  [shards(): lax.psum_scatter(grad_slots, axes, scatter_dimension=0, tiled=True)]
    all_gather x1 -> x0, waiting for transfers between devices: 26.4 us -> none  [shards(): slots = lax.all_gather(slot_weights.astype(BF16), axes, axis=0, tiled=True)]
    ppermute x0 -> x30, starting transfers between devices: none -> 23.1 us  [the longest x3 4.4 us: gather(): behind = lax.ppermute(behind, 'fsdp', self.backward)]
    unnamed x32 -> x58, local copies, waits for them, and re-layouts: 10.7 us -> 8.36 us
  transfers between devices with their start and end apart: 2 -> 30, of which waited for: 2 -> 17; matrix products, arithmetic and copies ran while one was open for 3% -> 5% of each run, Pallas kernels for 0% -> 0%
where the time goes in v2:
time: 227 us
  Pallas kernels  109 us (48%)
  waiting for transfers between devices  73.3 us (32%)
  starting transfers between devices  23.1 us (10%)
  local copies, waits for them, and re-layouts  9.75 us (4%)
  other arithmetic  7.75 us (3%)
  matrix products  2.86 us (1%)
    pallas_call x1, Pallas kernels, layer(): pl.pallas_call(functools.partial(layer_kernel, plan), grid=(steps,), in_s...  109 us
    ppermute x3, waiting for transfers between devices, gather(): behind = lax.ppermute(behind, 'fsdp', self.backward)  22.7 us
    ppermute x3, waiting for transfers between devices, scatter(): ahead = lax.ppermute(ahead, 'fsdp', self.forward)  18.5 us
    ppermute x3, waiting for transfers between devices, scatter(): behind = lax.ppermute(behind, 'fsdp', self.backward)  11.7 us
    unnamed x58, local copies, waits for them, and re-layouts  8.36 us
    ppermute x1, waiting for transfers between devices, scatter(): ahead = lax.ppermute(far[:m], 'fsdp', self.forward)  5 us
    ppermute x1, waiting for transfers between devices, gather(): stack.append(lax.ppermute(mine[None], 'dp', self.shift(-by)))  4.99 us
  transfers between devices with their start and end apart: 30, of which 17 were waited for; matrix products, arithmetic and copies ran while one was open for 5% of the time, Pallas kernels for 0%

profile of v2, /device:TPU:0, one launch (start us, length us, event | category | flops | bytes accessed | tf_op | source)
XLA Modules:
  0.0 227.0 jit_solution(17342879522295574694)
XLA Ops:
  1.5 1.3 multiply_reduce_fusion.1
  3.0 3.0 %collective-permute-start = (bf16[1,784,128]{2,1,0:T(8,128)(2,1)S(1)}, bf16[1,784,128]{2,1,0:T(8,128)(2,1)S(1)}, u32[]{:S(2)}, u32[]{:S(2)}) collective-permute-start(bf16[1,784,128]{2,1,0:T(8,128)(2,1)S(1)} %maximum_bitcast_fusion), channel_id=1, source_target_pairs={{0,16},{8,24},{16,0},{24,8},{1,17},{9,25},{17,1},{25,9},{2,18},{10... | collective-permute-start | bytes 602120 | tf_op jit(solution)/shard_map/ppermute | solution.py:175
  6.0 5.0 %collective-permute-done = bf16[1,784,128]{2,1,0:T(8,128)(2,1)S(1)} collective-permute-done((bf16[1,784,128]{2,1,0:T(8,128)(2,1)S(1)}, bf16[1,784,128]{2,1,0:T(8,128)(2,1)S(1)}, u32[]{:S(2)}, u32[]{:S(2)}) %collective-permute-start) | collective-permute-done | bytes 200736 | tf_op jit(solution)/shard_map/ppermute | solution.py:175
  11.1 1.8 collective-permute-start.2
  13.2 8.6 %collective-permute-done.2.rest_2_ = bf16[2,784,128]{2,1,0:T(8,128)(2,1)} collective-permute-done((bf16[2,784,128]{2,1,0:T(8,128)(2,1)S(1)}, bf16[2,784,128]{2,1,0:T(8,128)(2,1)}, u32[]{:S(2)}, u32[]{:S(2)}) %collective-permute-start.2) | collective-permute-done | bytes 401440 | tf_op jit(solution)/shard_map/ppermute | solution.py:182
  21.7 1.5 collective-permute-start.4
  23.8 7.8 %collective-permute-done.4.rest_4_ = bf16[2,784,128]{2,1,0:T(8,128)(2,1)} collective-permute-done((bf16[2,784,128]{2,1,0:T(8,128)(2,1)}, bf16[2,784,128]{2,1,0:T(8,128)(2,1)}, u32[]{:S(2)}, u32[]{:S(2)}) %collective-permute-start.4) | collective-permute-done | bytes 401440 | tf_op jit(solution)/shard_map/ppermute | solution.py:182
  31.6 1.1 collective-permute-start.6
  34.1 6.3 %collective-permute-done.6.rest_6_ = bf16[2,784,128]{2,1,0:T(8,128)(2,1)S(1)} collective-permute-done((bf16[2,784,128]{2,1,0:T(8,128)(2,1)}, bf16[2,784,128]{2,1,0:T(8,128)(2,1)S(1)}, u32[]{:S(2)}, u32[]{:S(2)}) %collective-permute-start.6) | collective-permute-done | bytes 401440 | tf_op jit(solution)/shard_map/ppermute | solution.py:182
  41.4 1.5 copy.42.patches
  42.9 1.5 copy.43.cot_patches
  46.8 1.2 collective-permute-start.7
  49.3 3.7 %collective-permute-done.8.rest_8_ = bf16[1,784,128]{2,1,0:T(8,128)(2,1)S(1)} collective-permute-done((bf16[1,784,128]{2,1,0:T(8,128)(2,1)S(1)}, bf16[1,784,128]{2,1,0:T(8,128)(2,1)S(1)}, u32[]{:S(2)}, u32[]{:S(2)}) %collective-permute-start.8) | collective-permute-done | bytes 200736 | tf_op jit(solution)/shard_map/ppermute | solution.py:185
  55.7 109.3 %layer.1 = (bf16[24,512]{1,0:T(8,128)(2,1)}, bf16[24,49,512]{2,1,0:T(8,128)(2,1)}, bf16[24,512]{1,0:T(8,128)(2,1)}, bf16[24,49,512]{2,1,0:T(8,128)(2,1)}, bf16[6...) custom-call(s32[192]{0:T(256)} %get-tuple-element.78.block_row, ...), custom_call_target="tpu_custom_call" | custom-call | tf_op jit(solution)/shard_map/layer/pallas_call | solution.py:695
  165.6 2.6 %collective-permute-done.20 = bf16[6,784,128]{2,1,0:T(8,128)(2,1)S(1)} collective-permute-done((bf16[6,784,128]{2,1,0:T(8,128)(2,1)}, bf16[6,784,128]{2,1,0:T(8,128)(2,1)S(1)}, u32[]{:S(2)}, u32[]{:S(2)}) %collective-permute-start.20) | collective-permute-done | bytes 1204256 | tf_op jit(solution)/shard_map/ppermute | solution.py:190
  168.2 1.1 add_convert_fusion.6
  169.4 1.2 collective-permute-start.21
  171.5 5.0 %collective-permute-done.21 = bf16[1,784,128]{2,1,0:T(8,128)(2,1)S(1)} collective-permute-done((bf16[1,784,128]{2,1,0:T(8,128)(2,1)S(1)}, bf16[1,784,128]{2,1,0:T(8,128)(2,1)S(1)}, u32[]{:S(2)}, u32[]{:S(2)}) %collective-permute-start.21) | collective-permute-done | bytes 200736 | tf_op jit(solution)/shard_map/ppermute | solution.py:199
  177.7 1.1 collective-permute-start.22
  179.8 8.2 %collective-permute-done.22 = bf16[2,784,128]{2,1,0:T(8,128)(2,1)S(1)} collective-permute-done((bf16[2,784,128]{2,1,0:T(8,128)(2,1)S(1)}, bf16[2,784,128]{2,1,0:T(8,128)(2,1)S(1)}, u32[]{:S(2)}, u32[]{:S(2)}) %collective-permute-start.22) | collective-permute-done | bytes 401440 | tf_op jit(solution)/shard_map/ppermute | solution.py:207
  188.1 1.3 collective-permute-start.23
  189.4 8.1 %collective-permute-done.23 = bf16[2,784,128]{2,1,0:T(8,128)(2,1)S(1)} collective-permute-done((bf16[2,784,128]{2,1,0:T(8,128)(2,1)S(1)}, bf16[2,784,128]{2,1,0:T(8,128)(2,1)S(1)}, u32[]{:S(2)}, u32[]{:S(2)}) %collective-permute-start.23) | collective-permute-done | bytes 401440 | tf_op jit(solution)/shard_map/ppermute | solution.py:207
  197.8 1.1 collective-permute-start.27
  199.9 7.2 %collective-permute-done.27 = bf16[2,784,128]{2,1,0:T(8,128)(2,1)S(1)} collective-permute-done((bf16[2,784,128]{2,1,0:T(8,128)(2,1)S(1)}, bf16[2,784,128]{2,1,0:T(8,128)(2,1)S(1)}, u32[]{:S(2)}, u32[]{:S(2)}) %collective-permute-start.27) | collective-permute-done | bytes 401440 | tf_op jit(solution)/shard_map/ppermute | solution.py:208
  207.3 1.1 collective-permute-start.28
  208.4 2.3 collective-permute-done.24
  210.7 4.5 %collective-permute-done.28 = bf16[2,784,128]{2,1,0:T(8,128)(2,1)S(1)} collective-permute-done((bf16[2,784,128]{2,1,0:T(8,128)(2,1)S(1)}, bf16[2,784,128]{2,1,0:T(8,128)(2,1)S(1)}, u32[]{:S(2)}, u32[]{:S(2)}) %collective-permute-start.28) | collective-permute-done | bytes 401440 | tf_op jit(solution)/shard_map/ppermute | solution.py:208
  215.5 1.1 collective-permute-start.29
  216.6 1.4 copy.50
  218.0 1.4 copy.51
  219.4 1.9 collective-permute-done.29
  226.0 1.0 multiply_add_fusion
  (120 shorter events, 20.8 us)
Async XLA Ops:
  0.6 39.8 %copy-start.21 = (s32[6,2]{0,1:T(2,128)S(1)}, s32[6,2]{0,1:T(2,128)}, u32[]{:S(2)}) copy-start(s32[6,2]{0,1:T(2,128)} %param.16) | copy-start | bytes 148
  0.7 40.8 %copy-start.6 = (bf16[24,49,512]{2,0,1:T(8,128)(2,1)S(1)}, bf16[24,49,512]{2,0,1:T(8,128)(2,1)}, u32[]{:S(2)}) copy-start(bf16[24,49,512]{2,0,1:T(8,128)(2,1)} %param.13) | copy-start | bytes 3612676
  3.0 8.0 %collective-permute-start = (bf16[1,784,128]{2,1,0:T(8,128)(2,1)S(1)}, bf16[1,784,128]{2,1,0:T(8,128)(2,1)S(1)}, u32[]{:S(2)}, u32[]{:S(2)}) collective-permute-start(bf16[1,784,128]{2,1,0:T(8,128)(2,1)S(1)} %maximum_bitcast_fusion), channel_id=1, source_target_pairs={{0,16},{8,24},{16,0},{24,8},{1,17},{9,25},{17,1},{25,9},{2,18},{10... | collective-permute-start | bytes 602120 | tf_op jit(solution)/shard_map/ppermute | solution.py:175
  11.1 10.6 %collective-permute-start.2 = (bf16[2,784,128]{2,1,0:T(8,128)(2,1)S(1)}, bf16[2,784,128]{2,1,0:T(8,128)(2,1)}, u32[]{:S(2)}, u32[]{:S(2)}) collective-permute-start(bf16[2,784,128]{2,1,0:T(8,128)(2,1)S(1)} %pad_maximum_fusion.rest_0_), channel_id=1, source_target_pairs={{0,1},{2,0},{4,2},{6,4},{7,6},{5,7},{3,5},{1,3},{8,9},{10,8},{12,1... | collective-permute-start | bytes 1204232 | tf_op jit(solution)/shard_map/ppermute | solution.py:182
  12.9 10.3 %collective-permute-start.1 = (bf16[2,784,128]{2,1,0:T(8,128)(2,1)S(1)}, bf16[2,784,128]{2,1,0:T(8,128)(2,1)}, u32[]{:S(2)}, u32[]{:S(2)}) collective-permute-start(bf16[2,784,128]{2,1,0:T(8,128)(2,1)S(1)} %pad_maximum_fusion.rest_0_), channel_id=1, source_target_pairs={{0,2},{2,4},{4,6},{6,7},{7,5},{5,3},{3,1},{1,0},{8,10},{10,12},{12... | collective-permute-start | bytes 1204232 | tf_op jit(solution)/shard_map/ppermute | solution.py:181
  21.7 9.9 %collective-permute-start.4 = (bf16[2,784,128]{2,1,0:T(8,128)(2,1)}, bf16[2,784,128]{2,1,0:T(8,128)(2,1)}, u32[]{:S(2)}, u32[]{:S(2)}) collective-permute-start(bf16[2,784,128]{2,1,0:T(8,128)(2,1)} %collective-permute-done.2.rest_2_), channel_id=1, source_target_pairs={{0,1},{2,0},{4,2},{6,4},{7,6},{5,7},{3,5},{1,3},{8,9},{10,8},{12,1... | collective-permute-start | bytes 1204232 | tf_op jit(solution)/shard_map/ppermute | solution.py:182
  23.2 9.6 %collective-permute-start.3 = (bf16[2,784,128]{2,1,0:T(8,128)(2,1)}, bf16[2,784,128]{2,1,0:T(8,128)(2,1)}, u32[]{:S(2)}, u32[]{:S(2)}) collective-permute-start(bf16[2,784,128]{2,1,0:T(8,128)(2,1)} %collective-permute-done.1.rest_1_), channel_id=1, source_target_pairs={{0,2},{2,4},{4,6},{6,7},{7,5},{5,3},{3,1},{1,0},{8,10},{10,12},{12... | collective-permute-start | bytes 1204232 | tf_op jit(solution)/shard_map/ppermute | solution.py:181
  31.6 8.8 %collective-permute-start.6 = (bf16[2,784,128]{2,1,0:T(8,128)(2,1)}, bf16[2,784,128]{2,1,0:T(8,128)(2,1)S(1)}, u32[]{:S(2)}, u32[]{:S(2)}) collective-permute-start(bf16[2,784,128]{2,1,0:T(8,128)(2,1)} %collective-permute-done.4.rest_4_), channel_id=1, source_target_pairs={{0,1},{2,0},{4,2},{6,4},{7,6},{5,7},{3,5},{1,3},{8,9},{10,8},{12,1... | collective-permute-start | bytes 1204232 | tf_op jit(solution)/shard_map/ppermute | solution.py:182
  32.7 11.7 %collective-permute-start.5 = (bf16[2,784,128]{2,1,0:T(8,128)(2,1)}, bf16[2,784,128]{2,1,0:T(8,128)(2,1)}, u32[]{:S(2)}, u32[]{:S(2)}) collective-permute-start(bf16[2,784,128]{2,1,0:T(8,128)(2,1)} %collective-permute-done.3.rest_3_), channel_id=1, source_target_pairs={{0,2},{2,4},{4,6},{6,7},{7,5},{5,3},{3,1},{1,0},{8,10},{10,12},{12... | collective-permute-start | bytes 1204232 | tf_op jit(solution)/shard_map/ppermute | solution.py:181
  33.6 12.3 %collective-permute-start.9 = (bf16[2,784,128]{2,1,0:T(8,128)(2,1)S(1)}, bf16[2,784,128]{2,1,0:T(8,128)(2,1)}, u32[]{:S(2)}, u32[]{:S(2)}) collective-permute-start(bf16[2,784,128]{2,1,0:T(8,128)(2,1)S(1)} %pad_maximum_fusion.rest_0_), channel_id=1, source_target_pairs={{0,8},{8,0},{16,24},{24,16},{1,9},{9,1},{17,25},{25,17},{2,10},{10... | collective-permute-start | bytes 1204232 | tf_op jit(solution)/shard_map/ppermute | solution.py:186
  33.6 13.2 %collective-permute-start.11 = (bf16[2,784,128]{2,1,0:T(8,128)(2,1)}, bf16[2,784,128]{2,1,0:T(8,128)(2,1)}, u32[]{:S(2)}, u32[]{:S(2)}) collective-permute-start(bf16[2,784,128]{2,1,0:T(8,128)(2,1)} %collective-permute-done.2.rest_2_), channel_id=1, source_target_pairs={{0,8},{8,0},{16,24},{24,16},{1,9},{9,1},{17,25},{25,17},{2,10},{10... | collective-permute-start | bytes 1204232 | tf_op jit(solution)/shard_map/ppermute | solution.py:186
  34.1 13.9 %collective-permute-start.10 = (bf16[2,784,128]{2,1,0:T(8,128)(2,1)}, bf16[2,784,128]{2,1,0:T(8,128)(2,1)}, u32[]{:S(2)}, u32[]{:S(2)}) collective-permute-start(bf16[2,784,128]{2,1,0:T(8,128)(2,1)} %collective-permute-done.1.rest_1_), channel_id=1, source_target_pairs={{0,8},{8,0},{16,24},{24,16},{1,9},{9,1},{17,25},{25,17},{2,10},{10... | collective-permute-start | bytes 1204232 | tf_op jit(solution)/shard_map/ppermute | solution.py:186
  40.4 7.6 %collective-permute-start.13 = (bf16[2,784,128]{2,1,0:T(8,128)(2,1)}, bf16[2,784,128]{2,1,0:T(8,128)(2,1)}, u32[]{:S(2)}, u32[]{:S(2)}) collective-permute-start(bf16[2,784,128]{2,1,0:T(8,128)(2,1)} %collective-permute-done.4.rest_4_), channel_id=1, source_target_pairs={{0,8},{8,0},{16,24},{24,16},{1,9},{9,1},{17,25},{25,17},{2,10},{10... | collective-permute-start | bytes 1204232 | tf_op jit(solution)/shard_map/ppermute | solution.py:186
  44.5 9.7 %collective-permute-start.12 = (bf16[2,784,128]{2,1,0:T(8,128)(2,1)}, bf16[2,784,128]{2,1,0:T(8,128)(2,1)S(1)}, u32[]{:S(2)}, u32[]{:S(2)}) collective-permute-start(bf16[2,784,128]{2,1,0:T(8,128)(2,1)} %collective-permute-done.3.rest_3_), channel_id=1, source_target_pairs={{0,8},{8,0},{16,24},{24,16},{1,9},{9,1},{17,25},{25,17},{2,10},{10... | collective-permute-start | bytes 1204232 | tf_op jit(solution)/shard_map/ppermute | solution.py:186
  45.9 7.0 %collective-permute-start.8 = (bf16[1,784,128]{2,1,0:T(8,128)(2,1)S(1)}, bf16[1,784,128]{2,1,0:T(8,128)(2,1)S(1)}, u32[]{:S(2)}, u32[]{:S(2)}) collective-permute-start(bf16[1,784,128]{2,1,0:T(8,128)(2,1)S(1)} %slice.98), channel_id=1, source_target_pairs={{0,1},{2,0},{4,2},{6,4},{7,6},{5,7},{3,5},{1,3},{8,9},{10,8},{12,1... | collective-permute-start | bytes 602120 | tf_op jit(solution)/shard_map/ppermute | solution.py:185
  46.8 6.7 %collective-permute-start.7 = (bf16[1,784,128]{2,1,0:T(8,128)(2,1)S(1)}, bf16[1,784,128]{2,1,0:T(8,128)(2,1)S(1)}, u32[]{:S(2)}, u32[]{:S(2)}) collective-permute-start(bf16[1,784,128]{2,1,0:T(8,128)(2,1)S(1)} %slice.97), channel_id=1, source_target_pairs={{0,2},{2,4},{4,6},{6,7},{7,5},{5,3},{3,1},{1,0},{8,10},{10,12},{12... | collective-permute-start | bytes 602120 | tf_op jit(solution)/shard_map/ppermute | solution.py:184
  48.0 6.4 %collective-permute-start.15 = (bf16[2,784,128]{2,1,0:T(8,128)(2,1)S(1)}, bf16[2,784,128]{2,1,0:T(8,128)(2,1)S(1)}, u32[]{:S(2)}, u32[]{:S(2)}) collective-permute-start(bf16[2,784,128]{2,1,0:T(8,128)(2,1)S(1)} %collective-permute-done.6.rest_6_), channel_id=1, source_target_pairs={{0,8},{8,0},{16,24},{24,16},{1,9},{9,1},{17,25},{25,17},{2,10},{10... | collective-permute-start | bytes 1204232 | tf_op jit(solution)/shard_map/ppermute | solution.py:186
  48.0 6.9 %collective-permute-start.14 = (bf16[2,784,128]{2,1,0:T(8,128)(2,1)}, bf16[2,784,128]{2,1,0:T(8,128)(2,1)S(1)}, u32[]{:S(2)}, u32[]{:S(2)}) collective-permute-start(bf16[2,784,128]{2,1,0:T(8,128)(2,1)} %collective-permute-done.5.rest_5_), channel_id=1, source_target_pairs={{0,8},{8,0},{16,24},{24,16},{1,9},{9,1},{17,25},{25,17},{2,10},{10... | collective-permute-start | bytes 1204232 | tf_op jit(solution)/shard_map/ppermute | solution.py:186
  52.9 1.4 collective-permute-start.17
  53.5 1.4 collective-permute-start.16
  165.1 3.2 %collective-permute-start.20 = (bf16[6,784,128]{2,1,0:T(8,128)(2,1)}, bf16[6,784,128]{2,1,0:T(8,128)(2,1)S(1)}, u32[]{:S(2)}, u32[]{:S(2)}) collective-permute-start(bf16[6,784,128]{2,1,0:T(8,128)(2,1)} %get-tuple-element.30), channel_id=1, source_target_pairs={{0,8},{8,0},{16,24},{24,16},{1,9},{9,1},{17,25},{25,17},{2,10},{10... | collective-permute-start | bytes 3612680 | tf_op jit(solution)/shard_map/ppermute | solution.py:190
  165.3 14.5 %collective-permute-start.19 = (bf16[8,784,128]{2,1,0:T(8,128)(2,1)}, bf16[8,784,128]{2,1,0:T(8,128)(2,1)S(1)}, u32[]{:S(2)}, u32[]{:S(2)}) collective-permute-start(bf16[8,784,128]{2,1,0:T(8,128)(2,1)} %get-tuple-element.28), channel_id=1, source_target_pairs={{0,8},{8,0},{16,24},{24,16},{1,9},{9,1},{17,25},{25,17},{2,10},{10... | collective-permute-start | bytes 4816904 | tf_op jit(solution)/shard_map/ppermute | solution.py:190
  169.4 7.1 %collective-permute-start.21 = (bf16[1,784,128]{2,1,0:T(8,128)(2,1)S(1)}, bf16[1,784,128]{2,1,0:T(8,128)(2,1)S(1)}, u32[]{:S(2)}, u32[]{:S(2)}) collective-permute-start(bf16[1,784,128]{2,1,0:T(8,128)(2,1)S(1)} %get-tuple-element.73), channel_id=1, source_target_pairs={{0,2},{2,4},{4,6},{6,7},{7,5},{5,3},{3,1},{1,0},{8,10},{10,12},{12... | collective-permute-start | bytes 602120 | tf_op jit(solution)/shard_map/ppermute | solution.py:199
  170.6 6.8 %collective-permute-start.25 = (bf16[1,784,128]{2,1,0:T(8,128)(2,1)S(1)}, bf16[1,784,128]{2,1,0:T(8,128)(2,1)S(1)}, u32[]{:S(2)}, u32[]{:S(2)}) collective-permute-start(bf16[1,784,128]{2,1,0:T(8,128)(2,1)S(1)} %get-tuple-element.74), channel_id=1, source_target_pairs={{0,1},{2,0},{4,2},{6,4},{7,6},{5,7},{3,5},{1,3},{8,9},{10,8},{12,1... | collective-permute-start | bytes 602120 | tf_op jit(solution)/shard_map/ppermute | solution.py:200
  177.7 10.3 %collective-permute-start.22 = (bf16[2,784,128]{2,1,0:T(8,128)(2,1)S(1)}, bf16[2,784,128]{2,1,0:T(8,128)(2,1)S(1)}, u32[]{:S(2)}, u32[]{:S(2)}) collective-permute-start(bf16[2,784,128]{2,1,0:T(8,128)(2,1)S(1)} %get-tuple-element.71), channel_id=1, source_target_pairs={{0,2},{2,4},{4,6},{6,7},{7,5},{5,3},{3,1},{1,0},{8,10},{10,12},{12... | collective-permute-start | bytes 1204232 | tf_op jit(solution)/shard_map/ppermute | solution.py:207
  178.8 10.6 %collective-permute-start.26 = (bf16[2,784,128]{2,1,0:T(8,128)(2,1)S(1)}, bf16[2,784,128]{2,1,0:T(8,128)(2,1)S(1)}, u32[]{:S(2)}, u32[]{:S(2)}) collective-permute-start(bf16[2,784,128]{2,1,0:T(8,128)(2,1)S(1)} %get-tuple-element.72), channel_id=1, source_target_pairs={{0,1},{2,0},{4,2},{6,4},{7,6},{5,7},{3,5},{1,3},{8,9},{10,8},{12,1... | collective-permute-start | bytes 1204232 | tf_op jit(solution)/shard_map/ppermute | solution.py:208
  188.1 9.3 %collective-permute-start.23 = (bf16[2,784,128]{2,1,0:T(8,128)(2,1)S(1)}, bf16[2,784,128]{2,1,0:T(8,128)(2,1)S(1)}, u32[]{:S(2)}, u32[]{:S(2)}) collective-permute-start(bf16[2,784,128]{2,1,0:T(8,128)(2,1)S(1)} %add_convert_fusion.4), channel_id=1, source_target_pairs={{0,2},{2,4},{4,6},{6,7},{7,5},{5,3},{3,1},{1,0},{8,10},{10,12},{12... | collective-permute-start | bytes 1204232 | tf_op jit(solution)/shard_map/ppermute | solution.py:207
  197.8 9.2 %collective-permute-start.27 = (bf16[2,784,128]{2,1,0:T(8,128)(2,1)S(1)}, bf16[2,784,128]{2,1,0:T(8,128)(2,1)S(1)}, u32[]{:S(2)}, u32[]{:S(2)}) collective-permute-start(bf16[2,784,128]{2,1,0:T(8,128)(2,1)S(1)} %get-tuple-element.70), channel_id=1, source_target_pairs={{0,1},{2,0},{4,2},{6,4},{7,6},{5,7},{3,5},{1,3},{8,9},{10,8},{12,1... | collective-permute-start | bytes 1204232 | tf_op jit(solution)/shard_map/ppermute | solution.py:208
  199.0 9.5 %collective-permute-start.18 = (bf16[2,784,128]{2,1,0:T(8,128)(2,1)S(1)}, bf16[2,784,128]{2,1,0:T(8,128)(2,1)S(1)}, u32[]{:S(2)}, u32[]{:S(2)}) collective-permute-start(bf16[2,784,128]{2,1,0:T(8,128)(2,1)S(1)} %copy-done.25), channel_id=1, source_target_pairs={{0,8},{8,0},{16,24},{24,16},{1,9},{9,1},{17,25},{25,17},{2,10},{10... | collective-permute-start | bytes 1204232 | tf_op jit(solution)/shard_map/ppermute | solution.py:190
  199.0 11.7 %collective-permute-start.24 = (bf16[2,784,128]{2,1,0:T(8,128)(2,1)S(1)}, bf16[2,784,128]{2,1,0:T(8,128)(2,1)S(1)}, u32[]{:S(2)}, u32[]{:S(2)}) collective-permute-start(bf16[2,784,128]{2,1,0:T(8,128)(2,1)S(1)} %get-tuple-element.69), channel_id=1, source_target_pairs={{0,2},{2,4},{4,6},{6,7},{7,5},{5,3},{3,1},{1,0},{8,10},{10,12},{12... | collective-permute-start | bytes 1204232 | tf_op jit(solution)/shard_map/ppermute | solution.py:207
  207.3 7.9 %collective-permute-start.28 = (bf16[2,784,128]{2,1,0:T(8,128)(2,1)S(1)}, bf16[2,784,128]{2,1,0:T(8,128)(2,1)S(1)}, u32[]{:S(2)}, u32[]{:S(2)}) collective-permute-start(bf16[2,784,128]{2,1,0:T(8,128)(2,1)S(1)} %add_convert_fusion), channel_id=1, source_target_pairs={{0,1},{2,0},{4,2},{6,4},{7,6},{5,7},{3,5},{1,3},{8,9},{10,8},{12,1... | collective-permute-start | bytes 1204232 | tf_op jit(solution)/shard_map/ppermute | solution.py:208
  215.5 5.8 %collective-permute-start.29 = (bf16[784,128]{1,0:T(8,128)(2,1)S(1)}, bf16[784,128]{1,0:T(8,128)(2,1)S(1)}, u32[]{:S(2)}, u32[]{:S(2)}) collective-permute-start(bf16[784,128]{1,0:T(8,128)(2,1)S(1)} %fusion.8), channel_id=1, source_target_pairs={{0,16},{8,24},{16,0},{24,8},{1,17},{9,25},{17,1},{25,9},{2,18},{10... | collective-permute-start | bytes 602120 | tf_op jit(solution)/shard_map/ppermute | solution.py:212
  (24 other events, 158.5 us)

commit v3 on v2

--- a/solution.py
+++ b/solution.py
@@ -66,15 +66,8 @@
 
 
 def gauss(values):
-    size = jnp.abs(values)
-    t = 1.0 / (1.0 + (0.3275911 * 0.7071067811865476) * size)
-    bell = jnp.exp(-0.5 * values * values)
-    poly = t * (
-        0.127414796
-        + t * (-0.142248368 + t * (0.7107068705 + t * (-0.7265760135 + t * 0.5307027145)))
-    )
-    tail = poly * bell
-    return jnp.where(values >= 0.0, 1.0 - tail, tail), bell * 0.3989422804014327
+    big_phi = 0.5 * (1.0 + lax.erf(values * 0.7071067811865476))
+    return big_phi, jnp.exp(-0.5 * values * values) * 0.3989422804014327
 
 
 def head_masks(rows, dtype):
@@ -467,7 +460,7 @@
             ctx[at, h * LANES : (h + 1) * LANES] = context.astype(BF16)
         return carry
 
-    lax.fori_loop(0, WINDOWS, window_attend, 0)
+    lax.fori_loop(0, WINDOWS, window_attend, 0, unroll=True)
 
     def perceptron(i, carry):
         at = pl.ds(pl.multiple_of(i * half, half), half)
@@ -483,8 +476,6 @@
         grad_final = g_fin[at, :]
         grad_b = grad_final.astype(BF16)
         acc[7:8, :] = acc[7:8, :] + jnp.sum(grad_final, axis=0, keepdims=True)
-        final = middle + row(7)
-        grad_a = jnp.zeros((half, D), F32)
         width = 256
         for c in range(FF // width):
             cols = slice(c * width, (c + 1) * width)
@@ -512,8 +503,21 @@
             acc_up[:, cols] = acc_up[:, cols] + jnp.sum(
                 grad_pre.astype(F32), axis=0, keepdims=True
             )
-            final = final + dot_nn(act_b, down)
-            grad_a = grad_a + dot_nt(grad_pre, up)
+        down = jnp.concatenate(
+            [
+                jnp.concatenate(
+                    [
+                        w_wide[k * SIDE : (k + 1) * SIDE, WIDE + r * SIDE : WIDE + (r + 1) * SIDE]
+                        for k in range(D // SIDE)
+                    ],
+                    axis=1,
+                )
+                for r in range(FF // SIDE)
+            ],
+            axis=0,
+        )
+        final = middle + row(7) + dot_nn(act[here, :], down)
+        grad_a = dot_nt(g_pre[here, :], w_wide[:, 4 * D : WIDE])
         mid[at, :] = final
         acc[2:3, :] = acc[2:3, :] + jnp.sum(grad_a * normed, axis=0, keepdims=True)
         acc[3:4, :] = acc[3:4, :] + jnp.sum(grad_a, axis=0, keepdims=True)
@@ -547,7 +551,7 @@
             g_mix[here, 2 * D + h * LANES : 2 * D + (h + 1) * LANES] = grad_v.astype(BF16)
         return carry
 
-    lax.fori_loop(0, WINDOWS, window_back, 0)
+    lax.fori_loop(0, WINDOWS, window_back, 0, unroll=True)
 
     def project_back(i, carry):
         at = pl.ds(pl.multiple_of(i * half, half), half)

time: 227 us -> 199 us (0.88)
  Pallas kernels: 109 us -> 81.4 us
    pallas_call x1, Pallas kernels: 109 us -> 81.4 us  [layer(): pl.pallas_call(functools.partial(layer_kernel, plan), grid=(steps,), in_s...]
where the time goes in v3:
time: 199 us
  Pallas kernels  81.4 us (41%)
  waiting for transfers between devices  73.1 us (37%)
  starting transfers between devices  23.2 us (12%)
  local copies, waits for them, and re-layouts  9.75 us (5%)
  other arithmetic  7.75 us (4%)
  matrix products  2.86 us (1%)
    pallas_call x1, Pallas kernels, layer(): pl.pallas_call(functools.partial(layer_kernel, plan), grid=(steps,), in_s...  81.4 us
    ppermute x3, waiting for transfers between devices, gather(): behind = lax.ppermute(behind, 'fsdp', self.backward)  22.7 us
    ppermute x3, waiting for transfers between devices, scatter(): ahead = lax.ppermute(ahead, 'fsdp', self.forward)  18.5 us
    ppermute x3, waiting for transfers between devices, scatter(): behind = lax.ppermute(behind, 'fsdp', self.backward)  11.7 us
    unnamed x58, local copies, waits for them, and re-layouts  8.36 us
    ppermute x1, waiting for transfers between devices, scatter(): ahead = lax.ppermute(far[:m], 'fsdp', self.forward)  5 us
    ppermute x1, waiting for transfers between devices, gather(): stack.append(lax.ppermute(mine[None], 'dp', self.shift(-by)))  4.99 us
    ppermute x3, starting transfers between devices, gather(): behind = lax.ppermute(behind, 'fsdp', self.backward)  4.4 us
  transfers between devices with their start and end apart: 30, of which 17 were waited for; matrix products, arithmetic and copies ran while one was open for 5% of the time, Pallas kernels for 0%

profile of v3, /device:TPU:0, one launch (start us, length us, event | category | flops | bytes accessed | tf_op | source)
XLA Modules:
  0.0 199.1 jit_solution(7253948109120593262)
XLA Ops:
  1.5 1.3 multiply_reduce_fusion.1
  3.0 3.0 %collective-permute-start = (bf16[1,784,128]{2,1,0:T(8,128)(2,1)S(1)}, bf16[1,784,128]{2,1,0:T(8,128)(2,1)S(1)}, u32[]{:S(2)}, u32[]{:S(2)}) collective-permute-start(bf16[1,784,128]{2,1,0:T(8,128)(2,1)S(1)} %maximum_bitcast_fusion), channel_id=1, source_target_pairs={{0,16},{8,24},{16,0},{24,8},{1,17},{9,25},{17,1},{25,9},{2,18},{10... | collective-permute-start | bytes 602120 | tf_op jit(solution)/shard_map/ppermute | solution.py:168
  6.0 5.0 %collective-permute-done = bf16[1,784,128]{2,1,0:T(8,128)(2,1)S(1)} collective-permute-done((bf16[1,784,128]{2,1,0:T(8,128)(2,1)S(1)}, bf16[1,784,128]{2,1,0:T(8,128)(2,1)S(1)}, u32[]{:S(2)}, u32[]{:S(2)}) %collective-permute-start) | collective-permute-done | bytes 200736 | tf_op jit(solution)/shard_map/ppermute | solution.py:168
  11.1 1.8 collective-permute-start.2
  13.2 8.6 %collective-permute-done.2.rest_2_ = bf16[2,784,128]{2,1,0:T(8,128)(2,1)} collective-permute-done((bf16[2,784,128]{2,1,0:T(8,128)(2,1)S(1)}, bf16[2,784,128]{2,1,0:T(8,128)(2,1)}, u32[]{:S(2)}, u32[]{:S(2)}) %collective-permute-start.2) | collective-permute-done | bytes 401440 | tf_op jit(solution)/shard_map/ppermute | solution.py:175
  21.7 1.5 collective-permute-start.4
  23.8 7.8 %collective-permute-done.4.rest_4_ = bf16[2,784,128]{2,1,0:T(8,128)(2,1)} collective-permute-done((bf16[2,784,128]{2,1,0:T(8,128)(2,1)}, bf16[2,784,128]{2,1,0:T(8,128)(2,1)}, u32[]{:S(2)}, u32[]{:S(2)}) %collective-permute-start.4) | collective-permute-done | bytes 401440 | tf_op jit(solution)/shard_map/ppermute | solution.py:175
  31.6 1.1 collective-permute-start.6
  34.1 6.3 %collective-permute-done.6.rest_6_ = bf16[2,784,128]{2,1,0:T(8,128)(2,1)S(1)} collective-permute-done((bf16[2,784,128]{2,1,0:T(8,128)(2,1)}, bf16[2,784,128]{2,1,0:T(8,128)(2,1)S(1)}, u32[]{:S(2)}, u32[]{:S(2)}) %collective-permute-start.6) | collective-permute-done | bytes 401440 | tf_op jit(solution)/shard_map/ppermute | solution.py:175
  41.4 1.5 copy.42.patches
  42.9 1.5 copy.43.cot_patches
  46.8 1.2 collective-permute-start.7
  49.3 3.7 %collective-permute-done.8.rest_8_ = bf16[1,784,128]{2,1,0:T(8,128)(2,1)S(1)} collective-permute-done((bf16[1,784,128]{2,1,0:T(8,128)(2,1)S(1)}, bf16[1,784,128]{2,1,0:T(8,128)(2,1)S(1)}, u32[]{:S(2)}, u32[]{:S(2)}) %collective-permute-start.8) | collective-permute-done | bytes 200736 | tf_op jit(solution)/shard_map/ppermute | solution.py:178
  55.7 81.4 %layer.1 = (bf16[24,512]{1,0:T(8,128)(2,1)}, bf16[24,49,512]{2,1,0:T(8,128)(2,1)}, bf16[24,512]{1,0:T(8,128)(2,1)}, bf16[24,49,512]{2,1,0:T(8,128)(2,1)}, bf16[6...) custom-call(s32[192]{0:T(256)} %get-tuple-element.78.block_row, ...), custom_call_target="tpu_custom_call" | custom-call | tf_op jit(solution)/shard_map/layer/pallas_call | solution.py:699
  137.7 2.6 %collective-permute-done.20 = bf16[6,784,128]{2,1,0:T(8,128)(2,1)S(1)} collective-permute-done((bf16[6,784,128]{2,1,0:T(8,128)(2,1)}, bf16[6,784,128]{2,1,0:T(8,128)(2,1)S(1)}, u32[]{:S(2)}, u32[]{:S(2)}) %collective-permute-start.20) | collective-permute-done | bytes 1204256 | tf_op jit(solution)/shard_map/ppermute | solution.py:183
  140.3 1.1 add_convert_fusion.6
  141.5 1.3 collective-permute-start.21
  143.6 5.0 %collective-permute-done.21 = bf16[1,784,128]{2,1,0:T(8,128)(2,1)S(1)} collective-permute-done((bf16[1,784,128]{2,1,0:T(8,128)(2,1)S(1)}, bf16[1,784,128]{2,1,0:T(8,128)(2,1)S(1)}, u32[]{:S(2)}, u32[]{:S(2)}) %collective-permute-start.21) | collective-permute-done | bytes 200736 | tf_op jit(solution)/shard_map/ppermute | solution.py:192
  149.8 1.1 collective-permute-start.22
  151.9 8.2 %collective-permute-done.22 = bf16[2,784,128]{2,1,0:T(8,128)(2,1)S(1)} collective-permute-done((bf16[2,784,128]{2,1,0:T(8,128)(2,1)S(1)}, bf16[2,784,128]{2,1,0:T(8,128)(2,1)S(1)}, u32[]{:S(2)}, u32[]{:S(2)}) %collective-permute-start.22) | collective-permute-done | bytes 401440 | tf_op jit(solution)/shard_map/ppermute | solution.py:200
  160.2 1.2 collective-permute-start.23
  161.4 8.1 %collective-permute-done.23 = bf16[2,784,128]{2,1,0:T(8,128)(2,1)S(1)} collective-permute-done((bf16[2,784,128]{2,1,0:T(8,128)(2,1)S(1)}, bf16[2,784,128]{2,1,0:T(8,128)(2,1)S(1)}, u32[]{:S(2)}, u32[]{:S(2)}) %collective-permute-start.23) | collective-permute-done | bytes 401440 | tf_op jit(solution)/shard_map/ppermute | solution.py:200
  169.9 1.2 collective-permute-start.27
  172.0 7.2 %collective-permute-done.27 = bf16[2,784,128]{2,1,0:T(8,128)(2,1)S(1)} collective-permute-done((bf16[2,784,128]{2,1,0:T(8,128)(2,1)S(1)}, bf16[2,784,128]{2,1,0:T(8,128)(2,1)S(1)}, u32[]{:S(2)}, u32[]{:S(2)}) %collective-permute-start.27) | collective-permute-done | bytes 401440 | tf_op jit(solution)/shard_map/ppermute | solution.py:201
  179.4 1.2 collective-permute-start.28
  180.5 2.3 %collective-permute-done.24 = bf16[2,784,128]{2,1,0:T(8,128)(2,1)S(1)} collective-permute-done((bf16[2,784,128]{2,1,0:T(8,128)(2,1)S(1)}, bf16[2,784,128]{2,1,0:T(8,128)(2,1)S(1)}, u32[]{:S(2)}, u32[]{:S(2)}) %collective-permute-start.24) | collective-permute-done | bytes 401440 | tf_op jit(solution)/shard_map/ppermute | solution.py:200
  182.8 4.5 %collective-permute-done.28 = bf16[2,784,128]{2,1,0:T(8,128)(2,1)S(1)} collective-permute-done((bf16[2,784,128]{2,1,0:T(8,128)(2,1)S(1)}, bf16[2,784,128]{2,1,0:T(8,128)(2,1)S(1)}, u32[]{:S(2)}, u32[]{:S(2)}) %collective-permute-start.28) | collective-permute-done | bytes 401440 | tf_op jit(solution)/shard_map/ppermute | solution.py:201
  187.5 1.3 collective-permute-start.29
  188.8 1.4 copy.50
  190.2 1.4 copy.51
  191.6 1.7 collective-permute-done.29
  198.1 1.0 multiply_add_fusion
  (120 shorter events, 20.8 us)
Async XLA Ops:
  0.6 39.8 %copy-start.21 = (s32[6,2]{0,1:T(2,128)S(1)}, s32[6,2]{0,1:T(2,128)}, u32[]{:S(2)}) copy-start(s32[6,2]{0,1:T(2,128)} %param.16) | copy-start | bytes 148
  0.7 40.8 %copy-start.6 = (bf16[24,49,512]{2,0,1:T(8,128)(2,1)S(1)}, bf16[24,49,512]{2,0,1:T(8,128)(2,1)}, u32[]{:S(2)}) copy-start(bf16[24,49,512]{2,0,1:T(8,128)(2,1)} %param.13) | copy-start | bytes 3612676
  3.0 8.0 %collective-permute-start = (bf16[1,784,128]{2,1,0:T(8,128)(2,1)S(1)}, bf16[1,784,128]{2,1,0:T(8,128)(2,1)S(1)}, u32[]{:S(2)}, u32[]{:S(2)}) collective-permute-start(bf16[1,784,128]{2,1,0:T(8,128)(2,1)S(1)} %maximum_bitcast_fusion), channel_id=1, source_target_pairs={{0,16},{8,24},{16,0},{24,8},{1,17},{9,25},{17,1},{25,9},{2,18},{10... | collective-permute-start | bytes 602120 | tf_op jit(solution)/shard_map/ppermute | solution.py:168
  11.1 10.6 %collective-permute-start.2 = (bf16[2,784,128]{2,1,0:T(8,128)(2,1)S(1)}, bf16[2,784,128]{2,1,0:T(8,128)(2,1)}, u32[]{:S(2)}, u32[]{:S(2)}) collective-permute-start(bf16[2,784,128]{2,1,0:T(8,128)(2,1)S(1)} %pad_maximum_fusion.rest_0_), channel_id=1, source_target_pairs={{0,1},{2,0},{4,2},{6,4},{7,6},{5,7},{3,5},{1,3},{8,9},{10,8},{12,1... | collective-permute-start | bytes 1204232 | tf_op jit(solution)/shard_map/ppermute | solution.py:175
  12.9 10.3 %collective-permute-start.1 = (bf16[2,784,128]{2,1,0:T(8,128)(2,1)S(1)}, bf16[2,784,128]{2,1,0:T(8,128)(2,1)}, u32[]{:S(2)}, u32[]{:S(2)}) collective-permute-start(bf16[2,784,128]{2,1,0:T(8,128)(2,1)S(1)} %pad_maximum_fusion.rest_0_), channel_id=1, source_target_pairs={{0,2},{2,4},{4,6},{6,7},{7,5},{5,3},{3,1},{1,0},{8,10},{10,12},{12... | collective-permute-start | bytes 1204232 | tf_op jit(solution)/shard_map/ppermute | solution.py:174
  21.7 9.9 %collective-permute-start.4 = (bf16[2,784,128]{2,1,0:T(8,128)(2,1)}, bf16[2,784,128]{2,1,0:T(8,128)(2,1)}, u32[]{:S(2)}, u32[]{:S(2)}) collective-permute-start(bf16[2,784,128]{2,1,0:T(8,128)(2,1)} %collective-permute-done.2.rest_2_), channel_id=1, source_target_pairs={{0,1},{2,0},{4,2},{6,4},{7,6},{5,7},{3,5},{1,3},{8,9},{10,8},{12,1... | collective-permute-start | bytes 1204232 | tf_op jit(solution)/shard_map/ppermute | solution.py:175
  23.2 9.6 %collective-permute-start.3 = (bf16[2,784,128]{2,1,0:T(8,128)(2,1)}, bf16[2,784,128]{2,1,0:T(8,128)(2,1)}, u32[]{:S(2)}, u32[]{:S(2)}) collective-permute-start(bf16[2,784,128]{2,1,0:T(8,128)(2,1)} %collective-permute-done.1.rest_1_), channel_id=1, source_target_pairs={{0,2},{2,4},{4,6},{6,7},{7,5},{5,3},{3,1},{1,0},{8,10},{10,12},{12... | collective-permute-start | bytes 1204232 | tf_op jit(solution)/shard_map/ppermute | solution.py:174
  31.6 8.8 %collective-permute-start.6 = (bf16[2,784,128]{2,1,0:T(8,128)(2,1)}, bf16[2,784,128]{2,1,0:T(8,128)(2,1)S(1)}, u32[]{:S(2)}, u32[]{:S(2)}) collective-permute-start(bf16[2,784,128]{2,1,0:T(8,128)(2,1)} %collective-permute-done.4.rest_4_), channel_id=1, source_target_pairs={{0,1},{2,0},{4,2},{6,4},{7,6},{5,7},{3,5},{1,3},{8,9},{10,8},{12,1... | collective-permute-start | bytes 1204232 | tf_op jit(solution)/shard_map/ppermute | solution.py:175
  32.7 11.7 %collective-permute-start.5 = (bf16[2,784,128]{2,1,0:T(8,128)(2,1)}, bf16[2,784,128]{2,1,0:T(8,128)(2,1)}, u32[]{:S(2)}, u32[]{:S(2)}) collective-permute-start(bf16[2,784,128]{2,1,0:T(8,128)(2,1)} %collective-permute-done.3.rest_3_), channel_id=1, source_target_pairs={{0,2},{2,4},{4,6},{6,7},{7,5},{5,3},{3,1},{1,0},{8,10},{10,12},{12... | collective-permute-start | bytes 1204232 | tf_op jit(solution)/shard_map/ppermute | solution.py:174
  33.6 12.3 %collective-permute-start.9 = (bf16[2,784,128]{2,1,0:T(8,128)(2,1)S(1)}, bf16[2,784,128]{2,1,0:T(8,128)(2,1)}, u32[]{:S(2)}, u32[]{:S(2)}) collective-permute-start(bf16[2,784,128]{2,1,0:T(8,128)(2,1)S(1)} %pad_maximum_fusion.rest_0_), channel_id=1, source_target_pairs={{0,8},{8,0},{16,24},{24,16},{1,9},{9,1},{17,25},{25,17},{2,10},{10... | collective-permute-start | bytes 1204232 | tf_op jit(solution)/shard_map/ppermute | solution.py:179
  33.6 13.2 %collective-permute-start.11 = (bf16[2,784,128]{2,1,0:T(8,128)(2,1)}, bf16[2,784,128]{2,1,0:T(8,128)(2,1)}, u32[]{:S(2)}, u32[]{:S(2)}) collective-permute-start(bf16[2,784,128]{2,1,0:T(8,128)(2,1)} %collective-permute-done.2.rest_2_), channel_id=1, source_target_pairs={{0,8},{8,0},{16,24},{24,16},{1,9},{9,1},{17,25},{25,17},{2,10},{10... | collective-permute-start | bytes 1204232 | tf_op jit(solution)/shard_map/ppermute | solution.py:179
  34.1 13.9 %collective-permute-start.10 = (bf16[2,784,128]{2,1,0:T(8,128)(2,1)}, bf16[2,784,128]{2,1,0:T(8,128)(2,1)}, u32[]{:S(2)}, u32[]{:S(2)}) collective-permute-start(bf16[2,784,128]{2,1,0:T(8,128)(2,1)} %collective-permute-done.1.rest_1_), channel_id=1, source_target_pairs={{0,8},{8,0},{16,24},{24,16},{1,9},{9,1},{17,25},{25,17},{2,10},{10... | collective-permute-start | bytes 1204232 | tf_op jit(solution)/shard_map/ppermute | solution.py:179
  40.4 7.6 %collective-permute-start.13 = (bf16[2,784,128]{2,1,0:T(8,128)(2,1)}, bf16[2,784,128]{2,1,0:T(8,128)(2,1)}, u32[]{:S(2)}, u32[]{:S(2)}) collective-permute-start(bf16[2,784,128]{2,1,0:T(8,128)(2,1)} %collective-permute-done.4.rest_4_), channel_id=1, source_target_pairs={{0,8},{8,0},{16,24},{24,16},{1,9},{9,1},{17,25},{25,17},{2,10},{10... | collective-permute-start | bytes 1204232 | tf_op jit(solution)/shard_map/ppermute | solution.py:179
  44.5 9.7 %collective-permute-start.12 = (bf16[2,784,128]{2,1,0:T(8,128)(2,1)}, bf16[2,784,128]{2,1,0:T(8,128)(2,1)S(1)}, u32[]{:S(2)}, u32[]{:S(2)}) collective-permute-start(bf16[2,784,128]{2,1,0:T(8,128)(2,1)} %collective-permute-done.3.rest_3_), channel_id=1, source_target_pairs={{0,8},{8,0},{16,24},{24,16},{1,9},{9,1},{17,25},{25,17},{2,10},{10... | collective-permute-start | bytes 1204232 | tf_op jit(solution)/shard_map/ppermute | solution.py:179
  45.9 7.0 %collective-permute-start.8 = (bf16[1,784,128]{2,1,0:T(8,128)(2,1)S(1)}, bf16[1,784,128]{2,1,0:T(8,128)(2,1)S(1)}, u32[]{:S(2)}, u32[]{:S(2)}) collective-permute-start(bf16[1,784,128]{2,1,0:T(8,128)(2,1)S(1)} %slice.98), channel_id=1, source_target_pairs={{0,1},{2,0},{4,2},{6,4},{7,6},{5,7},{3,5},{1,3},{8,9},{10,8},{12,1... | collective-permute-start | bytes 602120 | tf_op jit(solution)/shard_map/ppermute | solution.py:178
  46.8 6.7 %collective-permute-start.7 = (bf16[1,784,128]{2,1,0:T(8,128)(2,1)S(1)}, bf16[1,784,128]{2,1,0:T(8,128)(2,1)S(1)}, u32[]{:S(2)}, u32[]{:S(2)}) collective-permute-start(bf16[1,784,128]{2,1,0:T(8,128)(2,1)S(1)} %slice.97), channel_id=1, source_target_pairs={{0,2},{2,4},{4,6},{6,7},{7,5},{5,3},{3,1},{1,0},{8,10},{10,12},{12... | collective-permute-start | bytes 602120 | tf_op jit(solution)/shard_map/ppermute | solution.py:177
  48.0 6.4 %collective-permute-start.15 = (bf16[2,784,128]{2,1,0:T(8,128)(2,1)S(1)}, bf16[2,784,128]{2,1,0:T(8,128)(2,1)S(1)}, u32[]{:S(2)}, u32[]{:S(2)}) collective-permute-start(bf16[2,784,128]{2,1,0:T(8,128)(2,1)S(1)} %collective-permute-done.6.rest_6_), channel_id=1, source_target_pairs={{0,8},{8,0},{16,24},{24,16},{1,9},{9,1},{17,25},{25,17},{2,10},{10... | collective-permute-start | bytes 1204232 | tf_op jit(solution)/shard_map/ppermute | solution.py:179
  48.0 6.9 %collective-permute-start.14 = (bf16[2,784,128]{2,1,0:T(8,128)(2,1)}, bf16[2,784,128]{2,1,0:T(8,128)(2,1)S(1)}, u32[]{:S(2)}, u32[]{:S(2)}) collective-permute-start(bf16[2,784,128]{2,1,0:T(8,128)(2,1)} %collective-permute-done.5.rest_5_), channel_id=1, source_target_pairs={{0,8},{8,0},{16,24},{24,16},{1,9},{9,1},{17,25},{25,17},{2,10},{10... | collective-permute-start | bytes 1204232 | tf_op jit(solution)/shard_map/ppermute | solution.py:179
  52.9 1.4 collective-permute-start.17
  53.5 1.4 collective-permute-start.16
  137.1 3.2 %collective-permute-start.20 = (bf16[6,784,128]{2,1,0:T(8,128)(2,1)}, bf16[6,784,128]{2,1,0:T(8,128)(2,1)S(1)}, u32[]{:S(2)}, u32[]{:S(2)}) collective-permute-start(bf16[6,784,128]{2,1,0:T(8,128)(2,1)} %get-tuple-element.30), channel_id=1, source_target_pairs={{0,8},{8,0},{16,24},{24,16},{1,9},{9,1},{17,25},{25,17},{2,10},{10... | collective-permute-start | bytes 3612680 | tf_op jit(solution)/shard_map/ppermute | solution.py:183
  137.4 14.5 %collective-permute-start.19 = (bf16[8,784,128]{2,1,0:T(8,128)(2,1)}, bf16[8,784,128]{2,1,0:T(8,128)(2,1)S(1)}, u32[]{:S(2)}, u32[]{:S(2)}) collective-permute-start(bf16[8,784,128]{2,1,0:T(8,128)(2,1)} %get-tuple-element.28), channel_id=1, source_target_pairs={{0,8},{8,0},{16,24},{24,16},{1,9},{9,1},{17,25},{25,17},{2,10},{10... | collective-permute-start | bytes 4816904 | tf_op jit(solution)/shard_map/ppermute | solution.py:183
  141.5 7.1 %collective-permute-start.21 = (bf16[1,784,128]{2,1,0:T(8,128)(2,1)S(1)}, bf16[1,784,128]{2,1,0:T(8,128)(2,1)S(1)}, u32[]{:S(2)}, u32[]{:S(2)}) collective-permute-start(bf16[1,784,128]{2,1,0:T(8,128)(2,1)S(1)} %get-tuple-element.73), channel_id=1, source_target_pairs={{0,2},{2,4},{4,6},{6,7},{7,5},{5,3},{3,1},{1,0},{8,10},{10,12},{12... | collective-permute-start | bytes 602120 | tf_op jit(solution)/shard_map/ppermute | solution.py:192
  142.7 6.8 %collective-permute-start.25 = (bf16[1,784,128]{2,1,0:T(8,128)(2,1)S(1)}, bf16[1,784,128]{2,1,0:T(8,128)(2,1)S(1)}, u32[]{:S(2)}, u32[]{:S(2)}) collective-permute-start(bf16[1,784,128]{2,1,0:T(8,128)(2,1)S(1)} %get-tuple-element.74), channel_id=1, source_target_pairs={{0,1},{2,0},{4,2},{6,4},{7,6},{5,7},{3,5},{1,3},{8,9},{10,8},{12,1... | collective-permute-start | bytes 602120 | tf_op jit(solution)/shard_map/ppermute | solution.py:193
  149.8 10.2 %collective-permute-start.22 = (bf16[2,784,128]{2,1,0:T(8,128)(2,1)S(1)}, bf16[2,784,128]{2,1,0:T(8,128)(2,1)S(1)}, u32[]{:S(2)}, u32[]{:S(2)}) collective-permute-start(bf16[2,784,128]{2,1,0:T(8,128)(2,1)S(1)} %get-tuple-element.71), channel_id=1, source_target_pairs={{0,2},{2,4},{4,6},{6,7},{7,5},{5,3},{3,1},{1,0},{8,10},{10,12},{12... | collective-permute-start | bytes 1204232 | tf_op jit(solution)/shard_map/ppermute | solution.py:200
  150.9 10.5 %collective-permute-start.26 = (bf16[2,784,128]{2,1,0:T(8,128)(2,1)S(1)}, bf16[2,784,128]{2,1,0:T(8,128)(2,1)S(1)}, u32[]{:S(2)}, u32[]{:S(2)}) collective-permute-start(bf16[2,784,128]{2,1,0:T(8,128)(2,1)S(1)} %get-tuple-element.72), channel_id=1, source_target_pairs={{0,1},{2,0},{4,2},{6,4},{7,6},{5,7},{3,5},{1,3},{8,9},{10,8},{12,1... | collective-permute-start | bytes 1204232 | tf_op jit(solution)/shard_map/ppermute | solution.py:201
  160.2 9.3 %collective-permute-start.23 = (bf16[2,784,128]{2,1,0:T(8,128)(2,1)S(1)}, bf16[2,784,128]{2,1,0:T(8,128)(2,1)S(1)}, u32[]{:S(2)}, u32[]{:S(2)}) collective-permute-start(bf16[2,784,128]{2,1,0:T(8,128)(2,1)S(1)} %add_convert_fusion.4), channel_id=1, source_target_pairs={{0,2},{2,4},{4,6},{6,7},{7,5},{5,3},{3,1},{1,0},{8,10},{10,12},{12... | collective-permute-start | bytes 1204232 | tf_op jit(solution)/shard_map/ppermute | solution.py:200
  169.9 9.2 %collective-permute-start.27 = (bf16[2,784,128]{2,1,0:T(8,128)(2,1)S(1)}, bf16[2,784,128]{2,1,0:T(8,128)(2,1)S(1)}, u32[]{:S(2)}, u32[]{:S(2)}) collective-permute-start(bf16[2,784,128]{2,1,0:T(8,128)(2,1)S(1)} %get-tuple-element.70), channel_id=1, source_target_pairs={{0,1},{2,0},{4,2},{6,4},{7,6},{5,7},{3,5},{1,3},{8,9},{10,8},{12,1... | collective-permute-start | bytes 1204232 | tf_op jit(solution)/shard_map/ppermute | solution.py:201
  171.1 9.5 %collective-permute-start.18 = (bf16[2,784,128]{2,1,0:T(8,128)(2,1)S(1)}, bf16[2,784,128]{2,1,0:T(8,128)(2,1)S(1)}, u32[]{:S(2)}, u32[]{:S(2)}) collective-permute-start(bf16[2,784,128]{2,1,0:T(8,128)(2,1)S(1)} %copy-done.25), channel_id=1, source_target_pairs={{0,8},{8,0},{16,24},{24,16},{1,9},{9,1},{17,25},{25,17},{2,10},{10... | collective-permute-start | bytes 1204232 | tf_op jit(solution)/shard_map/ppermute | solution.py:183
  171.1 11.7 %collective-permute-start.24 = (bf16[2,784,128]{2,1,0:T(8,128)(2,1)S(1)}, bf16[2,784,128]{2,1,0:T(8,128)(2,1)S(1)}, u32[]{:S(2)}, u32[]{:S(2)}) collective-permute-start(bf16[2,784,128]{2,1,0:T(8,128)(2,1)S(1)} %get-tuple-element.69), channel_id=1, source_target_pairs={{0,2},{2,4},{4,6},{6,7},{7,5},{5,3},{3,1},{1,0},{8,10},{10,12},{12... | collective-permute-start | bytes 1204232 | tf_op jit(solution)/shard_map/ppermute | solution.py:200
  179.4 7.9 %collective-permute-start.28 = (bf16[2,784,128]{2,1,0:T(8,128)(2,1)S(1)}, bf16[2,784,128]{2,1,0:T(8,128)(2,1)S(1)}, u32[]{:S(2)}, u32[]{:S(2)}) collective-permute-start(bf16[2,784,128]{2,1,0:T(8,128)(2,1)S(1)} %add_convert_fusion), channel_id=1, source_target_pairs={{0,1},{2,0},{4,2},{6,4},{7,6},{5,7},{3,5},{1,3},{8,9},{10,8},{12,1... | collective-permute-start | bytes 1204232 | tf_op jit(solution)/shard_map/ppermute | solution.py:201
  187.5 5.8 %collective-permute-start.29 = (bf16[784,128]{1,0:T(8,128)(2,1)S(1)}, bf16[784,128]{1,0:T(8,128)(2,1)S(1)}, u32[]{:S(2)}, u32[]{:S(2)}) collective-permute-start(bf16[784,128]{1,0:T(8,128)(2,1)S(1)} %fusion.8), channel_id=1, source_target_pairs={{0,16},{8,24},{16,0},{24,8},{1,17},{9,25},{17,1},{25,9},{2,18},{10... | collective-permute-start | bytes 602120 | tf_op jit(solution)/shard_map/ppermute | solution.py:205
  (24 other events, 158.7 us)

commit v4 on v3

v4 whole, which is shorter than its diff:
```python
import functools
import math

import jax
import jax.numpy as jnp
from jax import lax
from jax.experimental import pallas as pl
from jax.experimental.pallas import tpu as pltpu
from jax.sharding import PartitionSpec as P

D = 512
HEAD = 32
FF = 2048
SIDE = 128
NBLOCKS = 192
LANES = 128
HEADS_PER = LANES // HEAD
GROUPS = D // LANES

EPS_NORM = 1e-05
EPS_MEAN = 1e-06
SHAMPOO_RATE = 0.5
SMALL_RATE = 0.3
EMA_DECAY = 0.8
STAT_DECAY = 0.5
SCORE_SCALE = HEAD ** (-0.5)
MASKED = -1e30

WINDOWS = 8
CHUNKS = 5
PAD = 64
REG_PAD = 32
WIDE = 4 * D + FF
ALL = WIDE + FF
Z_LEN = 4
TAIL = 16
VMEM_LIMIT = 60 * 1024 * 1024

F32 = jnp.float32
BF16 = jnp.bfloat16


def dot_nn(a, b):
    return lax.dot_general(a, b, (((1,), (0,)), ((), ())), preferred_element_type=F32)


def dot_nt(a, b):
    return lax.dot_general(a, b, (((1,), (1,)), ((), ())), preferred_element_type=F32)


def dot_tn(a, b):
    return lax.dot_general(a, b, (((0,), (0,)), ((), ())), preferred_element_type=F32)


def normalize(values):
    center = values - jnp.mean(values, axis=-1, keepdims=True)
    inverse = lax.rsqrt(jnp.mean(center * center, axis=-1, keepdims=True) + EPS_NORM)
    return center * inverse, inverse


def normalize_back(scaled, normed, inverse):
    return inverse * (
        scaled
        - jnp.mean(scaled, axis=-1, keepdims=True)
        - normed * jnp.mean(scaled * normed, axis=-1, keepdims=True)
    )


def gauss(values):
    big_phi = 0.5 * (1.0 + lax.erf(values * 0.7071067811865476))
    return big_phi, jnp.exp(-0.5 * values * values) * 0.3989422804014327


def head_masks(rows, dtype):
    lane = lax.broadcasted_iota(jnp.int32, (rows, LANES), 1) // HEAD
    return [(lane == j).astype(F32).astype(dtype) for j in range(HEADS_PER)]


def spread(values, masks):
    return jnp.concatenate([values * mask for mask in masks], axis=0)


def collect(stacked, masks, rows):
    total = stacked[:rows] * masks[0]
    for j in range(1, HEADS_PER):
        total = total + stacked[j * rows : (j + 1) * rows] * masks[j]
    return total


def attend(queries, keys, values, valid, masks_b, masks_f):
    rows = queries.shape[0]
    scores = dot_nt(keys, spread(queries, masks_b))
    scores = jnp.where(valid, scores, MASKED)
    highest = jnp.max(scores, axis=0, keepdims=True)
    weights = jnp.exp((scores - highest) * SCORE_SCALE)
    probs = weights * (1.0 / jnp.sum(weights, axis=0, keepdims=True))
    context = collect(dot_tn(probs.astype(BF16), values), masks_f, rows)
    return context, probs


def attend_back(queries, keys, values, probs, grad_context, masks_b, masks_f):
    rows = queries.shape[0]
    grad_wide = spread(grad_context, masks_b)
    grad_probs = dot_nt(values, grad_wide)
    row_dot = jnp.sum(probs * grad_probs, axis=0, keepdims=True)
    grad_scores = (probs * (grad_probs - row_dot)).astype(BF16)
    grad_q = collect(dot_tn(grad_scores, keys), masks_f, rows) * SCORE_SCALE
    grad_k = dot_nn(grad_scores, spread(queries, masks_b)) * SCORE_SCALE
    grad_v = dot_nn(probs.astype(BF16), grad_wide)
    return grad_q, grad_k, grad_v


class Plan:
    def __init__(self, n_dp, n_fsdp, own, entries):
        self.n_dp, self.n_fsdp, self.own, self.entries = n_dp, n_fsdp, own, entries
        self.x_len, self.ring = n_dp // 2, n_fsdp
        self.y_len = n_fsdp // Z_LEN
        self.devices = n_dp * n_fsdp
        self.empty = self.devices * own > NBLOCKS
        self.half = self.ring // 2
        starts = [(d * entries) % LANES for d in range(self.devices)]
        self.small_rows = max((at + entries - 1) // LANES + 1 for at in starts)
        order = [0] * self.ring
        for z in range(Z_LEN):
            for y in range(self.y_len):
                order[y * Z_LEN + (z if y % 2 == 0 else Z_LEN - 1 - z)] = z * self.y_len + y
        n = self.ring
        self.forward = [(order[i], order[(i + 1) % n]) for i in range(n)]
        self.backward = [(order[i], order[i - 1]) for i in range(n)]
        self.flip = [(i, i ^ 1) for i in range(n_dp)]
        self.gathered, self.scattered = [], []
        xs = range(self.x_len)
        h, m = self.half, self.x_len // 2
        for flip in (0, 1):
            put = lambda k, part: self.gathered.append([self.home(flip, k, x) for x in part])
            put(0, xs)
            for k in range(1, h):
                put(-k, xs)
                put(k, xs)
            put(-h, xs[:m])
            put(h, xs[m:])
            spots = [[h, h - 1, 1 - h]]
            spots.append([k for j in range(h - 2, 0, -1) for k in (j, -j)])
            spots.append([0])
            for group in spots:
                self.scattered.append([self.home(flip, k, x) for k in group for x in xs])
        self.spots = spots

    def home(self, flip, k, x):
        return (flip * self.ring + k % self.ring) * self.x_len + x % self.x_len

    def shift(self, by):
        return [(i, (i + 2 * by) % self.n_dp) for i in range(self.n_dp)]

    def device_of_homes(self, dp, fsdp):
        home = jnp.arange(self.devices, dtype=jnp.int32)
        x = (home % self.x_len + dp // 2) % self.x_len
        core = (home // (self.x_len * self.ring) + dp) % 2
        z, y = fsdp // self.y_len, fsdp % self.y_len
        here = y * Z_LEN + jnp.where(y % 2 == 0, z, Z_LEN - 1 - z)
        place = (home // self.x_len + here) % self.ring
        y, z = place // Z_LEN, place % Z_LEN
        z = jnp.where(y % 2 == 0, z, Z_LEN - 1 - z)
        return (x * 2 + core) * self.n_fsdp + z * self.y_len + y

    def gather(self, mine):
        stack = [mine[None]]
        for by in range(1, self.x_len):
            stack.append(lax.ppermute(mine[None], "dp", self.shift(-by)))
        first = jnp.concatenate(stack, axis=0)
        pieces = [first]
        ahead = behind = first
        m = self.x_len // 2
        for _ in range(1, self.half):
            ahead = lax.ppermute(ahead, "fsdp", self.forward)
            behind = lax.ppermute(behind, "fsdp", self.backward)
            pieces += [ahead, behind]
        pieces.append(lax.ppermute(ahead[:m], "fsdp", self.forward))
        pieces.append(lax.ppermute(behind[m:], "fsdp", self.backward))
        return pieces + [lax.ppermute(piece, "dp", self.flip) for piece in pieces]

    def scatter(self, sends):
        n = len(self.spots)
        mixed = [lax.ppermute(send, "dp", self.flip) for send in sends[n:]]
        parts = {}
        for spot, kept, came in zip(self.spots, sends[:n], mixed):
            for i, k in enumerate(spot):
                at = slice(i * self.x_len, (i + 1) * self.x_len)
                parts[k] = (kept[at], came[at])
        total = lambda k: parts[k][0].astype(F32) + parts[k][1].astype(F32)
        m = self.x_len // 2
        far = total(self.half).astype(BF16)
        ahead = lax.ppermute(far[:m], "fsdp", self.forward)
        behind = lax.ppermute(far[m:], "fsdp", self.backward)
        none = ((0, 0), (0, 0))
        ahead = jnp.pad(ahead, ((0, self.x_len - m),) + none)
        behind = jnp.pad(behind, ((m, 0),) + none)
        for k in range(self.half - 1, 0, -1):
            ahead = (total(k) + ahead.astype(F32)).astype(BF16)
            behind = (total(-k) + behind.astype(F32)).astype(BF16)
            ahead = lax.ppermute(ahead, "fsdp", self.forward)
            behind = lax.ppermute(behind, "fsdp", self.backward)
        mine = total(0) + ahead.astype(F32) + behind.astype(F32)
        result = mine[0]
        for by in range(1, self.x_len):
            came = lax.ppermute(mine[by].astype(BF16), "dp", self.shift(by))
            result = result + came.astype(F32)
        return result


def block_places(block):
    pick = jnp.where
    row = pick(block < 48, block // 12, pick(block < 64, (block - 48) // 4, (block - 64) // 16))
    col = pick(block < 48, block % 12, pick(block < 64, 12 + block % 4, 16 + block % 16))
    row = pick(block < 128, row, block % 4)
    col = pick(block < 128, col, 32 + (block - 128) // 4)
    return pick(block < NBLOCKS, row, 0), pick(block < NBLOCKS, col, ALL // SIDE)


def layer_kernel(
    plan,
    block_row,
    block_col,
    small_row,
    shape,
    regions,
    cot_regions,
    patches,
    cot_patches,
    *rest,
):
    n_in, n_out = len(plan.gathered), len(plan.scattered)
    pieces = rest[:n_in]
    outs = rest[n_in : n_in + 4]
    sends = rest[n_in + 4 : n_in + 4 + n_out]
    tables = (block_row, block_col, small_row, shape)
    layer_body(
        plan,
        tables,
        (regions, cot_regions, patches, cot_patches),
        pieces,
        outs,
        sends,
        *rest[n_in + 4 + n_out :],
    )


def layer_body(
    plan,
    tables,
    inputs,
    pieces,
    outs,
    sends,
    w_all,
    small_in,
    small,
    small_out,
    vecs,
    reg_in,
    reg_norm,
    reg_inv,
    reg_mix,
    reg_probs,
    reg_ctx,
    x_win,
    n_one,
    i_one,
    mix,
    probs_s,
    ctx,
    hold_a,
    hold_b,
    token,
    a_win_t,
    ctx_t,
    a_mlp_t,
    g_fin_t,
    g_mid,
    g_mix,
    act,
    g_pre,
    acc,
    acc_up,
    acc_mix,
    sem,
):
    block_row, block_col, small_row, shape = tables
    regions, cot_regions, patches, cot_patches = inputs
    out_regions, out_patches, grad_regions, grad_patches = outs
    n_reg = regions.shape[0]
    body = patches.shape[0]
    rows = body + n_reg
    tokens = rows // n_reg
    part = rows // CHUNKS
    chunk = lambda i: pl.ds(pl.multiple_of(i * part, part), part)
    stage = w_all

    def move(source, target, n):
        return pltpu.make_async_copy(source, target, sem.at[n])

    bring = [
        move(patches, hold_a, 0),
        move(cot_patches, hold_b, 1),
    ]
    for copy in bring:
        copy.start()
    for piece, homes in zip(pieces, plan.gathered):
        for j, home in enumerate(homes):
            move(piece.at[j, pl.ds(plan.own * SIDE, TAIL), :], small_in.at[home], 3).start()
    for piece, homes in zip(pieces, plan.gathered):
        for j, home in enumerate(homes):
            for i in range(plan.own):
                r = block_row[home * plan.own + i]
                c = block_col[home * plan.own + i]

                def fetch(piece=piece, j=j, i=i, r=r, c=c):
                    move(
                        piece.at[j, pl.ds(i * SIDE, SIDE), :],
                        w_all.at[
                            pl.ds(pl.multiple_of(r * SIDE, SIDE), SIDE),
                            pl.ds(pl.multiple_of(c * SIDE, SIDE), SIDE),
                        ],
                        4,
                    ).start()

                if plan.empty:
                    pl.when(c < ALL // SIDE)(fetch)
                else:
                    fetch()

    ends = []
    so_far = jnp.int32(0)
    for j in range(shape.shape[0]):
        so_far = so_far + shape[j, 0] * shape[j, 1]
        ends.append(so_far)
    live = (lax.broadcasted_iota(jnp.int32, (part, 1), 0) % n_reg < ends[-1]).astype(F32)

    def row(i):
        return vecs[i : i + 1, :D]

    acc[...] = jnp.zeros_like(acc)
    acc_up[...] = jnp.zeros_like(acc_up)
    acc_mix[...] = jnp.zeros_like(acc_mix)
    for h in range(3 * GROUPS):
        mix[h, rows:, :] = jnp.zeros((PAD * n_reg - rows, LANES), F32)
    for h in range(GROUPS):
        ctx[h, rows:, :] = jnp.zeros((PAD * n_reg - rows, LANES), F32)

    def norm_in(at):
        normed, inverse = normalize(x_win[at, :])
        n_one[at, :] = normed
        i_one[at, :] = inverse

    bring[0].wait()
    for i in range(CHUNKS):
        at = slice(i * part, min((i + 1) * part, body))
        x_win[at, :] = hold_a[at, :].astype(F32)
        norm_in(at)

    small[...] = jnp.zeros_like(small)
    move(small_in, small_in, 3).wait()
    for home in range(plan.devices):
        at = pl.ds(small_row[home], plan.small_rows)
        small[at, :] = small[at, :] + small_in[home].astype(F32)[: plan.small_rows, :]
    for i in range(8):
        vecs[i : i + 1, :D] = jnp.concatenate(
            [small[4 * i + j : 4 * i + j + 1, :] for j in range(4)], axis=1
        )
    vecs[8:9, :] = jnp.concatenate([small[32 + j : 33 + j, :] for j in range(16)], axis=1)
    reg_in[...] = jnp.zeros_like(reg_in)
    reg_in[:n_reg, :] = regions[...].astype(F32)
    normed, inverse = normalize(reg_in[...])
    reg_norm[...] = normed
    reg_inv[...] = inverse
    a_reg = (normed * row(0) + row(1)).astype(BF16)
    reg_mask_b = head_masks(REG_PAD, BF16)
    reg_mask_f = head_masks(REG_PAD, F32)
    filled = w_all.at[:, pl.ds(0, ALL)]
    move(filled, filled, 4).wait()

    w_out = w_all[:, 3 * D : 4 * D]
    mixed = dot_nn(a_reg, w_all[:, : 3 * D])
    reg_mix[:, :D] = (mixed[:, :D] + row(4)).astype(BF16)
    reg_mix[:, D : 2 * D] = mixed[:, D : 2 * D].astype(BF16)
    reg_mix[:, 2 * D :] = (mixed[:, 2 * D :] + row(5)).astype(BF16)
    spot = (REG_PAD, HEADS_PER * REG_PAD)
    key_at = lax.broadcasted_iota(jnp.int32, spot, 0)
    query_at = lax.broadcasted_iota(jnp.int32, spot, 1) % REG_PAD
    key_label = jnp.zeros(spot, jnp.int32)
    query_label = jnp.zeros(spot, jnp.int32)
    for end in ends:
        key_label = key_label + (key_at >= end).astype(jnp.int32)
        query_label = query_label + (query_at >= end).astype(jnp.int32)
    same = (key_label == query_label) & ((key_at < n_reg) == (query_at < n_reg))
    for h in range(GROUPS):
        context, probs = attend(
            reg_mix[:, h * LANES : (h + 1) * LANES],
            reg_mix[:, D + h * LANES : D + (h + 1) * LANES],
            reg_mix[:, 2 * D + h * LANES : 2 * D + (h + 1) * LANES],
            same,
            reg_mask_b,
            reg_mask_f,
        )
        reg_probs[h] = probs
        reg_ctx[:, h * LANES : (h + 1) * LANES] = context.astype(BF16)
    region_mid = reg_in[...] + dot_nn(reg_ctx[...], w_out) + row(6)
    x_win[body:, :] = region_mid[:n_reg, :]
    norm_in(slice(body, rows))

    bring[1].wait()
    token[:body, :] = hold_b[...]
    token[body:, :] = cot_regions[...]

    def project(i, carry):
        at = chunk(i)
        a_win = (n_one[at, :] * row(0) + row(1)).astype(BF16)
        a_win_t[i] = a_win.T
        for j, bias in ((0, row(4)), (1, None), (2, row(5))):
            mixed = dot_nn(a_win, w_all[:, j * D : (j + 1) * D])
            mixed = mixed if bias is None else mixed + bias
            for h in range(GROUPS):
                mix[j * GROUPS + h, at, :] = mixed[:, h * LANES : (h + 1) * LANES]
        return carry

    lax.fori_loop(0, CHUNKS, project, 0)

    masks_b = head_masks(PAD, BF16)
    masks_f = head_masks(PAD, F32)
    valid = lax.broadcasted_iota(jnp.int32, (PAD, HEADS_PER * PAD), 0) < tokens

    def window(w, h):
        return mix[h, pl.ds(w, PAD, stride=n_reg), :].astype(BF16)

    def window_attend(g, carry):
        for u in range(WINDOWS):
            w = g * WINDOWS + u
            for h in range(GROUPS):
                context, probs = attend(
                    window(w, h),
                    window(w, GROUPS + h),
                    window(w, 2 * GROUPS + h),
                    valid,
                    masks_b,
                    masks_f,
                )
                probs_s[w * GROUPS + h] = probs
                ctx[h, pl.ds(w, tokens, stride=n_reg), :] = context[:tokens]
        return carry

    lax.fori_loop(0, n_reg // WINDOWS, window_attend, 0)

    def perceptron(i, carry):
        at = chunk(i)
        context = jnp.concatenate([ctx[h, at, :] for h in range(GROUPS)], axis=1).astype(BF16)
        ctx_t[i] = context.T
        w_out = w_all[:, 3 * D : 4 * D]
        middle = x_win[at, :] + dot_nn(context, w_out) + row(6)
        normed, inverse = normalize(middle)
        a_mlp = (normed * row(2) + row(3)).astype(BF16)
        a_mlp_t[i] = a_mlp.T
        grad_final = token[at, :].astype(F32) * live
        grad_b = grad_final.astype(BF16)
        g_fin_t[i] = grad_b.T
        acc[7:8, :] = acc[7:8, :] + jnp.sum(grad_final, axis=0, keepdims=True)
        width = 256
        for c in range(FF // width):
            cols = slice(c * width, (c + 1) * width)
            up = w_all[:, 4 * D + c * width : 4 * D + (c + 1) * width]
            pre = dot_nn(a_mlp, up) + vecs[8:9, cols]
            big_phi, phi = gauss(pre)
            act[at, cols] = (pre * big_phi).astype(BF16)
            grad_pre = dot_nt(grad_b, down_rows(w_all, c * width, width))
            grad_pre = (grad_pre * (big_phi + pre * phi)).astype(BF16)
            g_pre[at, cols] = grad_pre
            acc_up[:, cols] = acc_up[:, cols] + jnp.sum(
                grad_pre.astype(F32), axis=0, keepdims=True
            )
        final = middle + row(7) + dot_nn(act[at, :], down_rows(w_all, 0, FF))
        token[at, :] = (final * live).astype(BF16)
        grad_a = dot_nt(g_pre[at, :], w_all[:, 4 * D : WIDE])
        acc[2:3, :] = acc[2:3, :] + jnp.sum(grad_a * normed, axis=0, keepdims=True)
        acc[3:4, :] = acc[3:4, :] + jnp.sum(grad_a, axis=0, keepdims=True)
        grad_mid = (grad_final + normalize_back(grad_a * row(2), normed, inverse)).astype(BF16)
        g_mid[at, :] = grad_mid
        acc[6:7, :] = acc[6:7, :] + jnp.sum(grad_mid.astype(F32), axis=0, keepdims=True)
        grad_ctx = dot_nt(grad_mid, w_out)
        for h in range(GROUPS):
            ctx[h, at, :] = grad_ctx[:, h * LANES : (h + 1) * LANES]
        return carry

    lax.fori_loop(0, CHUNKS, perceptron, 0)
    hold_a[...] = token[:body, :]
    out_regions[...] = token[body:, :]
    give = [move(hold_a, out_patches, 0), move(hold_b, grad_patches, 1)]
    give[0].start()

    def window_back(g, carry):
        for u in range(WINDOWS):
            w = g * WINDOWS + u
            for h in range(GROUPS):
                grads = attend_back(
                    window(w, h),
                    window(w, GROUPS + h),
                    window(w, 2 * GROUPS + h),
                    probs_s[w * GROUPS + h],
                    ctx[h, pl.ds(w, PAD, stride=n_reg), :].astype(BF16),
                    masks_b,
                    masks_f,
                )
                for j, grad in enumerate(grads):
                    mix[j * GROUPS + h, pl.ds(w, tokens, stride=n_reg), :] = grad[:tokens]
        return carry

    lax.fori_loop(0, n_reg // WINDOWS, window_back, 0)

    def project_back(i, carry):
        at = chunk(i)
        grad_mix = jnp.concatenate([mix[h, at, :] for h in range(3 * GROUPS)], axis=1).astype(BF16)
        g_mix[at, :] = grad_mix
        acc_mix[...] = acc_mix[...] + jnp.sum(grad_mix.astype(F32), axis=0, keepdims=True)
        grad_a = dot_nt(grad_mix, w_all[:, : 3 * D])
        normed = n_one[at, :]
        acc[0:1, :] = acc[0:1, :] + jnp.sum(grad_a * normed, axis=0, keepdims=True)
        acc[1:2, :] = acc[1:2, :] + jnp.sum(grad_a, axis=0, keepdims=True)
        token[at, :] = (
            g_mid[at, :].astype(F32) + normalize_back(grad_a * row(0), normed, i_one[at, :])
        ).astype(BF16)
        return carry

    lax.fori_loop(0, CHUNKS, project_back, 0)
    hold_b[...] = token[:body, :]
    give[1].start()

    w_out = w_all[:, 3 * D : 4 * D]
    none = jnp.zeros((REG_PAD - n_reg, D), F32)
    grad_mid_f = jnp.concatenate([token[body:, :].astype(F32), none], axis=0)
    grad_mid = grad_mid_f.astype(BF16)
    grad_ctx = dot_nt(grad_mid, w_out).astype(BF16)
    parts = ([], [], [])
    for h in range(GROUPS):
        grads = attend_back(
            reg_mix[:, h * LANES : (h + 1) * LANES],
            reg_mix[:, D + h * LANES : D + (h + 1) * LANES],
            reg_mix[:, 2 * D + h * LANES : 2 * D + (h + 1) * LANES],
            reg_probs[h],
            grad_ctx[:, h * LANES : (h + 1) * LANES],
            reg_mask_b,
            reg_mask_f,
        )
        for held, grad in zip(parts, grads):
            held.append(grad.astype(BF16))
    grad_mix = jnp.concatenate(parts[0] + parts[1] + parts[2], axis=1)
    grad_a = dot_nt(grad_mix, w_all[:, : 3 * D])
    normed = reg_norm[...]
    grad_regions[...] = (
        grad_mid_f + normalize_back(grad_a * row(0), normed, reg_inv[...])
    )[:n_reg, :].astype(BF16)
    bias_mix = acc_mix[...] + jnp.sum(grad_mix.astype(F32), axis=0, keepdims=True)
    rows_all = [
        acc[0:1, :] + jnp.sum(grad_a * normed, axis=0, keepdims=True),
        acc[1:2, :] + jnp.sum(grad_a, axis=0, keepdims=True),
        acc[2:3, :],
        acc[3:4, :],
        bias_mix[:, :D],
        bias_mix[:, 2 * D :],
        acc[6:7, :] + jnp.sum(grad_mid_f, axis=0, keepdims=True),
        acc[7:8, :],
    ]
    a_reg = (normed * row(0) + row(1)).astype(BF16)
    for i, values in enumerate(rows_all):
        for j in range(4):
            small[4 * i + j : 4 * i + j + 1, :] = values[:, j * LANES : (j + 1) * LANES]
    for j in range(FF // LANES):
        small[32 + j : 33 + j, :] = acc_up[:, j * LANES : (j + 1) * LANES]
    for home in range(plan.devices):
        held = small[pl.ds(small_row[home], plan.small_rows), :]
        small_out[home] = jnp.concatenate(
            [held, jnp.zeros((TAIL - plan.small_rows, LANES), F32)], axis=0
        ).astype(BF16)

    def contract(left, right, cols):
        total = dot_nn(left[0], right[:part, cols])
        for i in range(1, CHUNKS):
            total = total + dot_nn(left[i], right[i * part : (i + 1) * part, cols])
        return total

    width = 256
    for c in range(FF // width):
        cols = slice(c * width, (c + 1) * width)
        out = slice(4 * D + c * width, 4 * D + (c + 1) * width)
        stage[:, out] = contract(a_mlp_t, g_pre, cols).astype(BF16)
        flipped = contract(g_fin_t, act, cols).astype(BF16).T
        for j in range(width // SIDE):
            for k in range(D // SIDE):
                stage[
                    k * SIDE : (k + 1) * SIDE,
                    WIDE + c * width + j * SIDE : WIDE + c * width + (j + 1) * SIDE,
                ] = flipped[j * SIDE : (j + 1) * SIDE, k * SIDE : (k + 1) * SIDE]
    for c in range(3 * D // width):
        cols = slice(c * width, (c + 1) * width)
        stage[:, cols] = (
            contract(a_win_t, g_mix, cols) + dot_tn(a_reg, grad_mix[:, cols])
        ).astype(BF16)
    for c in range(D // width):
        cols = slice(c * width, (c + 1) * width)
        stage[:, 3 * D + c * width : 3 * D + (c + 1) * width] = (
            contract(ctx_t, g_mid, cols) + dot_tn(reg_ctx[...], grad_mid[:, cols])
        ).astype(BF16)
    if plan.empty:
        stage[:SIDE, ALL:] = jnp.zeros((SIDE, SIDE), BF16)
    for n, (send, homes) in enumerate(zip(sends, plan.scattered)):
        for j, home in enumerate(homes):
            move(small_out.at[home], send.at[j, pl.ds(plan.own * SIDE, TAIL), :], 5 + n).start()
            for i in range(plan.own):
                r = block_row[home * plan.own + i]
                c = block_col[home * plan.own + i]
                move(
                    stage.at[
                        pl.ds(pl.multiple_of(r * SIDE, SIDE), SIDE),
                        pl.ds(pl.multiple_of(c * SIDE, SIDE), SIDE),
                    ],
                    send.at[j, pl.ds(i * SIDE, SIDE), :],
                    5 + n,
                ).start()
    for copy in give:
        copy.wait()
    for n, send in enumerate(sends):
        move(send, send, 5 + n).wait()


def down_rows(w_all, start, count):
    return jnp.concatenate(
        [
            jnp.concatenate(
                [
                    w_all[k * SIDE : (k + 1) * SIDE, WIDE + r * SIDE : WIDE + (r + 1) * SIDE]
                    for k in range(D // SIDE)
                ],
                axis=1,
            )
            for r in range(start // SIDE, (start + count) // SIDE)
        ],
        axis=0,
    )


def layer(plan, block_row, block_col, small_row, shape, regions, cot_regions, patches, cot_patches, pieces):
    n_reg = regions.shape[0]
    rows = patches.shape[0] + n_reg
    part = rows // CHUNKS
    length = pieces[0].shape[1]
    vec = lambda r, c, dtype=F32: pltpu.VMEM((r, c), dtype)
    cube = lambda n, r, c, dtype=F32: pltpu.VMEM((n, r, c), dtype)
    in_smem = pl.BlockSpec(memory_space=pltpu.SMEM)
    in_vmem = pl.BlockSpec(memory_space=pltpu.VMEM)
    in_place = pl.BlockSpec(memory_space=pl.ANY)
    like = lambda a: jax.ShapeDtypeStruct(a.shape, BF16)
    return pl.pallas_call(
        functools.partial(layer_kernel, plan),
        in_specs=[in_smem] * 4 + [in_vmem, in_vmem, in_place, in_place] + [in_place] * len(pieces),
        out_specs=[in_vmem, in_place, in_vmem, in_place] + [in_place] * len(plan.scattered),
        out_shape=[like(regions), like(patches), like(regions), like(patches)]
        + [jax.ShapeDtypeStruct((len(h), length, LANES), BF16) for h in plan.scattered],
        scratch_shapes=[
            vec(D, ALL + SIDE, BF16),
            cube(plan.devices, TAIL, LANES, BF16),
            vec(56, LANES),
            cube(plan.devices, TAIL, LANES, BF16),
            vec(16, FF),
            vec(REG_PAD, D),
            vec(REG_PAD, D),
            vec(REG_PAD, 1),
            vec(REG_PAD, 3 * D, BF16),
            cube(GROUPS, REG_PAD, HEADS_PER * REG_PAD),
            vec(REG_PAD, D, BF16),
            vec(rows, D),
            vec(rows, D),
            vec(rows, 1),
            cube(3 * GROUPS, PAD * n_reg, LANES),
            cube(n_reg * GROUPS, PAD, HEADS_PER * PAD),
            cube(GROUPS, PAD * n_reg, LANES),
            vec(rows - n_reg, D, BF16),
            vec(rows - n_reg, D, BF16),
            vec(rows, D, BF16),
            cube(CHUNKS, D, part, BF16),
            cube(CHUNKS, D, part, BF16),
            cube(CHUNKS, D, part, BF16),
            cube(CHUNKS, D, part, BF16),
            vec(rows, D, BF16),
            vec(rows, 3 * D, BF16),
            vec(rows, FF, BF16),
            vec(rows, FF, BF16),
            vec(8, D),
            vec(1, FF),
            vec(1, 3 * D),
            pltpu.SemaphoreType.DMA((5 + len(plan.scattered),)),
        ],
        compiler_params=pltpu.CompilerParams(vmem_limit_bytes=VMEM_LIMIT),
        name="layer",
    )(block_row, block_col, small_row, shape, regions, cot_regions, patches, cot_patches, *pieces)


def shards(
    regions,
    patches,
    cot_regions,
    cot_patches,
    image_shape,
    owner,
    slot_weights,
    small,
    stats,
    roots,
    ema_slots,
    ema_small,
):
    axes = ("dp", "fsdp")
    devices = lax.axis_size(axes)
    entries = small.shape[0]
    own = slot_weights.shape[0]
    plan = Plan(lax.axis_size("dp"), lax.axis_size("fsdp"), own, entries)
    offset = lax.rem(lax.axis_index(axes) * entries, LANES)
    tail = lax.dynamic_update_slice(jnp.zeros(TAIL * LANES, BF16), small.astype(BF16), (offset,))
    mine = jnp.concatenate(
        [slot_weights.astype(BF16).reshape(own * SIDE, LANES), tail.reshape(TAIL, LANES)], axis=0
    )
    pieces = plan.gather(mine)
    by_token = lambda a: jnp.swapaxes(a, 0, 1).reshape(-1, D)
    homes = plan.device_of_homes(lax.axis_index("dp"), lax.axis_index("fsdp"))
    spots = (homes[:, None] * own + jnp.arange(own, dtype=jnp.int32)[None, :]).reshape(-1)
    numbers = jnp.arange(owner.shape[0], dtype=jnp.int32)
    block = jnp.sum(jnp.where(owner[None, :] == spots[:, None], numbers[None, :], 0), axis=1)
    block_row, block_col = block_places(block)
    small_row = homes * entries // LANES
    out_regions, out_patches, grad_regions, grad_patches, *sends = layer(
        plan,
        block_row,
        block_col,
        small_row,
        image_shape,
        regions,
        cot_regions,
        by_token(patches),
        by_token(cot_patches),
        pieces,
    )
    by_window = lambda a: jnp.swapaxes(a.reshape(-1, regions.shape[0], D), 0, 1)
    out_patches, grad_patches = by_window(out_patches), by_window(grad_patches)
    received = plan.scatter(sends)
    grad_slot = received[: own * SIDE].reshape(own, SIDE, SIDE)
    grad_small = lax.dynamic_slice(received[own * SIDE :].reshape(-1), (offset,), (entries,))
    precise = lax.Precision.HIGHEST
    left_stat = jnp.einsum("sij,skj->sik", grad_slot, grad_slot, precision=precise)
    right_stat = jnp.einsum("sji,sjk->sik", grad_slot, grad_slot, precision=precise)
    new_stats = STAT_DECAY * stats + (1.0 - STAT_DECAY) * jnp.stack([left_stat, right_stat], axis=1)
    direction = jnp.einsum("sij,sjk->sik", roots[:, 0], grad_slot, precision=precise)
    direction = jnp.einsum("sij,sjk->sik", direction, roots[:, 1], precision=precise)
    weight_rms = jnp.sqrt(
        jnp.mean(slot_weights * slot_weights, axis=(1, 2), keepdims=True) + EPS_MEAN
    )
    step_rms = jnp.sqrt(jnp.mean(direction * direction, axis=(1, 2), keepdims=True) + EPS_MEAN)
    new_slots = slot_weights - SHAMPOO_RATE * (weight_rms / step_rms) * direction
    token_count = regions.shape[0] * (patches.shape[1] + 1) * devices
    new_small = small - SMALL_RATE / math.sqrt(token_count) * grad_small
    new_ema_slots = EMA_DECAY * ema_slots + (1.0 - EMA_DECAY) * new_slots
    new_ema_small = EMA_DECAY * ema_small + (1.0 - EMA_DECAY) * new_small
    return (
        out_regions,
        out_patches,
        grad_regions,
        grad_patches,
        grad_slot,
        grad_small,
        new_stats,
        new_slots,
        new_small,
        new_ema_slots,
        new_ema_small,
    )


def solution(mesh):
    both = ("dp", "fsdp")
    ranks = (2, 3, 2, 3, 2, None, 3, 1, 4, 4, 3, 1)
    outs = (2, 3, 2, 3, 3, 1, 4, 3, 1, 3, 1)
    spec = lambda rank: P() if rank is None else P(both, *([None] * (rank - 1)))
    return jax.shard_map(
        shards,
        mesh=mesh,
        in_specs=tuple(spec(r) for r in ranks),
        out_specs=tuple(spec(r) for r in outs),
        check_vma=False,
    )
```

time: 199 us -> 182 us (0.915)
  Pallas kernels: 81.4 us -> 68.1 us
  local copies, waits for them, and re-layouts: 9.75 us -> 3.09 us
    pallas_call x1, Pallas kernels: 81.4 us -> 68.1 us  [layer(): pl.pallas_call(functools.partial(layer_kernel, plan), in_specs=[in_smem]...]
    unnamed x58, local copies, waits for them, and re-layouts: 8.36 us -> 2.61 us
    ppermute x1, waiting for transfers between devices: 1.72 us -> 4.16 us  [scatter(): came = lax.ppermute(mine[by].astype(BF16), 'dp', self.shift(by))]
  transfers between devices with their start and end apart: 30 -> 30, of which waited for: 17 -> 16; matrix products, arithmetic and copies ran while one was open for 5% -> 2% of each run, Pallas kernels for 0% -> 0%
where the time goes in v4:
time: 182 us
  waiting for transfers between devices  74.6 us (41%)
  Pallas kernels  68.1 us (37%)
  starting transfers between devices  24.6 us (14%)
  other arithmetic  7.63 us (4%)
  local copies, waits for them, and re-layouts  3.09 us (2%)
  matrix products  2.89 us (2%)
    pallas_call x1, Pallas kernels, layer(): pl.pallas_call(functools.partial(layer_kernel, plan), in_specs=[in_smem]...  68.1 us
    ppermute x3, waiting for transfers between devices, gather(): behind = lax.ppermute(behind, 'fsdp', self.backward)  22.1 us
    ppermute x3, waiting for transfers between devices, scatter(): ahead = lax.ppermute(ahead, 'fsdp', self.forward)  18.8 us
    ppermute x3, waiting for transfers between devices, scatter(): behind = lax.ppermute(behind, 'fsdp', self.backward)  10.8 us
    ppermute x1, waiting for transfers between devices, scatter(): ahead = lax.ppermute(far[:m], 'fsdp', self.forward)  5.22 us
    ppermute x1, waiting for transfers between devices, gather(): stack.append(lax.ppermute(mine[None], 'dp', self.shift(-by)))  4.99 us
    ppermute x3, starting transfers between devices, gather(): behind = lax.ppermute(behind, 'fsdp', self.backward)  4.62 us
    ppermute x3, starting transfers between devices, scatter(): behind = lax.ppermute(behind, 'fsdp', self.backward)  4.44 us
  transfers between devices with their start and end apart: 30, of which 16 were waited for; matrix products, arithmetic and copies ran while one was open for 2% of the time, Pallas kernels for 0%

profile of v4, /device:TPU:0, one launch (start us, length us, event | category | flops | bytes accessed | tf_op | source)
XLA Modules:
  0.0 181.9 jit_solution(4178509701199394710)
XLA Ops:
  1.3 1.3 multiply_reduce_fusion.1
  2.9 3.0 %collective-permute-start = (bf16[1,784,128]{2,1,0:T(8,128)(2,1)S(1)}, bf16[1,784,128]{2,1,0:T(8,128)(2,1)S(1)}, u32[]{:S(2)}, u32[]{:S(2)}) collective-permute-start(bf16[1,784,128]{2,1,0:T(8,128)(2,1)S(1)} %maximum_bitcast_fusion), channel_id=1, source_target_pairs={{0,16},{8,24},{16,0},{24,8},{1,17},{9,25},{17,1},{25,9},{2,18},{10... | collective-permute-start | bytes 602120 | tf_op jit(solution)/shard_map/ppermute | solution.py:169
  5.9 5.0 %collective-permute-done = bf16[1,784,128]{2,1,0:T(8,128)(2,1)S(1)} collective-permute-done((bf16[1,784,128]{2,1,0:T(8,128)(2,1)S(1)}, bf16[1,784,128]{2,1,0:T(8,128)(2,1)S(1)}, u32[]{:S(2)}, u32[]{:S(2)}) %collective-permute-start) | collective-permute-done | bytes 200736 | tf_op jit(solution)/shard_map/ppermute | solution.py:169
  10.9 1.8 %collective-permute-start.2 = (bf16[2,784,128]{2,1,0:T(8,128)(2,1)S(1)}, bf16[2,784,128]{2,1,0:T(8,128)(2,1)S(1)}, u32[]{:S(2)}, u32[]{:S(2)}) collective-permute-start(bf16[2,784,128]{2,1,0:T(8,128)(2,1)S(1)} %pad_maximum_fusion.rest_0_), channel_id=1, source_target_pairs={{0,1},{2,0},{4,2},{6,4},{7,6},{5,7},{3,5},{1,3},{8,9},{10,8},{12,1... | collective-permute-start | bytes 1204232 | tf_op jit(solution)/shard_map/ppermute | solution.py:176
  13.0 8.4 %collective-permute-done.2.rest_2_ = bf16[2,784,128]{2,1,0:T(8,128)(2,1)S(1)} collective-permute-done((bf16[2,784,128]{2,1,0:T(8,128)(2,1)S(1)}, bf16[2,784,128]{2,1,0:T(8,128)(2,1)S(1)}, u32[]{:S(2)}, u32[]{:S(2)}) %collective-permute-start.2) | collective-permute-done | bytes 401440 | tf_op jit(solution)/shard_map/ppermute | solution.py:176
  21.5 1.5 collective-permute-start.4
  23.5 7.5 %collective-permute-done.4.rest_4_ = bf16[2,784,128]{2,1,0:T(8,128)(2,1)S(1)} collective-permute-done((bf16[2,784,128]{2,1,0:T(8,128)(2,1)S(1)}, bf16[2,784,128]{2,1,0:T(8,128)(2,1)S(1)}, u32[]{:S(2)}, u32[]{:S(2)}) %collective-permute-start.4) | collective-permute-done | bytes 401440 | tf_op jit(solution)/shard_map/ppermute | solution.py:176
  31.0 1.3 collective-permute-start.6
  33.6 6.1 %collective-permute-done.6.rest_6_ = bf16[2,784,128]{2,1,0:T(8,128)(2,1)S(1)} collective-permute-done((bf16[2,784,128]{2,1,0:T(8,128)(2,1)S(1)}, bf16[2,784,128]{2,1,0:T(8,128)(2,1)S(1)}, u32[]{:S(2)}, u32[]{:S(2)}) %collective-permute-start.6) | collective-permute-done | bytes 401440 | tf_op jit(solution)/shard_map/ppermute | solution.py:176
  41.2 1.1 collective-permute-start.8
  42.4 0.9 collective-permute-start.7
  44.6 3.7 %collective-permute-done.8.rest_8_ = bf16[1,784,128]{2,1,0:T(8,128)(2,1)S(1)} collective-permute-done((bf16[1,784,128]{2,1,0:T(8,128)(2,1)S(1)}, bf16[1,784,128]{2,1,0:T(8,128)(2,1)S(1)}, u32[]{:S(2)}, u32[]{:S(2)}) %collective-permute-start.8) | collective-permute-done | bytes 200736 | tf_op jit(solution)/shard_map/ppermute | solution.py:179
  48.2 1.0 collective-permute-done.7.rest_7_
  51.7 68.1 %layer.1 = (bf16[24,512]{1,0:T(8,128)(2,1)}, bf16[1176,512]{1,0:T(8,128)(2,1)}, bf16[24,512]{1,0:T(8,128)(2,1)}, bf16[1176,512]{1,0:T(8,128)(2,1)}, bf16[6,784,1...) custom-call(s32[192]{0:T(256)} %get-tuple-element.78.block_row, ...), custom_call_target="tpu_custom_call" | custom-call | tf_op jit(solution)/shard_map/layer/pallas_call | solution.py:659
  120.4 2.6 %collective-permute-done.20 = bf16[6,784,128]{2,1,0:T(8,128)(2,1)S(1)} collective-permute-done((bf16[6,784,128]{2,1,0:T(8,128)(2,1)}, bf16[6,784,128]{2,1,0:T(8,128)(2,1)S(1)}, u32[]{:S(2)}, u32[]{:S(2)}) %collective-permute-start.20) | collective-permute-done | bytes 1204256 | tf_op jit(solution)/shard_map/ppermute | solution.py:184
  123.0 1.1 add_convert_fusion.6
  125.0 1.3 collective-permute-start.25
  126.3 5.2 %collective-permute-done.21 = bf16[1,784,128]{2,1,0:T(8,128)(2,1)S(1)} collective-permute-done((bf16[1,784,128]{2,1,0:T(8,128)(2,1)S(1)}, bf16[1,784,128]{2,1,0:T(8,128)(2,1)S(1)}, u32[]{:S(2)}, u32[]{:S(2)}) %collective-permute-start.21) | collective-permute-done | bytes 200736 | tf_op jit(solution)/shard_map/ppermute | solution.py:193
  132.2 1.5 collective-permute-start.22
  134.3 8.3 %collective-permute-done.22 = bf16[2,784,128]{2,1,0:T(8,128)(2,1)S(1)} collective-permute-done((bf16[2,784,128]{2,1,0:T(8,128)(2,1)S(1)}, bf16[2,784,128]{2,1,0:T(8,128)(2,1)S(1)}, u32[]{:S(2)}, u32[]{:S(2)}) %collective-permute-start.22) | collective-permute-done | bytes 401440 | tf_op jit(solution)/shard_map/ppermute | solution.py:201
  142.8 1.3 collective-permute-start.23
  144.1 8.2 %collective-permute-done.23 = bf16[2,784,128]{2,1,0:T(8,128)(2,1)S(1)} collective-permute-done((bf16[2,784,128]{2,1,0:T(8,128)(2,1)S(1)}, bf16[2,784,128]{2,1,0:T(8,128)(2,1)S(1)}, u32[]{:S(2)}, u32[]{:S(2)}) %collective-permute-start.23) | collective-permute-done | bytes 401440 | tf_op jit(solution)/shard_map/ppermute | solution.py:201
  152.7 1.8 collective-permute-start.27
  154.8 6.9 %collective-permute-done.27 = bf16[2,784,128]{2,1,0:T(8,128)(2,1)S(1)} collective-permute-done((bf16[2,784,128]{2,1,0:T(8,128)(2,1)S(1)}, bf16[2,784,128]{2,1,0:T(8,128)(2,1)S(1)}, u32[]{:S(2)}, u32[]{:S(2)}) %collective-permute-start.27) | collective-permute-done | bytes 401440 | tf_op jit(solution)/shard_map/ppermute | solution.py:202
  161.9 2.1 %collective-permute-start.28 = (bf16[2,784,128]{2,1,0:T(8,128)(2,1)S(1)}, bf16[2,784,128]{2,1,0:T(8,128)(2,1)S(1)}, u32[]{:S(2)}, u32[]{:S(2)}) collective-permute-start(bf16[2,784,128]{2,1,0:T(8,128)(2,1)S(1)} %add_convert_fusion), channel_id=1, source_target_pairs={{0,1},{2,0},{4,2},{6,4},{7,6},{5,7},{3,5},{1,3},{8,9},{10,8},{12,1... | collective-permute-start | bytes 1204232 | tf_op jit(solution)/shard_map/ppermute | solution.py:202
  163.9 2.2 %collective-permute-done.24 = bf16[2,784,128]{2,1,0:T(8,128)(2,1)S(1)} collective-permute-done((bf16[2,784,128]{2,1,0:T(8,128)(2,1)S(1)}, bf16[2,784,128]{2,1,0:T(8,128)(2,1)S(1)}, u32[]{:S(2)}, u32[]{:S(2)}) %collective-permute-start.24) | collective-permute-done | bytes 401440 | tf_op jit(solution)/shard_map/ppermute | solution.py:201
  166.2 3.9 %collective-permute-done.28 = bf16[2,784,128]{2,1,0:T(8,128)(2,1)S(1)} collective-permute-done((bf16[2,784,128]{2,1,0:T(8,128)(2,1)S(1)}, bf16[2,784,128]{2,1,0:T(8,128)(2,1)S(1)}, u32[]{:S(2)}, u32[]{:S(2)}) %collective-permute-start.28) | collective-permute-done | bytes 401440 | tf_op jit(solution)/shard_map/ppermute | solution.py:202
  170.3 1.6 collective-permute-start.29
  171.9 4.2 %collective-permute-done.29 = bf16[784,128]{1,0:T(8,128)(2,1)S(1)} collective-permute-done((bf16[784,128]{1,0:T(8,128)(2,1)S(1)}, bf16[784,128]{1,0:T(8,128)(2,1)S(1)}, u32[]{:S(2)}, u32[]{:S(2)}) %collective-permute-start.29) | collective-permute-done | bytes 200736 | tf_op jit(solution)/shard_map/ppermute | solution.py:206
  177.0 0.9 convolution_bitcast_fusion.1
  179.3 0.9 copy.40
  180.9 1.0 multiply_add_fusion
  (120 shorter events, 14.9 us)
Async XLA Ops:
  2.6 41.8 %copy-start.24 = (s32[192]{0:T(256)S(1)}, s32[192]{0:T(256)}, u32[]{:S(2)}) copy-start(s32[192]{0:T(256)} %param.17) | copy-start | bytes 2308
  2.9 8.0 %collective-permute-start = (bf16[1,784,128]{2,1,0:T(8,128)(2,1)S(1)}, bf16[1,784,128]{2,1,0:T(8,128)(2,1)S(1)}, u32[]{:S(2)}, u32[]{:S(2)}) collective-permute-start(bf16[1,784,128]{2,1,0:T(8,128)(2,1)S(1)} %maximum_bitcast_fusion), channel_id=1, source_target_pairs={{0,16},{8,24},{16,0},{24,8},{1,17},{9,25},{17,1},{25,9},{2,18},{10... | collective-permute-start | bytes 602120 | tf_op jit(solution)/shard_map/ppermute | solution.py:169
  10.9 40.6 %copy-start.1 = (bf16[2,784,128]{2,1,0:T(8,128)(2,1)}, bf16[2,784,128]{2,1,0:T(8,128)(2,1)S(1)}, u32[]{:S(2)}) copy-start(bf16[2,784,128]{2,1,0:T(8,128)(2,1)S(1)} %pad_maximum_fusion.rest_0_) | copy-start | bytes 1204228
  10.9 10.5 %collective-permute-start.2 = (bf16[2,784,128]{2,1,0:T(8,128)(2,1)S(1)}, bf16[2,784,128]{2,1,0:T(8,128)(2,1)S(1)}, u32[]{:S(2)}, u32[]{:S(2)}) collective-permute-start(bf16[2,784,128]{2,1,0:T(8,128)(2,1)S(1)} %pad_maximum_fusion.rest_0_), channel_id=1, source_target_pairs={{0,1},{2,0},{4,2},{6,4},{7,6},{5,7},{3,5},{1,3},{8,9},{10,8},{12,1... | collective-permute-start | bytes 1204232 | tf_op jit(solution)/shard_map/ppermute | solution.py:176
  12.8 10.2 %collective-permute-start.1 = (bf16[2,784,128]{2,1,0:T(8,128)(2,1)S(1)}, bf16[2,784,128]{2,1,0:T(8,128)(2,1)S(1)}, u32[]{:S(2)}, u32[]{:S(2)}) collective-permute-start(bf16[2,784,128]{2,1,0:T(8,128)(2,1)S(1)} %pad_maximum_fusion.rest_0_), channel_id=1, source_target_pairs={{0,2},{2,4},{4,6},{6,7},{7,5},{5,3},{3,1},{1,0},{8,10},{10,12},{12... | collective-permute-start | bytes 1204232 | tf_op jit(solution)/shard_map/ppermute | solution.py:175
  21.5 9.6 %collective-permute-start.4 = (bf16[2,784,128]{2,1,0:T(8,128)(2,1)S(1)}, bf16[2,784,128]{2,1,0:T(8,128)(2,1)S(1)}, u32[]{:S(2)}, u32[]{:S(2)}) collective-permute-start(bf16[2,784,128]{2,1,0:T(8,128)(2,1)S(1)} %collective-permute-done.2.rest_2_), channel_id=1, source_target_pairs={{0,1},{2,0},{4,2},{6,4},{7,6},{5,7},{3,5},{1,3},{8,9},{10,8},{12,1... | collective-permute-start | bytes 1204232 | tf_op jit(solution)/shard_map/ppermute | solution.py:176
  22.9 9.5 %collective-permute-start.3 = (bf16[2,784,128]{2,1,0:T(8,128)(2,1)S(1)}, bf16[2,784,128]{2,1,0:T(8,128)(2,1)S(1)}, u32[]{:S(2)}, u32[]{:S(2)}) collective-permute-start(bf16[2,784,128]{2,1,0:T(8,128)(2,1)S(1)} %collective-permute-done.1.rest_1_), channel_id=1, source_target_pairs={{0,2},{2,4},{4,6},{6,7},{7,5},{5,3},{3,1},{1,0},{8,10},{10,12},{12... | collective-permute-start | bytes 1204232 | tf_op jit(solution)/shard_map/ppermute | solution.py:175
  31.0 8.6 %collective-permute-start.6 = (bf16[2,784,128]{2,1,0:T(8,128)(2,1)S(1)}, bf16[2,784,128]{2,1,0:T(8,128)(2,1)S(1)}, u32[]{:S(2)}, u32[]{:S(2)}) collective-permute-start(bf16[2,784,128]{2,1,0:T(8,128)(2,1)S(1)} %collective-permute-done.4.rest_4_), channel_id=1, source_target_pairs={{0,1},{2,0},{4,2},{6,4},{7,6},{5,7},{3,5},{1,3},{8,9},{10,8},{12,1... | collective-permute-start | bytes 1204232 | tf_op jit(solution)/shard_map/ppermute | solution.py:176
  32.4 8.3 %collective-permute-start.5 = (bf16[2,784,128]{2,1,0:T(8,128)(2,1)S(1)}, bf16[2,784,128]{2,1,0:T(8,128)(2,1)S(1)}, u32[]{:S(2)}, u32[]{:S(2)}) collective-permute-start(bf16[2,784,128]{2,1,0:T(8,128)(2,1)S(1)} %collective-permute-done.3.rest_3_), channel_id=1, source_target_pairs={{0,2},{2,4},{4,6},{6,7},{7,5},{5,3},{3,1},{1,0},{8,10},{10,12},{12... | collective-permute-start | bytes 1204232 | tf_op jit(solution)/shard_map/ppermute | solution.py:175
  33.1 8.1 %collective-permute-start.9 = (bf16[2,784,128]{2,1,0:T(8,128)(2,1)S(1)}, bf16[2,784,128]{2,1,0:T(8,128)(2,1)S(1)}, u32[]{:S(2)}, u32[]{:S(2)}) collective-permute-start(bf16[2,784,128]{2,1,0:T(8,128)(2,1)S(1)} %pad_maximum_fusion.rest_0_), channel_id=1, source_target_pairs={{0,8},{8,0},{16,24},{24,16},{1,9},{9,1},{17,25},{25,17},{2,10},{10... | collective-permute-start | bytes 1204232 | tf_op jit(solution)/shard_map/ppermute | solution.py:180
  33.1 9.3 %collective-permute-start.11 = (bf16[2,784,128]{2,1,0:T(8,128)(2,1)S(1)}, bf16[2,784,128]{2,1,0:T(8,128)(2,1)}, u32[]{:S(2)}, u32[]{:S(2)}) collective-permute-start(bf16[2,784,128]{2,1,0:T(8,128)(2,1)S(1)} %collective-permute-done.2.rest_2_), channel_id=1, source_target_pairs={{0,8},{8,0},{16,24},{24,16},{1,9},{9,1},{17,25},{25,17},{2,10},{10... | collective-permute-start | bytes 1204232 | tf_op jit(solution)/shard_map/ppermute | solution.py:180
  33.6 9.7 %collective-permute-start.10 = (bf16[2,784,128]{2,1,0:T(8,128)(2,1)S(1)}, bf16[2,784,128]{2,1,0:T(8,128)(2,1)}, u32[]{:S(2)}, u32[]{:S(2)}) collective-permute-start(bf16[2,784,128]{2,1,0:T(8,128)(2,1)S(1)} %collective-permute-done.1.rest_1_), channel_id=1, source_target_pairs={{0,8},{8,0},{16,24},{24,16},{1,9},{9,1},{17,25},{25,17},{2,10},{10... | collective-permute-start | bytes 1204232 | tf_op jit(solution)/shard_map/ppermute | solution.py:180
  39.7 3.6 %collective-permute-start.13 = (bf16[2,784,128]{2,1,0:T(8,128)(2,1)S(1)}, bf16[2,784,128]{2,1,0:T(8,128)(2,1)}, u32[]{:S(2)}, u32[]{:S(2)}) collective-permute-start(bf16[2,784,128]{2,1,0:T(8,128)(2,1)S(1)} %collective-permute-done.4.rest_4_), channel_id=1, source_target_pairs={{0,8},{8,0},{16,24},{24,16},{1,9},{9,1},{17,25},{25,17},{2,10},{10... | collective-permute-start | bytes 1204232 | tf_op jit(solution)/shard_map/ppermute | solution.py:180
  40.7 9.2 %collective-permute-start.12 = (bf16[2,784,128]{2,1,0:T(8,128)(2,1)S(1)}, bf16[2,784,128]{2,1,0:T(8,128)(2,1)S(1)}, u32[]{:S(2)}, u32[]{:S(2)}) collective-permute-start(bf16[2,784,128]{2,1,0:T(8,128)(2,1)S(1)} %collective-permute-done.3.rest_3_), channel_id=1, source_target_pairs={{0,8},{8,0},{16,24},{24,16},{1,9},{9,1},{17,25},{25,17},{2,10},{10... | collective-permute-start | bytes 1204232 | tf_op jit(solution)/shard_map/ppermute | solution.py:180
  41.2 7.0 %collective-permute-start.8 = (bf16[1,784,128]{2,1,0:T(8,128)(2,1)S(1)}, bf16[1,784,128]{2,1,0:T(8,128)(2,1)S(1)}, u32[]{:S(2)}, u32[]{:S(2)}) collective-permute-start(bf16[1,784,128]{2,1,0:T(8,128)(2,1)S(1)} %slice.98), channel_id=1, source_target_pairs={{0,1},{2,0},{4,2},{6,4},{7,6},{5,7},{3,5},{1,3},{8,9},{10,8},{12,1... | collective-permute-start | bytes 602120 | tf_op jit(solution)/shard_map/ppermute | solution.py:179
  42.4 6.9 %collective-permute-start.7 = (bf16[1,784,128]{2,1,0:T(8,128)(2,1)S(1)}, bf16[1,784,128]{2,1,0:T(8,128)(2,1)S(1)}, u32[]{:S(2)}, u32[]{:S(2)}) collective-permute-start(bf16[1,784,128]{2,1,0:T(8,128)(2,1)S(1)} %slice.97), channel_id=1, source_target_pairs={{0,2},{2,4},{4,6},{6,7},{7,5},{5,3},{3,1},{1,0},{8,10},{10,12},{12... | collective-permute-start | bytes 602120 | tf_op jit(solution)/shard_map/ppermute | solution.py:178
  43.3 6.6 %collective-permute-start.15 = (bf16[2,784,128]{2,1,0:T(8,128)(2,1)S(1)}, bf16[2,784,128]{2,1,0:T(8,128)(2,1)S(1)}, u32[]{:S(2)}, u32[]{:S(2)}) collective-permute-start(bf16[2,784,128]{2,1,0:T(8,128)(2,1)S(1)} %collective-permute-done.6.rest_6_), channel_id=1, source_target_pairs={{0,8},{8,0},{16,24},{24,16},{1,9},{9,1},{17,25},{25,17},{2,10},{10... | collective-permute-start | bytes 1204232 | tf_op jit(solution)/shard_map/ppermute | solution.py:180
  43.3 7.4 %collective-permute-start.14 = (bf16[2,784,128]{2,1,0:T(8,128)(2,1)S(1)}, bf16[2,784,128]{2,1,0:T(8,128)(2,1)S(1)}, u32[]{:S(2)}, u32[]{:S(2)}) collective-permute-start(bf16[2,784,128]{2,1,0:T(8,128)(2,1)S(1)} %collective-permute-done.5.rest_5_), channel_id=1, source_target_pairs={{0,8},{8,0},{16,24},{24,16},{1,9},{9,1},{17,25},{25,17},{2,10},{10... | collective-permute-start | bytes 1204232 | tf_op jit(solution)/shard_map/ppermute | solution.py:180
  48.2 1.7 collective-permute-start.17
  49.3 1.4 collective-permute-start.16
  119.8 3.2 %collective-permute-start.20 = (bf16[6,784,128]{2,1,0:T(8,128)(2,1)}, bf16[6,784,128]{2,1,0:T(8,128)(2,1)S(1)}, u32[]{:S(2)}, u32[]{:S(2)}) collective-permute-start(bf16[6,784,128]{2,1,0:T(8,128)(2,1)} %get-tuple-element.30), channel_id=1, source_target_pairs={{0,8},{8,0},{16,24},{24,16},{1,9},{9,1},{17,25},{25,17},{2,10},{10... | collective-permute-start | bytes 3612680 | tf_op jit(solution)/shard_map/ppermute | solution.py:184
  120.3 14.0 %collective-permute-start.19 = (bf16[8,784,128]{2,1,0:T(8,128)(2,1)}, bf16[8,784,128]{2,1,0:T(8,128)(2,1)S(1)}, u32[]{:S(2)}, u32[]{:S(2)}) collective-permute-start(bf16[8,784,128]{2,1,0:T(8,128)(2,1)} %get-tuple-element.28), channel_id=1, source_target_pairs={{0,8},{8,0},{16,24},{24,16},{1,9},{9,1},{17,25},{25,17},{2,10},{10... | collective-permute-start | bytes 4816904 | tf_op jit(solution)/shard_map/ppermute | solution.py:184
  124.2 7.3 %collective-permute-start.21 = (bf16[1,784,128]{2,1,0:T(8,128)(2,1)S(1)}, bf16[1,784,128]{2,1,0:T(8,128)(2,1)S(1)}, u32[]{:S(2)}, u32[]{:S(2)}) collective-permute-start(bf16[1,784,128]{2,1,0:T(8,128)(2,1)S(1)} %get-tuple-element.73), channel_id=1, source_target_pairs={{0,2},{2,4},{4,6},{6,7},{7,5},{5,3},{3,1},{1,0},{8,10},{10,12},{12... | collective-permute-start | bytes 602120 | tf_op jit(solution)/shard_map/ppermute | solution.py:193
  125.0 6.9 %collective-permute-start.25 = (bf16[1,784,128]{2,1,0:T(8,128)(2,1)S(1)}, bf16[1,784,128]{2,1,0:T(8,128)(2,1)S(1)}, u32[]{:S(2)}, u32[]{:S(2)}) collective-permute-start(bf16[1,784,128]{2,1,0:T(8,128)(2,1)S(1)} %get-tuple-element.74), channel_id=1, source_target_pairs={{0,1},{2,0},{4,2},{6,4},{7,6},{5,7},{3,5},{1,3},{8,9},{10,8},{12,1... | collective-permute-start | bytes 602120 | tf_op jit(solution)/shard_map/ppermute | solution.py:194
  132.2 10.4 %collective-permute-start.22 = (bf16[2,784,128]{2,1,0:T(8,128)(2,1)S(1)}, bf16[2,784,128]{2,1,0:T(8,128)(2,1)S(1)}, u32[]{:S(2)}, u32[]{:S(2)}) collective-permute-start(bf16[2,784,128]{2,1,0:T(8,128)(2,1)S(1)} %get-tuple-element.71), channel_id=1, source_target_pairs={{0,2},{2,4},{4,6},{6,7},{7,5},{5,3},{3,1},{1,0},{8,10},{10,12},{12... | collective-permute-start | bytes 1204232 | tf_op jit(solution)/shard_map/ppermute | solution.py:201
  133.7 10.4 %collective-permute-start.26 = (bf16[2,784,128]{2,1,0:T(8,128)(2,1)S(1)}, bf16[2,784,128]{2,1,0:T(8,128)(2,1)S(1)}, u32[]{:S(2)}, u32[]{:S(2)}) collective-permute-start(bf16[2,784,128]{2,1,0:T(8,128)(2,1)S(1)} %get-tuple-element.72), channel_id=1, source_target_pairs={{0,1},{2,0},{4,2},{6,4},{7,6},{5,7},{3,5},{1,3},{8,9},{10,8},{12,1... | collective-permute-start | bytes 1204232 | tf_op jit(solution)/shard_map/ppermute | solution.py:202
  142.8 9.5 %collective-permute-start.23 = (bf16[2,784,128]{2,1,0:T(8,128)(2,1)S(1)}, bf16[2,784,128]{2,1,0:T(8,128)(2,1)S(1)}, u32[]{:S(2)}, u32[]{:S(2)}) collective-permute-start(bf16[2,784,128]{2,1,0:T(8,128)(2,1)S(1)} %add_convert_fusion.4), channel_id=1, source_target_pairs={{0,2},{2,4},{4,6},{6,7},{7,5},{5,3},{3,1},{1,0},{8,10},{10,12},{12... | collective-permute-start | bytes 1204232 | tf_op jit(solution)/shard_map/ppermute | solution.py:201
  152.7 9.0 %collective-permute-start.27 = (bf16[2,784,128]{2,1,0:T(8,128)(2,1)S(1)}, bf16[2,784,128]{2,1,0:T(8,128)(2,1)S(1)}, u32[]{:S(2)}, u32[]{:S(2)}) collective-permute-start(bf16[2,784,128]{2,1,0:T(8,128)(2,1)S(1)} %get-tuple-element.70), channel_id=1, source_target_pairs={{0,1},{2,0},{4,2},{6,4},{7,6},{5,7},{3,5},{1,3},{8,9},{10,8},{12,1... | collective-permute-start | bytes 1204232 | tf_op jit(solution)/shard_map/ppermute | solution.py:202
  154.5 9.5 %collective-permute-start.18 = (bf16[2,784,128]{2,1,0:T(8,128)(2,1)S(1)}, bf16[2,784,128]{2,1,0:T(8,128)(2,1)S(1)}, u32[]{:S(2)}, u32[]{:S(2)}) collective-permute-start(bf16[2,784,128]{2,1,0:T(8,128)(2,1)S(1)} %copy-done.27), channel_id=1, source_target_pairs={{0,8},{8,0},{16,24},{24,16},{1,9},{9,1},{17,25},{25,17},{2,10},{10... | collective-permute-start | bytes 1204232 | tf_op jit(solution)/shard_map/ppermute | solution.py:184
  154.5 11.7 %collective-permute-start.24 = (bf16[2,784,128]{2,1,0:T(8,128)(2,1)S(1)}, bf16[2,784,128]{2,1,0:T(8,128)(2,1)S(1)}, u32[]{:S(2)}, u32[]{:S(2)}) collective-permute-start(bf16[2,784,128]{2,1,0:T(8,128)(2,1)S(1)} %get-tuple-element.69), channel_id=1, source_target_pairs={{0,2},{2,4},{4,6},{6,7},{7,5},{5,3},{3,1},{1,0},{8,10},{10,12},{12... | collective-permute-start | bytes 1204232 | tf_op jit(solution)/shard_map/ppermute | solution.py:201
  161.9 8.2 %collective-permute-start.28 = (bf16[2,784,128]{2,1,0:T(8,128)(2,1)S(1)}, bf16[2,784,128]{2,1,0:T(8,128)(2,1)S(1)}, u32[]{:S(2)}, u32[]{:S(2)}) collective-permute-start(bf16[2,784,128]{2,1,0:T(8,128)(2,1)S(1)} %add_convert_fusion), channel_id=1, source_target_pairs={{0,1},{2,0},{4,2},{6,4},{7,6},{5,7},{3,5},{1,3},{8,9},{10,8},{12,1... | collective-permute-start | bytes 1204232 | tf_op jit(solution)/shard_map/ppermute | solution.py:202
  170.3 5.8 %collective-permute-start.29 = (bf16[784,128]{1,0:T(8,128)(2,1)S(1)}, bf16[784,128]{1,0:T(8,128)(2,1)S(1)}, u32[]{:S(2)}, u32[]{:S(2)}) collective-permute-start(bf16[784,128]{1,0:T(8,128)(2,1)S(1)} %fusion.8), channel_id=1, source_target_pairs={{0,16},{8,24},{16,0},{24,8},{1,17},{9,25},{17,1},{25,9},{2,18},{10... | collective-permute-start | bytes 602120 | tf_op jit(solution)/shard_map/ppermute | solution.py:206
  (26 other events, 251.8 us)

commit v5 on v4

--- a/solution.py
+++ b/solution.py
@@ -128,23 +128,74 @@
         self.forward = [(order[i], order[(i + 1) % n]) for i in range(n)]
         self.backward = [(order[i], order[i - 1]) for i in range(n)]
         self.flip = [(i, i ^ 1) for i in range(n_dp)]
+        self.far_slots = own // 2 if self.x_len == 2 else 0
+        self.near = (own - self.far_slots) * SIDE + TAIL
+        self.far = self.far_slots * SIDE
+        self.piece = self.x_len * self.near + self.far
+        self.cut = self.piece // 2
+        h = self.half
         self.gathered, self.scattered = [], []
-        xs = range(self.x_len)
-        h, m = self.half, self.x_len // 2
         for flip in (0, 1):
-            put = lambda k, part: self.gathered.append([self.home(flip, k, x) for x in part])
-            put(0, xs)
+            ring = lambda k: self.segments(flip, k)
+            add = lambda *parts: self.gathered.append(self.joined(parts))
+            add((ring(0), self.piece))
+            if self.far:
+                add(self.crossed(flip, 0))
             for k in range(1, h):
-                put(-k, xs)
-                put(k, xs)
-            put(-h, xs[:m])
-            put(h, xs[m:])
-            spots = [[h, h - 1, 1 - h]]
-            spots.append([k for j in range(h - 2, 0, -1) for k in (j, -j)])
-            spots.append([0])
-            for group in spots:
-                self.scattered.append([self.home(flip, k, x) for k in group for x in xs])
-        self.spots = spots
+                add((ring(-k), self.piece))
+                add((ring(k), self.piece))
+                if self.far:
+                    add(self.crossed(flip, -k), self.crossed(flip, k))
+            add((self.clip(ring(-h), 0, self.cut), self.cut))
+            add((self.clip(ring(h), self.cut, self.piece), self.piece - self.cut))
+            if self.far:
+                add(self.crossed(flip, h))
+        self.spots = [[h], [h - 1, 1 - h]]
+        self.spots += [[k, -k] for k in range(h - 2, 1, -1)]
+        self.spots += [[1, -1, 0]]
+        for flip in (0, 1):
+            for group in self.spots:
+                parts = []
+                for k in group:
+                    parts.append((self.segments(flip, k), self.piece))
+                    if self.far:
+                        parts.append(self.crossed(flip, k))
+                self.scattered.append(self.joined(parts))
+
+    def slots_at(self, home, start, first, count):
+        return [(start + i * SIDE, SIDE, home, first + i, 0) for i in range(count)]
+
+    def segments(self, flip, k):
+        near_slots = self.own - self.far_slots
+        found, at = [], 0
+        for x in range(self.x_len):
+            home = self.home(flip, k, x)
+            found += self.slots_at(home, at, 0, near_slots)
+            found.append((at + near_slots * SIDE, TAIL, home, None, 0))
+            at += self.near
+            if x == 0:
+                found += self.slots_at(home, at, near_slots, self.far_slots)
+                at += self.far
+        return found
+
+    def crossed(self, flip, k):
+        home = self.home(flip, k, 1)
+        return self.slots_at(home, 0, self.own - self.far_slots, self.far_slots), self.far
+
+    def clip(self, found, low, high):
+        kept = []
+        for at, rows, home, slot, inner in found:
+            start, stop = max(at, low), min(at + rows, high)
+            if start < stop:
+                kept.append((start - low, stop - start, home, slot, inner + start - at))
+        return kept
+
+    def joined(self, parts):
+        found, at = [], 0
+        for part, rows in parts:
+            found += [(at + row, *others) for row, *others in part]
+            at += rows
+        return found, at
 
     def home(self, flip, k, x):
         return (flip * self.ring + k % self.ring) * self.x_len + x % self.x_len
@@ -164,48 +215,70 @@
         return (x * 2 + core) * self.n_fsdp + z * self.y_len + y
 
     def gather(self, mine):
-        stack = [mine[None]]
+        cross = lambda a: lax.ppermute(a, "dp", self.shift(1))
+        near, far = mine[: self.near], mine[self.near :]
+        stack = [mine]
         for by in range(1, self.x_len):
-            stack.append(lax.ppermute(mine[None], "dp", self.shift(-by)))
+            stack.append(lax.ppermute(near, "dp", self.shift(-by)))
         first = jnp.concatenate(stack, axis=0)
         pieces = [first]
+        if self.far:
+            pieces.append(cross(far))
+        middle = slice(self.near, self.near + self.far)
         ahead = behind = first
-        m = self.x_len // 2
         for _ in range(1, self.half):
             ahead = lax.ppermute(ahead, "fsdp", self.forward)
             behind = lax.ppermute(behind, "fsdp", self.backward)
             pieces += [ahead, behind]
-        pieces.append(lax.ppermute(ahead[:m], "fsdp", self.forward))
-        pieces.append(lax.ppermute(behind[m:], "fsdp", self.backward))
+            if self.far:
+                pieces.append(cross(jnp.concatenate([ahead[middle], behind[middle]], axis=0)))
+        low = lax.ppermute(ahead[: self.cut], "fsdp", self.forward)
+        high = lax.ppermute(behind[self.cut :], "fsdp", self.backward)
+        pieces += [low, high]
+        if self.far:
+            ends = [low[self.near :], high[: self.near + self.far - self.cut]]
+            pieces.append(cross(jnp.concatenate(ends, axis=0)))
         return pieces + [lax.ppermute(piece, "dp", self.flip) for piece in pieces]
 
     def scatter(self, sends):
+        cross = lambda a: lax.ppermute(a, "dp", self.shift(1))
         n = len(self.spots)
         mixed = [lax.ppermute(send, "dp", self.flip) for send in sends[n:]]
+        long = self.piece + self.far
         parts = {}
         for spot, kept, came in zip(self.spots, sends[:n], mixed):
+            sums = {}
             for i, k in enumerate(spot):
-                at = slice(i * self.x_len, (i + 1) * self.x_len)
-                parts[k] = (kept[at], came[at])
-        total = lambda k: parts[k][0].astype(F32) + parts[k][1].astype(F32)
-        m = self.x_len // 2
-        far = total(self.half).astype(BF16)
-        ahead = lax.ppermute(far[:m], "fsdp", self.forward)
-        behind = lax.ppermute(far[m:], "fsdp", self.backward)
-        none = ((0, 0), (0, 0))
-        ahead = jnp.pad(ahead, ((0, self.x_len - m),) + none)
-        behind = jnp.pad(behind, ((m, 0),) + none)
+                at = slice(i * long, i * long + self.piece)
+                sums[k] = kept[at].astype(F32) + came[at].astype(F32)
+            if self.far:
+                outer = []
+                for i, k in enumerate(spot):
+                    at = slice(i * long + self.piece, (i + 1) * long)
+                    outer.append((kept[at].astype(F32) + came[at].astype(F32)).astype(BF16))
+                got = cross(jnp.concatenate(outer, axis=0) if len(outer) > 1 else outer[0])
+                below = self.piece - self.near - self.far
+                for i, k in enumerate(spot):
+                    inner = got[i * self.far : (i + 1) * self.far].astype(F32)
+                    sums[k] = sums[k] + jnp.pad(inner, ((self.near, below), (0, 0)))
+            parts.update(sums)
+        start = parts[self.half].astype(BF16)
+        ahead = lax.ppermute(start[: self.cut], "fsdp", self.forward)
+        behind = lax.ppermute(start[self.cut :], "fsdp", self.backward)
+        ahead = jnp.pad(ahead, ((0, self.piece - self.cut), (0, 0)))
+        behind = jnp.pad(behind, ((self.cut, 0), (0, 0)))
         for k in range(self.half - 1, 0, -1):
-            ahead = (total(k) + ahead.astype(F32)).astype(BF16)
-            behind = (total(-k) + behind.astype(F32)).astype(BF16)
+            ahead = (parts[k] + ahead.astype(F32)).astype(BF16)
+            behind = (parts[-k] + behind.astype(F32)).astype(BF16)
             ahead = lax.ppermute(ahead, "fsdp", self.forward)
             behind = lax.ppermute(behind, "fsdp", self.backward)
-        mine = total(0) + ahead.astype(F32) + behind.astype(F32)
-        result = mine[0]
+        mine = parts[0] + ahead.astype(F32) + behind.astype(F32)
+        inside = self.near + self.far
+        result, came = mine[:inside], []
         for by in range(1, self.x_len):
-            came = lax.ppermute(mine[by].astype(BF16), "dp", self.shift(by))
-            result = result + came.astype(F32)
-        return result
+            at = slice(inside + (by - 1) * self.near, inside + by * self.near)
+            came.append(lax.ppermute(mine[at].astype(BF16), "dp", self.shift(by)))
+        return result, came
 
 
 def block_places(block):
@@ -305,29 +378,32 @@
     ]
     for copy in bring:
         copy.start()
-    for piece, homes in zip(pieces, plan.gathered):
-        for j, home in enumerate(homes):
-            move(piece.at[j, pl.ds(plan.own * SIDE, TAIL), :], small_in.at[home], 3).start()
-    for piece, homes in zip(pieces, plan.gathered):
-        for j, home in enumerate(homes):
-            for i in range(plan.own):
-                r = block_row[home * plan.own + i]
-                c = block_col[home * plan.own + i]
-
-                def fetch(piece=piece, j=j, i=i, r=r, c=c):
-                    move(
-                        piece.at[j, pl.ds(i * SIDE, SIDE), :],
-                        w_all.at[
-                            pl.ds(pl.multiple_of(r * SIDE, SIDE), SIDE),
-                            pl.ds(pl.multiple_of(c * SIDE, SIDE), SIDE),
-                        ],
-                        4,
-                    ).start()
-
-                if plan.empty:
-                    pl.when(c < ALL // SIDE)(fetch)
-                else:
-                    fetch()
+    for piece, (found, _) in zip(pieces, plan.gathered):
+        for at, count, home, slot, inner in found:
+            if slot is None:
+                target = small_in.at[home, pl.ds(inner, count), :]
+                move(piece.at[pl.ds(at, count), :], target, 3).start()
+    for piece, (found, _) in zip(pieces, plan.gathered):
+        for at, count, home, slot, inner in found:
+            if slot is None:
+                continue
+            r = block_row[home * plan.own + slot]
+            c = block_col[home * plan.own + slot]
+
+            def fetch(piece=piece, at=at, count=count, inner=inner, r=r, c=c):
+                move(
+                    piece.at[pl.ds(at, count), :],
+                    w_all.at[
+                        pl.ds(pl.multiple_of(r * SIDE + inner, TAIL), count),
+                        pl.ds(pl.multiple_of(c * SIDE, SIDE), SIDE),
+                    ],
+                    4,
+                ).start()
+
+            if plan.empty:
+                pl.when(c < ALL // SIDE)(fetch)
+            else:
+                fetch()
 
     ends = []
     so_far = jnp.int32(0)
@@ -609,20 +685,19 @@
         ).astype(BF16)
     if plan.empty:
         stage[:SIDE, ALL:] = jnp.zeros((SIDE, SIDE), BF16)
-    for n, (send, homes) in enumerate(zip(sends, plan.scattered)):
-        for j, home in enumerate(homes):
-            move(small_out.at[home], send.at[j, pl.ds(plan.own * SIDE, TAIL), :], 5 + n).start()
-            for i in range(plan.own):
-                r = block_row[home * plan.own + i]
-                c = block_col[home * plan.own + i]
-                move(
-                    stage.at[
-                        pl.ds(pl.multiple_of(r * SIDE, SIDE), SIDE),
-                        pl.ds(pl.multiple_of(c * SIDE, SIDE), SIDE),
-                    ],
-                    send.at[j, pl.ds(i * SIDE, SIDE), :],
-                    5 + n,
-                ).start()
+    for n, (send, (found, _)) in enumerate(zip(sends, plan.scattered)):
+        for at, count, home, slot, inner in found:
+            target = send.at[pl.ds(at, count), :]
+            if slot is None:
+                move(small_out.at[home], target, 5 + n).start()
+                continue
+            r = block_row[home * plan.own + slot]
+            c = block_col[home * plan.own + slot]
+            block = stage.at[
+                pl.ds(pl.multiple_of(r * SIDE, SIDE), SIDE),
+                pl.ds(pl.multiple_of(c * SIDE, SIDE), SIDE),
+            ]
+            move(block, target, 5 + n).start()
     for copy in give:
         copy.wait()
     for n, send in enumerate(sends):
@@ -649,7 +724,6 @@
     n_reg = regions.shape[0]
     rows = patches.shape[0] + n_reg
     part = rows // CHUNKS
-    length = pieces[0].shape[1]
     vec = lambda r, c, dtype=F32: pltpu.VMEM((r, c), dtype)
     cube = lambda n, r, c, dtype=F32: pltpu.VMEM((n, r, c), dtype)
     in_smem = pl.BlockSpec(memory_space=pltpu.SMEM)
@@ -661,7 +735,7 @@
         in_specs=[in_smem] * 4 + [in_vmem, in_vmem, in_place, in_place] + [in_place] * len(pieces),
         out_specs=[in_vmem, in_place, in_vmem, in_place] + [in_place] * len(plan.scattered),
         out_shape=[like(regions), like(patches), like(regions), like(patches)]
-        + [jax.ShapeDtypeStruct((len(h), length, LANES), BF16) for h in plan.scattered],
+        + [jax.ShapeDtypeStruct((n, LANES), BF16) for _, n in plan.scattered],
         scratch_shapes=[
             vec(D, ALL + SIDE, BF16),
             cube(plan.devices, TAIL, LANES, BF16),
@@ -701,6 +775,44 @@
     )(block_row, block_col, small_row, shape, regions, cot_regions, patches, cot_patches, *pieces)
 
 
+def update_kernel(plan, summed, *rest):
+    count = plan.x_len - 1
+    came = rest[:count]
+    weights, stats, roots, ema, grads, new_stats, new_weights, new_ema = rest[count:]
+
+    def mean_square(values):
+        return jnp.mean(values * values, axis=(0, 1), keepdims=True) + EPS_MEAN
+
+    for i in range(plan.own):
+        if i < plan.own - plan.far_slots:
+            at = slice(i * SIDE, (i + 1) * SIDE)
+            grad = summed[at, :]
+            for part in came:
+                grad = grad + part[at, :].astype(F32)
+        else:
+            grad = summed[TAIL + i * SIDE : TAIL + (i + 1) * SIDE, :]
+        grads[i] = grad
+        grad_b = grad.astype(BF16)
+        new_stats[i, 0] = STAT_DECAY * stats[i, 0] + (1.0 - STAT_DECAY) * dot_nt(grad_b, grad_b)
+        new_stats[i, 1] = STAT_DECAY * stats[i, 1] + (1.0 - STAT_DECAY) * dot_tn(grad_b, grad_b)
+        half_way = dot_nn(roots[i, 0].astype(BF16), grad_b)
+        direction = dot_nn(half_way.astype(BF16), roots[i, 1].astype(BF16))
+        weight = weights[i]
+        ratio = jnp.sqrt(mean_square(weight)) / jnp.sqrt(mean_square(direction))
+        fresh = weight - SHAMPOO_RATE * ratio * direction
+        new_weights[i] = fresh
+        new_ema[i] = EMA_DECAY * ema[i] + (1.0 - EMA_DECAY) * fresh
+
+
+def update(plan, summed, came, weights, stats, roots, ema):
+    like = lambda a: jax.ShapeDtypeStruct(a.shape, F32)
+    return pl.pallas_call(
+        functools.partial(update_kernel, plan),
+        out_shape=[like(weights), like(stats), like(weights), like(weights)],
+        name="update",
+    )(summed, *came, weights, stats, roots, ema)
+
+
 def shards(
     regions,
     patches,
@@ -722,8 +834,14 @@
     plan = Plan(lax.axis_size("dp"), lax.axis_size("fsdp"), own, entries)
     offset = lax.rem(lax.axis_index(axes) * entries, LANES)
     tail = lax.dynamic_update_slice(jnp.zeros(TAIL * LANES, BF16), small.astype(BF16), (offset,))
+    held = slot_weights.astype(BF16).reshape(own * SIDE, LANES)
     mine = jnp.concatenate(
-        [slot_weights.astype(BF16).reshape(own * SIDE, LANES), tail.reshape(TAIL, LANES)], axis=0
+        [
+            held[: plan.near - TAIL],
+            tail.reshape(TAIL, LANES),
+            held[plan.near - TAIL :],
+        ],
+        axis=0,
     )
     pieces = plan.gather(mine)
     by_token = lambda a: jnp.swapaxes(a, 0, 1).reshape(-1, D)
@@ -747,23 +865,17 @@
     )
     by_window = lambda a: jnp.swapaxes(a.reshape(-1, regions.shape[0], D), 0, 1)
     out_patches, grad_patches = by_window(out_patches), by_window(grad_patches)
-    received = plan.scatter(sends)
-    grad_slot = received[: own * SIDE].reshape(own, SIDE, SIDE)
-    grad_small = lax.dynamic_slice(received[own * SIDE :].reshape(-1), (offset,), (entries,))
-    precise = lax.Precision.HIGHEST
-    left_stat = jnp.einsum("sij,skj->sik", grad_slot, grad_slot, precision=precise)
-    right_stat = jnp.einsum("sji,sjk->sik", grad_slot, grad_slot, precision=precise)
-    new_stats = STAT_DECAY * stats + (1.0 - STAT_DECAY) * jnp.stack([left_stat, right_stat], axis=1)
-    direction = jnp.einsum("sij,sjk->sik", roots[:, 0], grad_slot, precision=precise)
-    direction = jnp.einsum("sij,sjk->sik", direction, roots[:, 1], precision=precise)
-    weight_rms = jnp.sqrt(
-        jnp.mean(slot_weights * slot_weights, axis=(1, 2), keepdims=True) + EPS_MEAN
+    summed, came = plan.scatter(sends)
+    token_count = regions.shape[0] * (patches.shape[1] + 1) * devices
+    grad_slot, new_stats, new_slots, new_ema_slots = update(
+        plan, summed, came, slot_weights, stats, roots, ema_slots
     )
-    step_rms = jnp.sqrt(jnp.mean(direction * direction, axis=(1, 2), keepdims=True) + EPS_MEAN)
-    new_slots = slot_weights - SHAMPOO_RATE * (weight_rms / step_rms) * direction
-    token_count = regions.shape[0] * (patches.shape[1] + 1) * devices
+    small_at = slice(plan.near - TAIL, plan.near)
+    rows_small = summed[small_at]
+    for part in came:
+        rows_small = rows_small + part[small_at].astype(F32)
+    grad_small = lax.dynamic_slice(rows_small.reshape(-1), (offset,), (entries,))
     new_small = small - SMALL_RATE / math.sqrt(token_count) * grad_small
-    new_ema_slots = EMA_DECAY * ema_slots + (1.0 - EMA_DECAY) * new_slots
     new_ema_small = EMA_DECAY * ema_small + (1.0 - EMA_DECAY) * new_small
     return (
         out_regions,

time: 182 us -> 185 us (1.016)
  waiting for transfers between devices: 74.6 us -> 65.7 us
  starting transfers between devices: 24.6 us -> 32.8 us
  Pallas kernels: 68.1 us -> 72 us
  matrix products: 2.89 us -> 0 us
  local copies, waits for them, and re-layouts: 3.09 us -> 4.94 us
    ppermute x3, waiting for transfers between devices: 10.8 us -> 1.24 us  [scatter(): behind = lax.ppermute(behind, 'fsdp', self.backward)]
    ppermute x6 -> x15, starting transfers between devices: 8.79 us -> 18.3 us  [the longest x5 5.24 us: gather(): cross = lambda a: lax.ppermute(a, 'dp', self.shift(1))]
    ppermute x3, waiting for transfers between devices: 22.1 us -> 13 us  [gather(): behind = lax.ppermute(behind, 'fsdp', self.backward)]
    ppermute x6 -> x15, waiting for transfers between devices: 19.5 us -> 27.2 us  [the longest x4 8.95 us: scatter(): cross = lambda a: lax.ppermute(a, 'dp', self.shift(1))]
    ppermute x3, waiting for transfers between devices: 0.01 us -> 4.35 us  [gather(): ahead = lax.ppermute(ahead, 'fsdp', self.forward)]
    pallas_call x0 -> x1, Pallas kernels: none -> 3.93 us  [update(): pl.pallas_call(functools.partial(update_kernel, plan), out_shape=[like(we...]
    dot_general x4 -> x0, matrix products: 2.89 us -> none  [the longest x1 0.93 us: shards(): jnp.einsum('sij,skj->sik', grad_slot, grad_slot, precision=precise)]
    ppermute x3, starting transfers between devices: 3.1 us -> 0.86 us  [scatter(): ahead = lax.ppermute(ahead, 'fsdp', self.forward)]
  transfers between devices with their start and end apart: 30 -> 45, of which waited for: 16 -> 21; matrix products, arithmetic and copies ran while one was open for 2% -> 4% of each run, Pallas kernels for 0% -> 0%
where the time goes in v5:
time: 185 us; the launch traced here: 184 us
  Pallas kernels  72 us (39%)
  waiting for transfers between devices  65.7 us (36%)
  starting transfers between devices  32.8 us (18%)
  other arithmetic  7.76 us (4%)
  local copies, waits for them, and re-layouts  4.94 us (3%)
    pallas_call x1, Pallas kernels, layer(): pl.pallas_call(functools.partial(layer_kernel, plan), in_specs=[in_smem]...  68 us
    ppermute x3, waiting for transfers between devices, scatter(): ahead = lax.ppermute(ahead, 'fsdp', self.forward)  17.9 us
    ppermute x3, waiting for transfers between devices, gather(): behind = lax.ppermute(behind, 'fsdp', self.backward)  13 us
    ppermute x4, waiting for transfers between devices, scatter(): cross = lambda a: lax.ppermute(a, 'dp', self.shift(1))  8.95 us
    ppermute x5, waiting for transfers between devices, gather(): cross = lambda a: lax.ppermute(a, 'dp', self.shift(1))  7.2 us
    ppermute x3, starting transfers between devices, scatter(): behind = lax.ppermute(behind, 'fsdp', self.backward)  5.37 us
    ppermute x5, starting transfers between devices, gather(): cross = lambda a: lax.ppermute(a, 'dp', self.shift(1))  5.24 us
    ppermute x4, starting transfers between devices, scatter(): cross = lambda a: lax.ppermute(a, 'dp', self.shift(1))  4.66 us
  transfers between devices with their start and end apart: 45, of which 21 were waited for; matrix products, arithmetic and copies ran while one was open for 4% of the time, Pallas kernels for 0%

profile of v5, /device:TPU:0, one launch (start us, length us, event | category | flops | bytes accessed | tf_op | source)
XLA Modules:
  0.0 184.4 jit_solution(3179976708300710275)
XLA Ops:
  2.7 3.0 %collective-permute-start = (bf16[400,128]{1,0:T(8,128)(2,1)S(1)}, bf16[400,128]{1,0:T(8,128)(2,1)S(1)}, u32[]{:S(2)}, u32[]{:S(2)}) collective-permute-start(bf16[400,128]{1,0:T(8,128)(2,1)S(1)} %pad_maximum_fusion.7), channel_id=1, source_target_pairs={{0,16},{8,24},{16,0},{24,8},{1,17},{9,25},{17,1},{25,9},{2,18},{10... | collective-permute-start | bytes 307208 | tf_op jit(solution)/shard_map/ppermute | solution.py:222
  5.7 2.9 %collective-permute-done = bf16[400,128]{1,0:T(8,128)(2,1)S(1)} collective-permute-done((bf16[400,128]{1,0:T(8,128)(2,1)S(1)}, bf16[400,128]{1,0:T(8,128)(2,1)S(1)}, u32[]{:S(2)}, u32[]{:S(2)}) %collective-permute-start) | collective-permute-done | bytes 102432 | tf_op jit(solution)/shard_map/ppermute | solution.py:222
  8.6 1.9 %collective-permute-start.3 = (bf16[1184,128]{1,0:T(8,128)(2,1)S(1)}, bf16[1184,128]{1,0:T(8,128)(2,1)S(1)}, u32[]{:S(2)}, u32[]{:S(2)}) collective-permute-start(bf16[1184,128]{1,0:T(8,128)(2,1)S(1)} %pad_maximum_fusion.rest_0_), channel_id=1, source_target_pairs={{0,1},{2,0},{4,2},{6,4},{7,6},{5,7},{3,5},{1,3},{8,9},{10,8},{12,1... | collective-permute-start | bytes 909320 | tf_op jit(solution)/shard_map/ppermute | solution.py:231
  10.7 6.3 %collective-permute-done.3.rest_3_ = bf16[1184,128]{1,0:T(8,128)(2,1)S(1)} collective-permute-done((bf16[1184,128]{1,0:T(8,128)(2,1)S(1)}, bf16[1184,128]{1,0:T(8,128)(2,1)S(1)}, u32[]{:S(2)}, u32[]{:S(2)}) %collective-permute-start.3) | collective-permute-done | bytes 303136 | tf_op jit(solution)/shard_map/ppermute | solution.py:231
  17.0 1.2 collective-permute-start.6
  19.0 5.4 %collective-permute-done.6.rest_6_ = bf16[1184,128]{1,0:T(8,128)(2,1)S(1)} collective-permute-done((bf16[1184,128]{1,0:T(8,128)(2,1)S(1)}, bf16[1184,128]{1,0:T(8,128)(2,1)S(1)}, u32[]{:S(2)}, u32[]{:S(2)}) %collective-permute-start.6) | collective-permute-done | bytes 303136 | tf_op jit(solution)/shard_map/ppermute | solution.py:231
  25.3 2.0 %collective-permute-start.1 = (bf16[384,128]{1,0:T(8,128)(2,1)S(1)}, bf16[384,128]{1,0:T(8,128)(2,1)S(1)}, u32[]{:S(2)}, u32[]{:S(2)}) collective-permute-start(bf16[384,128]{1,0:T(8,128)(2,1)S(1)} %bitcast.22), channel_id=1, source_target_pairs={{0,16},{8,24},{16,0},{24,8},{1,17},{9,25},{17,1},{25,9},{2,18},{10... | collective-permute-start | bytes 294920 | tf_op jit(solution)/shard_map/ppermute | solution.py:218
  28.7 1.2 collective-permute-done.1.rest_1_
  30.0 1.3 collective-permute-done.9.rest_9_
  32.7 4.3 %collective-permute-done.8.rest_8_ = bf16[1184,128]{1,0:T(8,128)(2,1)S(1)} collective-permute-done((bf16[1184,128]{1,0:T(8,128)(2,1)S(1)}, bf16[1184,128]{1,0:T(8,128)(2,1)S(1)}, u32[]{:S(2)}, u32[]{:S(2)}) %collective-permute-start.8) | collective-permute-done | bytes 303136 | tf_op jit(solution)/shard_map/ppermute | solution.py:230
  38.4 1.6 collective-permute-start.12
  41.4 3.5 %collective-permute-done.12.rest_12_ = bf16[592,128]{1,0:T(8,128)(2,1)S(1)} collective-permute-done((bf16[592,128]{1,0:T(8,128)(2,1)}, bf16[592,128]{1,0:T(8,128)(2,1)S(1)}, u32[]{:S(2)}, u32[]{:S(2)}) %collective-permute-start.12) | collective-permute-done | bytes 151584 | tf_op jit(solution)/shard_map/ppermute | solution.py:236
  44.9 2.0 %collective-permute-done.11.rest_11_ = bf16[592,128]{1,0:T(8,128)(2,1)S(1)} collective-permute-done((bf16[592,128]{1,0:T(8,128)(2,1)}, bf16[592,128]{1,0:T(8,128)(2,1)S(1)}, u32[]{:S(2)}, u32[]{:S(2)}) %collective-permute-start.11) | collective-permute-done | bytes 151584 | tf_op jit(solution)/shard_map/ppermute | solution.py:235
  50.5 4.7 %collective-permute-done.10.rest_10_ = bf16[768,128]{1,0:T(8,128)(2,1)S(1)} collective-permute-done((bf16[768,128]{1,0:T(8,128)(2,1)S(1)}, bf16[768,128]{1,0:T(8,128)(2,1)S(1)}, u32[]{:S(2)}, u32[]{:S(2)}) %collective-permute-start.10) | collective-permute-done | bytes 196640 | tf_op jit(solution)/shard_map/ppermute | solution.py:218
  55.3 1.2 collective-permute-done.13.rest_13_
  59.9 68.0 %layer.1 = (bf16[24,512]{1,0:T(8,128)(2,1)}, bf16[1176,512]{1,0:T(8,128)(2,1)}, bf16[24,512]{1,0:T(8,128)(2,1)}, bf16[1176,512]{1,0:T(8,128)(2,1)}, bf16[1568,12...) custom-call(s32[192]{0:T(256)} %get-tuple-element.71.block_row, ...), custom_call_target="tpu_custom_call" | custom-call | tf_op jit(solution)/shard_map/layer/pallas_call | solution.py:733
  128.4 1.6 collective-permute-done.34
  130.9 1.3 collective-permute-start.35
  132.8 3.3 %collective-permute-done.35 = bf16[384,128]{1,0:T(8,128)(2,1)S(1)} collective-permute-done((bf16[384,128]{1,0:T(8,128)(2,1)S(1)}, bf16[384,128]{1,0:T(8,128)(2,1)S(1)}, u32[]{:S(2)}, u32[]{:S(2)}) %collective-permute-start.35) | collective-permute-done | bytes 98336 | tf_op jit(solution)/shard_map/ppermute | solution.py:244
  137.6 1.6 collective-permute-start.40
  139.3 1.2 collective-permute-start.33
  141.6 5.7 %collective-permute-done.33 = bf16[768,128]{1,0:T(8,128)(2,1)S(1)} collective-permute-done((bf16[768,128]{1,0:T(8,128)(2,1)S(1)}, bf16[768,128]{1,0:T(8,128)(2,1)S(1)}, u32[]{:S(2)}, u32[]{:S(2)}) %collective-permute-start.33) | collective-permute-done | bytes 196640 | tf_op jit(solution)/shard_map/ppermute | solution.py:244
  148.0 1.6 collective-permute-start.41
  149.8 1.2 collective-permute-start.29
  151.0 5.3 %collective-permute-done.37 = bf16[1184,128]{1,0:T(8,128)(2,1)S(1)} collective-permute-done((bf16[1184,128]{1,0:T(8,128)(2,1)S(1)}, bf16[1184,128]{1,0:T(8,128)(2,1)S(1)}, u32[]{:S(2)}, u32[]{:S(2)}) %collective-permute-start.37) | collective-permute-done | bytes 303136 | tf_op jit(solution)/shard_map/ppermute | solution.py:273
  157.4 2.0 %collective-permute-start.42 = (bf16[1184,128]{1,0:T(8,128)(2,1)S(1)}, bf16[1184,128]{1,0:T(8,128)(2,1)S(1)}, u32[]{:S(2)}, u32[]{:S(2)}) collective-permute-start(bf16[1184,128]{1,0:T(8,128)(2,1)S(1)} %get-tuple-element.52), channel_id=1, source_target_pairs={{0,1},{2,0},{4,2},{6,4},{7,6},{5,7},{3,5},{1,3},{8,9},{10,8},{12,1... | collective-permute-start | bytes 909320 | tf_op jit(solution)/shard_map/ppermute | solution.py:274
  159.5 7.8 %collective-permute-done.38 = bf16[1184,128]{1,0:T(8,128)(2,1)S(1)} collective-permute-done((bf16[1184,128]{1,0:T(8,128)(2,1)S(1)}, bf16[1184,128]{1,0:T(8,128)(2,1)S(1)}, u32[]{:S(2)}, u32[]{:S(2)}) %collective-permute-start.38) | collective-permute-done | bytes 303136 | tf_op jit(solution)/shard_map/ppermute | solution.py:273
  168.1 1.8 collective-permute-start.43
  169.9 4.8 %collective-permute-done.39 = bf16[1184,128]{1,0:T(8,128)(2,1)S(1)} collective-permute-done((bf16[1184,128]{1,0:T(8,128)(2,1)S(1)}, bf16[1184,128]{1,0:T(8,128)(2,1)S(1)}, u32[]{:S(2)}, u32[]{:S(2)}) %collective-permute-start.39) | collective-permute-done | bytes 303136 | tf_op jit(solution)/shard_map/ppermute | solution.py:273
  175.1 1.3 collective-permute-start.44
  177.1 2.7 %collective-permute-done.44.rest_0_ = bf16[400,128]{1,0:T(8,128)(2,1)S(1)} collective-permute-done((bf16[400,128]{1,0:T(8,128)(2,1)S(1)}, bf16[400,128]{1,0:T(8,128)(2,1)S(1)}, u32[]{:S(2)}, u32[]{:S(2)}) %collective-permute-start.44) | collective-permute-done | bytes 102432 | tf_op jit(solution)/shard_map/ppermute | solution.py:280
  180.5 3.9 %update.1 = (f32[6,128,128]{2,1,0:T(8,128)}, f32[6,2,128,128]{3,2,1,0:T(8,128)}, f32[6,128,128]{2,1,0:T(8,128)}, f32[6,128,128]{2,1,0:T(8,128)}) custom-call(f32[784,128]{1,0:T(8,128)} %slice.277.summed, bf16[400,128]{1,0:T(8,128)(2,1)} %copy-done.23, f32[6,128,128]{2,1,0:T(8,128)} %rest_1_.1, f32[6,2,128,128]{3,2,1,0:T(8,128)} %rest_2_.1, ...), custom_call_target="tpu_custom_call" | custom-call | tf_op jit(solution)/shard_map/update/pallas_call | solution.py:809
  (172 shorter events, 25.5 us)
Async XLA Ops:
  8.6 8.4 %collective-permute-start.3 = (bf16[1184,128]{1,0:T(8,128)(2,1)S(1)}, bf16[1184,128]{1,0:T(8,128)(2,1)S(1)}, u32[]{:S(2)}, u32[]{:S(2)}) collective-permute-start(bf16[1184,128]{1,0:T(8,128)(2,1)S(1)} %pad_maximum_fusion.rest_0_), channel_id=1, source_target_pairs={{0,1},{2,0},{4,2},{6,4},{7,6},{5,7},{3,5},{1,3},{8,9},{10,8},{12,1... | collective-permute-start | bytes 909320 | tf_op jit(solution)/shard_map/ppermute | solution.py:231
  10.4 7.8 %collective-permute-start.2 = (bf16[1184,128]{1,0:T(8,128)(2,1)S(1)}, bf16[1184,128]{1,0:T(8,128)(2,1)S(1)}, u32[]{:S(2)}, u32[]{:S(2)}) collective-permute-start(bf16[1184,128]{1,0:T(8,128)(2,1)S(1)} %pad_maximum_fusion.rest_0_), channel_id=1, source_target_pairs={{0,2},{2,4},{4,6},{6,7},{7,5},{5,3},{3,1},{1,0},{8,10},{10,12},{12... | collective-permute-start | bytes 909320 | tf_op jit(solution)/shard_map/ppermute | solution.py:230
  17.0 7.4 %collective-permute-start.6 = (bf16[1184,128]{1,0:T(8,128)(2,1)S(1)}, bf16[1184,128]{1,0:T(8,128)(2,1)S(1)}, u32[]{:S(2)}, u32[]{:S(2)}) collective-permute-start(bf16[1184,128]{1,0:T(8,128)(2,1)S(1)} %collective-permute-done.3.rest_3_), channel_id=1, source_target_pairs={{0,1},{2,0},{4,2},{6,4},{7,6},{5,7},{3,5},{1,3},{8,9},{10,8},{12,1... | collective-permute-start | bytes 909320 | tf_op jit(solution)/shard_map/ppermute | solution.py:231
  18.2 9.1 %collective-permute-start.5 = (bf16[1184,128]{1,0:T(8,128)(2,1)S(1)}, bf16[1184,128]{1,0:T(8,128)(2,1)S(1)}, u32[]{:S(2)}, u32[]{:S(2)}) collective-permute-start(bf16[1184,128]{1,0:T(8,128)(2,1)S(1)} %collective-permute-done.2.rest_2_), channel_id=1, source_target_pairs={{0,2},{2,4},{4,6},{6,7},{7,5},{5,3},{3,1},{1,0},{8,10},{10,12},{12... | collective-permute-start | bytes 909320 | tf_op jit(solution)/shard_map/ppermute | solution.py:230
  24.5 6.8 %collective-permute-start.9 = (bf16[1184,128]{1,0:T(8,128)(2,1)S(1)}, bf16[1184,128]{1,0:T(8,128)(2,1)S(1)}, u32[]{:S(2)}, u32[]{:S(2)}) collective-permute-start(bf16[1184,128]{1,0:T(8,128)(2,1)S(1)} %collective-permute-done.6.rest_6_), channel_id=1, source_target_pairs={{0,1},{2,0},{4,2},{6,4},{7,6},{5,7},{3,5},{1,3},{8,9},{10,8},{12,1... | collective-permute-start | bytes 909320 | tf_op jit(solution)/shard_map/ppermute | solution.py:231
  27.3 11.0 %collective-permute-start.14 = (bf16[1184,128]{1,0:T(8,128)(2,1)S(1)}, bf16[1184,128]{1,0:T(8,128)(2,1)S(1)}, u32[]{:S(2)}, u32[]{:S(2)}) collective-permute-start(bf16[1184,128]{1,0:T(8,128)(2,1)S(1)} %pad_maximum_fusion.rest_0_), channel_id=1, source_target_pairs={{0,8},{8,0},{16,24},{24,16},{1,9},{9,1},{17,25},{25,17},{2,10},{10... | collective-permute-start | bytes 909320 | tf_op jit(solution)/shard_map/ppermute | solution.py:241
  27.4 9.6 %collective-permute-start.8 = (bf16[1184,128]{1,0:T(8,128)(2,1)S(1)}, bf16[1184,128]{1,0:T(8,128)(2,1)S(1)}, u32[]{:S(2)}, u32[]{:S(2)}) collective-permute-start(bf16[1184,128]{1,0:T(8,128)(2,1)S(1)} %collective-permute-done.5.rest_5_), channel_id=1, source_target_pairs={{0,2},{2,4},{4,6},{6,7},{7,5},{5,3},{3,1},{1,0},{8,10},{10,12},{12... | collective-permute-start | bytes 909320 | tf_op jit(solution)/shard_map/ppermute | solution.py:230
  28.0 12.0 %collective-permute-start.4 = (bf16[768,128]{1,0:T(8,128)(2,1)S(1)}, bf16[768,128]{1,0:T(8,128)(2,1)S(1)}, u32[]{:S(2)}, u32[]{:S(2)}) collective-permute-start(bf16[768,128]{1,0:T(8,128)(2,1)S(1)} %pad_maximum_fusion.2), channel_id=1, source_target_pairs={{0,16},{8,24},{16,0},{24,8},{1,17},{9,25},{17,1},{25,9},{2,18},{10... | collective-permute-start | bytes 589832 | tf_op jit(solution)/shard_map/ppermute | solution.py:218
  29.9 7.8 %collective-permute-start.15 = (bf16[384,128]{1,0:T(8,128)(2,1)S(1)}, bf16[384,128]{1,0:T(8,128)(2,1)S(1)}, u32[]{:S(2)}, u32[]{:S(2)}) collective-permute-start(bf16[384,128]{1,0:T(8,128)(2,1)S(1)} %collective-permute-done.1.rest_1_), channel_id=1, source_target_pairs={{0,8},{8,0},{16,24},{24,16},{1,9},{9,1},{17,25},{25,17},{2,10},{10... | collective-permute-start | bytes 294920 | tf_op jit(solution)/shard_map/ppermute | solution.py:241
  31.3 10.1 %collective-permute-start.17 = (bf16[1184,128]{1,0:T(8,128)(2,1)S(1)}, bf16[1184,128]{1,0:T(8,128)(2,1)S(1)}, u32[]{:S(2)}, u32[]{:S(2)}) collective-permute-start(bf16[1184,128]{1,0:T(8,128)(2,1)S(1)} %collective-permute-done.3.rest_3_), channel_id=1, source_target_pairs={{0,8},{8,0},{16,24},{24,16},{1,9},{9,1},{17,25},{25,17},{2,10},{10... | collective-permute-start | bytes 909320 | tf_op jit(solution)/shard_map/ppermute | solution.py:241
  37.0 10.5 %collective-permute-start.16 = (bf16[1184,128]{1,0:T(8,128)(2,1)S(1)}, bf16[1184,128]{1,0:T(8,128)(2,1)S(1)}, u32[]{:S(2)}, u32[]{:S(2)}) collective-permute-start(bf16[1184,128]{1,0:T(8,128)(2,1)S(1)} %collective-permute-done.2.rest_2_), channel_id=1, source_target_pairs={{0,8},{8,0},{16,24},{24,16},{1,9},{9,1},{17,25},{25,17},{2,10},{10... | collective-permute-start | bytes 909320 | tf_op jit(solution)/shard_map/ppermute | solution.py:241
  37.7 9.2 %collective-permute-start.7 = (bf16[768,128]{1,0:T(8,128)(2,1)}, bf16[768,128]{1,0:T(8,128)(2,1)}, u32[]{:S(2)}, u32[]{:S(2)}) collective-permute-start(bf16[768,128]{1,0:T(8,128)(2,1)} %pad_maximum_fusion.3), channel_id=1, source_target_pairs={{0,16},{8,24},{16,0},{24,8},{1,17},{9,25},{17,1},{25,9},{2,18},{10... | collective-permute-start | bytes 589832 | tf_op jit(solution)/shard_map/ppermute | solution.py:218
  41.4 7.4 %collective-permute-start.18 = (bf16[768,128]{1,0:T(8,128)(2,1)}, bf16[768,128]{1,0:T(8,128)(2,1)S(1)}, u32[]{:S(2)}, u32[]{:S(2)}) collective-permute-start(bf16[768,128]{1,0:T(8,128)(2,1)} %copy-done.19), channel_id=1, source_target_pairs={{0,8},{8,0},{16,24},{24,16},{1,9},{9,1},{17,25},{25,17},{2,10},{10... | collective-permute-start | bytes 589832 | tf_op jit(solution)/shard_map/ppermute | solution.py:241
  47.5 7.8 %collective-permute-start.10 = (bf16[768,128]{1,0:T(8,128)(2,1)S(1)}, bf16[768,128]{1,0:T(8,128)(2,1)S(1)}, u32[]{:S(2)}, u32[]{:S(2)}) collective-permute-start(bf16[768,128]{1,0:T(8,128)(2,1)S(1)} %pad_maximum_fusion.4), channel_id=1, source_target_pairs={{0,16},{8,24},{16,0},{24,8},{1,17},{9,25},{17,1},{25,9},{2,18},{10... | collective-permute-start | bytes 589832 | tf_op jit(solution)/shard_map/ppermute | solution.py:218
  48.7 7.8 %collective-permute-start.13 = (bf16[384,128]{1,0:T(8,128)(2,1)S(1)}, bf16[384,128]{1,0:T(8,128)(2,1)S(1)}, u32[]{:S(2)}, u32[]{:S(2)}) collective-permute-start(bf16[384,128]{1,0:T(8,128)(2,1)S(1)} %pad_maximum_fusion.8), channel_id=1, source_target_pairs={{0,16},{8,24},{16,0},{24,8},{1,17},{9,25},{17,1},{25,9},{2,18},{10... | collective-permute-start | bytes 294920 | tf_op jit(solution)/shard_map/ppermute | solution.py:218
  49.9 9.0 %collective-permute-start.23 = (bf16[1184,128]{1,0:T(8,128)(2,1)S(1)}, bf16[1184,128]{1,0:T(8,128)(2,1)S(1)}, u32[]{:S(2)}, u32[]{:S(2)}) collective-permute-start(bf16[1184,128]{1,0:T(8,128)(2,1)S(1)} %collective-permute-done.9.rest_9_), channel_id=1, source_target_pairs={{0,8},{8,0},{16,24},{24,16},{1,9},{9,1},{17,25},{25,17},{2,10},{10... | collective-permute-start | bytes 909320 | tf_op jit(solution)/shard_map/ppermute | solution.py:241
  50.0 8.9 %collective-permute-start.22 = (bf16[1184,128]{1,0:T(8,128)(2,1)S(1)}, bf16[1184,128]{1,0:T(8,128)(2,1)S(1)}, u32[]{:S(2)}, u32[]{:S(2)}) collective-permute-start(bf16[1184,128]{1,0:T(8,128)(2,1)S(1)} %collective-permute-done.8.rest_8_), channel_id=1, source_target_pairs={{0,8},{8,0},{16,24},{24,16},{1,9},{9,1},{17,25},{25,17},{2,10},{10... | collective-permute-start | bytes 909320 | tf_op jit(solution)/shard_map/ppermute | solution.py:241
  50.5 7.4 %collective-permute-start.26 = (bf16[592,128]{1,0:T(8,128)(2,1)S(1)}, bf16[592,128]{1,0:T(8,128)(2,1)}, u32[]{:S(2)}, u32[]{:S(2)}) collective-permute-start(bf16[592,128]{1,0:T(8,128)(2,1)S(1)} %collective-permute-done.12.rest_12_), channel_id=1, source_target_pairs={{0,8},{8,0},{16,24},{24,16},{1,9},{9,1},{17,25},{25,17},{2,10},{10... | collective-permute-start | bytes 454664 | tf_op jit(solution)/shard_map/ppermute | solution.py:241
  132.2 7.0 %collective-permute-start.32 = (bf16[3136,128]{1,0:T(8,128)(2,1)}, bf16[3136,128]{1,0:T(8,128)(2,1)S(1)}, u32[]{:S(2)}, u32[]{:S(2)}) collective-permute-start(bf16[3136,128]{1,0:T(8,128)(2,1)} %get-tuple-element.36), channel_id=1, source_target_pairs={{0,8},{8,0},{16,24},{24,16},{1,9},{9,1},{17,25},{25,17},{2,10},{10... | collective-permute-start | bytes 2408456 | tf_op jit(solution)/shard_map/ppermute | solution.py:246
  132.2 8.3 %collective-permute-start.30 = (bf16[3136,128]{1,0:T(8,128)(2,1)}, bf16[3136,128]{1,0:T(8,128)(2,1)S(1)}, u32[]{:S(2)}, u32[]{:S(2)}) collective-permute-start(bf16[3136,128]{1,0:T(8,128)(2,1)} %get-tuple-element.34), channel_id=1, source_target_pairs={{0,8},{8,0},{16,24},{24,16},{1,9},{9,1},{17,25},{25,17},{2,10},{10... | collective-permute-start | bytes 2408456 | tf_op jit(solution)/shard_map/ppermute | solution.py:246
  132.7 16.9 %collective-permute-start.28 = (bf16[4704,128]{1,0:T(8,128)(2,1)}, bf16[4704,128]{1,0:T(8,128)(2,1)S(1)}, u32[]{:S(2)}, u32[]{:S(2)}) collective-permute-start(bf16[4704,128]{1,0:T(8,128)(2,1)} %get-tuple-element.32), channel_id=1, source_target_pairs={{0,8},{8,0},{16,24},{24,16},{1,9},{9,1},{17,25},{25,17},{2,10},{10... | collective-permute-start | bytes 3612680 | tf_op jit(solution)/shard_map/ppermute | solution.py:246
  137.1 10.1 %collective-permute-start.36 = (bf16[592,128]{1,0:T(8,128)(2,1)S(1)}, bf16[592,128]{1,0:T(8,128)(2,1)S(1)}, u32[]{:S(2)}, u32[]{:S(2)}) collective-permute-start(bf16[592,128]{1,0:T(8,128)(2,1)S(1)} %get-tuple-element.59), channel_id=1, source_target_pairs={{0,2},{2,4},{4,6},{6,7},{7,5},{5,3},{3,1},{1,0},{8,10},{10,12},{12... | collective-permute-start | bytes 454664 | tf_op jit(solution)/shard_map/ppermute | solution.py:266
  137.6 9.6 %collective-permute-start.40 = (bf16[592,128]{1,0:T(8,128)(2,1)S(1)}, bf16[592,128]{1,0:T(8,128)(2,1)S(1)}, u32[]{:S(2)}, u32[]{:S(2)}) collective-permute-start(bf16[592,128]{1,0:T(8,128)(2,1)S(1)} %get-tuple-element.60), channel_id=1, source_target_pairs={{0,1},{2,0},{4,2},{6,4},{7,6},{5,7},{3,5},{1,3},{8,9},{10,8},{12,1... | collective-permute-start | bytes 454664 | tf_op jit(solution)/shard_map/ppermute | solution.py:267
  139.3 7.9 %collective-permute-start.33 = (bf16[768,128]{1,0:T(8,128)(2,1)S(1)}, bf16[768,128]{1,0:T(8,128)(2,1)S(1)}, u32[]{:S(2)}, u32[]{:S(2)}) collective-permute-start(bf16[768,128]{1,0:T(8,128)(2,1)S(1)} %pad_maximum_fusion.6), channel_id=1, source_target_pairs={{0,16},{8,24},{16,0},{24,8},{1,17},{9,25},{17,1},{25,9},{2,18},{10... | collective-permute-start | bytes 589832 | tf_op jit(solution)/shard_map/ppermute | solution.py:244
  140.6 9.0 %collective-permute-start.31 = (bf16[768,128]{1,0:T(8,128)(2,1)S(1)}, bf16[768,128]{1,0:T(8,128)(2,1)S(1)}, u32[]{:S(2)}, u32[]{:S(2)}) collective-permute-start(bf16[768,128]{1,0:T(8,128)(2,1)S(1)} %pad_maximum_fusion.5), channel_id=1, source_target_pairs={{0,16},{8,24},{16,0},{24,8},{1,17},{9,25},{17,1},{25,9},{2,18},{10... | collective-permute-start | bytes 589832 | tf_op jit(solution)/shard_map/ppermute | solution.py:244
  147.5 8.8 %collective-permute-start.37 = (bf16[1184,128]{1,0:T(8,128)(2,1)S(1)}, bf16[1184,128]{1,0:T(8,128)(2,1)S(1)}, u32[]{:S(2)}, u32[]{:S(2)}) collective-permute-start(bf16[1184,128]{1,0:T(8,128)(2,1)S(1)} %get-tuple-element.53), channel_id=1, source_target_pairs={{0,2},{2,4},{4,6},{6,7},{7,5},{5,3},{3,1},{1,0},{8,10},{10,12},{12... | collective-permute-start | bytes 909320 | tf_op jit(solution)/shard_map/ppermute | solution.py:273
  148.0 9.1 %collective-permute-start.41 = (bf16[1184,128]{1,0:T(8,128)(2,1)S(1)}, bf16[1184,128]{1,0:T(8,128)(2,1)S(1)}, u32[]{:S(2)}, u32[]{:S(2)}) collective-permute-start(bf16[1184,128]{1,0:T(8,128)(2,1)S(1)} %get-tuple-element.54), channel_id=1, source_target_pairs={{0,1},{2,0},{4,2},{6,4},{7,6},{5,7},{3,5},{1,3},{8,9},{10,8},{12,1... | collective-permute-start | bytes 909320 | tf_op jit(solution)/shard_map/ppermute | solution.py:274
  149.8 9.7 %collective-permute-start.29 = (bf16[1152,128]{1,0:T(8,128)(2,1)S(1)}, bf16[1152,128]{1,0:T(8,128)(2,1)S(1)}, u32[]{:S(2)}, u32[]{:S(2)}) collective-permute-start(bf16[1152,128]{1,0:T(8,128)(2,1)S(1)} %pad_maximum_fusion.1), channel_id=1, source_target_pairs={{0,16},{8,24},{16,0},{24,8},{1,17},{9,25},{17,1},{25,9},{2,18},{10... | collective-permute-start | bytes 884744 | tf_op jit(solution)/shard_map/ppermute | solution.py:244
  157.4 10.0 %collective-permute-start.38 = (bf16[1184,128]{1,0:T(8,128)(2,1)S(1)}, bf16[1184,128]{1,0:T(8,128)(2,1)S(1)}, u32[]{:S(2)}, u32[]{:S(2)}) collective-permute-start(bf16[1184,128]{1,0:T(8,128)(2,1)S(1)} %get-tuple-element.51), channel_id=1, source_target_pairs={{0,2},{2,4},{4,6},{6,7},{7,5},{5,3},{3,1},{1,0},{8,10},{10,12},{12... | collective-permute-start | bytes 909320 | tf_op jit(solution)/shard_map/ppermute | solution.py:273
  157.4 10.1 %collective-permute-start.42 = (bf16[1184,128]{1,0:T(8,128)(2,1)S(1)}, bf16[1184,128]{1,0:T(8,128)(2,1)S(1)}, u32[]{:S(2)}, u32[]{:S(2)}) collective-permute-start(bf16[1184,128]{1,0:T(8,128)(2,1)S(1)} %get-tuple-element.52), channel_id=1, source_target_pairs={{0,1},{2,0},{4,2},{6,4},{7,6},{5,7},{3,5},{1,3},{8,9},{10,8},{12,1... | collective-permute-start | bytes 909320 | tf_op jit(solution)/shard_map/ppermute | solution.py:274
  167.8 6.9 %collective-permute-start.39 = (bf16[1184,128]{1,0:T(8,128)(2,1)S(1)}, bf16[1184,128]{1,0:T(8,128)(2,1)S(1)}, u32[]{:S(2)}, u32[]{:S(2)}) collective-permute-start(bf16[1184,128]{1,0:T(8,128)(2,1)S(1)} %get-tuple-element.46), channel_id=1, source_target_pairs={{0,2},{2,4},{4,6},{6,7},{7,5},{5,3},{3,1},{1,0},{8,10},{10,12},{12... | collective-permute-start | bytes 909320 | tf_op jit(solution)/shard_map/ppermute | solution.py:273
  168.1 6.8 %collective-permute-start.43 = (bf16[1184,128]{1,0:T(8,128)(2,1)S(1)}, bf16[1184,128]{1,0:T(8,128)(2,1)S(1)}, u32[]{:S(2)}, u32[]{:S(2)}) collective-permute-start(bf16[1184,128]{1,0:T(8,128)(2,1)S(1)} %get-tuple-element.47), channel_id=1, source_target_pairs={{0,1},{2,0},{4,2},{6,4},{7,6},{5,7},{3,5},{1,3},{8,9},{10,8},{12,1... | collective-permute-start | bytes 909320 | tf_op jit(solution)/shard_map/ppermute | solution.py:274
  (45 other events, 438.7 us)

commit v6 on v5

--- a/solution.py
+++ b/solution.py
@@ -217,33 +217,42 @@
     def gather(self, mine):
         cross = lambda a: lax.ppermute(a, "dp", self.shift(1))
         near, far = mine[: self.near], mine[self.near :]
+        turn = lambda a: lax.ppermute(a, "dp", self.flip)
         stack = [mine]
         for by in range(1, self.x_len):
             stack.append(lax.ppermute(near, "dp", self.shift(-by)))
         first = jnp.concatenate(stack, axis=0)
-        pieces = [first]
-        if self.far:
-            pieces.append(cross(far))
+        pieces, turned = [first], []
         middle = slice(self.near, self.near + self.far)
         ahead = behind = first
-        for _ in range(1, self.half):
-            ahead = lax.ppermute(ahead, "fsdp", self.forward)
-            behind = lax.ppermute(behind, "fsdp", self.backward)
-            pieces += [ahead, behind]
-            if self.far:
-                pieces.append(cross(jnp.concatenate([ahead[middle], behind[middle]], axis=0)))
-        low = lax.ppermute(ahead[: self.cut], "fsdp", self.forward)
-        high = lax.ppermute(behind[self.cut :], "fsdp", self.backward)
-        pieces += [low, high]
+        to_cross = far
+        for k in range(1, self.half + 1):
+            if k < self.half:
+                ahead = lax.ppermute(ahead, "fsdp", self.forward)
+                behind = lax.ppermute(behind, "fsdp", self.backward)
+            else:
+                ahead = lax.ppermute(ahead[: self.cut], "fsdp", self.forward)
+                behind = lax.ppermute(behind[self.cut :], "fsdp", self.backward)
+            beside = [cross(to_cross)] if self.far else []
+            fresh = [turn(piece) for piece in pieces[len(turned) :]]
+            ahead, behind, *rest = lax.optimization_barrier((ahead, behind, *beside, *fresh))
+            pieces += rest[: len(beside)] + [ahead, behind]
+            turned += rest[len(beside) :]
+            if k < self.half:
+                to_cross = jnp.concatenate([ahead[middle], behind[middle]], axis=0)
         if self.far:
-            ends = [low[self.near :], high[: self.near + self.far - self.cut]]
+            ends = [ahead[self.near :], behind[: self.near + self.far - self.cut]]
             pieces.append(cross(jnp.concatenate(ends, axis=0)))
-        return pieces + [lax.ppermute(piece, "dp", self.flip) for piece in pieces]
+        return pieces + turned + [turn(piece) for piece in pieces[len(turned) :]]
 
     def scatter(self, sends):
         cross = lambda a: lax.ppermute(a, "dp", self.shift(1))
         n = len(self.spots)
-        mixed = [lax.ppermute(send, "dp", self.flip) for send in sends[n:]]
+        mixed = []
+        for i, send in enumerate(sends[n:]):
+            if i >= 2:
+                send, mixed[i - 1] = lax.optimization_barrier((send, mixed[i - 1]))
+            mixed.append(lax.ppermute(send, "dp", self.flip))
         long = self.piece + self.far
         parts = {}
         for spot, kept, came in zip(self.spots, sends[:n], mixed):

time: 185 us -> 183 us (0.989)
    ppermute x3, waiting for transfers between devices: 13 us -> 4.08 us  [gather(): behind = lax.ppermute(behind, 'fsdp', self.backward)]
    ppermute x5, waiting for transfers between devices: 7.2 us -> 15.6 us  [gather(): cross = lambda a: lax.ppermute(a, 'dp', self.shift(1))]
    ppermute x3, waiting for transfers between devices: 17.9 us -> 11 us  [scatter(): ahead = lax.ppermute(ahead, 'fsdp', self.forward)]
    ppermute x3, starting transfers between devices: 0.86 us -> 5.03 us  [scatter(): ahead = lax.ppermute(ahead, 'fsdp', self.forward)]
    ppermute x3, starting transfers between devices: 5.37 us -> 1.2 us  [scatter(): behind = lax.ppermute(behind, 'fsdp', self.backward)]
    ppermute x3, waiting for transfers between devices: 1.24 us -> 4.98 us  [scatter(): behind = lax.ppermute(behind, 'fsdp', self.backward)]
    ppermute x20, waiting for transfers between devices: 7.43 us -> 10.1 us  [the longest x14 3.52 us: gather(): turn = lambda a: lax.ppermute(a, 'dp', self.flip)]
    ppermute x4, starting transfers between devices: 4.66 us -> 2.46 us  [scatter(): cross = lambda a: lax.ppermute(a, 'dp', self.shift(1))]
  transfers between devices with their start and end apart: 45 -> 45, of which waited for: 21 -> 28; matrix products, arithmetic and copies ran while one was open for 4% -> 4% of each run, Pallas kernels for 0% -> 0%
where the time goes in v6:
time: 183 us; the launch traced here: 182 us
  Pallas kernels  72 us (39%)
  waiting for transfers between devices  66.7 us (36%)
  starting transfers between devices  32 us (17%)
  other arithmetic  7.04 us (4%)
  local copies, waits for them, and re-layouts  3.32 us (2%)
    pallas_call x1, Pallas kernels, layer(): pl.pallas_call(functools.partial(layer_kernel, plan), in_specs=[in_smem]...  68 us
    ppermute x5, waiting for transfers between devices, gather(): cross = lambda a: lax.ppermute(a, 'dp', self.shift(1))  15.6 us
    ppermute x3, waiting for transfers between devices, scatter(): ahead = lax.ppermute(ahead, 'fsdp', self.forward)  11 us
    ppermute x4, waiting for transfers between devices, scatter(): cross = lambda a: lax.ppermute(a, 'dp', self.shift(1))  10.5 us
    ppermute x5, starting transfers between devices, gather(): cross = lambda a: lax.ppermute(a, 'dp', self.shift(1))  6.02 us
    ppermute x3, starting transfers between devices, scatter(): ahead = lax.ppermute(ahead, 'fsdp', self.forward)  5.03 us
    ppermute x3, waiting for transfers between devices, scatter(): behind = lax.ppermute(behind, 'fsdp', self.backward)  4.98 us
    ppermute x3, waiting for transfers between devices, gather(): ahead = lax.ppermute(ahead, 'fsdp', self.forward)  4.68 us
  transfers between devices with their start and end apart: 45, of which 28 were waited for; matrix products, arithmetic and copies ran while one was open for 4% of the time, Pallas kernels for 0%

profile of v6, /device:TPU:0, one launch (start us, length us, event | category | flops | bytes accessed | tf_op | source)
XLA Modules:
  0.0 182.3 jit_solution(12516593263090736547)
XLA Ops:
  2.7 3.0 %collective-permute-start = (bf16[400,128]{1,0:T(8,128)(2,1)S(1)}, bf16[400,128]{1,0:T(8,128)(2,1)S(1)}, u32[]{:S(2)}, u32[]{:S(2)}) collective-permute-start(bf16[400,128]{1,0:T(8,128)(2,1)S(1)} %pad_maximum_fusion.7), channel_id=1, source_target_pairs={{0,16},{8,24},{16,0},{24,8},{1,17},{9,25},{17,1},{25,9},{2,18},{10... | collective-permute-start | bytes 307208 | tf_op jit(solution)/shard_map/ppermute | solution.py:223
  5.7 2.9 %collective-permute-done = bf16[400,128]{1,0:T(8,128)(2,1)S(1)} collective-permute-done((bf16[400,128]{1,0:T(8,128)(2,1)S(1)}, bf16[400,128]{1,0:T(8,128)(2,1)S(1)}, u32[]{:S(2)}, u32[]{:S(2)}) %collective-permute-start) | collective-permute-done | bytes 102432 | tf_op jit(solution)/shard_map/ppermute | solution.py:223
  8.7 1.9 %collective-permute-start.2 = (bf16[1184,128]{1,0:T(8,128)(2,1)S(1)}, bf16[1184,128]{1,0:T(8,128)(2,1)S(1)}, u32[]{:S(2)}, u32[]{:S(2)}) collective-permute-start(bf16[1184,128]{1,0:T(8,128)(2,1)S(1)} %pad_maximum_fusion.rest_0_), channel_id=1, source_target_pairs={{0,1},{2,0},{4,2},{6,4},{7,6},{5,7},{3,5},{1,3},{8,9},{10,8},{12,1... | collective-permute-start | bytes 909320 | tf_op jit(solution)/shard_map/ppermute | solution.py:232
  10.7 1.8 collective-permute-start.3
  12.5 2.9 %collective-permute-done.3.rest_1_ = bf16[384,128]{1,0:T(8,128)(2,1)S(1)} collective-permute-done((bf16[384,128]{1,0:T(8,128)(2,1)S(1)}, bf16[384,128]{1,0:T(8,128)(2,1)S(1)}, u32[]{:S(2)}, u32[]{:S(2)}) %collective-permute-start.3) | collective-permute-done | bytes 98336 | tf_op jit(solution)/shard_map/ppermute | solution.py:218
  15.5 2.9 %collective-permute-done.2.rest_3_ = bf16[1184,128]{1,0:T(8,128)(2,1)S(1)} collective-permute-done((bf16[1184,128]{1,0:T(8,128)(2,1)S(1)}, bf16[1184,128]{1,0:T(8,128)(2,1)S(1)}, u32[]{:S(2)}, u32[]{:S(2)}) %collective-permute-start.2) | collective-permute-done | bytes 303136 | tf_op jit(solution)/shard_map/ppermute | solution.py:232
  20.5 1.7 collective-permute-start.6
  25.0 5.5 %collective-permute-done.7.rest_4_ = bf16[768,128]{1,0:T(8,128)(2,1)S(1)} collective-permute-done((bf16[768,128]{1,0:T(8,128)(2,1)S(1)}, bf16[768,128]{1,0:T(8,128)(2,1)S(1)}, u32[]{:S(2)}, u32[]{:S(2)}) %collective-permute-start.7) | collective-permute-done | bytes 196640 | tf_op jit(solution)/shard_map/ppermute | solution.py:218
  30.6 1.6 collective-permute-start.13
  34.4 2.5 %collective-permute-done.13.rest_7_ = bf16[768,128]{1,0:T(8,128)(2,1)} collective-permute-done((bf16[768,128]{1,0:T(8,128)(2,1)S(1)}, bf16[768,128]{1,0:T(8,128)(2,1)}, u32[]{:S(2)}, u32[]{:S(2)}) %collective-permute-start.13) | collective-permute-done | bytes 196640 | tf_op jit(solution)/shard_map/ppermute | solution.py:218
  36.9 1.6 collective-permute-done.14.rest_18_
  38.5 3.3 %collective-permute-done.11.rest_8_ = bf16[1184,128]{1,0:T(8,128)(2,1)S(1)} collective-permute-done((bf16[1184,128]{1,0:T(8,128)(2,1)S(1)}, bf16[1184,128]{1,0:T(8,128)(2,1)S(1)}, u32[]{:S(2)}, u32[]{:S(2)}) %collective-permute-start.11) | collective-permute-done | bytes 303136 | tf_op jit(solution)/shard_map/ppermute | solution.py:231
  48.7 2.6 %collective-permute-done.17.rest_11_ = bf16[592,128]{1,0:T(8,128)(2,1)S(1)} collective-permute-done((bf16[592,128]{1,0:T(8,128)(2,1)}, bf16[592,128]{1,0:T(8,128)(2,1)S(1)}, u32[]{:S(2)}, u32[]{:S(2)}) %collective-permute-start.17) | collective-permute-done | bytes 151584 | tf_op jit(solution)/shard_map/ppermute | solution.py:234
  51.3 1.7 collective-permute-done.19.rest_10_
  55.6 3.0 %collective-permute-done.23.rest_13_ = bf16[384,128]{1,0:T(8,128)(2,1)S(1)} collective-permute-done((bf16[384,128]{1,0:T(8,128)(2,1)S(1)}, bf16[384,128]{1,0:T(8,128)(2,1)S(1)}, u32[]{:S(2)}, u32[]{:S(2)}) %collective-permute-start.23) | collective-permute-done | bytes 98336 | tf_op jit(solution)/shard_map/ppermute | solution.py:218
  60.5 68.0 %layer.1 = (bf16[24,512]{1,0:T(8,128)(2,1)}, bf16[1176,512]{1,0:T(8,128)(2,1)}, bf16[24,512]{1,0:T(8,128)(2,1)}, bf16[1176,512]{1,0:T(8,128)(2,1)}, bf16[1568,12...) custom-call(s32[192]{0:T(256)} %get-tuple-element.123.block_row, ...), custom_call_target="tpu_custom_call" | custom-call | tf_op jit(solution)/shard_map/layer/pallas_call | solution.py:742
  129.1 2.6 %collective-permute-done.34 = bf16[1568,128]{1,0:T(8,128)(2,1)S(1)} collective-permute-done((bf16[1568,128]{1,0:T(8,128)(2,1)}, bf16[1568,128]{1,0:T(8,128)(2,1)S(1)}, u32[]{:S(2)}, u32[]{:S(2)}) %collective-permute-start.34) | collective-permute-done | bytes 401440 | tf_op jit(solution)/shard_map/ppermute | solution.py:255
  133.3 4.3 %collective-permute-done.35 = bf16[384,128]{1,0:T(8,128)(2,1)S(1)} collective-permute-done((bf16[384,128]{1,0:T(8,128)(2,1)S(1)}, bf16[384,128]{1,0:T(8,128)(2,1)S(1)}, u32[]{:S(2)}, u32[]{:S(2)}) %collective-permute-start.35) | collective-permute-done | bytes 98336 | tf_op jit(solution)/shard_map/ppermute | solution.py:249
  139.4 1.6 collective-permute-start.36
  141.5 3.5 %collective-permute-done.33 = bf16[768,128]{1,0:T(8,128)(2,1)S(1)} collective-permute-done((bf16[768,128]{1,0:T(8,128)(2,1)S(1)}, bf16[768,128]{1,0:T(8,128)(2,1)S(1)}, u32[]{:S(2)}, u32[]{:S(2)}) %collective-permute-start.33) | collective-permute-done | bytes 196640 | tf_op jit(solution)/shard_map/ppermute | solution.py:249
  146.5 1.6 collective-permute-start.37
  148.5 2.3 %collective-permute-done.32 = bf16[768,128]{1,0:T(8,128)(2,1)S(1)} collective-permute-done((bf16[768,128]{1,0:T(8,128)(2,1)S(1)}, bf16[768,128]{1,0:T(8,128)(2,1)S(1)}, u32[]{:S(2)}, u32[]{:S(2)}) %collective-permute-start.32) | collective-permute-done | bytes 196640 | tf_op jit(solution)/shard_map/ppermute | solution.py:249
  151.6 1.9 %collective-permute-done.37 = bf16[1184,128]{1,0:T(8,128)(2,1)S(1)} collective-permute-done((bf16[1184,128]{1,0:T(8,128)(2,1)S(1)}, bf16[1184,128]{1,0:T(8,128)(2,1)S(1)}, u32[]{:S(2)}, u32[]{:S(2)}) %collective-permute-start.37) | collective-permute-done | bytes 303136 | tf_op jit(solution)/shard_map/ppermute | solution.py:282
  155.1 1.6 collective-permute-start.38
  157.8 4.3 %collective-permute-done.38 = bf16[1184,128]{1,0:T(8,128)(2,1)S(1)} collective-permute-done((bf16[1184,128]{1,0:T(8,128)(2,1)S(1)}, bf16[1184,128]{1,0:T(8,128)(2,1)S(1)}, u32[]{:S(2)}, u32[]{:S(2)}) %collective-permute-start.38) | collective-permute-done | bytes 303136 | tf_op jit(solution)/shard_map/ppermute | solution.py:282
  162.0 1.8 %collective-permute-done.42 = bf16[1184,128]{1,0:T(8,128)(2,1)S(1)} collective-permute-done((bf16[1184,128]{1,0:T(8,128)(2,1)S(1)}, bf16[1184,128]{1,0:T(8,128)(2,1)S(1)}, u32[]{:S(2)}, u32[]{:S(2)}) %collective-permute-start.42) | collective-permute-done | bytes 303136 | tf_op jit(solution)/shard_map/ppermute | solution.py:283
  164.1 1.8 %collective-permute-start.39 = (bf16[1184,128]{1,0:T(8,128)(2,1)S(1)}, bf16[1184,128]{1,0:T(8,128)(2,1)S(1)}, u32[]{:S(2)}, u32[]{:S(2)}) collective-permute-start(bf16[1184,128]{1,0:T(8,128)(2,1)S(1)} %get-tuple-element.98), channel_id=1, source_target_pairs={{0,2},{2,4},{4,6},{6,7},{7,5},{5,3},{3,1},{1,0},{8,10},{10,12},{12... | collective-permute-start | bytes 909320 | tf_op jit(solution)/shard_map/ppermute | solution.py:282
  166.2 4.8 %collective-permute-done.39 = bf16[1184,128]{1,0:T(8,128)(2,1)S(1)} collective-permute-done((bf16[1184,128]{1,0:T(8,128)(2,1)S(1)}, bf16[1184,128]{1,0:T(8,128)(2,1)S(1)}, u32[]{:S(2)}, u32[]{:S(2)}) %collective-permute-start.39) | collective-permute-done | bytes 303136 | tf_op jit(solution)/shard_map/ppermute | solution.py:282
  171.0 1.8 collective-permute-done.43
  173.0 1.6 collective-permute-start.44
  175.3 2.4 %collective-permute-done.44.rest_0_ = bf16[400,128]{1,0:T(8,128)(2,1)S(1)} collective-permute-done((bf16[400,128]{1,0:T(8,128)(2,1)S(1)}, bf16[400,128]{1,0:T(8,128)(2,1)S(1)}, u32[]{:S(2)}, u32[]{:S(2)}) %collective-permute-start.44) | collective-permute-done | bytes 102432 | tf_op jit(solution)/shard_map/ppermute | solution.py:289
  178.4 3.9 %update.1 = (f32[6,128,128]{2,1,0:T(8,128)}, f32[6,2,128,128]{3,2,1,0:T(8,128)}, f32[6,128,128]{2,1,0:T(8,128)}, f32[6,128,128]{2,1,0:T(8,128)}) custom-call(f32[784,128]{1,0:T(8,128)} %slice.259.summed, bf16[400,128]{1,0:T(8,128)(2,1)} %copy-done.22, f32[6,128,128]{2,1,0:T(8,128)} %rest_1_.1, f32[6,2,128,128]{3,2,1,0:T(8,128)} %rest_2_.1, ...), custom_call_target="tpu_custom_call" | custom-call | tf_op jit(solution)/shard_map/update/pallas_call | solution.py:818
  (172 shorter events, 32.5 us)
Async XLA Ops:
  2.7 5.9 %collective-permute-start = (bf16[400,128]{1,0:T(8,128)(2,1)S(1)}, bf16[400,128]{1,0:T(8,128)(2,1)S(1)}, u32[]{:S(2)}, u32[]{:S(2)}) collective-permute-start(bf16[400,128]{1,0:T(8,128)(2,1)S(1)} %pad_maximum_fusion.7), channel_id=1, source_target_pairs={{0,16},{8,24},{16,0},{24,8},{1,17},{9,25},{17,1},{25,9},{2,18},{10... | collective-permute-start | bytes 307208 | tf_op jit(solution)/shard_map/ppermute | solution.py:223
  8.6 6.9 %collective-permute-start.4 = (bf16[1184,128]{1,0:T(8,128)(2,1)S(1)}, bf16[1184,128]{1,0:T(8,128)(2,1)S(1)}, u32[]{:S(2)}, u32[]{:S(2)}) collective-permute-start(bf16[1184,128]{1,0:T(8,128)(2,1)S(1)} %pad_maximum_fusion.rest_0_), channel_id=1, source_target_pairs={{0,8},{8,0},{16,24},{24,16},{1,9},{9,1},{17,25},{25,17},{2,10},{10... | collective-permute-start | bytes 909320 | tf_op jit(solution)/shard_map/ppermute | solution.py:220
  8.7 9.7 %collective-permute-start.2 = (bf16[1184,128]{1,0:T(8,128)(2,1)S(1)}, bf16[1184,128]{1,0:T(8,128)(2,1)S(1)}, u32[]{:S(2)}, u32[]{:S(2)}) collective-permute-start(bf16[1184,128]{1,0:T(8,128)(2,1)S(1)} %pad_maximum_fusion.rest_0_), channel_id=1, source_target_pairs={{0,1},{2,0},{4,2},{6,4},{7,6},{5,7},{3,5},{1,3},{8,9},{10,8},{12,1... | collective-permute-start | bytes 909320 | tf_op jit(solution)/shard_map/ppermute | solution.py:232
  10.5 9.3 %collective-permute-start.1 = (bf16[1184,128]{1,0:T(8,128)(2,1)S(1)}, bf16[1184,128]{1,0:T(8,128)(2,1)S(1)}, u32[]{:S(2)}, u32[]{:S(2)}) collective-permute-start(bf16[1184,128]{1,0:T(8,128)(2,1)S(1)} %pad_maximum_fusion.rest_0_), channel_id=1, source_target_pairs={{0,2},{2,4},{4,6},{6,7},{7,5},{5,3},{3,1},{1,0},{8,10},{10,12},{12... | collective-permute-start | bytes 909320 | tf_op jit(solution)/shard_map/ppermute | solution.py:231
  19.8 10.7 %collective-permute-start.9 = (bf16[1184,128]{1,0:T(8,128)(2,1)S(1)}, bf16[1184,128]{1,0:T(8,128)(2,1)S(1)}, u32[]{:S(2)}, u32[]{:S(2)}) collective-permute-start(bf16[1184,128]{1,0:T(8,128)(2,1)S(1)} %collective-permute-done.1.rest_2_), channel_id=1, source_target_pairs={{0,8},{8,0},{16,24},{24,16},{1,9},{9,1},{17,25},{25,17},{2,10},{10... | collective-permute-start | bytes 909320 | tf_op jit(solution)/shard_map/ppermute | solution.py:220
  19.9 10.6 %collective-permute-start.5 = (bf16[1184,128]{1,0:T(8,128)(2,1)S(1)}, bf16[1184,128]{1,0:T(8,128)(2,1)S(1)}, u32[]{:S(2)}, u32[]{:S(2)}) collective-permute-start(bf16[1184,128]{1,0:T(8,128)(2,1)S(1)} %collective-permute-done.1.rest_2_), channel_id=1, source_target_pairs={{0,2},{2,4},{4,6},{6,7},{7,5},{5,3},{3,1},{1,0},{8,10},{10,12},{12... | collective-permute-start | bytes 909320 | tf_op jit(solution)/shard_map/ppermute | solution.py:231
  20.3 10.2 %collective-permute-start.10 = (bf16[1184,128]{1,0:T(8,128)(2,1)S(1)}, bf16[1184,128]{1,0:T(8,128)(2,1)S(1)}, u32[]{:S(2)}, u32[]{:S(2)}) collective-permute-start(bf16[1184,128]{1,0:T(8,128)(2,1)S(1)} %collective-permute-done.2.rest_3_), channel_id=1, source_target_pairs={{0,8},{8,0},{16,24},{24,16},{1,9},{9,1},{17,25},{25,17},{2,10},{10... | collective-permute-start | bytes 909320 | tf_op jit(solution)/shard_map/ppermute | solution.py:220
  20.5 10.0 %collective-permute-start.6 = (bf16[1184,128]{1,0:T(8,128)(2,1)S(1)}, bf16[1184,128]{1,0:T(8,128)(2,1)S(1)}, u32[]{:S(2)}, u32[]{:S(2)}) collective-permute-start(bf16[1184,128]{1,0:T(8,128)(2,1)S(1)} %collective-permute-done.2.rest_3_), channel_id=1, source_target_pairs={{0,1},{2,0},{4,2},{6,4},{7,6},{5,7},{3,5},{1,3},{8,9},{10,8},{12,1... | collective-permute-start | bytes 909320 | tf_op jit(solution)/shard_map/ppermute | solution.py:232
  23.5 7.0 %collective-permute-start.7 = (bf16[768,128]{1,0:T(8,128)(2,1)S(1)}, bf16[768,128]{1,0:T(8,128)(2,1)S(1)}, u32[]{:S(2)}, u32[]{:S(2)}) collective-permute-start(bf16[768,128]{1,0:T(8,128)(2,1)S(1)} %pad_maximum_fusion.2), channel_id=1, source_target_pairs={{0,16},{8,24},{16,0},{24,8},{1,17},{9,25},{17,1},{25,9},{2,18},{10... | collective-permute-start | bytes 589832 | tf_op jit(solution)/shard_map/ppermute | solution.py:218
  30.6 6.3 %collective-permute-start.13 = (bf16[768,128]{1,0:T(8,128)(2,1)S(1)}, bf16[768,128]{1,0:T(8,128)(2,1)}, u32[]{:S(2)}, u32[]{:S(2)}) collective-permute-start(bf16[768,128]{1,0:T(8,128)(2,1)S(1)} %pad_maximum_fusion.3), channel_id=1, source_target_pairs={{0,16},{8,24},{16,0},{24,8},{1,17},{9,25},{17,1},{25,9},{2,18},{10... | collective-permute-start | bytes 589832 | tf_op jit(solution)/shard_map/ppermute | solution.py:218
  32.1 6.3 %collective-permute-start.15 = (bf16[1184,128]{1,0:T(8,128)(2,1)S(1)}, bf16[1184,128]{1,0:T(8,128)(2,1)S(1)}, u32[]{:S(2)}, u32[]{:S(2)}) collective-permute-start(bf16[1184,128]{1,0:T(8,128)(2,1)S(1)} %collective-permute-done.5.rest_5_), channel_id=1, source_target_pairs={{0,8},{8,0},{16,24},{24,16},{1,9},{9,1},{17,25},{25,17},{2,10},{10... | collective-permute-start | bytes 909320 | tf_op jit(solution)/shard_map/ppermute | solution.py:220
  32.1 9.6 %collective-permute-start.11 = (bf16[1184,128]{1,0:T(8,128)(2,1)S(1)}, bf16[1184,128]{1,0:T(8,128)(2,1)S(1)}, u32[]{:S(2)}, u32[]{:S(2)}) collective-permute-start(bf16[1184,128]{1,0:T(8,128)(2,1)S(1)} %collective-permute-done.5.rest_5_), channel_id=1, source_target_pairs={{0,2},{2,4},{4,6},{6,7},{7,5},{5,3},{3,1},{1,0},{8,10},{10,12},{12... | collective-permute-start | bytes 909320 | tf_op jit(solution)/shard_map/ppermute | solution.py:231
  33.3 8.4 %collective-permute-start.16 = (bf16[1184,128]{1,0:T(8,128)(2,1)S(1)}, bf16[1184,128]{1,0:T(8,128)(2,1)}, u32[]{:S(2)}, u32[]{:S(2)}) collective-permute-start(bf16[1184,128]{1,0:T(8,128)(2,1)S(1)} %collective-permute-done.6.rest_6_), channel_id=1, source_target_pairs={{0,8},{8,0},{16,24},{24,16},{1,9},{9,1},{17,25},{25,17},{2,10},{10... | collective-permute-start | bytes 909320 | tf_op jit(solution)/shard_map/ppermute | solution.py:220
  33.5 9.4 %collective-permute-start.12 = (bf16[1184,128]{1,0:T(8,128)(2,1)S(1)}, bf16[1184,128]{1,0:T(8,128)(2,1)S(1)}, u32[]{:S(2)}, u32[]{:S(2)}) collective-permute-start(bf16[1184,128]{1,0:T(8,128)(2,1)S(1)} %collective-permute-done.6.rest_6_), channel_id=1, source_target_pairs={{0,1},{2,0},{4,2},{6,4},{7,6},{5,7},{3,5},{1,3},{8,9},{10,8},{12,1... | collective-permute-start | bytes 909320 | tf_op jit(solution)/shard_map/ppermute | solution.py:232
  44.6 8.4 %collective-permute-start.21 = (bf16[1184,128]{1,0:T(8,128)(2,1)S(1)}, bf16[1184,128]{1,0:T(8,128)(2,1)}, u32[]{:S(2)}, u32[]{:S(2)}) collective-permute-start(bf16[1184,128]{1,0:T(8,128)(2,1)S(1)} %collective-permute-done.11.rest_8_), channel_id=1, source_target_pairs={{0,8},{8,0},{16,24},{24,16},{1,9},{9,1},{17,25},{25,17},{2,10},{10... | collective-permute-start | bytes 909320 | tf_op jit(solution)/shard_map/ppermute | solution.py:220
  44.7 8.4 %collective-permute-start.22 = (bf16[1184,128]{1,0:T(8,128)(2,1)S(1)}, bf16[1184,128]{1,0:T(8,128)(2,1)S(1)}, u32[]{:S(2)}, u32[]{:S(2)}) collective-permute-start(bf16[1184,128]{1,0:T(8,128)(2,1)S(1)} %collective-permute-done.12.rest_9_), channel_id=1, source_target_pairs={{0,8},{8,0},{16,24},{24,16},{1,9},{9,1},{17,25},{25,17},{2,10},{10... | collective-permute-start | bytes 909320 | tf_op jit(solution)/shard_map/ppermute | solution.py:220
  45.2 6.1 %collective-permute-start.17 = (bf16[592,128]{1,0:T(8,128)(2,1)}, bf16[592,128]{1,0:T(8,128)(2,1)S(1)}, u32[]{:S(2)}, u32[]{:S(2)}) collective-permute-start(bf16[592,128]{1,0:T(8,128)(2,1)} %slice.189), channel_id=1, source_target_pairs={{0,2},{2,4},{4,6},{6,7},{7,5},{5,3},{3,1},{1,0},{8,10},{10,12},{12... | collective-permute-start | bytes 454664 | tf_op jit(solution)/shard_map/ppermute | solution.py:234
  46.3 6.7 %collective-permute-start.19 = (bf16[768,128]{1,0:T(8,128)(2,1)S(1)}, bf16[768,128]{1,0:T(8,128)(2,1)S(1)}, u32[]{:S(2)}, u32[]{:S(2)}) collective-permute-start(bf16[768,128]{1,0:T(8,128)(2,1)S(1)} %pad_maximum_fusion.4), channel_id=1, source_target_pairs={{0,16},{8,24},{16,0},{24,8},{1,17},{9,25},{17,1},{25,9},{2,18},{10... | collective-permute-start | bytes 589832 | tf_op jit(solution)/shard_map/ppermute | solution.py:218
  53.1 6.0 %collective-permute-start.25 = (bf16[592,128]{1,0:T(8,128)(2,1)S(1)}, bf16[592,128]{1,0:T(8,128)(2,1)}, u32[]{:S(2)}, u32[]{:S(2)}) collective-permute-start(bf16[592,128]{1,0:T(8,128)(2,1)S(1)} %collective-permute-done.17.rest_11_), channel_id=1, source_target_pairs={{0,8},{8,0},{16,24},{24,16},{1,9},{9,1},{17,25},{25,17},{2,10},{10... | collective-permute-start | bytes 454664 | tf_op jit(solution)/shard_map/ppermute | solution.py:220
  53.2 5.9 %collective-permute-start.26 = (bf16[592,128]{1,0:T(8,128)(2,1)S(1)}, bf16[592,128]{1,0:T(8,128)(2,1)S(1)}, u32[]{:S(2)}, u32[]{:S(2)}) collective-permute-start(bf16[592,128]{1,0:T(8,128)(2,1)S(1)} %collective-permute-done.18.rest_12_), channel_id=1, source_target_pairs={{0,8},{8,0},{16,24},{24,16},{1,9},{9,1},{17,25},{25,17},{2,10},{10... | collective-permute-start | bytes 454664 | tf_op jit(solution)/shard_map/ppermute | solution.py:220
  133.3 8.2 %collective-permute-start.29 = (bf16[3136,128]{1,0:T(8,128)(2,1)}, bf16[3136,128]{1,0:T(8,128)(2,1)S(1)}, u32[]{:S(2)}, u32[]{:S(2)}) collective-permute-start(bf16[3136,128]{1,0:T(8,128)(2,1)} %get-tuple-element.83), channel_id=1, source_target_pairs={{0,8},{8,0},{16,24},{24,16},{1,9},{9,1},{17,25},{25,17},{2,10},{10... | collective-permute-start | bytes 2408456 | tf_op jit(solution)/shard_map/ppermute | solution.py:255
  138.7 6.2 %collective-permute-start.33 = (bf16[768,128]{1,0:T(8,128)(2,1)S(1)}, bf16[768,128]{1,0:T(8,128)(2,1)S(1)}, u32[]{:S(2)}, u32[]{:S(2)}) collective-permute-start(bf16[768,128]{1,0:T(8,128)(2,1)S(1)} %pad_maximum_fusion.6), channel_id=1, source_target_pairs={{0,16},{8,24},{16,0},{24,8},{1,17},{9,25},{17,1},{25,9},{2,18},{10... | collective-permute-start | bytes 589832 | tf_op jit(solution)/shard_map/ppermute | solution.py:249
  139.4 6.3 %collective-permute-start.36 = (bf16[592,128]{1,0:T(8,128)(2,1)S(1)}, bf16[592,128]{1,0:T(8,128)(2,1)S(1)}, u32[]{:S(2)}, u32[]{:S(2)}) collective-permute-start(bf16[592,128]{1,0:T(8,128)(2,1)S(1)} %get-tuple-element.111), channel_id=1, source_target_pairs={{0,2},{2,4},{4,6},{6,7},{7,5},{5,3},{3,1},{1,0},{8,10},{10,12},{12... | collective-permute-start | bytes 454664 | tf_op jit(solution)/shard_map/ppermute | solution.py:275
  141.5 9.3 %collective-permute-start.30 = (bf16[4704,128]{1,0:T(8,128)(2,1)S(1)}, bf16[4704,128]{1,0:T(8,128)(2,1)S(1)}, u32[]{:S(2)}, u32[]{:S(2)}) collective-permute-start(bf16[4704,128]{1,0:T(8,128)(2,1)S(1)} %copy-done.31), channel_id=1, source_target_pairs={{0,8},{8,0},{16,24},{24,16},{1,9},{9,1},{17,25},{25,17},{2,10},{10... | collective-permute-start | bytes 3612680 | tf_op jit(solution)/shard_map/ppermute | solution.py:255
  145.1 5.7 %collective-permute-start.32 = (bf16[768,128]{1,0:T(8,128)(2,1)S(1)}, bf16[768,128]{1,0:T(8,128)(2,1)S(1)}, u32[]{:S(2)}, u32[]{:S(2)}) collective-permute-start(bf16[768,128]{1,0:T(8,128)(2,1)S(1)} %pad_maximum_fusion.5), channel_id=1, source_target_pairs={{0,16},{8,24},{16,0},{24,8},{1,17},{9,25},{17,1},{25,9},{2,18},{10... | collective-permute-start | bytes 589832 | tf_op jit(solution)/shard_map/ppermute | solution.py:249
  146.5 7.1 %collective-permute-start.37 = (bf16[1184,128]{1,0:T(8,128)(2,1)S(1)}, bf16[1184,128]{1,0:T(8,128)(2,1)S(1)}, u32[]{:S(2)}, u32[]{:S(2)}) collective-permute-start(bf16[1184,128]{1,0:T(8,128)(2,1)S(1)} %get-tuple-element.105), channel_id=1, source_target_pairs={{0,2},{2,4},{4,6},{6,7},{7,5},{5,3},{3,1},{1,0},{8,10},{10,12},{12... | collective-permute-start | bytes 909320 | tf_op jit(solution)/shard_map/ppermute | solution.py:282
  148.1 6.8 %collective-permute-start.41 = (bf16[1184,128]{1,0:T(8,128)(2,1)S(1)}, bf16[1184,128]{1,0:T(8,128)(2,1)S(1)}, u32[]{:S(2)}, u32[]{:S(2)}) collective-permute-start(bf16[1184,128]{1,0:T(8,128)(2,1)S(1)} %get-tuple-element.106), channel_id=1, source_target_pairs={{0,1},{2,0},{4,2},{6,4},{7,6},{5,7},{3,5},{1,3},{8,9},{10,8},{12,1... | collective-permute-start | bytes 909320 | tf_op jit(solution)/shard_map/ppermute | solution.py:283
  150.9 6.8 %collective-permute-start.31 = (bf16[1152,128]{1,0:T(8,128)(2,1)S(1)}, bf16[1152,128]{1,0:T(8,128)(2,1)S(1)}, u32[]{:S(2)}, u32[]{:S(2)}) collective-permute-start(bf16[1152,128]{1,0:T(8,128)(2,1)S(1)} %pad_maximum_fusion.1), channel_id=1, source_target_pairs={{0,16},{8,24},{16,0},{24,8},{1,17},{9,25},{17,1},{25,9},{2,18},{10... | collective-permute-start | bytes 884744 | tf_op jit(solution)/shard_map/ppermute | solution.py:249
  155.1 6.9 %collective-permute-start.38 = (bf16[1184,128]{1,0:T(8,128)(2,1)S(1)}, bf16[1184,128]{1,0:T(8,128)(2,1)S(1)}, u32[]{:S(2)}, u32[]{:S(2)}) collective-permute-start(bf16[1184,128]{1,0:T(8,128)(2,1)S(1)} %get-tuple-element.103), channel_id=1, source_target_pairs={{0,2},{2,4},{4,6},{6,7},{7,5},{5,3},{3,1},{1,0},{8,10},{10,12},{12... | collective-permute-start | bytes 909320 | tf_op jit(solution)/shard_map/ppermute | solution.py:282
  156.7 7.1 %collective-permute-start.42 = (bf16[1184,128]{1,0:T(8,128)(2,1)S(1)}, bf16[1184,128]{1,0:T(8,128)(2,1)S(1)}, u32[]{:S(2)}, u32[]{:S(2)}) collective-permute-start(bf16[1184,128]{1,0:T(8,128)(2,1)S(1)} %get-tuple-element.104), channel_id=1, source_target_pairs={{0,1},{2,0},{4,2},{6,4},{7,6},{5,7},{3,5},{1,3},{8,9},{10,8},{12,1... | collective-permute-start | bytes 909320 | tf_op jit(solution)/shard_map/ppermute | solution.py:283
  164.1 6.9 %collective-permute-start.39 = (bf16[1184,128]{1,0:T(8,128)(2,1)S(1)}, bf16[1184,128]{1,0:T(8,128)(2,1)S(1)}, u32[]{:S(2)}, u32[]{:S(2)}) collective-permute-start(bf16[1184,128]{1,0:T(8,128)(2,1)S(1)} %get-tuple-element.98), channel_id=1, source_target_pairs={{0,2},{2,4},{4,6},{6,7},{7,5},{5,3},{3,1},{1,0},{8,10},{10,12},{12... | collective-permute-start | bytes 909320 | tf_op jit(solution)/shard_map/ppermute | solution.py:282
  166.0 6.8 %collective-permute-start.43 = (bf16[1184,128]{1,0:T(8,128)(2,1)S(1)}, bf16[1184,128]{1,0:T(8,128)(2,1)S(1)}, u32[]{:S(2)}, u32[]{:S(2)}) collective-permute-start(bf16[1184,128]{1,0:T(8,128)(2,1)S(1)} %get-tuple-element.99), channel_id=1, source_target_pairs={{0,1},{2,0},{4,2},{6,4},{7,6},{5,7},{3,5},{1,3},{8,9},{10,8},{12,1... | collective-permute-start | bytes 909320 | tf_op jit(solution)/shard_map/ppermute | solution.py:283
  (45 other events, 489.0 us)

commit v7 on v5

--- a/solution.py
+++ b/solution.py
@@ -111,7 +111,7 @@
 
 
 class Plan:
-    def __init__(self, n_dp, n_fsdp, own, entries):
+    def __init__(self, n_dp, n_fsdp, own, entries, far_slots):
         self.n_dp, self.n_fsdp, self.own, self.entries = n_dp, n_fsdp, own, entries
         self.x_len, self.ring = n_dp // 2, n_fsdp
         self.y_len = n_fsdp // Z_LEN
@@ -128,7 +128,7 @@
         self.forward = [(order[i], order[(i + 1) % n]) for i in range(n)]
         self.backward = [(order[i], order[i - 1]) for i in range(n)]
         self.flip = [(i, i ^ 1) for i in range(n_dp)]
-        self.far_slots = own // 2 if self.x_len == 2 else 0
+        self.far_slots = far_slots if self.x_len == 2 else 0
         self.near = (own - self.far_slots) * SIDE + TAIL
         self.far = self.far_slots * SIDE
         self.piece = self.x_len * self.near + self.far
@@ -215,35 +215,27 @@
         return (x * 2 + core) * self.n_fsdp + z * self.y_len + y
 
     def gather(self, mine):
-        cross = lambda a: lax.ppermute(a, "dp", self.shift(1))
-        near, far = mine[: self.near], mine[self.near :]
         stack = [mine]
         for by in range(1, self.x_len):
-            stack.append(lax.ppermute(near, "dp", self.shift(-by)))
-        first = jnp.concatenate(stack, axis=0)
-        pieces = [first]
-        if self.far:
-            pieces.append(cross(far))
-        middle = slice(self.near, self.near + self.far)
-        ahead = behind = first
+            stack.append(lax.ppermute(mine, "dp", self.shift(-by)))
+        ahead = behind = jnp.concatenate(stack, axis=0)
+        pieces = [ahead]
         for _ in range(1, self.half):
             ahead = lax.ppermute(ahead, "fsdp", self.forward)
             behind = lax.ppermute(behind, "fsdp", self.backward)
             pieces += [ahead, behind]
-            if self.far:
-                pieces.append(cross(jnp.concatenate([ahead[middle], behind[middle]], axis=0)))
-        low = lax.ppermute(ahead[: self.cut], "fsdp", self.forward)
-        high = lax.ppermute(behind[self.cut :], "fsdp", self.backward)
-        pieces += [low, high]
-        if self.far:
-            ends = [low[self.near :], high[: self.near + self.far - self.cut]]
-            pieces.append(cross(jnp.concatenate(ends, axis=0)))
+        pieces.append(lax.ppermute(ahead[: self.cut], "fsdp", self.forward))
+        pieces.append(lax.ppermute(behind[self.cut :], "fsdp", self.backward))
         return pieces + [lax.ppermute(piece, "dp", self.flip) for piece in pieces]
 
     def scatter(self, sends):
         cross = lambda a: lax.ppermute(a, "dp", self.shift(1))
         n = len(self.spots)
-        mixed = [lax.ppermute(send, "dp", self.flip) for send in sends[n:]]
+        mixed = []
+        for i, send in enumerate(sends[n:]):
+            if i >= 2:
+                send, mixed[i - 1] = lax.optimization_barrier((send, mixed[i - 1]))
+            mixed.append(lax.ppermute(send, "dp", self.flip))
         long = self.piece + self.far
         parts = {}
         for spot, kept, came in zip(self.spots, sends[:n], mixed):
@@ -291,7 +283,7 @@
 
 
 def layer_kernel(
-    plan,
+    plans,
     block_row,
     block_col,
     small_row,
@@ -302,13 +294,13 @@
     cot_patches,
     *rest,
 ):
-    n_in, n_out = len(plan.gathered), len(plan.scattered)
+    n_in, n_out = len(plans[0].gathered), len(plans[1].scattered)
     pieces = rest[:n_in]
     outs = rest[n_in : n_in + 4]
     sends = rest[n_in + 4 : n_in + 4 + n_out]
     tables = (block_row, block_col, small_row, shape)
     layer_body(
-        plan,
+        plans,
         tables,
         (regions, cot_regions, patches, cot_patches),
         pieces,
@@ -319,7 +311,7 @@
 
 
 def layer_body(
-    plan,
+    plans,
     tables,
     inputs,
     pieces,
@@ -358,6 +350,7 @@
     acc_mix,
     sem,
 ):
+    plan_in, plan = plans
     block_row, block_col, small_row, shape = tables
     regions, cot_regions, patches, cot_patches = inputs
     out_regions, out_patches, grad_regions, grad_patches = outs
@@ -378,12 +371,12 @@
     ]
     for copy in bring:
         copy.start()
-    for piece, (found, _) in zip(pieces, plan.gathered):
+    for piece, (found, _) in zip(pieces, plan_in.gathered):
         for at, count, home, slot, inner in found:
             if slot is None:
                 target = small_in.at[home, pl.ds(inner, count), :]
                 move(piece.at[pl.ds(at, count), :], target, 3).start()
-    for piece, (found, _) in zip(pieces, plan.gathered):
+    for piece, (found, _) in zip(pieces, plan_in.gathered):
         for at, count, home, slot, inner in found:
             if slot is None:
                 continue
@@ -720,10 +713,11 @@
     )
 
 
-def layer(plan, block_row, block_col, small_row, shape, regions, cot_regions, patches, cot_patches, pieces):
+def layer(plans, block_row, block_col, small_row, shape, regions, cot_regions, patches, cot_patches, pieces):
     n_reg = regions.shape[0]
     rows = patches.shape[0] + n_reg
     part = rows // CHUNKS
+    plan = plans[1]
     vec = lambda r, c, dtype=F32: pltpu.VMEM((r, c), dtype)
     cube = lambda n, r, c, dtype=F32: pltpu.VMEM((n, r, c), dtype)
     in_smem = pl.BlockSpec(memory_space=pltpu.SMEM)
@@ -731,7 +725,7 @@
     in_place = pl.BlockSpec(memory_space=pl.ANY)
     like = lambda a: jax.ShapeDtypeStruct(a.shape, BF16)
     return pl.pallas_call(
-        functools.partial(layer_kernel, plan),
+        functools.partial(layer_kernel, plans),
         in_specs=[in_smem] * 4 + [in_vmem, in_vmem, in_place, in_place] + [in_place] * len(pieces),
         out_specs=[in_vmem, in_place, in_vmem, in_place] + [in_place] * len(plan.scattered),
         out_shape=[like(regions), like(patches), like(regions), like(patches)]
@@ -831,19 +825,14 @@
     devices = lax.axis_size(axes)
     entries = small.shape[0]
     own = slot_weights.shape[0]
-    plan = Plan(lax.axis_size("dp"), lax.axis_size("fsdp"), own, entries)
+    sizes = (lax.axis_size("dp"), lax.axis_size("fsdp"), own, entries)
+    plan_in, plan = Plan(*sizes, 0), Plan(*sizes, own // 2)
     offset = lax.rem(lax.axis_index(axes) * entries, LANES)
     tail = lax.dynamic_update_slice(jnp.zeros(TAIL * LANES, BF16), small.astype(BF16), (offset,))
-    held = slot_weights.astype(BF16).reshape(own * SIDE, LANES)
     mine = jnp.concatenate(
-        [
-            held[: plan.near - TAIL],
-            tail.reshape(TAIL, LANES),
-            held[plan.near - TAIL :],
-        ],
-        axis=0,
+        [slot_weights.astype(BF16).reshape(own * SIDE, LANES), tail.reshape(TAIL, LANES)], axis=0
     )
-    pieces = plan.gather(mine)
+    pieces = plan_in.gather(mine)
     by_token = lambda a: jnp.swapaxes(a, 0, 1).reshape(-1, D)
     homes = plan.device_of_homes(lax.axis_index("dp"), lax.axis_index("fsdp"))
     spots = (homes[:, None] * own + jnp.arange(own, dtype=jnp.int32)[None, :]).reshape(-1)
@@ -852,7 +841,7 @@
     block_row, block_col = block_places(block)
     small_row = homes * entries // LANES
     out_regions, out_patches, grad_regions, grad_patches, *sends = layer(
-        plan,
+        (plan_in, plan),
         block_row,
         block_col,
         small_row,

time: 185 us -> 173 us (0.935)
  waiting for transfers between devices: 65.7 us -> 61.4 us
  starting transfers between devices: 32.8 us -> 28.6 us
  local copies, waits for them, and re-layouts: 4.94 us -> 2.86 us
    ppermute x3, waiting for transfers between devices: 13 us -> 22.1 us  [gather(): behind = lax.ppermute(behind, 'fsdp', self.backward)]
    ppermute x3, waiting for transfers between devices: 17.9 us -> 10.6 us  [scatter(): ahead = lax.ppermute(ahead, 'fsdp', self.forward)]
    ppermute x12 -> x7, starting transfers between devices: 11.3 us -> 5.74 us  [the longest x1 3 us: gather(): stack.append(lax.ppermute(mine, 'dp', self.shift(-by)))]
    ppermute x12 -> x7, waiting for transfers between devices: 17.1 us -> 12.3 us  [the longest x1 4.99 us: gather(): stack.append(lax.ppermute(mine, 'dp', self.shift(-by)))]
    ppermute x3, waiting for transfers between devices: 4.35 us -> 0.01 us  [gather(): ahead = lax.ppermute(ahead, 'fsdp', self.forward)]
    ppermute x3, starting transfers between devices: 0.86 us -> 3.96 us  [scatter(): ahead = lax.ppermute(ahead, 'fsdp', self.forward)]
    ppermute x3, starting transfers between devices: 5.37 us -> 2.27 us  [scatter(): behind = lax.ppermute(behind, 'fsdp', self.backward)]
    ppermute x3, waiting for transfers between devices: 1.24 us -> 3.31 us  [scatter(): behind = lax.ppermute(behind, 'fsdp', self.backward)]
  transfers between devices with their start and end apart: 45 -> 35, of which waited for: 21 -> 19; matrix products, arithmetic and copies ran while one was open for 4% -> 3% of each run, Pallas kernels for 0% -> 0%
where the time goes in v7:
time: 173 us
  Pallas kernels  72 us (42%)
  waiting for transfers between devices  61.4 us (35%)
  starting transfers between devices  28.6 us (17%)
  other arithmetic  7.05 us (4%)
  local copies, waits for them, and re-layouts  2.86 us (2%)
    pallas_call x1, Pallas kernels, layer(): pl.pallas_call(functools.partial(layer_kernel, plans), in_specs=[in_smem]...  68.1 us
    ppermute x3, waiting for transfers between devices, gather(): behind = lax.ppermute(behind, 'fsdp', self.backward)  22.1 us
    ppermute x3, waiting for transfers between devices, scatter(): ahead = lax.ppermute(ahead, 'fsdp', self.forward)  10.6 us
    ppermute x4, waiting for transfers between devices, scatter(): cross = lambda a: lax.ppermute(a, 'dp', self.shift(1))  8.9 us
    ppermute x4, starting transfers between devices, scatter(): cross = lambda a: lax.ppermute(a, 'dp', self.shift(1))  6.24 us
    ppermute x1, waiting for transfers between devices, gather(): stack.append(lax.ppermute(mine, 'dp', self.shift(-by)))  4.99 us
    ppermute x3, starting transfers between devices, gather(): behind = lax.ppermute(behind, 'fsdp', self.backward)  4.62 us
    ppermute x3, starting transfers between devices, scatter(): ahead = lax.ppermute(ahead, 'fsdp', self.forward)  3.96 us
  transfers between devices with their start and end apart: 35, of which 19 were waited for; matrix products, arithmetic and copies ran while one was open for 3% of the time, Pallas kernels for 0%

profile of v7, /device:TPU:0, one launch (start us, length us, event | category | flops | bytes accessed | tf_op | source)
XLA Modules:
  0.0 172.9 jit_solution(8804702621380285438)
XLA Ops:
  2.7 3.0 %collective-permute-start = (bf16[784,128]{1,0:T(8,128)(2,1)S(1)}, bf16[784,128]{1,0:T(8,128)(2,1)S(1)}, u32[]{:S(2)}, u32[]{:S(2)}) collective-permute-start(bf16[784,128]{1,0:T(8,128)(2,1)S(1)} %pad_maximum_fusion.2), channel_id=1, source_target_pairs={{0,16},{8,24},{16,0},{24,8},{1,17},{9,25},{17,1},{25,9},{2,18},{10... | collective-permute-start | bytes 602120 | tf_op jit(solution)/shard_map/ppermute | solution.py:220
  5.7 5.0 %collective-permute-done = bf16[784,128]{1,0:T(8,128)(2,1)S(1)} collective-permute-done((bf16[784,128]{1,0:T(8,128)(2,1)S(1)}, bf16[784,128]{1,0:T(8,128)(2,1)S(1)}, u32[]{:S(2)}, u32[]{:S(2)}) %collective-permute-start) | collective-permute-done | bytes 200736 | tf_op jit(solution)/shard_map/ppermute | solution.py:220
  10.7 1.8 %collective-permute-start.2 = (bf16[1568,128]{1,0:T(8,128)(2,1)S(1)}, bf16[1568,128]{1,0:T(8,128)(2,1)S(1)}, u32[]{:S(2)}, u32[]{:S(2)}) collective-permute-start(bf16[1568,128]{1,0:T(8,128)(2,1)S(1)} %pad_maximum_fusion.rest_0_), channel_id=1, source_target_pairs={{0,1},{2,0},{4,2},{6,4},{7,6},{5,7},{3,5},{1,3},{8,9},{10,8},{12,1... | collective-permute-start | bytes 1204232 | tf_op jit(solution)/shard_map/ppermute | solution.py:225
  12.8 8.4 %collective-permute-done.2.rest_2_ = bf16[1568,128]{1,0:T(8,128)(2,1)S(1)} collective-permute-done((bf16[1568,128]{1,0:T(8,128)(2,1)S(1)}, bf16[1568,128]{1,0:T(8,128)(2,1)S(1)}, u32[]{:S(2)}, u32[]{:S(2)}) %collective-permute-start.2) | collective-permute-done | bytes 401440 | tf_op jit(solution)/shard_map/ppermute | solution.py:225
  21.2 1.5 collective-permute-start.4
  23.3 7.5 %collective-permute-done.4.rest_4_ = bf16[1568,128]{1,0:T(8,128)(2,1)S(1)} collective-permute-done((bf16[1568,128]{1,0:T(8,128)(2,1)S(1)}, bf16[1568,128]{1,0:T(8,128)(2,1)S(1)}, u32[]{:S(2)}, u32[]{:S(2)}) %collective-permute-start.4) | collective-permute-done | bytes 401440 | tf_op jit(solution)/shard_map/ppermute | solution.py:225
  30.8 1.3 collective-permute-start.6
  33.3 6.1 %collective-permute-done.6.rest_6_ = bf16[1568,128]{1,0:T(8,128)(2,1)S(1)} collective-permute-done((bf16[1568,128]{1,0:T(8,128)(2,1)S(1)}, bf16[1568,128]{1,0:T(8,128)(2,1)S(1)}, u32[]{:S(2)}, u32[]{:S(2)}) %collective-permute-start.6) | collective-permute-done | bytes 401440 | tf_op jit(solution)/shard_map/ppermute | solution.py:225
  41.0 1.1 collective-permute-start.8
  44.3 3.7 %collective-permute-done.8.rest_8_ = bf16[784,128]{1,0:T(8,128)(2,1)S(1)} collective-permute-done((bf16[784,128]{1,0:T(8,128)(2,1)S(1)}, bf16[784,128]{1,0:T(8,128)(2,1)S(1)}, u32[]{:S(2)}, u32[]{:S(2)}) %collective-permute-start.8) | collective-permute-done | bytes 200736 | tf_op jit(solution)/shard_map/ppermute | solution.py:228
  48.0 1.1 collective-permute-done.7.rest_7_
  51.4 68.1 %layer.1 = (bf16[24,512]{1,0:T(8,128)(2,1)}, bf16[1176,512]{1,0:T(8,128)(2,1)}, bf16[24,512]{1,0:T(8,128)(2,1)}, bf16[1176,512]{1,0:T(8,128)(2,1)}, bf16[1568,12...) custom-call(s32[192]{0:T(256)} %get-tuple-element.77.block_row, ...), custom_call_target="tpu_custom_call" | custom-call | tf_op jit(solution)/shard_map/layer/pallas_call | solution.py:727
  120.1 2.6 %collective-permute-done.24 = bf16[1568,128]{1,0:T(8,128)(2,1)S(1)} collective-permute-done((bf16[1568,128]{1,0:T(8,128)(2,1)}, bf16[1568,128]{1,0:T(8,128)(2,1)S(1)}, u32[]{:S(2)}, u32[]{:S(2)}) %collective-permute-start.24) | collective-permute-done | bytes 401440 | tf_op jit(solution)/shard_map/ppermute | solution.py:238
  123.7 1.6 collective-permute-start.25
  125.3 3.5 %collective-permute-done.25 = bf16[384,128]{1,0:T(8,128)(2,1)S(1)} collective-permute-done((bf16[384,128]{1,0:T(8,128)(2,1)S(1)}, bf16[384,128]{1,0:T(8,128)(2,1)S(1)}, u32[]{:S(2)}, u32[]{:S(2)}) %collective-permute-start.25) | collective-permute-done | bytes 98336 | tf_op jit(solution)/shard_map/ppermute | solution.py:232
  128.8 1.1 add_convert_fusion.6
  130.0 1.6 collective-permute-start.23
  132.1 1.5 collective-permute-start.30
  133.6 2.8 %collective-permute-done.23 = bf16[768,128]{1,0:T(8,128)(2,1)S(1)} collective-permute-done((bf16[768,128]{1,0:T(8,128)(2,1)S(1)}, bf16[768,128]{1,0:T(8,128)(2,1)S(1)}, u32[]{:S(2)}, u32[]{:S(2)}) %collective-permute-start.23) | collective-permute-done | bytes 196640 | tf_op jit(solution)/shard_map/ppermute | solution.py:232
  136.5 1.6 collective-permute-start.22
  139.2 1.2 collective-permute-start.31
  140.4 1.8 %collective-permute-done.22 = bf16[768,128]{1,0:T(8,128)(2,1)S(1)} collective-permute-done((bf16[768,128]{1,0:T(8,128)(2,1)S(1)}, bf16[768,128]{1,0:T(8,128)(2,1)S(1)}, u32[]{:S(2)}, u32[]{:S(2)}) %collective-permute-start.22) | collective-permute-done | bytes 196640 | tf_op jit(solution)/shard_map/ppermute | solution.py:232
  142.4 1.6 collective-permute-start.21
  144.0 1.9 %collective-permute-done.27 = bf16[1184,128]{1,0:T(8,128)(2,1)S(1)} collective-permute-done((bf16[1184,128]{1,0:T(8,128)(2,1)S(1)}, bf16[1184,128]{1,0:T(8,128)(2,1)S(1)}, u32[]{:S(2)}, u32[]{:S(2)}) %collective-permute-start.27) | collective-permute-done | bytes 303136 | tf_op jit(solution)/shard_map/ppermute | solution.py:265
  146.3 1.6 collective-permute-start.28
  149.2 3.9 %collective-permute-done.28 = bf16[1184,128]{1,0:T(8,128)(2,1)S(1)} collective-permute-done((bf16[1184,128]{1,0:T(8,128)(2,1)S(1)}, bf16[1184,128]{1,0:T(8,128)(2,1)S(1)}, u32[]{:S(2)}, u32[]{:S(2)}) %collective-permute-start.28) | collective-permute-done | bytes 303136 | tf_op jit(solution)/shard_map/ppermute | solution.py:265
  153.1 1.7 collective-permute-done.32
  155.1 1.5 collective-permute-start.29
  157.2 4.8 %collective-permute-done.29 = bf16[1184,128]{1,0:T(8,128)(2,1)S(1)} collective-permute-done((bf16[1184,128]{1,0:T(8,128)(2,1)S(1)}, bf16[1184,128]{1,0:T(8,128)(2,1)S(1)}, u32[]{:S(2)}, u32[]{:S(2)}) %collective-permute-start.29) | collective-permute-done | bytes 303136 | tf_op jit(solution)/shard_map/ppermute | solution.py:265
  162.0 1.4 collective-permute-done.33
  165.0 3.3 %collective-permute-done.34.rest_0_ = bf16[400,128]{1,0:T(8,128)(2,1)S(1)} collective-permute-done((bf16[400,128]{1,0:T(8,128)(2,1)S(1)}, bf16[400,128]{1,0:T(8,128)(2,1)S(1)}, u32[]{:S(2)}, u32[]{:S(2)}) %collective-permute-start.34) | collective-permute-done | bytes 102432 | tf_op jit(solution)/shard_map/ppermute | solution.py:272
  169.0 3.9 %update.1 = (f32[6,128,128]{2,1,0:T(8,128)}, f32[6,2,128,128]{3,2,1,0:T(8,128)}, f32[6,128,128]{2,1,0:T(8,128)}, f32[6,128,128]{2,1,0:T(8,128)}) custom-call(f32[784,128]{1,0:T(8,128)} %slice.209.summed, bf16[400,128]{1,0:T(8,128)(2,1)} %copy-done.18, f32[6,128,128]{2,1,0:T(8,128)} %rest_1_.1, f32[6,2,128,128]{3,2,1,0:T(8,128)} %rest_2_.1, ...), custom_call_target="tpu_custom_call" | custom-call | tf_op jit(solution)/shard_map/update/pallas_call | solution.py:803
  (123 shorter events, 18.4 us)
Async XLA Ops:
  2.7 8.0 %collective-permute-start = (bf16[784,128]{1,0:T(8,128)(2,1)S(1)}, bf16[784,128]{1,0:T(8,128)(2,1)S(1)}, u32[]{:S(2)}, u32[]{:S(2)}) collective-permute-start(bf16[784,128]{1,0:T(8,128)(2,1)S(1)} %pad_maximum_fusion.2), channel_id=1, source_target_pairs={{0,16},{8,24},{16,0},{24,8},{1,17},{9,25},{17,1},{25,9},{2,18},{10... | collective-permute-start | bytes 602120 | tf_op jit(solution)/shard_map/ppermute | solution.py:220
  10.7 10.5 %collective-permute-start.2 = (bf16[1568,128]{1,0:T(8,128)(2,1)S(1)}, bf16[1568,128]{1,0:T(8,128)(2,1)S(1)}, u32[]{:S(2)}, u32[]{:S(2)}) collective-permute-start(bf16[1568,128]{1,0:T(8,128)(2,1)S(1)} %pad_maximum_fusion.rest_0_), channel_id=1, source_target_pairs={{0,1},{2,0},{4,2},{6,4},{7,6},{5,7},{3,5},{1,3},{8,9},{10,8},{12,1... | collective-permute-start | bytes 1204232 | tf_op jit(solution)/shard_map/ppermute | solution.py:225
  12.5 10.2 %collective-permute-start.1 = (bf16[1568,128]{1,0:T(8,128)(2,1)S(1)}, bf16[1568,128]{1,0:T(8,128)(2,1)S(1)}, u32[]{:S(2)}, u32[]{:S(2)}) collective-permute-start(bf16[1568,128]{1,0:T(8,128)(2,1)S(1)} %pad_maximum_fusion.rest_0_), channel_id=1, source_target_pairs={{0,2},{2,4},{4,6},{6,7},{7,5},{5,3},{3,1},{1,0},{8,10},{10,12},{12... | collective-permute-start | bytes 1204232 | tf_op jit(solution)/shard_map/ppermute | solution.py:224
  21.2 9.6 %collective-permute-start.4 = (bf16[1568,128]{1,0:T(8,128)(2,1)S(1)}, bf16[1568,128]{1,0:T(8,128)(2,1)S(1)}, u32[]{:S(2)}, u32[]{:S(2)}) collective-permute-start(bf16[1568,128]{1,0:T(8,128)(2,1)S(1)} %collective-permute-done.2.rest_2_), channel_id=1, source_target_pairs={{0,1},{2,0},{4,2},{6,4},{7,6},{5,7},{3,5},{1,3},{8,9},{10,8},{12,1... | collective-permute-start | bytes 1204232 | tf_op jit(solution)/shard_map/ppermute | solution.py:225
  22.7 9.5 %collective-permute-start.3 = (bf16[1568,128]{1,0:T(8,128)(2,1)S(1)}, bf16[1568,128]{1,0:T(8,128)(2,1)S(1)}, u32[]{:S(2)}, u32[]{:S(2)}) collective-permute-start(bf16[1568,128]{1,0:T(8,128)(2,1)S(1)} %collective-permute-done.1.rest_1_), channel_id=1, source_target_pairs={{0,2},{2,4},{4,6},{6,7},{7,5},{5,3},{3,1},{1,0},{8,10},{10,12},{12... | collective-permute-start | bytes 1204232 | tf_op jit(solution)/shard_map/ppermute | solution.py:224
  30.8 8.6 %collective-permute-start.6 = (bf16[1568,128]{1,0:T(8,128)(2,1)S(1)}, bf16[1568,128]{1,0:T(8,128)(2,1)S(1)}, u32[]{:S(2)}, u32[]{:S(2)}) collective-permute-start(bf16[1568,128]{1,0:T(8,128)(2,1)S(1)} %collective-permute-done.4.rest_4_), channel_id=1, source_target_pairs={{0,1},{2,0},{4,2},{6,4},{7,6},{5,7},{3,5},{1,3},{8,9},{10,8},{12,1... | collective-permute-start | bytes 1204232 | tf_op jit(solution)/shard_map/ppermute | solution.py:225
  32.2 8.3 %collective-permute-start.5 = (bf16[1568,128]{1,0:T(8,128)(2,1)S(1)}, bf16[1568,128]{1,0:T(8,128)(2,1)S(1)}, u32[]{:S(2)}, u32[]{:S(2)}) collective-permute-start(bf16[1568,128]{1,0:T(8,128)(2,1)S(1)} %collective-permute-done.3.rest_3_), channel_id=1, source_target_pairs={{0,2},{2,4},{4,6},{6,7},{7,5},{5,3},{3,1},{1,0},{8,10},{10,12},{12... | collective-permute-start | bytes 1204232 | tf_op jit(solution)/shard_map/ppermute | solution.py:224
  32.8 8.1 %collective-permute-start.9 = (bf16[1568,128]{1,0:T(8,128)(2,1)S(1)}, bf16[1568,128]{1,0:T(8,128)(2,1)S(1)}, u32[]{:S(2)}, u32[]{:S(2)}) collective-permute-start(bf16[1568,128]{1,0:T(8,128)(2,1)S(1)} %pad_maximum_fusion.rest_0_), channel_id=1, source_target_pairs={{0,8},{8,0},{16,24},{24,16},{1,9},{9,1},{17,25},{25,17},{2,10},{10... | collective-permute-start | bytes 1204232 | tf_op jit(solution)/shard_map/ppermute | solution.py:229
  32.8 9.3 %collective-permute-start.11 = (bf16[1568,128]{1,0:T(8,128)(2,1)S(1)}, bf16[1568,128]{1,0:T(8,128)(2,1)}, u32[]{:S(2)}, u32[]{:S(2)}) collective-permute-start(bf16[1568,128]{1,0:T(8,128)(2,1)S(1)} %collective-permute-done.2.rest_2_), channel_id=1, source_target_pairs={{0,8},{8,0},{16,24},{24,16},{1,9},{9,1},{17,25},{25,17},{2,10},{10... | collective-permute-start | bytes 1204232 | tf_op jit(solution)/shard_map/ppermute | solution.py:229
  33.3 9.7 %collective-permute-start.10 = (bf16[1568,128]{1,0:T(8,128)(2,1)S(1)}, bf16[1568,128]{1,0:T(8,128)(2,1)}, u32[]{:S(2)}, u32[]{:S(2)}) collective-permute-start(bf16[1568,128]{1,0:T(8,128)(2,1)S(1)} %collective-permute-done.1.rest_1_), channel_id=1, source_target_pairs={{0,8},{8,0},{16,24},{24,16},{1,9},{9,1},{17,25},{25,17},{2,10},{10... | collective-permute-start | bytes 1204232 | tf_op jit(solution)/shard_map/ppermute | solution.py:229
  39.4 3.6 %collective-permute-start.13 = (bf16[1568,128]{1,0:T(8,128)(2,1)S(1)}, bf16[1568,128]{1,0:T(8,128)(2,1)}, u32[]{:S(2)}, u32[]{:S(2)}) collective-permute-start(bf16[1568,128]{1,0:T(8,128)(2,1)S(1)} %collective-permute-done.4.rest_4_), channel_id=1, source_target_pairs={{0,8},{8,0},{16,24},{24,16},{1,9},{9,1},{17,25},{25,17},{2,10},{10... | collective-permute-start | bytes 1204232 | tf_op jit(solution)/shard_map/ppermute | solution.py:229
  40.4 9.3 %collective-permute-start.12 = (bf16[1568,128]{1,0:T(8,128)(2,1)S(1)}, bf16[1568,128]{1,0:T(8,128)(2,1)S(1)}, u32[]{:S(2)}, u32[]{:S(2)}) collective-permute-start(bf16[1568,128]{1,0:T(8,128)(2,1)S(1)} %collective-permute-done.3.rest_3_), channel_id=1, source_target_pairs={{0,8},{8,0},{16,24},{24,16},{1,9},{9,1},{17,25},{25,17},{2,10},{10... | collective-permute-start | bytes 1204232 | tf_op jit(solution)/shard_map/ppermute | solution.py:229
  41.0 7.0 %collective-permute-start.8 = (bf16[784,128]{1,0:T(8,128)(2,1)S(1)}, bf16[784,128]{1,0:T(8,128)(2,1)S(1)}, u32[]{:S(2)}, u32[]{:S(2)}) collective-permute-start(bf16[784,128]{1,0:T(8,128)(2,1)S(1)} %slice.191), channel_id=1, source_target_pairs={{0,1},{2,0},{4,2},{6,4},{7,6},{5,7},{3,5},{1,3},{8,9},{10,8},{12,1... | collective-permute-start | bytes 602120 | tf_op jit(solution)/shard_map/ppermute | solution.py:228
  42.1 6.9 %collective-permute-start.7 = (bf16[784,128]{1,0:T(8,128)(2,1)S(1)}, bf16[784,128]{1,0:T(8,128)(2,1)S(1)}, u32[]{:S(2)}, u32[]{:S(2)}) collective-permute-start(bf16[784,128]{1,0:T(8,128)(2,1)S(1)} %slice.190), channel_id=1, source_target_pairs={{0,2},{2,4},{4,6},{6,7},{7,5},{5,3},{3,1},{1,0},{8,10},{10,12},{12... | collective-permute-start | bytes 602120 | tf_op jit(solution)/shard_map/ppermute | solution.py:227
  43.1 6.6 %collective-permute-start.15 = (bf16[1568,128]{1,0:T(8,128)(2,1)S(1)}, bf16[1568,128]{1,0:T(8,128)(2,1)S(1)}, u32[]{:S(2)}, u32[]{:S(2)}) collective-permute-start(bf16[1568,128]{1,0:T(8,128)(2,1)S(1)} %collective-permute-done.6.rest_6_), channel_id=1, source_target_pairs={{0,8},{8,0},{16,24},{24,16},{1,9},{9,1},{17,25},{25,17},{2,10},{10... | collective-permute-start | bytes 1204232 | tf_op jit(solution)/shard_map/ppermute | solution.py:229
  43.1 7.4 %collective-permute-start.14 = (bf16[1568,128]{1,0:T(8,128)(2,1)S(1)}, bf16[1568,128]{1,0:T(8,128)(2,1)S(1)}, u32[]{:S(2)}, u32[]{:S(2)}) collective-permute-start(bf16[1568,128]{1,0:T(8,128)(2,1)S(1)} %collective-permute-done.5.rest_5_), channel_id=1, source_target_pairs={{0,8},{8,0},{16,24},{24,16},{1,9},{9,1},{17,25},{25,17},{2,10},{10... | collective-permute-start | bytes 1204232 | tf_op jit(solution)/shard_map/ppermute | solution.py:229
  119.5 5.7 %collective-permute-start.18 = (bf16[3136,128]{1,0:T(8,128)(2,1)}, bf16[3136,128]{1,0:T(8,128)(2,1)S(1)}, u32[]{:S(2)}, u32[]{:S(2)}) collective-permute-start(bf16[3136,128]{1,0:T(8,128)(2,1)} %get-tuple-element.38), channel_id=1, source_target_pairs={{0,8},{8,0},{16,24},{24,16},{1,9},{9,1},{17,25},{25,17},{2,10},{10... | collective-permute-start | bytes 2408456 | tf_op jit(solution)/shard_map/ppermute | solution.py:238
  123.7 5.1 %collective-permute-start.25 = (bf16[384,128]{1,0:T(8,128)(2,1)S(1)}, bf16[384,128]{1,0:T(8,128)(2,1)S(1)}, u32[]{:S(2)}, u32[]{:S(2)}) collective-permute-start(bf16[384,128]{1,0:T(8,128)(2,1)S(1)} %add_convert_fusion.7), channel_id=1, source_target_pairs={{0,16},{8,24},{16,0},{24,8},{1,17},{9,25},{17,1},{25,9},{2,18},{10... | collective-permute-start | bytes 294920 | tf_op jit(solution)/shard_map/ppermute | solution.py:232
  125.2 8.4 %collective-permute-start.19 = (bf16[3136,128]{1,0:T(8,128)(2,1)}, bf16[3136,128]{1,0:T(8,128)(2,1)S(1)}, u32[]{:S(2)}, u32[]{:S(2)}) collective-permute-start(bf16[3136,128]{1,0:T(8,128)(2,1)} %get-tuple-element.39), channel_id=1, source_target_pairs={{0,8},{8,0},{16,24},{24,16},{1,9},{9,1},{17,25},{25,17},{2,10},{10... | collective-permute-start | bytes 2408456 | tf_op jit(solution)/shard_map/ppermute | solution.py:238
  130.0 6.4 %collective-permute-start.23 = (bf16[768,128]{1,0:T(8,128)(2,1)S(1)}, bf16[768,128]{1,0:T(8,128)(2,1)S(1)}, u32[]{:S(2)}, u32[]{:S(2)}) collective-permute-start(bf16[768,128]{1,0:T(8,128)(2,1)S(1)} %pad_maximum_fusion.4), channel_id=1, source_target_pairs={{0,16},{8,24},{16,0},{24,8},{1,17},{9,25},{17,1},{25,9},{2,18},{10... | collective-permute-start | bytes 589832 | tf_op jit(solution)/shard_map/ppermute | solution.py:232
  131.5 6.5 %collective-permute-start.26 = (bf16[592,128]{1,0:T(8,128)(2,1)S(1)}, bf16[592,128]{1,0:T(8,128)(2,1)S(1)}, u32[]{:S(2)}, u32[]{:S(2)}) collective-permute-start(bf16[592,128]{1,0:T(8,128)(2,1)S(1)} %get-tuple-element.67), channel_id=1, source_target_pairs={{0,2},{2,4},{4,6},{6,7},{7,5},{5,3},{3,1},{1,0},{8,10},{10,12},{12... | collective-permute-start | bytes 454664 | tf_op jit(solution)/shard_map/ppermute | solution.py:258
  132.1 5.9 %collective-permute-start.30 = (bf16[592,128]{1,0:T(8,128)(2,1)S(1)}, bf16[592,128]{1,0:T(8,128)(2,1)S(1)}, u32[]{:S(2)}, u32[]{:S(2)}) collective-permute-start(bf16[592,128]{1,0:T(8,128)(2,1)S(1)} %get-tuple-element.68), channel_id=1, source_target_pairs={{0,1},{2,0},{4,2},{6,4},{7,6},{5,7},{3,5},{1,3},{8,9},{10,8},{12,1... | collective-permute-start | bytes 454664 | tf_op jit(solution)/shard_map/ppermute | solution.py:259
  133.6 8.6 %collective-permute-start.20 = (bf16[4704,128]{1,0:T(8,128)(2,1)S(1)}, bf16[4704,128]{1,0:T(8,128)(2,1)S(1)}, u32[]{:S(2)}, u32[]{:S(2)}) collective-permute-start(bf16[4704,128]{1,0:T(8,128)(2,1)S(1)} %copy-done.23), channel_id=1, source_target_pairs={{0,8},{8,0},{16,24},{24,16},{1,9},{9,1},{17,25},{25,17},{2,10},{10... | collective-permute-start | bytes 3612680 | tf_op jit(solution)/shard_map/ppermute | solution.py:238
  136.5 5.7 %collective-permute-start.22 = (bf16[768,128]{1,0:T(8,128)(2,1)S(1)}, bf16[768,128]{1,0:T(8,128)(2,1)S(1)}, u32[]{:S(2)}, u32[]{:S(2)}) collective-permute-start(bf16[768,128]{1,0:T(8,128)(2,1)S(1)} %pad_maximum_fusion.3), channel_id=1, source_target_pairs={{0,16},{8,24},{16,0},{24,8},{1,17},{9,25},{17,1},{25,9},{2,18},{10... | collective-permute-start | bytes 589832 | tf_op jit(solution)/shard_map/ppermute | solution.py:232
  138.3 7.5 %collective-permute-start.27 = (bf16[1184,128]{1,0:T(8,128)(2,1)S(1)}, bf16[1184,128]{1,0:T(8,128)(2,1)S(1)}, u32[]{:S(2)}, u32[]{:S(2)}) collective-permute-start(bf16[1184,128]{1,0:T(8,128)(2,1)S(1)} %get-tuple-element.61), channel_id=1, source_target_pairs={{0,2},{2,4},{4,6},{6,7},{7,5},{5,3},{3,1},{1,0},{8,10},{10,12},{12... | collective-permute-start | bytes 909320 | tf_op jit(solution)/shard_map/ppermute | solution.py:265
  139.2 6.8 %collective-permute-start.31 = (bf16[1184,128]{1,0:T(8,128)(2,1)S(1)}, bf16[1184,128]{1,0:T(8,128)(2,1)S(1)}, u32[]{:S(2)}, u32[]{:S(2)}) collective-permute-start(bf16[1184,128]{1,0:T(8,128)(2,1)S(1)} %get-tuple-element.62), channel_id=1, source_target_pairs={{0,1},{2,0},{4,2},{6,4},{7,6},{5,7},{3,5},{1,3},{8,9},{10,8},{12,1... | collective-permute-start | bytes 909320 | tf_op jit(solution)/shard_map/ppermute | solution.py:266
  142.4 6.8 %collective-permute-start.21 = (bf16[1152,128]{1,0:T(8,128)(2,1)S(1)}, bf16[1152,128]{1,0:T(8,128)(2,1)S(1)}, u32[]{:S(2)}, u32[]{:S(2)}) collective-permute-start(bf16[1152,128]{1,0:T(8,128)(2,1)S(1)} %pad_maximum_fusion.1), channel_id=1, source_target_pairs={{0,16},{8,24},{16,0},{24,8},{1,17},{9,25},{17,1},{25,9},{2,18},{10... | collective-permute-start | bytes 884744 | tf_op jit(solution)/shard_map/ppermute | solution.py:232
  146.3 6.9 %collective-permute-start.28 = (bf16[1184,128]{1,0:T(8,128)(2,1)S(1)}, bf16[1184,128]{1,0:T(8,128)(2,1)S(1)}, u32[]{:S(2)}, u32[]{:S(2)}) collective-permute-start(bf16[1184,128]{1,0:T(8,128)(2,1)S(1)} %get-tuple-element.59), channel_id=1, source_target_pairs={{0,2},{2,4},{4,6},{6,7},{7,5},{5,3},{3,1},{1,0},{8,10},{10,12},{12... | collective-permute-start | bytes 909320 | tf_op jit(solution)/shard_map/ppermute | solution.py:265
  147.9 7.0 %collective-permute-start.32 = (bf16[1184,128]{1,0:T(8,128)(2,1)S(1)}, bf16[1184,128]{1,0:T(8,128)(2,1)S(1)}, u32[]{:S(2)}, u32[]{:S(2)}) collective-permute-start(bf16[1184,128]{1,0:T(8,128)(2,1)S(1)} %get-tuple-element.60), channel_id=1, source_target_pairs={{0,1},{2,0},{4,2},{6,4},{7,6},{5,7},{3,5},{1,3},{8,9},{10,8},{12,1... | collective-permute-start | bytes 909320 | tf_op jit(solution)/shard_map/ppermute | solution.py:266
  155.1 6.9 %collective-permute-start.29 = (bf16[1184,128]{1,0:T(8,128)(2,1)S(1)}, bf16[1184,128]{1,0:T(8,128)(2,1)S(1)}, u32[]{:S(2)}, u32[]{:S(2)}) collective-permute-start(bf16[1184,128]{1,0:T(8,128)(2,1)S(1)} %get-tuple-element.54), channel_id=1, source_target_pairs={{0,2},{2,4},{4,6},{6,7},{7,5},{5,3},{3,1},{1,0},{8,10},{10,12},{12... | collective-permute-start | bytes 909320 | tf_op jit(solution)/shard_map/ppermute | solution.py:265
  156.6 6.8 %collective-permute-start.33 = (bf16[1184,128]{1,0:T(8,128)(2,1)S(1)}, bf16[1184,128]{1,0:T(8,128)(2,1)S(1)}, u32[]{:S(2)}, u32[]{:S(2)}) collective-permute-start(bf16[1184,128]{1,0:T(8,128)(2,1)S(1)} %get-tuple-element.55), channel_id=1, source_target_pairs={{0,1},{2,0},{4,2},{6,4},{7,6},{5,7},{3,5},{1,3},{8,9},{10,8},{12,1... | collective-permute-start | bytes 909320 | tf_op jit(solution)/shard_map/ppermute | solution.py:266
  163.6 4.7 %collective-permute-start.34 = (bf16[400,128]{1,0:T(8,128)(2,1)S(1)}, bf16[400,128]{1,0:T(8,128)(2,1)S(1)}, u32[]{:S(2)}, u32[]{:S(2)}) collective-permute-start(bf16[400,128]{1,0:T(8,128)(2,1)S(1)} %slice.250), channel_id=1, source_target_pairs={{0,16},{8,24},{16,0},{24,8},{1,17},{9,25},{17,1},{25,9},{2,18},{10... | collective-permute-start | bytes 307208 | tf_op jit(solution)/shard_map/ppermute | solution.py:272
  (27 other events, 310.2 us)

commit v8 on v7

--- a/solution.py
+++ b/solution.py
@@ -98,16 +98,16 @@
     return context, probs
 
 
-def attend_back(queries, keys, values, probs, grad_context, masks_b, masks_f):
-    rows = queries.shape[0]
+def scores_back(values, probs, grad_context, masks_b):
     grad_wide = spread(grad_context, masks_b)
     grad_probs = dot_nt(values, grad_wide)
     row_dot = jnp.sum(probs * grad_probs, axis=0, keepdims=True)
-    grad_scores = (probs * (grad_probs - row_dot)).astype(BF16)
-    grad_q = collect(dot_tn(grad_scores, keys), masks_f, rows) * SCORE_SCALE
-    grad_k = dot_nn(grad_scores, spread(queries, masks_b)) * SCORE_SCALE
-    grad_v = dot_nn(probs.astype(BF16), grad_wide)
-    return grad_q, grad_k, grad_v
+    return probs * (grad_probs - row_dot), dot_nn(probs.astype(BF16), grad_wide)
+
+
+def operands_back(queries, keys, grad_scores, masks_b, masks_f):
+    grad_q = collect(dot_tn(grad_scores, keys), masks_f, queries.shape[0])
+    return grad_q * SCORE_SCALE, dot_nn(grad_scores, spread(queries, masks_b)) * SCORE_SCALE
 
 
 class Plan:
@@ -568,12 +568,21 @@
         for u in range(WINDOWS):
             w = g * WINDOWS + u
             for h in range(GROUPS):
-                grads = attend_back(
-                    window(w, h),
-                    window(w, GROUPS + h),
+                grad_scores, grad_v = scores_back(
                     window(w, 2 * GROUPS + h),
                     probs_s[w * GROUPS + h],
                     ctx[h, pl.ds(w, PAD, stride=n_reg), :].astype(BF16),
+                    masks_b,
+                )
+                probs_s[w * GROUPS + h] = grad_scores
+                mix[2 * GROUPS + h, pl.ds(w, tokens, stride=n_reg), :] = grad_v[:tokens]
+        for u in range(WINDOWS):
+            w = g * WINDOWS + u
+            for h in range(GROUPS):
+                grads = operands_back(
+                    window(w, h),
+                    window(w, GROUPS + h),
+                    probs_s[w * GROUPS + h].astype(BF16),
                     masks_b,
                     masks_f,
                 )
@@ -608,16 +617,20 @@
     grad_ctx = dot_nt(grad_mid, w_out).astype(BF16)
     parts = ([], [], [])
     for h in range(GROUPS):
-        grads = attend_back(
-            reg_mix[:, h * LANES : (h + 1) * LANES],
-            reg_mix[:, D + h * LANES : D + (h + 1) * LANES],
+        grad_scores, grad_v = scores_back(
             reg_mix[:, 2 * D + h * LANES : 2 * D + (h + 1) * LANES],
             reg_probs[h],
             grad_ctx[:, h * LANES : (h + 1) * LANES],
             reg_mask_b,
+        )
+        grads = operands_back(
+            reg_mix[:, h * LANES : (h + 1) * LANES],
+            reg_mix[:, D + h * LANES : D + (h + 1) * LANES],
+            grad_scores.astype(BF16),
+            reg_mask_b,
             reg_mask_f,
         )
-        for held, grad in zip(parts, grads):
+        for held, grad in zip(parts, (*grads, grad_v)):
             held.append(grad.astype(BF16))
     grad_mix = jnp.concatenate(parts[0] + parts[1] + parts[2], axis=1)
     grad_a = dot_nt(grad_mix, w_all[:, : 3 * D])

time: 173 us -> 161 us (0.931)
  Pallas kernels: 72 us -> 60 us
    pallas_call x1, Pallas kernels: 68.1 us -> 56.1 us  [layer(): pl.pallas_call(functools.partial(layer_kernel, plans), in_specs=[in_smem]...]
  transfers between devices with their start and end apart: 35 -> 35, of which waited for: 19 -> 19; matrix products, arithmetic and copies ran while one was open for 3% -> 4% of each run, Pallas kernels for 0% -> 0%
where the time goes in v8:
time: 161 us
  waiting for transfers between devices  61.3 us (38%)
  Pallas kernels  60 us (37%)
  starting transfers between devices  28.6 us (18%)
  other arithmetic  7.05 us (4%)
  local copies, waits for them, and re-layouts  2.86 us (2%)
    pallas_call x1, Pallas kernels, layer(): pl.pallas_call(functools.partial(layer_kernel, plans), in_specs=[in_smem]...  56.1 us
    ppermute x3, waiting for transfers between devices, gather(): behind = lax.ppermute(behind, 'fsdp', self.backward)  22.1 us
    ppermute x3, waiting for transfers between devices, scatter(): ahead = lax.ppermute(ahead, 'fsdp', self.forward)  10.6 us
    ppermute x4, waiting for transfers between devices, scatter(): cross = lambda a: lax.ppermute(a, 'dp', self.shift(1))  8.87 us
    ppermute x4, starting transfers between devices, scatter(): cross = lambda a: lax.ppermute(a, 'dp', self.shift(1))  6.26 us
    ppermute x1, waiting for transfers between devices, gather(): stack.append(lax.ppermute(mine, 'dp', self.shift(-by)))  4.99 us
    ppermute x3, starting transfers between devices, gather(): behind = lax.ppermute(behind, 'fsdp', self.backward)  4.62 us
    ppermute x3, starting transfers between devices, scatter(): ahead = lax.ppermute(ahead, 'fsdp', self.forward)  3.96 us
  transfers between devices with their start and end apart: 35, of which 19 were waited for; matrix products, arithmetic and copies ran while one was open for 4% of the time, Pallas kernels for 0%

profile of v8, /device:TPU:0, one launch (start us, length us, event | category | flops | bytes accessed | tf_op | source)
XLA Modules:
  0.0 160.9 jit_solution(17096570014843223040)
XLA Ops:
  2.7 3.0 %collective-permute-start = (bf16[784,128]{1,0:T(8,128)(2,1)S(1)}, bf16[784,128]{1,0:T(8,128)(2,1)S(1)}, u32[]{:S(2)}, u32[]{:S(2)}) collective-permute-start(bf16[784,128]{1,0:T(8,128)(2,1)S(1)} %pad_maximum_fusion.2), channel_id=1, source_target_pairs={{0,16},{8,24},{16,0},{24,8},{1,17},{9,25},{17,1},{25,9},{2,18},{10... | collective-permute-start | bytes 602120 | tf_op jit(solution)/shard_map/ppermute | solution.py:220
  5.7 5.0 %collective-permute-done = bf16[784,128]{1,0:T(8,128)(2,1)S(1)} collective-permute-done((bf16[784,128]{1,0:T(8,128)(2,1)S(1)}, bf16[784,128]{1,0:T(8,128)(2,1)S(1)}, u32[]{:S(2)}, u32[]{:S(2)}) %collective-permute-start) | collective-permute-done | bytes 200736 | tf_op jit(solution)/shard_map/ppermute | solution.py:220
  10.7 1.8 %collective-permute-start.2 = (bf16[1568,128]{1,0:T(8,128)(2,1)S(1)}, bf16[1568,128]{1,0:T(8,128)(2,1)S(1)}, u32[]{:S(2)}, u32[]{:S(2)}) collective-permute-start(bf16[1568,128]{1,0:T(8,128)(2,1)S(1)} %pad_maximum_fusion.rest_0_), channel_id=1, source_target_pairs={{0,1},{2,0},{4,2},{6,4},{7,6},{5,7},{3,5},{1,3},{8,9},{10,8},{12,1... | collective-permute-start | bytes 1204232 | tf_op jit(solution)/shard_map/ppermute | solution.py:225
  12.8 8.4 %collective-permute-done.2.rest_2_ = bf16[1568,128]{1,0:T(8,128)(2,1)S(1)} collective-permute-done((bf16[1568,128]{1,0:T(8,128)(2,1)S(1)}, bf16[1568,128]{1,0:T(8,128)(2,1)S(1)}, u32[]{:S(2)}, u32[]{:S(2)}) %collective-permute-start.2) | collective-permute-done | bytes 401440 | tf_op jit(solution)/shard_map/ppermute | solution.py:225
  21.2 1.5 collective-permute-start.4
  23.3 7.5 %collective-permute-done.4.rest_4_ = bf16[1568,128]{1,0:T(8,128)(2,1)S(1)} collective-permute-done((bf16[1568,128]{1,0:T(8,128)(2,1)S(1)}, bf16[1568,128]{1,0:T(8,128)(2,1)S(1)}, u32[]{:S(2)}, u32[]{:S(2)}) %collective-permute-start.4) | collective-permute-done | bytes 401440 | tf_op jit(solution)/shard_map/ppermute | solution.py:225
  30.8 1.3 collective-permute-start.6
  33.3 6.1 %collective-permute-done.6.rest_6_ = bf16[1568,128]{1,0:T(8,128)(2,1)S(1)} collective-permute-done((bf16[1568,128]{1,0:T(8,128)(2,1)S(1)}, bf16[1568,128]{1,0:T(8,128)(2,1)S(1)}, u32[]{:S(2)}, u32[]{:S(2)}) %collective-permute-start.6) | collective-permute-done | bytes 401440 | tf_op jit(solution)/shard_map/ppermute | solution.py:225
  41.0 1.1 collective-permute-start.8
  44.3 3.7 %collective-permute-done.8.rest_8_ = bf16[784,128]{1,0:T(8,128)(2,1)S(1)} collective-permute-done((bf16[784,128]{1,0:T(8,128)(2,1)S(1)}, bf16[784,128]{1,0:T(8,128)(2,1)S(1)}, u32[]{:S(2)}, u32[]{:S(2)}) %collective-permute-start.8) | collective-permute-done | bytes 200736 | tf_op jit(solution)/shard_map/ppermute | solution.py:228
  48.0 1.1 collective-permute-done.7.rest_7_
  51.4 56.1 %layer.1 = (bf16[24,512]{1,0:T(8,128)(2,1)}, bf16[1176,512]{1,0:T(8,128)(2,1)}, bf16[24,512]{1,0:T(8,128)(2,1)}, bf16[1176,512]{1,0:T(8,128)(2,1)}, bf16[1568,12...) custom-call(s32[192]{0:T(256)} %get-tuple-element.77.block_row, ...), custom_call_target="tpu_custom_call" | custom-call | tf_op jit(solution)/shard_map/layer/pallas_call | solution.py:740
  108.1 2.6 %collective-permute-done.24 = bf16[1568,128]{1,0:T(8,128)(2,1)S(1)} collective-permute-done((bf16[1568,128]{1,0:T(8,128)(2,1)}, bf16[1568,128]{1,0:T(8,128)(2,1)S(1)}, u32[]{:S(2)}, u32[]{:S(2)}) %collective-permute-start.24) | collective-permute-done | bytes 401440 | tf_op jit(solution)/shard_map/ppermute | solution.py:238
  111.6 1.6 collective-permute-start.25
  113.3 3.5 %collective-permute-done.25 = bf16[384,128]{1,0:T(8,128)(2,1)S(1)} collective-permute-done((bf16[384,128]{1,0:T(8,128)(2,1)S(1)}, bf16[384,128]{1,0:T(8,128)(2,1)S(1)}, u32[]{:S(2)}, u32[]{:S(2)}) %collective-permute-start.25) | collective-permute-done | bytes 98336 | tf_op jit(solution)/shard_map/ppermute | solution.py:232
  116.7 1.1 add_convert_fusion.6
  117.9 1.6 collective-permute-start.23
  120.1 1.5 collective-permute-start.30
  121.6 2.8 %collective-permute-done.23 = bf16[768,128]{1,0:T(8,128)(2,1)S(1)} collective-permute-done((bf16[768,128]{1,0:T(8,128)(2,1)S(1)}, bf16[768,128]{1,0:T(8,128)(2,1)S(1)}, u32[]{:S(2)}, u32[]{:S(2)}) %collective-permute-start.23) | collective-permute-done | bytes 196640 | tf_op jit(solution)/shard_map/ppermute | solution.py:232
  124.5 1.6 collective-permute-start.22
  127.2 1.2 collective-permute-start.31
  128.4 1.8 %collective-permute-done.22 = bf16[768,128]{1,0:T(8,128)(2,1)S(1)} collective-permute-done((bf16[768,128]{1,0:T(8,128)(2,1)S(1)}, bf16[768,128]{1,0:T(8,128)(2,1)S(1)}, u32[]{:S(2)}, u32[]{:S(2)}) %collective-permute-start.22) | collective-permute-done | bytes 196640 | tf_op jit(solution)/shard_map/ppermute | solution.py:232
  130.3 1.6 collective-permute-start.21
  131.9 1.9 %collective-permute-done.27 = bf16[1184,128]{1,0:T(8,128)(2,1)S(1)} collective-permute-done((bf16[1184,128]{1,0:T(8,128)(2,1)S(1)}, bf16[1184,128]{1,0:T(8,128)(2,1)S(1)}, u32[]{:S(2)}, u32[]{:S(2)}) %collective-permute-start.27) | collective-permute-done | bytes 303136 | tf_op jit(solution)/shard_map/ppermute | solution.py:265
  134.2 1.6 %collective-permute-start.28 = (bf16[1184,128]{1,0:T(8,128)(2,1)S(1)}, bf16[1184,128]{1,0:T(8,128)(2,1)S(1)}, u32[]{:S(2)}, u32[]{:S(2)}) collective-permute-start(bf16[1184,128]{1,0:T(8,128)(2,1)S(1)} %get-tuple-element.59), channel_id=1, source_target_pairs={{0,2},{2,4},{4,6},{6,7},{7,5},{5,3},{3,1},{1,0},{8,10},{10,12},{12... | collective-permute-start | bytes 909320 | tf_op jit(solution)/shard_map/ppermute | solution.py:265
  137.2 3.9 %collective-permute-done.28 = bf16[1184,128]{1,0:T(8,128)(2,1)S(1)} collective-permute-done((bf16[1184,128]{1,0:T(8,128)(2,1)S(1)}, bf16[1184,128]{1,0:T(8,128)(2,1)S(1)}, u32[]{:S(2)}, u32[]{:S(2)}) %collective-permute-start.28) | collective-permute-done | bytes 303136 | tf_op jit(solution)/shard_map/ppermute | solution.py:265
  141.1 1.7 %collective-permute-done.32 = bf16[1184,128]{1,0:T(8,128)(2,1)S(1)} collective-permute-done((bf16[1184,128]{1,0:T(8,128)(2,1)S(1)}, bf16[1184,128]{1,0:T(8,128)(2,1)S(1)}, u32[]{:S(2)}, u32[]{:S(2)}) %collective-permute-start.32) | collective-permute-done | bytes 303136 | tf_op jit(solution)/shard_map/ppermute | solution.py:266
  143.1 1.5 collective-permute-start.29
  145.2 4.8 %collective-permute-done.29 = bf16[1184,128]{1,0:T(8,128)(2,1)S(1)} collective-permute-done((bf16[1184,128]{1,0:T(8,128)(2,1)S(1)}, bf16[1184,128]{1,0:T(8,128)(2,1)S(1)}, u32[]{:S(2)}, u32[]{:S(2)}) %collective-permute-start.29) | collective-permute-done | bytes 303136 | tf_op jit(solution)/shard_map/ppermute | solution.py:265
  150.0 1.4 collective-permute-done.33
  152.9 3.3 %collective-permute-done.34.rest_0_ = bf16[400,128]{1,0:T(8,128)(2,1)S(1)} collective-permute-done((bf16[400,128]{1,0:T(8,128)(2,1)S(1)}, bf16[400,128]{1,0:T(8,128)(2,1)S(1)}, u32[]{:S(2)}, u32[]{:S(2)}) %collective-permute-start.34) | collective-permute-done | bytes 102432 | tf_op jit(solution)/shard_map/ppermute | solution.py:272
  157.0 3.9 %update.1 = (f32[6,128,128]{2,1,0:T(8,128)}, f32[6,2,128,128]{3,2,1,0:T(8,128)}, f32[6,128,128]{2,1,0:T(8,128)}, f32[6,128,128]{2,1,0:T(8,128)}) custom-call(f32[784,128]{1,0:T(8,128)} %slice.209.summed, bf16[400,128]{1,0:T(8,128)(2,1)} %copy-done.18, f32[6,128,128]{2,1,0:T(8,128)} %rest_1_.1, f32[6,2,128,128]{3,2,1,0:T(8,128)} %rest_2_.1, ...), custom_call_target="tpu_custom_call" | custom-call | tf_op jit(solution)/shard_map/update/pallas_call | solution.py:816
  (123 shorter events, 18.4 us)
Async XLA Ops:
  2.7 8.0 %collective-permute-start = (bf16[784,128]{1,0:T(8,128)(2,1)S(1)}, bf16[784,128]{1,0:T(8,128)(2,1)S(1)}, u32[]{:S(2)}, u32[]{:S(2)}) collective-permute-start(bf16[784,128]{1,0:T(8,128)(2,1)S(1)} %pad_maximum_fusion.2), channel_id=1, source_target_pairs={{0,16},{8,24},{16,0},{24,8},{1,17},{9,25},{17,1},{25,9},{2,18},{10... | collective-permute-start | bytes 602120 | tf_op jit(solution)/shard_map/ppermute | solution.py:220
  10.7 10.5 %collective-permute-start.2 = (bf16[1568,128]{1,0:T(8,128)(2,1)S(1)}, bf16[1568,128]{1,0:T(8,128)(2,1)S(1)}, u32[]{:S(2)}, u32[]{:S(2)}) collective-permute-start(bf16[1568,128]{1,0:T(8,128)(2,1)S(1)} %pad_maximum_fusion.rest_0_), channel_id=1, source_target_pairs={{0,1},{2,0},{4,2},{6,4},{7,6},{5,7},{3,5},{1,3},{8,9},{10,8},{12,1... | collective-permute-start | bytes 1204232 | tf_op jit(solution)/shard_map/ppermute | solution.py:225
  12.5 10.2 %collective-permute-start.1 = (bf16[1568,128]{1,0:T(8,128)(2,1)S(1)}, bf16[1568,128]{1,0:T(8,128)(2,1)S(1)}, u32[]{:S(2)}, u32[]{:S(2)}) collective-permute-start(bf16[1568,128]{1,0:T(8,128)(2,1)S(1)} %pad_maximum_fusion.rest_0_), channel_id=1, source_target_pairs={{0,2},{2,4},{4,6},{6,7},{7,5},{5,3},{3,1},{1,0},{8,10},{10,12},{12... | collective-permute-start | bytes 1204232 | tf_op jit(solution)/shard_map/ppermute | solution.py:224
  21.2 9.6 %collective-permute-start.4 = (bf16[1568,128]{1,0:T(8,128)(2,1)S(1)}, bf16[1568,128]{1,0:T(8,128)(2,1)S(1)}, u32[]{:S(2)}, u32[]{:S(2)}) collective-permute-start(bf16[1568,128]{1,0:T(8,128)(2,1)S(1)} %collective-permute-done.2.rest_2_), channel_id=1, source_target_pairs={{0,1},{2,0},{4,2},{6,4},{7,6},{5,7},{3,5},{1,3},{8,9},{10,8},{12,1... | collective-permute-start | bytes 1204232 | tf_op jit(solution)/shard_map/ppermute | solution.py:225
  22.7 9.5 %collective-permute-start.3 = (bf16[1568,128]{1,0:T(8,128)(2,1)S(1)}, bf16[1568,128]{1,0:T(8,128)(2,1)S(1)}, u32[]{:S(2)}, u32[]{:S(2)}) collective-permute-start(bf16[1568,128]{1,0:T(8,128)(2,1)S(1)} %collective-permute-done.1.rest_1_), channel_id=1, source_target_pairs={{0,2},{2,4},{4,6},{6,7},{7,5},{5,3},{3,1},{1,0},{8,10},{10,12},{12... | collective-permute-start | bytes 1204232 | tf_op jit(solution)/shard_map/ppermute | solution.py:224
  30.8 8.6 %collective-permute-start.6 = (bf16[1568,128]{1,0:T(8,128)(2,1)S(1)}, bf16[1568,128]{1,0:T(8,128)(2,1)S(1)}, u32[]{:S(2)}, u32[]{:S(2)}) collective-permute-start(bf16[1568,128]{1,0:T(8,128)(2,1)S(1)} %collective-permute-done.4.rest_4_), channel_id=1, source_target_pairs={{0,1},{2,0},{4,2},{6,4},{7,6},{5,7},{3,5},{1,3},{8,9},{10,8},{12,1... | collective-permute-start | bytes 1204232 | tf_op jit(solution)/shard_map/ppermute | solution.py:225
  32.2 8.3 %collective-permute-start.5 = (bf16[1568,128]{1,0:T(8,128)(2,1)S(1)}, bf16[1568,128]{1,0:T(8,128)(2,1)S(1)}, u32[]{:S(2)}, u32[]{:S(2)}) collective-permute-start(bf16[1568,128]{1,0:T(8,128)(2,1)S(1)} %collective-permute-done.3.rest_3_), channel_id=1, source_target_pairs={{0,2},{2,4},{4,6},{6,7},{7,5},{5,3},{3,1},{1,0},{8,10},{10,12},{12... | collective-permute-start | bytes 1204232 | tf_op jit(solution)/shard_map/ppermute | solution.py:224
  32.8 8.1 %collective-permute-start.9 = (bf16[1568,128]{1,0:T(8,128)(2,1)S(1)}, bf16[1568,128]{1,0:T(8,128)(2,1)S(1)}, u32[]{:S(2)}, u32[]{:S(2)}) collective-permute-start(bf16[1568,128]{1,0:T(8,128)(2,1)S(1)} %pad_maximum_fusion.rest_0_), channel_id=1, source_target_pairs={{0,8},{8,0},{16,24},{24,16},{1,9},{9,1},{17,25},{25,17},{2,10},{10... | collective-permute-start | bytes 1204232 | tf_op jit(solution)/shard_map/ppermute | solution.py:229
  32.8 9.3 %collective-permute-start.11 = (bf16[1568,128]{1,0:T(8,128)(2,1)S(1)}, bf16[1568,128]{1,0:T(8,128)(2,1)}, u32[]{:S(2)}, u32[]{:S(2)}) collective-permute-start(bf16[1568,128]{1,0:T(8,128)(2,1)S(1)} %collective-permute-done.2.rest_2_), channel_id=1, source_target_pairs={{0,8},{8,0},{16,24},{24,16},{1,9},{9,1},{17,25},{25,17},{2,10},{10... | collective-permute-start | bytes 1204232 | tf_op jit(solution)/shard_map/ppermute | solution.py:229
  33.3 9.7 %collective-permute-start.10 = (bf16[1568,128]{1,0:T(8,128)(2,1)S(1)}, bf16[1568,128]{1,0:T(8,128)(2,1)}, u32[]{:S(2)}, u32[]{:S(2)}) collective-permute-start(bf16[1568,128]{1,0:T(8,128)(2,1)S(1)} %collective-permute-done.1.rest_1_), channel_id=1, source_target_pairs={{0,8},{8,0},{16,24},{24,16},{1,9},{9,1},{17,25},{25,17},{2,10},{10... | collective-permute-start | bytes 1204232 | tf_op jit(solution)/shard_map/ppermute | solution.py:229
  39.4 3.6 %collective-permute-start.13 = (bf16[1568,128]{1,0:T(8,128)(2,1)S(1)}, bf16[1568,128]{1,0:T(8,128)(2,1)}, u32[]{:S(2)}, u32[]{:S(2)}) collective-permute-start(bf16[1568,128]{1,0:T(8,128)(2,1)S(1)} %collective-permute-done.4.rest_4_), channel_id=1, source_target_pairs={{0,8},{8,0},{16,24},{24,16},{1,9},{9,1},{17,25},{25,17},{2,10},{10... | collective-permute-start | bytes 1204232 | tf_op jit(solution)/shard_map/ppermute | solution.py:229
  40.4 9.3 %collective-permute-start.12 = (bf16[1568,128]{1,0:T(8,128)(2,1)S(1)}, bf16[1568,128]{1,0:T(8,128)(2,1)S(1)}, u32[]{:S(2)}, u32[]{:S(2)}) collective-permute-start(bf16[1568,128]{1,0:T(8,128)(2,1)S(1)} %collective-permute-done.3.rest_3_), channel_id=1, source_target_pairs={{0,8},{8,0},{16,24},{24,16},{1,9},{9,1},{17,25},{25,17},{2,10},{10... | collective-permute-start | bytes 1204232 | tf_op jit(solution)/shard_map/ppermute | solution.py:229
  41.0 7.0 %collective-permute-start.8 = (bf16[784,128]{1,0:T(8,128)(2,1)S(1)}, bf16[784,128]{1,0:T(8,128)(2,1)S(1)}, u32[]{:S(2)}, u32[]{:S(2)}) collective-permute-start(bf16[784,128]{1,0:T(8,128)(2,1)S(1)} %slice.191), channel_id=1, source_target_pairs={{0,1},{2,0},{4,2},{6,4},{7,6},{5,7},{3,5},{1,3},{8,9},{10,8},{12,1... | collective-permute-start | bytes 602120 | tf_op jit(solution)/shard_map/ppermute | solution.py:228
  42.1 6.9 %collective-permute-start.7 = (bf16[784,128]{1,0:T(8,128)(2,1)S(1)}, bf16[784,128]{1,0:T(8,128)(2,1)S(1)}, u32[]{:S(2)}, u32[]{:S(2)}) collective-permute-start(bf16[784,128]{1,0:T(8,128)(2,1)S(1)} %slice.190), channel_id=1, source_target_pairs={{0,2},{2,4},{4,6},{6,7},{7,5},{5,3},{3,1},{1,0},{8,10},{10,12},{12... | collective-permute-start | bytes 602120 | tf_op jit(solution)/shard_map/ppermute | solution.py:227
  43.1 6.6 %collective-permute-start.15 = (bf16[1568,128]{1,0:T(8,128)(2,1)S(1)}, bf16[1568,128]{1,0:T(8,128)(2,1)S(1)}, u32[]{:S(2)}, u32[]{:S(2)}) collective-permute-start(bf16[1568,128]{1,0:T(8,128)(2,1)S(1)} %collective-permute-done.6.rest_6_), channel_id=1, source_target_pairs={{0,8},{8,0},{16,24},{24,16},{1,9},{9,1},{17,25},{25,17},{2,10},{10... | collective-permute-start | bytes 1204232 | tf_op jit(solution)/shard_map/ppermute | solution.py:229
  43.1 7.4 %collective-permute-start.14 = (bf16[1568,128]{1,0:T(8,128)(2,1)S(1)}, bf16[1568,128]{1,0:T(8,128)(2,1)S(1)}, u32[]{:S(2)}, u32[]{:S(2)}) collective-permute-start(bf16[1568,128]{1,0:T(8,128)(2,1)S(1)} %collective-permute-done.5.rest_5_), channel_id=1, source_target_pairs={{0,8},{8,0},{16,24},{24,16},{1,9},{9,1},{17,25},{25,17},{2,10},{10... | collective-permute-start | bytes 1204232 | tf_op jit(solution)/shard_map/ppermute | solution.py:229
  107.5 5.7 %collective-permute-start.18 = (bf16[3136,128]{1,0:T(8,128)(2,1)}, bf16[3136,128]{1,0:T(8,128)(2,1)S(1)}, u32[]{:S(2)}, u32[]{:S(2)}) collective-permute-start(bf16[3136,128]{1,0:T(8,128)(2,1)} %get-tuple-element.38), channel_id=1, source_target_pairs={{0,8},{8,0},{16,24},{24,16},{1,9},{9,1},{17,25},{25,17},{2,10},{10... | collective-permute-start | bytes 2408456 | tf_op jit(solution)/shard_map/ppermute | solution.py:238
  111.6 5.1 %collective-permute-start.25 = (bf16[384,128]{1,0:T(8,128)(2,1)S(1)}, bf16[384,128]{1,0:T(8,128)(2,1)S(1)}, u32[]{:S(2)}, u32[]{:S(2)}) collective-permute-start(bf16[384,128]{1,0:T(8,128)(2,1)S(1)} %add_convert_fusion.7), channel_id=1, source_target_pairs={{0,16},{8,24},{16,0},{24,8},{1,17},{9,25},{17,1},{25,9},{2,18},{10... | collective-permute-start | bytes 294920 | tf_op jit(solution)/shard_map/ppermute | solution.py:232
  113.2 8.4 %collective-permute-start.19 = (bf16[3136,128]{1,0:T(8,128)(2,1)}, bf16[3136,128]{1,0:T(8,128)(2,1)S(1)}, u32[]{:S(2)}, u32[]{:S(2)}) collective-permute-start(bf16[3136,128]{1,0:T(8,128)(2,1)} %get-tuple-element.39), channel_id=1, source_target_pairs={{0,8},{8,0},{16,24},{24,16},{1,9},{9,1},{17,25},{25,17},{2,10},{10... | collective-permute-start | bytes 2408456 | tf_op jit(solution)/shard_map/ppermute | solution.py:238
  117.9 6.4 %collective-permute-start.23 = (bf16[768,128]{1,0:T(8,128)(2,1)S(1)}, bf16[768,128]{1,0:T(8,128)(2,1)S(1)}, u32[]{:S(2)}, u32[]{:S(2)}) collective-permute-start(bf16[768,128]{1,0:T(8,128)(2,1)S(1)} %pad_maximum_fusion.4), channel_id=1, source_target_pairs={{0,16},{8,24},{16,0},{24,8},{1,17},{9,25},{17,1},{25,9},{2,18},{10... | collective-permute-start | bytes 589832 | tf_op jit(solution)/shard_map/ppermute | solution.py:232
  119.5 6.5 %collective-permute-start.26 = (bf16[592,128]{1,0:T(8,128)(2,1)S(1)}, bf16[592,128]{1,0:T(8,128)(2,1)S(1)}, u32[]{:S(2)}, u32[]{:S(2)}) collective-permute-start(bf16[592,128]{1,0:T(8,128)(2,1)S(1)} %get-tuple-element.67), channel_id=1, source_target_pairs={{0,2},{2,4},{4,6},{6,7},{7,5},{5,3},{3,1},{1,0},{8,10},{10,12},{12... | collective-permute-start | bytes 454664 | tf_op jit(solution)/shard_map/ppermute | solution.py:258
  120.1 5.9 %collective-permute-start.30 = (bf16[592,128]{1,0:T(8,128)(2,1)S(1)}, bf16[592,128]{1,0:T(8,128)(2,1)S(1)}, u32[]{:S(2)}, u32[]{:S(2)}) collective-permute-start(bf16[592,128]{1,0:T(8,128)(2,1)S(1)} %get-tuple-element.68), channel_id=1, source_target_pairs={{0,1},{2,0},{4,2},{6,4},{7,6},{5,7},{3,5},{1,3},{8,9},{10,8},{12,1... | collective-permute-start | bytes 454664 | tf_op jit(solution)/shard_map/ppermute | solution.py:259
  121.6 8.6 %collective-permute-start.20 = (bf16[4704,128]{1,0:T(8,128)(2,1)S(1)}, bf16[4704,128]{1,0:T(8,128)(2,1)S(1)}, u32[]{:S(2)}, u32[]{:S(2)}) collective-permute-start(bf16[4704,128]{1,0:T(8,128)(2,1)S(1)} %copy-done.23), channel_id=1, source_target_pairs={{0,8},{8,0},{16,24},{24,16},{1,9},{9,1},{17,25},{25,17},{2,10},{10... | collective-permute-start | bytes 3612680 | tf_op jit(solution)/shard_map/ppermute | solution.py:238
  124.5 5.7 %collective-permute-start.22 = (bf16[768,128]{1,0:T(8,128)(2,1)S(1)}, bf16[768,128]{1,0:T(8,128)(2,1)S(1)}, u32[]{:S(2)}, u32[]{:S(2)}) collective-permute-start(bf16[768,128]{1,0:T(8,128)(2,1)S(1)} %pad_maximum_fusion.3), channel_id=1, source_target_pairs={{0,16},{8,24},{16,0},{24,8},{1,17},{9,25},{17,1},{25,9},{2,18},{10... | collective-permute-start | bytes 589832 | tf_op jit(solution)/shard_map/ppermute | solution.py:232
  126.3 7.5 %collective-permute-start.27 = (bf16[1184,128]{1,0:T(8,128)(2,1)S(1)}, bf16[1184,128]{1,0:T(8,128)(2,1)S(1)}, u32[]{:S(2)}, u32[]{:S(2)}) collective-permute-start(bf16[1184,128]{1,0:T(8,128)(2,1)S(1)} %get-tuple-element.61), channel_id=1, source_target_pairs={{0,2},{2,4},{4,6},{6,7},{7,5},{5,3},{3,1},{1,0},{8,10},{10,12},{12... | collective-permute-start | bytes 909320 | tf_op jit(solution)/shard_map/ppermute | solution.py:265
  127.2 6.8 %collective-permute-start.31 = (bf16[1184,128]{1,0:T(8,128)(2,1)S(1)}, bf16[1184,128]{1,0:T(8,128)(2,1)S(1)}, u32[]{:S(2)}, u32[]{:S(2)}) collective-permute-start(bf16[1184,128]{1,0:T(8,128)(2,1)S(1)} %get-tuple-element.62), channel_id=1, source_target_pairs={{0,1},{2,0},{4,2},{6,4},{7,6},{5,7},{3,5},{1,3},{8,9},{10,8},{12,1... | collective-permute-start | bytes 909320 | tf_op jit(solution)/shard_map/ppermute | solution.py:266
  130.3 6.8 %collective-permute-start.21 = (bf16[1152,128]{1,0:T(8,128)(2,1)S(1)}, bf16[1152,128]{1,0:T(8,128)(2,1)S(1)}, u32[]{:S(2)}, u32[]{:S(2)}) collective-permute-start(bf16[1152,128]{1,0:T(8,128)(2,1)S(1)} %pad_maximum_fusion.1), channel_id=1, source_target_pairs={{0,16},{8,24},{16,0},{24,8},{1,17},{9,25},{17,1},{25,9},{2,18},{10... | collective-permute-start | bytes 884744 | tf_op jit(solution)/shard_map/ppermute | solution.py:232
  134.2 6.9 %collective-permute-start.28 = (bf16[1184,128]{1,0:T(8,128)(2,1)S(1)}, bf16[1184,128]{1,0:T(8,128)(2,1)S(1)}, u32[]{:S(2)}, u32[]{:S(2)}) collective-permute-start(bf16[1184,128]{1,0:T(8,128)(2,1)S(1)} %get-tuple-element.59), channel_id=1, source_target_pairs={{0,2},{2,4},{4,6},{6,7},{7,5},{5,3},{3,1},{1,0},{8,10},{10,12},{12... | collective-permute-start | bytes 909320 | tf_op jit(solution)/shard_map/ppermute | solution.py:265
  135.9 7.0 %collective-permute-start.32 = (bf16[1184,128]{1,0:T(8,128)(2,1)S(1)}, bf16[1184,128]{1,0:T(8,128)(2,1)S(1)}, u32[]{:S(2)}, u32[]{:S(2)}) collective-permute-start(bf16[1184,128]{1,0:T(8,128)(2,1)S(1)} %get-tuple-element.60), channel_id=1, source_target_pairs={{0,1},{2,0},{4,2},{6,4},{7,6},{5,7},{3,5},{1,3},{8,9},{10,8},{12,1... | collective-permute-start | bytes 909320 | tf_op jit(solution)/shard_map/ppermute | solution.py:266
  143.1 6.9 %collective-permute-start.29 = (bf16[1184,128]{1,0:T(8,128)(2,1)S(1)}, bf16[1184,128]{1,0:T(8,128)(2,1)S(1)}, u32[]{:S(2)}, u32[]{:S(2)}) collective-permute-start(bf16[1184,128]{1,0:T(8,128)(2,1)S(1)} %get-tuple-element.54), channel_id=1, source_target_pairs={{0,2},{2,4},{4,6},{6,7},{7,5},{5,3},{3,1},{1,0},{8,10},{10,12},{12... | collective-permute-start | bytes 909320 | tf_op jit(solution)/shard_map/ppermute | solution.py:265
  144.6 6.8 %collective-permute-start.33 = (bf16[1184,128]{1,0:T(8,128)(2,1)S(1)}, bf16[1184,128]{1,0:T(8,128)(2,1)S(1)}, u32[]{:S(2)}, u32[]{:S(2)}) collective-permute-start(bf16[1184,128]{1,0:T(8,128)(2,1)S(1)} %get-tuple-element.55), channel_id=1, source_target_pairs={{0,1},{2,0},{4,2},{6,4},{7,6},{5,7},{3,5},{1,3},{8,9},{10,8},{12,1... | collective-permute-start | bytes 909320 | tf_op jit(solution)/shard_map/ppermute | solution.py:266
  151.6 4.7 %collective-permute-start.34 = (bf16[400,128]{1,0:T(8,128)(2,1)S(1)}, bf16[400,128]{1,0:T(8,128)(2,1)S(1)}, u32[]{:S(2)}, u32[]{:S(2)}) collective-permute-start(bf16[400,128]{1,0:T(8,128)(2,1)S(1)} %slice.250), channel_id=1, source_target_pairs={{0,16},{8,24},{16,0},{24,8},{1,17},{9,25},{17,1},{25,9},{2,18},{10... | collective-permute-start | bytes 307208 | tf_op jit(solution)/shard_map/ppermute | solution.py:272
  (27 other events, 310.2 us)

commit v9 on v8

--- a/solution.py
+++ b/solution.py
@@ -342,7 +342,6 @@
     a_mlp_t,
     g_fin_t,
     g_mid,
-    g_mix,
     act,
     g_pre,
     acc,
@@ -359,7 +358,7 @@
     rows = body + n_reg
     tokens = rows // n_reg
     part = rows // CHUNKS
-    chunk = lambda i: pl.ds(pl.multiple_of(i * part, part), part)
+    chunk = lambda i: slice(i * part, (i + 1) * part)
     stage = w_all
 
     def move(source, target, n):
@@ -481,7 +480,7 @@
     token[:body, :] = hold_b[...]
     token[body:, :] = cot_regions[...]
 
-    def project(i, carry):
+    def project(i):
         at = chunk(i)
         a_win = (n_one[at, :] * row(0) + row(1)).astype(BF16)
         a_win_t[i] = a_win.T
@@ -490,9 +489,9 @@
             mixed = mixed if bias is None else mixed + bias
             for h in range(GROUPS):
                 mix[j * GROUPS + h, at, :] = mixed[:, h * LANES : (h + 1) * LANES]
-        return carry
-
-    lax.fori_loop(0, CHUNKS, project, 0)
+
+    for i in range(CHUNKS):
+        project(i)
 
     masks_b = head_masks(PAD, BF16)
     masks_f = head_masks(PAD, F32)
@@ -519,7 +518,7 @@
 
     lax.fori_loop(0, n_reg // WINDOWS, window_attend, 0)
 
-    def perceptron(i, carry):
+    def perceptron(i):
         at = chunk(i)
         context = jnp.concatenate([ctx[h, at, :] for h in range(GROUPS)], axis=1).astype(BF16)
         ctx_t[i] = context.T
@@ -556,9 +555,9 @@
         grad_ctx = dot_nt(grad_mid, w_out)
         for h in range(GROUPS):
             ctx[h, at, :] = grad_ctx[:, h * LANES : (h + 1) * LANES]
-        return carry
-
-    lax.fori_loop(0, CHUNKS, perceptron, 0)
+
+    for i in range(CHUNKS):
+        perceptron(i)
     hold_a[...] = token[:body, :]
     out_regions[...] = token[body:, :]
     give = [move(hold_a, out_patches, 0), move(hold_b, grad_patches, 1)]
@@ -592,10 +591,9 @@
 
     lax.fori_loop(0, n_reg // WINDOWS, window_back, 0)
 
-    def project_back(i, carry):
+    def project_back(i):
         at = chunk(i)
         grad_mix = jnp.concatenate([mix[h, at, :] for h in range(3 * GROUPS)], axis=1).astype(BF16)
-        g_mix[at, :] = grad_mix
         acc_mix[...] = acc_mix[...] + jnp.sum(grad_mix.astype(F32), axis=0, keepdims=True)
         grad_a = dot_nt(grad_mix, w_all[:, : 3 * D])
         normed = n_one[at, :]
@@ -604,9 +602,9 @@
         token[at, :] = (
             g_mid[at, :].astype(F32) + normalize_back(grad_a * row(0), normed, i_one[at, :])
         ).astype(BF16)
-        return carry
-
-    lax.fori_loop(0, CHUNKS, project_back, 0)
+
+    for i in range(CHUNKS):
+        project_back(i)
     hold_b[...] = token[:body, :]
     give[1].start()
 
@@ -661,18 +659,22 @@
             [held, jnp.zeros((TAIL - plan.small_rows, LANES), F32)], axis=0
         ).astype(BF16)
 
-    def contract(left, right, cols):
-        total = dot_nn(left[0], right[:part, cols])
+    def contract(left, right):
+        total = dot_nn(left[0], right(chunk(0)))
         for i in range(1, CHUNKS):
-            total = total + dot_nn(left[i], right[i * part : (i + 1) * part, cols])
+            total = total + dot_nn(left[i], right(chunk(i)))
         return total
+
+    def mix_columns(at, start, count):
+        held = range(start // LANES, (start + count) // LANES)
+        return jnp.concatenate([mix[h, at, :] for h in held], axis=1).astype(BF16)
 
     width = 256
     for c in range(FF // width):
         cols = slice(c * width, (c + 1) * width)
         out = slice(4 * D + c * width, 4 * D + (c + 1) * width)
-        stage[:, out] = contract(a_mlp_t, g_pre, cols).astype(BF16)
-        flipped = contract(g_fin_t, act, cols).astype(BF16).T
+        stage[:, out] = contract(a_mlp_t, lambda at: g_pre[at, cols]).astype(BF16)
+        flipped = contract(g_fin_t, lambda at: act[at, cols]).astype(BF16).T
         for j in range(width // SIDE):
             for k in range(D // SIDE):
                 stage[
@@ -682,12 +684,12 @@
     for c in range(3 * D // width):
         cols = slice(c * width, (c + 1) * width)
         stage[:, cols] = (
-            contract(a_win_t, g_mix, cols) + dot_tn(a_reg, grad_mix[:, cols])
+            contract(a_win_t, lambda at: mix_columns(at, c * width, width)) + dot_tn(a_reg, grad_mix[:, cols])
         ).astype(BF16)
     for c in range(D // width):
         cols = slice(c * width, (c + 1) * width)
         stage[:, 3 * D + c * width : 3 * D + (c + 1) * width] = (
-            contract(ctx_t, g_mid, cols) + dot_tn(reg_ctx[...], grad_mid[:, cols])
+            contract(ctx_t, lambda at: g_mid[at, cols]) + dot_tn(reg_ctx[...], grad_mid[:, cols])
         ).astype(BF16)
     if plan.empty:
         stage[:SIDE, ALL:] = jnp.zeros((SIDE, SIDE), BF16)
@@ -769,7 +771,6 @@
             cube(CHUNKS, D, part, BF16),
             cube(CHUNKS, D, part, BF16),
             vec(rows, D, BF16),
-            vec(rows, 3 * D, BF16),
             vec(rows, FF, BF16),
             vec(rows, FF, BF16),
             vec(8, D),

time: 161 us -> 171 us (1.062)
  Pallas kernels: 60 us -> 69 us
    pallas_call x1, Pallas kernels: 56.1 us -> 65 us  [layer(): pl.pallas_call(functools.partial(layer_kernel, plans), in_specs=[in_smem]...]
  transfers between devices with their start and end apart: 35 -> 35, of which waited for: 19 -> 19; matrix products, arithmetic and copies ran while one was open for 4% -> 3% of each run, Pallas kernels for 0% -> 0%
where the time goes in v9:
time: 171 us; the launch traced here: 170 us
  Pallas kernels  69 us (40%)
  waiting for transfers between devices  61.3 us (36%)
  starting transfers between devices  28.8 us (17%)
  other arithmetic  7.05 us (4%)
  local copies, waits for them, and re-layouts  2.86 us (2%)
    pallas_call x1, Pallas kernels, layer(): pl.pallas_call(functools.partial(layer_kernel, plans), in_specs=[in_smem]...  65 us
    ppermute x3, waiting for transfers between devices, gather(): behind = lax.ppermute(behind, 'fsdp', self.backward)  22.1 us
    ppermute x3, waiting for transfers between devices, scatter(): ahead = lax.ppermute(ahead, 'fsdp', self.forward)  10.8 us
    ppermute x4, waiting for transfers between devices, scatter(): cross = lambda a: lax.ppermute(a, 'dp', self.shift(1))  8.48 us
    ppermute x4, starting transfers between devices, scatter(): cross = lambda a: lax.ppermute(a, 'dp', self.shift(1))  6.27 us
    ppermute x1, waiting for transfers between devices, gather(): stack.append(lax.ppermute(mine, 'dp', self.shift(-by)))  4.99 us
    ppermute x3, starting transfers between devices, gather(): behind = lax.ppermute(behind, 'fsdp', self.backward)  4.62 us
    ppermute x3, starting transfers between devices, scatter(): ahead = lax.ppermute(ahead, 'fsdp', self.forward)  4.16 us
  transfers between devices with their start and end apart: 35, of which 19 were waited for; matrix products, arithmetic and copies ran while one was open for 3% of the time, Pallas kernels for 0%

profile of v9, /device:TPU:0, one launch (start us, length us, event | category | flops | bytes accessed | tf_op | source)
XLA Modules:
  0.0 170.3 jit_solution(1595343231796551105)
XLA Ops:
  2.7 3.0 %collective-permute-start = (bf16[784,128]{1,0:T(8,128)(2,1)S(1)}, bf16[784,128]{1,0:T(8,128)(2,1)S(1)}, u32[]{:S(2)}, u32[]{:S(2)}) collective-permute-start(bf16[784,128]{1,0:T(8,128)(2,1)S(1)} %pad_maximum_fusion.2), channel_id=1, source_target_pairs={{0,16},{8,24},{16,0},{24,8},{1,17},{9,25},{17,1},{25,9},{2,18},{10... | collective-permute-start | bytes 602120 | tf_op jit(solution)/shard_map/ppermute | solution.py:220
  5.7 5.0 %collective-permute-done = bf16[784,128]{1,0:T(8,128)(2,1)S(1)} collective-permute-done((bf16[784,128]{1,0:T(8,128)(2,1)S(1)}, bf16[784,128]{1,0:T(8,128)(2,1)S(1)}, u32[]{:S(2)}, u32[]{:S(2)}) %collective-permute-start) | collective-permute-done | bytes 200736 | tf_op jit(solution)/shard_map/ppermute | solution.py:220
  10.7 1.8 %collective-permute-start.2 = (bf16[1568,128]{1,0:T(8,128)(2,1)S(1)}, bf16[1568,128]{1,0:T(8,128)(2,1)S(1)}, u32[]{:S(2)}, u32[]{:S(2)}) collective-permute-start(bf16[1568,128]{1,0:T(8,128)(2,1)S(1)} %pad_maximum_fusion.rest_0_), channel_id=1, source_target_pairs={{0,1},{2,0},{4,2},{6,4},{7,6},{5,7},{3,5},{1,3},{8,9},{10,8},{12,1... | collective-permute-start | bytes 1204232 | tf_op jit(solution)/shard_map/ppermute | solution.py:225
  12.8 8.4 %collective-permute-done.2.rest_2_ = bf16[1568,128]{1,0:T(8,128)(2,1)S(1)} collective-permute-done((bf16[1568,128]{1,0:T(8,128)(2,1)S(1)}, bf16[1568,128]{1,0:T(8,128)(2,1)S(1)}, u32[]{:S(2)}, u32[]{:S(2)}) %collective-permute-start.2) | collective-permute-done | bytes 401440 | tf_op jit(solution)/shard_map/ppermute | solution.py:225
  21.2 1.5 collective-permute-start.4
  23.3 7.5 %collective-permute-done.4.rest_4_ = bf16[1568,128]{1,0:T(8,128)(2,1)S(1)} collective-permute-done((bf16[1568,128]{1,0:T(8,128)(2,1)S(1)}, bf16[1568,128]{1,0:T(8,128)(2,1)S(1)}, u32[]{:S(2)}, u32[]{:S(2)}) %collective-permute-start.4) | collective-permute-done | bytes 401440 | tf_op jit(solution)/shard_map/ppermute | solution.py:225
  30.8 1.3 collective-permute-start.6
  33.3 6.1 %collective-permute-done.6.rest_6_ = bf16[1568,128]{1,0:T(8,128)(2,1)S(1)} collective-permute-done((bf16[1568,128]{1,0:T(8,128)(2,1)S(1)}, bf16[1568,128]{1,0:T(8,128)(2,1)S(1)}, u32[]{:S(2)}, u32[]{:S(2)}) %collective-permute-start.6) | collective-permute-done | bytes 401440 | tf_op jit(solution)/shard_map/ppermute | solution.py:225
  41.0 1.1 collective-permute-start.8
  44.3 3.7 %collective-permute-done.8.rest_8_ = bf16[784,128]{1,0:T(8,128)(2,1)S(1)} collective-permute-done((bf16[784,128]{1,0:T(8,128)(2,1)S(1)}, bf16[784,128]{1,0:T(8,128)(2,1)S(1)}, u32[]{:S(2)}, u32[]{:S(2)}) %collective-permute-start.8) | collective-permute-done | bytes 200736 | tf_op jit(solution)/shard_map/ppermute | solution.py:228
  48.0 1.1 collective-permute-done.7.rest_7_
  51.4 65.0 %layer.1 = (bf16[24,512]{1,0:T(8,128)(2,1)}, bf16[1176,512]{1,0:T(8,128)(2,1)}, bf16[24,512]{1,0:T(8,128)(2,1)}, bf16[1176,512]{1,0:T(8,128)(2,1)}, bf16[1568,12...) custom-call(s32[192]{0:T(256)} %get-tuple-element.77.block_row, ...), custom_call_target="tpu_custom_call" | custom-call | tf_op jit(solution)/shard_map/layer/pallas_call | solution.py:742
  117.0 2.6 %collective-permute-done.24 = bf16[1568,128]{1,0:T(8,128)(2,1)S(1)} collective-permute-done((bf16[1568,128]{1,0:T(8,128)(2,1)}, bf16[1568,128]{1,0:T(8,128)(2,1)S(1)}, u32[]{:S(2)}, u32[]{:S(2)}) %collective-permute-start.24) | collective-permute-done | bytes 401440 | tf_op jit(solution)/shard_map/ppermute | solution.py:238
  120.6 1.6 collective-permute-start.25
  122.3 3.5 %collective-permute-done.25 = bf16[384,128]{1,0:T(8,128)(2,1)S(1)} collective-permute-done((bf16[384,128]{1,0:T(8,128)(2,1)S(1)}, bf16[384,128]{1,0:T(8,128)(2,1)S(1)}, u32[]{:S(2)}, u32[]{:S(2)}) %collective-permute-start.25) | collective-permute-done | bytes 98336 | tf_op jit(solution)/shard_map/ppermute | solution.py:232
  125.7 1.1 add_convert_fusion.6
  126.9 1.6 collective-permute-start.23
  129.1 1.7 collective-permute-start.30
  130.8 2.6 %collective-permute-done.23 = bf16[768,128]{1,0:T(8,128)(2,1)S(1)} collective-permute-done((bf16[768,128]{1,0:T(8,128)(2,1)S(1)}, bf16[768,128]{1,0:T(8,128)(2,1)S(1)}, u32[]{:S(2)}, u32[]{:S(2)}) %collective-permute-start.23) | collective-permute-done | bytes 196640 | tf_op jit(solution)/shard_map/ppermute | solution.py:232
  133.5 1.6 collective-permute-start.22
  135.3 1.1 collective-permute-start.27
  137.4 1.8 %collective-permute-done.22 = bf16[768,128]{1,0:T(8,128)(2,1)S(1)} collective-permute-done((bf16[768,128]{1,0:T(8,128)(2,1)S(1)}, bf16[768,128]{1,0:T(8,128)(2,1)S(1)}, u32[]{:S(2)}, u32[]{:S(2)}) %collective-permute-start.22) | collective-permute-done | bytes 196640 | tf_op jit(solution)/shard_map/ppermute | solution.py:232
  139.3 1.6 collective-permute-start.21
  140.9 1.9 %collective-permute-done.27 = bf16[1184,128]{1,0:T(8,128)(2,1)S(1)} collective-permute-done((bf16[1184,128]{1,0:T(8,128)(2,1)S(1)}, bf16[1184,128]{1,0:T(8,128)(2,1)S(1)}, u32[]{:S(2)}, u32[]{:S(2)}) %collective-permute-start.27) | collective-permute-done | bytes 303136 | tf_op jit(solution)/shard_map/ppermute | solution.py:265
  143.4 1.6 collective-permute-start.28
  146.2 4.1 %collective-permute-done.28 = bf16[1184,128]{1,0:T(8,128)(2,1)S(1)} collective-permute-done((bf16[1184,128]{1,0:T(8,128)(2,1)S(1)}, bf16[1184,128]{1,0:T(8,128)(2,1)S(1)}, u32[]{:S(2)}, u32[]{:S(2)}) %collective-permute-start.28) | collective-permute-done | bytes 303136 | tf_op jit(solution)/shard_map/ppermute | solution.py:265
  150.3 1.7 %collective-permute-done.32 = bf16[1184,128]{1,0:T(8,128)(2,1)S(1)} collective-permute-done((bf16[1184,128]{1,0:T(8,128)(2,1)S(1)}, bf16[1184,128]{1,0:T(8,128)(2,1)S(1)}, u32[]{:S(2)}, u32[]{:S(2)}) %collective-permute-start.32) | collective-permute-done | bytes 303136 | tf_op jit(solution)/shard_map/ppermute | solution.py:266
  152.3 1.5 collective-permute-start.29
  154.4 4.8 %collective-permute-done.29 = bf16[1184,128]{1,0:T(8,128)(2,1)S(1)} collective-permute-done((bf16[1184,128]{1,0:T(8,128)(2,1)S(1)}, bf16[1184,128]{1,0:T(8,128)(2,1)S(1)}, u32[]{:S(2)}, u32[]{:S(2)}) %collective-permute-start.29) | collective-permute-done | bytes 303136 | tf_op jit(solution)/shard_map/ppermute | solution.py:265
  159.1 1.4 collective-permute-done.33
  162.1 3.3 %collective-permute-done.34.rest_0_ = bf16[400,128]{1,0:T(8,128)(2,1)S(1)} collective-permute-done((bf16[400,128]{1,0:T(8,128)(2,1)S(1)}, bf16[400,128]{1,0:T(8,128)(2,1)S(1)}, u32[]{:S(2)}, u32[]{:S(2)}) %collective-permute-start.34) | collective-permute-done | bytes 102432 | tf_op jit(solution)/shard_map/ppermute | solution.py:272
  166.2 3.9 %update.1 = (f32[6,128,128]{2,1,0:T(8,128)}, f32[6,2,128,128]{3,2,1,0:T(8,128)}, f32[6,128,128]{2,1,0:T(8,128)}, f32[6,128,128]{2,1,0:T(8,128)}) custom-call(f32[784,128]{1,0:T(8,128)} %slice.209.summed, bf16[400,128]{1,0:T(8,128)(2,1)} %copy-done.18, f32[6,128,128]{2,1,0:T(8,128)} %rest_1_.1, f32[6,2,128,128]{3,2,1,0:T(8,128)} %rest_2_.1, ...), custom_call_target="tpu_custom_call" | custom-call | tf_op jit(solution)/shard_map/update/pallas_call | solution.py:817
  (123 shorter events, 18.6 us)
Async XLA Ops:
  2.7 8.0 %collective-permute-start = (bf16[784,128]{1,0:T(8,128)(2,1)S(1)}, bf16[784,128]{1,0:T(8,128)(2,1)S(1)}, u32[]{:S(2)}, u32[]{:S(2)}) collective-permute-start(bf16[784,128]{1,0:T(8,128)(2,1)S(1)} %pad_maximum_fusion.2), channel_id=1, source_target_pairs={{0,16},{8,24},{16,0},{24,8},{1,17},{9,25},{17,1},{25,9},{2,18},{10... | collective-permute-start | bytes 602120 | tf_op jit(solution)/shard_map/ppermute | solution.py:220
  10.7 10.5 %collective-permute-start.2 = (bf16[1568,128]{1,0:T(8,128)(2,1)S(1)}, bf16[1568,128]{1,0:T(8,128)(2,1)S(1)}, u32[]{:S(2)}, u32[]{:S(2)}) collective-permute-start(bf16[1568,128]{1,0:T(8,128)(2,1)S(1)} %pad_maximum_fusion.rest_0_), channel_id=1, source_target_pairs={{0,1},{2,0},{4,2},{6,4},{7,6},{5,7},{3,5},{1,3},{8,9},{10,8},{12,1... | collective-permute-start | bytes 1204232 | tf_op jit(solution)/shard_map/ppermute | solution.py:225
  12.5 10.2 %collective-permute-start.1 = (bf16[1568,128]{1,0:T(8,128)(2,1)S(1)}, bf16[1568,128]{1,0:T(8,128)(2,1)S(1)}, u32[]{:S(2)}, u32[]{:S(2)}) collective-permute-start(bf16[1568,128]{1,0:T(8,128)(2,1)S(1)} %pad_maximum_fusion.rest_0_), channel_id=1, source_target_pairs={{0,2},{2,4},{4,6},{6,7},{7,5},{5,3},{3,1},{1,0},{8,10},{10,12},{12... | collective-permute-start | bytes 1204232 | tf_op jit(solution)/shard_map/ppermute | solution.py:224
  21.2 9.6 %collective-permute-start.4 = (bf16[1568,128]{1,0:T(8,128)(2,1)S(1)}, bf16[1568,128]{1,0:T(8,128)(2,1)S(1)}, u32[]{:S(2)}, u32[]{:S(2)}) collective-permute-start(bf16[1568,128]{1,0:T(8,128)(2,1)S(1)} %collective-permute-done.2.rest_2_), channel_id=1, source_target_pairs={{0,1},{2,0},{4,2},{6,4},{7,6},{5,7},{3,5},{1,3},{8,9},{10,8},{12,1... | collective-permute-start | bytes 1204232 | tf_op jit(solution)/shard_map/ppermute | solution.py:225
  22.7 9.5 %collective-permute-start.3 = (bf16[1568,128]{1,0:T(8,128)(2,1)S(1)}, bf16[1568,128]{1,0:T(8,128)(2,1)S(1)}, u32[]{:S(2)}, u32[]{:S(2)}) collective-permute-start(bf16[1568,128]{1,0:T(8,128)(2,1)S(1)} %collective-permute-done.1.rest_1_), channel_id=1, source_target_pairs={{0,2},{2,4},{4,6},{6,7},{7,5},{5,3},{3,1},{1,0},{8,10},{10,12},{12... | collective-permute-start | bytes 1204232 | tf_op jit(solution)/shard_map/ppermute | solution.py:224
  30.8 8.6 %collective-permute-start.6 = (bf16[1568,128]{1,0:T(8,128)(2,1)S(1)}, bf16[1568,128]{1,0:T(8,128)(2,1)S(1)}, u32[]{:S(2)}, u32[]{:S(2)}) collective-permute-start(bf16[1568,128]{1,0:T(8,128)(2,1)S(1)} %collective-permute-done.4.rest_4_), channel_id=1, source_target_pairs={{0,1},{2,0},{4,2},{6,4},{7,6},{5,7},{3,5},{1,3},{8,9},{10,8},{12,1... | collective-permute-start | bytes 1204232 | tf_op jit(solution)/shard_map/ppermute | solution.py:225
  32.2 8.3 %collective-permute-start.5 = (bf16[1568,128]{1,0:T(8,128)(2,1)S(1)}, bf16[1568,128]{1,0:T(8,128)(2,1)S(1)}, u32[]{:S(2)}, u32[]{:S(2)}) collective-permute-start(bf16[1568,128]{1,0:T(8,128)(2,1)S(1)} %collective-permute-done.3.rest_3_), channel_id=1, source_target_pairs={{0,2},{2,4},{4,6},{6,7},{7,5},{5,3},{3,1},{1,0},{8,10},{10,12},{12... | collective-permute-start | bytes 1204232 | tf_op jit(solution)/shard_map/ppermute | solution.py:224
  32.8 8.1 %collective-permute-start.9 = (bf16[1568,128]{1,0:T(8,128)(2,1)S(1)}, bf16[1568,128]{1,0:T(8,128)(2,1)S(1)}, u32[]{:S(2)}, u32[]{:S(2)}) collective-permute-start(bf16[1568,128]{1,0:T(8,128)(2,1)S(1)} %pad_maximum_fusion.rest_0_), channel_id=1, source_target_pairs={{0,8},{8,0},{16,24},{24,16},{1,9},{9,1},{17,25},{25,17},{2,10},{10... | collective-permute-start | bytes 1204232 | tf_op jit(solution)/shard_map/ppermute | solution.py:229
  32.8 9.3 %collective-permute-start.11 = (bf16[1568,128]{1,0:T(8,128)(2,1)S(1)}, bf16[1568,128]{1,0:T(8,128)(2,1)}, u32[]{:S(2)}, u32[]{:S(2)}) collective-permute-start(bf16[1568,128]{1,0:T(8,128)(2,1)S(1)} %collective-permute-done.2.rest_2_), channel_id=1, source_target_pairs={{0,8},{8,0},{16,24},{24,16},{1,9},{9,1},{17,25},{25,17},{2,10},{10... | collective-permute-start | bytes 1204232 | tf_op jit(solution)/shard_map/ppermute | solution.py:229
  33.3 9.7 %collective-permute-start.10 = (bf16[1568,128]{1,0:T(8,128)(2,1)S(1)}, bf16[1568,128]{1,0:T(8,128)(2,1)}, u32[]{:S(2)}, u32[]{:S(2)}) collective-permute-start(bf16[1568,128]{1,0:T(8,128)(2,1)S(1)} %collective-permute-done.1.rest_1_), channel_id=1, source_target_pairs={{0,8},{8,0},{16,24},{24,16},{1,9},{9,1},{17,25},{25,17},{2,10},{10... | collective-permute-start | bytes 1204232 | tf_op jit(solution)/shard_map/ppermute | solution.py:229
  39.4 3.6 %collective-permute-start.13 = (bf16[1568,128]{1,0:T(8,128)(2,1)S(1)}, bf16[1568,128]{1,0:T(8,128)(2,1)}, u32[]{:S(2)}, u32[]{:S(2)}) collective-permute-start(bf16[1568,128]{1,0:T(8,128)(2,1)S(1)} %collective-permute-done.4.rest_4_), channel_id=1, source_target_pairs={{0,8},{8,0},{16,24},{24,16},{1,9},{9,1},{17,25},{25,17},{2,10},{10... | collective-permute-start | bytes 1204232 | tf_op jit(solution)/shard_map/ppermute | solution.py:229
  40.4 9.3 %collective-permute-start.12 = (bf16[1568,128]{1,0:T(8,128)(2,1)S(1)}, bf16[1568,128]{1,0:T(8,128)(2,1)S(1)}, u32[]{:S(2)}, u32[]{:S(2)}) collective-permute-start(bf16[1568,128]{1,0:T(8,128)(2,1)S(1)} %collective-permute-done.3.rest_3_), channel_id=1, source_target_pairs={{0,8},{8,0},{16,24},{24,16},{1,9},{9,1},{17,25},{25,17},{2,10},{10... | collective-permute-start | bytes 1204232 | tf_op jit(solution)/shard_map/ppermute | solution.py:229
  41.0 7.0 %collective-permute-start.8 = (bf16[784,128]{1,0:T(8,128)(2,1)S(1)}, bf16[784,128]{1,0:T(8,128)(2,1)S(1)}, u32[]{:S(2)}, u32[]{:S(2)}) collective-permute-start(bf16[784,128]{1,0:T(8,128)(2,1)S(1)} %slice.191), channel_id=1, source_target_pairs={{0,1},{2,0},{4,2},{6,4},{7,6},{5,7},{3,5},{1,3},{8,9},{10,8},{12,1... | collective-permute-start | bytes 602120 | tf_op jit(solution)/shard_map/ppermute | solution.py:228
  42.1 6.9 %collective-permute-start.7 = (bf16[784,128]{1,0:T(8,128)(2,1)S(1)}, bf16[784,128]{1,0:T(8,128)(2,1)S(1)}, u32[]{:S(2)}, u32[]{:S(2)}) collective-permute-start(bf16[784,128]{1,0:T(8,128)(2,1)S(1)} %slice.190), channel_id=1, source_target_pairs={{0,2},{2,4},{4,6},{6,7},{7,5},{5,3},{3,1},{1,0},{8,10},{10,12},{12... | collective-permute-start | bytes 602120 | tf_op jit(solution)/shard_map/ppermute | solution.py:227
  43.1 6.6 %collective-permute-start.15 = (bf16[1568,128]{1,0:T(8,128)(2,1)S(1)}, bf16[1568,128]{1,0:T(8,128)(2,1)S(1)}, u32[]{:S(2)}, u32[]{:S(2)}) collective-permute-start(bf16[1568,128]{1,0:T(8,128)(2,1)S(1)} %collective-permute-done.6.rest_6_), channel_id=1, source_target_pairs={{0,8},{8,0},{16,24},{24,16},{1,9},{9,1},{17,25},{25,17},{2,10},{10... | collective-permute-start | bytes 1204232 | tf_op jit(solution)/shard_map/ppermute | solution.py:229
  43.1 7.4 %collective-permute-start.14 = (bf16[1568,128]{1,0:T(8,128)(2,1)S(1)}, bf16[1568,128]{1,0:T(8,128)(2,1)S(1)}, u32[]{:S(2)}, u32[]{:S(2)}) collective-permute-start(bf16[1568,128]{1,0:T(8,128)(2,1)S(1)} %collective-permute-done.5.rest_5_), channel_id=1, source_target_pairs={{0,8},{8,0},{16,24},{24,16},{1,9},{9,1},{17,25},{25,17},{2,10},{10... | collective-permute-start | bytes 1204232 | tf_op jit(solution)/shard_map/ppermute | solution.py:229
  116.5 5.7 %collective-permute-start.18 = (bf16[3136,128]{1,0:T(8,128)(2,1)}, bf16[3136,128]{1,0:T(8,128)(2,1)S(1)}, u32[]{:S(2)}, u32[]{:S(2)}) collective-permute-start(bf16[3136,128]{1,0:T(8,128)(2,1)} %get-tuple-element.38), channel_id=1, source_target_pairs={{0,8},{8,0},{16,24},{24,16},{1,9},{9,1},{17,25},{25,17},{2,10},{10... | collective-permute-start | bytes 2408456 | tf_op jit(solution)/shard_map/ppermute | solution.py:238
  120.6 5.1 %collective-permute-start.25 = (bf16[384,128]{1,0:T(8,128)(2,1)S(1)}, bf16[384,128]{1,0:T(8,128)(2,1)S(1)}, u32[]{:S(2)}, u32[]{:S(2)}) collective-permute-start(bf16[384,128]{1,0:T(8,128)(2,1)S(1)} %add_convert_fusion.7), channel_id=1, source_target_pairs={{0,16},{8,24},{16,0},{24,8},{1,17},{9,25},{17,1},{25,9},{2,18},{10... | collective-permute-start | bytes 294920 | tf_op jit(solution)/shard_map/ppermute | solution.py:232
  122.2 8.6 %collective-permute-start.19 = (bf16[3136,128]{1,0:T(8,128)(2,1)}, bf16[3136,128]{1,0:T(8,128)(2,1)S(1)}, u32[]{:S(2)}, u32[]{:S(2)}) collective-permute-start(bf16[3136,128]{1,0:T(8,128)(2,1)} %get-tuple-element.39), channel_id=1, source_target_pairs={{0,8},{8,0},{16,24},{24,16},{1,9},{9,1},{17,25},{25,17},{2,10},{10... | collective-permute-start | bytes 2408456 | tf_op jit(solution)/shard_map/ppermute | solution.py:238
  126.9 6.4 %collective-permute-start.23 = (bf16[768,128]{1,0:T(8,128)(2,1)S(1)}, bf16[768,128]{1,0:T(8,128)(2,1)S(1)}, u32[]{:S(2)}, u32[]{:S(2)}) collective-permute-start(bf16[768,128]{1,0:T(8,128)(2,1)S(1)} %pad_maximum_fusion.4), channel_id=1, source_target_pairs={{0,16},{8,24},{16,0},{24,8},{1,17},{9,25},{17,1},{25,9},{2,18},{10... | collective-permute-start | bytes 589832 | tf_op jit(solution)/shard_map/ppermute | solution.py:232
  128.5 6.5 %collective-permute-start.26 = (bf16[592,128]{1,0:T(8,128)(2,1)S(1)}, bf16[592,128]{1,0:T(8,128)(2,1)S(1)}, u32[]{:S(2)}, u32[]{:S(2)}) collective-permute-start(bf16[592,128]{1,0:T(8,128)(2,1)S(1)} %get-tuple-element.67), channel_id=1, source_target_pairs={{0,2},{2,4},{4,6},{6,7},{7,5},{5,3},{3,1},{1,0},{8,10},{10,12},{12... | collective-permute-start | bytes 454664 | tf_op jit(solution)/shard_map/ppermute | solution.py:258
  129.1 5.9 %collective-permute-start.30 = (bf16[592,128]{1,0:T(8,128)(2,1)S(1)}, bf16[592,128]{1,0:T(8,128)(2,1)S(1)}, u32[]{:S(2)}, u32[]{:S(2)}) collective-permute-start(bf16[592,128]{1,0:T(8,128)(2,1)S(1)} %get-tuple-element.68), channel_id=1, source_target_pairs={{0,1},{2,0},{4,2},{6,4},{7,6},{5,7},{3,5},{1,3},{8,9},{10,8},{12,1... | collective-permute-start | bytes 454664 | tf_op jit(solution)/shard_map/ppermute | solution.py:259
  130.8 8.4 %collective-permute-start.20 = (bf16[4704,128]{1,0:T(8,128)(2,1)S(1)}, bf16[4704,128]{1,0:T(8,128)(2,1)S(1)}, u32[]{:S(2)}, u32[]{:S(2)}) collective-permute-start(bf16[4704,128]{1,0:T(8,128)(2,1)S(1)} %copy-done.23), channel_id=1, source_target_pairs={{0,8},{8,0},{16,24},{24,16},{1,9},{9,1},{17,25},{25,17},{2,10},{10... | collective-permute-start | bytes 3612680 | tf_op jit(solution)/shard_map/ppermute | solution.py:238
  133.5 5.7 %collective-permute-start.22 = (bf16[768,128]{1,0:T(8,128)(2,1)S(1)}, bf16[768,128]{1,0:T(8,128)(2,1)S(1)}, u32[]{:S(2)}, u32[]{:S(2)}) collective-permute-start(bf16[768,128]{1,0:T(8,128)(2,1)S(1)} %pad_maximum_fusion.3), channel_id=1, source_target_pairs={{0,16},{8,24},{16,0},{24,8},{1,17},{9,25},{17,1},{25,9},{2,18},{10... | collective-permute-start | bytes 589832 | tf_op jit(solution)/shard_map/ppermute | solution.py:232
  135.3 7.5 %collective-permute-start.27 = (bf16[1184,128]{1,0:T(8,128)(2,1)S(1)}, bf16[1184,128]{1,0:T(8,128)(2,1)S(1)}, u32[]{:S(2)}, u32[]{:S(2)}) collective-permute-start(bf16[1184,128]{1,0:T(8,128)(2,1)S(1)} %get-tuple-element.61), channel_id=1, source_target_pairs={{0,2},{2,4},{4,6},{6,7},{7,5},{5,3},{3,1},{1,0},{8,10},{10,12},{12... | collective-permute-start | bytes 909320 | tf_op jit(solution)/shard_map/ppermute | solution.py:265
  136.3 6.8 %collective-permute-start.31 = (bf16[1184,128]{1,0:T(8,128)(2,1)S(1)}, bf16[1184,128]{1,0:T(8,128)(2,1)S(1)}, u32[]{:S(2)}, u32[]{:S(2)}) collective-permute-start(bf16[1184,128]{1,0:T(8,128)(2,1)S(1)} %get-tuple-element.62), channel_id=1, source_target_pairs={{0,1},{2,0},{4,2},{6,4},{7,6},{5,7},{3,5},{1,3},{8,9},{10,8},{12,1... | collective-permute-start | bytes 909320 | tf_op jit(solution)/shard_map/ppermute | solution.py:266
  139.3 6.8 %collective-permute-start.21 = (bf16[1152,128]{1,0:T(8,128)(2,1)S(1)}, bf16[1152,128]{1,0:T(8,128)(2,1)S(1)}, u32[]{:S(2)}, u32[]{:S(2)}) collective-permute-start(bf16[1152,128]{1,0:T(8,128)(2,1)S(1)} %pad_maximum_fusion.1), channel_id=1, source_target_pairs={{0,16},{8,24},{16,0},{24,8},{1,17},{9,25},{17,1},{25,9},{2,18},{10... | collective-permute-start | bytes 884744 | tf_op jit(solution)/shard_map/ppermute | solution.py:232
  143.4 6.9 %collective-permute-start.28 = (bf16[1184,128]{1,0:T(8,128)(2,1)S(1)}, bf16[1184,128]{1,0:T(8,128)(2,1)S(1)}, u32[]{:S(2)}, u32[]{:S(2)}) collective-permute-start(bf16[1184,128]{1,0:T(8,128)(2,1)S(1)} %get-tuple-element.59), channel_id=1, source_target_pairs={{0,2},{2,4},{4,6},{6,7},{7,5},{5,3},{3,1},{1,0},{8,10},{10,12},{12... | collective-permute-start | bytes 909320 | tf_op jit(solution)/shard_map/ppermute | solution.py:265
  145.1 7.0 %collective-permute-start.32 = (bf16[1184,128]{1,0:T(8,128)(2,1)S(1)}, bf16[1184,128]{1,0:T(8,128)(2,1)S(1)}, u32[]{:S(2)}, u32[]{:S(2)}) collective-permute-start(bf16[1184,128]{1,0:T(8,128)(2,1)S(1)} %get-tuple-element.60), channel_id=1, source_target_pairs={{0,1},{2,0},{4,2},{6,4},{7,6},{5,7},{3,5},{1,3},{8,9},{10,8},{12,1... | collective-permute-start | bytes 909320 | tf_op jit(solution)/shard_map/ppermute | solution.py:266
  152.3 6.9 %collective-permute-start.29 = (bf16[1184,128]{1,0:T(8,128)(2,1)S(1)}, bf16[1184,128]{1,0:T(8,128)(2,1)S(1)}, u32[]{:S(2)}, u32[]{:S(2)}) collective-permute-start(bf16[1184,128]{1,0:T(8,128)(2,1)S(1)} %get-tuple-element.54), channel_id=1, source_target_pairs={{0,2},{2,4},{4,6},{6,7},{7,5},{5,3},{3,1},{1,0},{8,10},{10,12},{12... | collective-permute-start | bytes 909320 | tf_op jit(solution)/shard_map/ppermute | solution.py:265
  153.8 6.8 %collective-permute-start.33 = (bf16[1184,128]{1,0:T(8,128)(2,1)S(1)}, bf16[1184,128]{1,0:T(8,128)(2,1)S(1)}, u32[]{:S(2)}, u32[]{:S(2)}) collective-permute-start(bf16[1184,128]{1,0:T(8,128)(2,1)S(1)} %get-tuple-element.55), channel_id=1, source_target_pairs={{0,1},{2,0},{4,2},{6,4},{7,6},{5,7},{3,5},{1,3},{8,9},{10,8},{12,1... | collective-permute-start | bytes 909320 | tf_op jit(solution)/shard_map/ppermute | solution.py:266
  160.8 4.7 %collective-permute-start.34 = (bf16[400,128]{1,0:T(8,128)(2,1)S(1)}, bf16[400,128]{1,0:T(8,128)(2,1)S(1)}, u32[]{:S(2)}, u32[]{:S(2)}) collective-permute-start(bf16[400,128]{1,0:T(8,128)(2,1)S(1)} %slice.250), channel_id=1, source_target_pairs={{0,16},{8,24},{16,0},{24,8},{1,17},{9,25},{17,1},{25,9},{2,18},{10... | collective-permute-start | bytes 307208 | tf_op jit(solution)/shard_map/ppermute | solution.py:272
  (27 other events, 310.4 us)
